TPU v7x, 32 devices: a whole 2x2x4 slice. The times are simulated.
32 devices in a mesh: fsdp: 8 (over z, x), seq: 4 (over y, core).
Axes of the slice: x: 2, y: 2, z: 4, core: 2. Of those that a mesh axis runs over, the one named last changes fastest.
Arguments:
- tokens: bfloat16 [32768, 1024], P(('fsdp', 'seq')), may hold values from -6 to 6
- cotangent: bfloat16 [32768, 1024], P(('fsdp', 'seq')), may hold values from -6 to 6
- query_weight: bfloat16 [1024, 1024], P('fsdp'), may hold values from -0.1875 to 0.1875
- key_weight: bfloat16 [1024, 1024], P('fsdp'), may hold values from -0.1875 to 0.1875
- value_weight: bfloat16 [1024, 1024], P('fsdp'), may hold values from -0.1875 to 0.1875
- output_weight: bfloat16 [1024, 1024], P('fsdp'), may hold values from -6 to 6
- gate_weight: bfloat16 [1024, 2816], P('fsdp'), may hold values from -0.1875 to 0.1875
- up_weight: bfloat16 [1024, 2816], P('fsdp'), may hold values from -0.1875 to 0.1875
- down_weight: bfloat16 [2816, 1024], P(None, 'fsdp'), may hold values from -0.109375 to 0.109375
- attention_gain: bfloat16 [1024], P('fsdp'), may hold values from 0.5 to 1.5
- feedforward_gain: bfloat16 [1024], P('fsdp'), may hold values from 0.5 to 1.5
- cache_keys: bfloat16 [8, 8, 2048, 128], P('fsdp', 'seq'), may hold values from -6 to 6
- cache_values: bfloat16 [8, 8, 2048, 128], P('fsdp', 'seq'), may hold values from -6 to 6
- memory_rows: int32 [8, 8, 32, 128], P('fsdp', 'seq'), may hold values from 0 to 2047
- memory_docs: int32 [8, 8, 32, 128], P('fsdp', 'seq'), may hold values from 0 to 1
Outputs:
- result: bfloat16 [32768, 1024], P(('fsdp', 'seq'))
- grad_tokens: bfloat16 [32768, 1024], P(('fsdp', 'seq'))
- grad_query_weight: float32 [1024, 1024], P('fsdp')
- grad_key_weight: float32 [1024, 1024], P('fsdp')
- grad_value_weight: float32 [1024, 1024], P('fsdp')
- grad_output_weight: float32 [1024, 1024], P('fsdp')
- grad_gate_weight: float32 [1024, 2816], P('fsdp')
- grad_up_weight: float32 [1024, 2816], P('fsdp')
- grad_down_weight: float32 [2816, 1024], P(None, 'fsdp')
- grad_attention_gain: float32 [1024], P('fsdp')
- grad_feedforward_gain: float32 [1024], P('fsdp')
Inputs may be any that keep to these rules, and one draw needn't show every extreme that they name: `memory_rows`: a row of a cache of 2048 rows. `memory_docs`: 0 picks the sequence's own cache, 1 the cache of the sequence before it in the batch (the last sequence for the first).
All inputs are finite; a program needn't handle non-finite values.
Results may differ from a plain program's by a relative error of at most 0.018.
Values may be sent and summed in bfloat16 or wider, within the bound.
No kernel may reach another device: no remote copies, remote signals or barrier semaphores. Data moves between devices by JAX's collectives and lax.ppermute only.
A program may use at most 384 MiB of HBM per device.

v0:
```python
import jax
import jax.numpy as jnp
from jax import lax
from jax.sharding import PartitionSpec as P

epsilon = 1e-06


def from_behind(array, axis, by):
    count = lax.axis_size(axis)
    return lax.ppermute(array, axis, [(i, (i + by) % count) for i in range(count)])


def rms_scale(values, gain_row):
    return (
        values * lax.rsqrt(jnp.mean(values * values, axis=-1, keepdims=True) + epsilon) * gain_row
    )


def rotate(tensor, positions, direction):
    half_dim = tensor.shape[-1] // 2
    frequency = 10000.0 ** (-2.0 * jnp.arange(half_dim, dtype=jnp.float32) / tensor.shape[-1])
    angles = positions.astype(jnp.float32)[:, None] * frequency[None, :]
    cosine = jnp.cos(angles)[:, None, :]
    sine_table = direction * jnp.sin(angles)[:, None, :]
    first_half = tensor[..., :half_dim]
    second_half = tensor[..., half_dim:]
    return jnp.concatenate(
        [
            first_half * cosine - second_half * sine_table,
            second_half * cosine + first_half * sine_table,
        ],
        axis=-1,
    )


def matmul(first_op, second_op):
    return jnp.dot(first_op, second_op, preferred_element_type=jnp.float32)


def inner_rows(first_op, second_op):
    return lax.dot_general(
        first_op, second_op, (((0,), (0,)), ((), ())), preferred_element_type=jnp.float32
    )


def outer_cols(first_op, second_op):
    return lax.dot_general(
        first_op, second_op, (((1,), (1,)), ((), ())), preferred_element_type=jnp.float32
    )


def block_scores(block_index, block_rows, query_heads, key_heads, picked_keys, score_scale):
    head_local = query_heads.shape[1]
    head_dim = query_heads.shape[2]
    mem_block = query_heads.shape[0] // picked_keys.shape[1]
    mem_count = picked_keys.shape[2]
    group_count = block_rows // mem_block
    row_start = block_index * block_rows
    key_end = row_start + block_rows
    query_slab = query_heads[row_start:key_end]
    local_scores = (
        jnp.einsum(
            "qhd,khd->hqk", query_slab, key_heads[:key_end], preferred_element_type=jnp.float32
        )
        * score_scale
    )
    causal = jnp.arange(key_end)[None, :] <= (row_start + jnp.arange(block_rows))[:, None]
    local_scores = jnp.where(causal[None], local_scores, -jnp.inf)
    first_group = block_index * group_count
    grouped = query_slab.reshape(group_count, mem_block, head_local, head_dim)
    memory_keys = picked_keys[:, first_group : first_group + group_count]
    memory_scores = (
        jnp.einsum("bqhd,hbmd->hbqm", grouped, memory_keys, preferred_element_type=jnp.float32)
        * score_scale
    )
    return (query_slab, local_scores, memory_scores.reshape(head_local, block_rows, mem_count))


def body(
    tokens,
    cotangent,
    query_weight,
    key_weight,
    value_weight,
    output_weight,
    gate_weight,
    up_weight,
    down_weight,
    attention_gain,
    feedforward_gain,
    cache_keys,
    cache_values,
    memory_rows,
    memory_docs,
):
    seq_count = lax.axis_size("seq")
    tok_rows, model_width = tokens.shape
    head_local = cache_keys.shape[1]
    rows_cache = cache_keys.shape[2]
    head_dim = cache_keys.shape[3]
    head_count = head_local * seq_count
    seq_len = tok_rows * seq_count
    mem_block = seq_len // memory_rows.shape[2]
    mem_count = memory_rows.shape[3]
    block_rows = min(512, seq_len)
    group_count = block_rows // mem_block
    block_total = seq_len // block_rows
    score_scale = head_dim ** (-0.5)
    positions = lax.axis_index("seq") * tok_rows + jnp.arange(tok_rows, dtype=jnp.int32)
    (
        query_full,
        key_full,
        value_full,
        output_full,
        gate_full,
        up_full,
        down_full,
        gain_one,
        gain_two,
    ) = (
        lax.all_gather(query_weight, "fsdp", axis=0, tiled=True),
        lax.all_gather(key_weight, "fsdp", axis=0, tiled=True),
        lax.all_gather(value_weight, "fsdp", axis=0, tiled=True),
        lax.all_gather(output_weight, "fsdp", axis=0, tiled=True),
        lax.all_gather(gate_weight, "fsdp", axis=0, tiled=True),
        lax.all_gather(up_weight, "fsdp", axis=0, tiled=True),
        lax.all_gather(down_weight, "fsdp", axis=1, tiled=True),
        lax.all_gather(attention_gain, "fsdp", axis=0, tiled=True),
        lax.all_gather(feedforward_gain, "fsdp", axis=0, tiled=True),
    )
    inputs = tokens.astype(jnp.float32)
    normed_one = rms_scale(inputs, gain_one.astype(jnp.float32)).astype(jnp.bfloat16)
    query_lin = matmul(normed_one, query_full).reshape(tok_rows, head_count, head_dim)
    key_lin = matmul(normed_one, key_full).reshape(tok_rows, head_count, head_dim)
    query_tok = rotate(query_lin, positions, 1.0).astype(jnp.bfloat16)
    key_tok = rotate(key_lin, positions, 1.0).astype(jnp.bfloat16)
    value_tok = (
        matmul(normed_one, value_full).astype(jnp.bfloat16).reshape(tok_rows, head_count, head_dim)
    )
    query_heads, key_heads, value_heads = (
        lax.all_to_all(query_tok, "seq", split_axis=1, concat_axis=0, tiled=True),
        lax.all_to_all(key_tok, "seq", split_axis=1, concat_axis=0, tiled=True),
        lax.all_to_all(value_tok, "seq", split_axis=1, concat_axis=0, tiled=True),
    )
    partner_keys, partner_values = from_behind((cache_keys, cache_values), "fsdp", 1)
    chosen_rows = memory_docs[0] * rows_cache + memory_rows[0]
    picker = jax.vmap(lambda source, chosen: source[chosen])
    picked_keys = picker(jnp.concatenate([cache_keys[0], partner_keys[0]], axis=1), chosen_rows)
    picked_values = picker(
        jnp.concatenate([cache_values[0], partner_values[0]], axis=1), chosen_rows
    )
    attended_blocks = []
    log_totals = []
    for block_index in range(block_total):
        key_end = (block_index + 1) * block_rows
        first_group = block_index * group_count
        query_slab, local_scores, memory_scores = block_scores(
            block_index, block_rows, query_heads, key_heads, picked_keys, score_scale
        )
        row_top = jnp.maximum(
            jnp.max(local_scores, axis=-1, keepdims=True),
            jnp.max(memory_scores, axis=-1, keepdims=True),
        )
        local_exp = jnp.exp(local_scores - row_top)
        memory_exp = jnp.exp(memory_scores - row_top)
        row_total = jnp.sum(local_exp, axis=-1, keepdims=True) + jnp.sum(
            memory_exp, axis=-1, keepdims=True
        )
        local_prob = (local_exp / row_total).astype(jnp.bfloat16)
        memory_prob = (
            (memory_exp / row_total)
            .astype(jnp.bfloat16)
            .reshape(head_local, group_count, mem_block, mem_count)
        )
        local_part = jnp.einsum(
            "hqk,khd->qhd", local_prob, value_heads[:key_end], preferred_element_type=jnp.float32
        )
        memory_part = jnp.einsum(
            "hbqm,hbmd->bqhd",
            memory_prob,
            picked_values[:, first_group : first_group + group_count],
            preferred_element_type=jnp.float32,
        )
        attended_blocks.append(
            (local_part + memory_part.reshape(block_rows, head_local, head_dim)).astype(
                jnp.bfloat16
            )
        )
        log_totals.append(row_top + jnp.log(row_total))
    attended_heads = jnp.concatenate(attended_blocks, axis=0)
    attended = lax.all_to_all(
        attended_heads, "seq", split_axis=0, concat_axis=1, tiled=True
    ).reshape(tok_rows, model_width)
    residual = inputs + matmul(attended, output_full)
    normed_two = rms_scale(residual, gain_two.astype(jnp.float32)).astype(jnp.bfloat16)
    gate_lin = matmul(normed_two, gate_full)
    up_lin = matmul(normed_two, up_full)
    hidden = (jax.nn.silu(gate_lin) * up_lin).astype(jnp.bfloat16)
    result = (residual + matmul(hidden, down_full)).astype(jnp.bfloat16)
    (
        query_full,
        key_full,
        value_full,
        output_full,
        gate_full,
        up_full,
        down_full,
        gain_one,
        gain_two,
    ) = (
        lax.all_gather(query_weight, "fsdp", axis=0, tiled=True),
        lax.all_gather(key_weight, "fsdp", axis=0, tiled=True),
        lax.all_gather(value_weight, "fsdp", axis=0, tiled=True),
        lax.all_gather(output_weight, "fsdp", axis=0, tiled=True),
        lax.all_gather(gate_weight, "fsdp", axis=0, tiled=True),
        lax.all_gather(up_weight, "fsdp", axis=0, tiled=True),
        lax.all_gather(down_weight, "fsdp", axis=1, tiled=True),
        lax.all_gather(attention_gain, "fsdp", axis=0, tiled=True),
        lax.all_gather(feedforward_gain, "fsdp", axis=0, tiled=True),
    )
    grad_down = inner_rows(hidden, cotangent)
    grad_hidden = outer_cols(cotangent, down_full)
    _, swiglu_pull = jax.vjp(lambda gate_in, up_in: jax.nn.silu(gate_in) * up_in, gate_lin, up_lin)
    grad_gate, grad_up = swiglu_pull(grad_hidden)
    grad_gate = grad_gate.astype(jnp.bfloat16)
    grad_up = grad_up.astype(jnp.bfloat16)
    grad_gate_w = inner_rows(normed_two, grad_gate)
    grad_up_w = inner_rows(normed_two, grad_up)
    grad_normed_two = outer_cols(grad_gate, gate_full) + outer_cols(grad_up, up_full)
    _, norm_pull_two = jax.vjp(rms_scale, residual, gain_two.astype(jnp.float32))
    grad_resid_norm, grad_gain_two = norm_pull_two(grad_normed_two)
    grad_residual = cotangent.astype(jnp.float32) + grad_resid_norm
    grad_branch = grad_residual.astype(jnp.bfloat16)
    grad_output_w = inner_rows(attended, grad_branch)
    grad_mixed = (
        outer_cols(grad_branch, output_full)
        .astype(jnp.bfloat16)
        .reshape(tok_rows, head_count, head_dim)
    )
    grad_heads = lax.all_to_all(grad_mixed, "seq", split_axis=1, concat_axis=0, tiled=True)
    grad_key_heads = jnp.zeros((seq_len, head_local, head_dim), jnp.float32)
    grad_value_heads = jnp.zeros((seq_len, head_local, head_dim), jnp.float32)
    grad_query_blocks = []
    for block_index in range(block_total):
        row_start = block_index * block_rows
        key_end = row_start + block_rows
        first_group = block_index * group_count
        query_slab, local_scores, memory_scores = block_scores(
            block_index, block_rows, query_heads, key_heads, picked_keys, score_scale
        )
        local_prob = jnp.exp(local_scores - log_totals[block_index])
        memory_prob = jnp.exp(memory_scores - log_totals[block_index])
        grad_slab = grad_heads[row_start:key_end]
        grad_grouped = grad_slab.reshape(group_count, mem_block, head_local, head_dim)
        memory_keys = picked_keys[:, first_group : first_group + group_count]
        memory_values = picked_values[:, first_group : first_group + group_count]
        local_dp = jnp.einsum(
            "qhd,khd->hqk", grad_slab, value_heads[:key_end], preferred_element_type=jnp.float32
        )
        memory_dp = jnp.einsum(
            "bqhd,hbmd->hbqm", grad_grouped, memory_values, preferred_element_type=jnp.float32
        ).reshape(head_local, block_rows, mem_count)
        row_delta = jnp.sum(local_prob * local_dp, axis=-1, keepdims=True) + jnp.sum(
            memory_prob * memory_dp, axis=-1, keepdims=True
        )
        local_ds = (local_prob * (local_dp - row_delta)).astype(jnp.bfloat16)
        memory_ds = (
            (memory_prob * (memory_dp - row_delta))
            .astype(jnp.bfloat16)
            .reshape(head_local, group_count, mem_block, mem_count)
        )
        local_grad_q = jnp.einsum(
            "hqk,khd->qhd", local_ds, key_heads[:key_end], preferred_element_type=jnp.float32
        )
        memory_grad_q = jnp.einsum(
            "hbqm,hbmd->bqhd", memory_ds, memory_keys, preferred_element_type=jnp.float32
        ).reshape(block_rows, head_local, head_dim)
        grad_query_blocks.append((local_grad_q + memory_grad_q) * score_scale)
        grad_key_heads = grad_key_heads.at[:key_end].add(
            jnp.einsum("hqk,qhd->khd", local_ds, query_slab, preferred_element_type=jnp.float32)
            * score_scale
        )
        grad_value_heads = grad_value_heads.at[:key_end].add(
            jnp.einsum(
                "hqk,qhd->khd",
                local_prob.astype(jnp.bfloat16),
                grad_slab,
                preferred_element_type=jnp.float32,
            )
        )
    grad_query_heads = jnp.concatenate(grad_query_blocks, axis=0)
    back_query, back_key, back_value = (
        lax.all_to_all(
            grad_query_heads.astype(jnp.bfloat16), "seq", split_axis=0, concat_axis=1, tiled=True
        ),
        lax.all_to_all(
            grad_key_heads.astype(jnp.bfloat16), "seq", split_axis=0, concat_axis=1, tiled=True
        ),
        lax.all_to_all(
            grad_value_heads.astype(jnp.bfloat16), "seq", split_axis=0, concat_axis=1, tiled=True
        ),
    )
    grad_query_lin = (
        rotate(back_query.astype(jnp.float32), positions, -1.0)
        .astype(jnp.bfloat16)
        .reshape(tok_rows, model_width)
    )
    grad_key_lin = (
        rotate(back_key.astype(jnp.float32), positions, -1.0)
        .astype(jnp.bfloat16)
        .reshape(tok_rows, model_width)
    )
    grad_value_lin = back_value.reshape(tok_rows, model_width)
    grad_query_w = inner_rows(normed_one, grad_query_lin)
    grad_key_w = inner_rows(normed_one, grad_key_lin)
    grad_value_w = inner_rows(normed_one, grad_value_lin)
    grad_normed_one = (
        outer_cols(grad_query_lin, query_full)
        + outer_cols(grad_key_lin, key_full)
        + outer_cols(grad_value_lin, value_full)
    )
    _, norm_pull_one = jax.vjp(rms_scale, inputs, gain_one.astype(jnp.float32))
    grad_norm_input, grad_gain_one = norm_pull_one(grad_normed_one)
    grad_tokens = (grad_residual + grad_norm_input).astype(jnp.bfloat16)
    shards = (
        lax.psum_scatter(grad_query_w, "fsdp", scatter_dimension=0, tiled=True),
        lax.psum_scatter(grad_key_w, "fsdp", scatter_dimension=0, tiled=True),
        lax.psum_scatter(grad_value_w, "fsdp", scatter_dimension=0, tiled=True),
        lax.psum_scatter(grad_output_w, "fsdp", scatter_dimension=0, tiled=True),
        lax.psum_scatter(grad_gate_w, "fsdp", scatter_dimension=0, tiled=True),
        lax.psum_scatter(grad_up_w, "fsdp", scatter_dimension=0, tiled=True),
        lax.psum_scatter(grad_down, "fsdp", scatter_dimension=1, tiled=True),
        lax.psum_scatter(grad_gain_one, "fsdp", scatter_dimension=0, tiled=True),
        lax.psum_scatter(grad_gain_two, "fsdp", scatter_dimension=0, tiled=True),
    )
    summed = (
        lax.psum(shards[0].astype(jnp.bfloat16), "seq").astype(jnp.float32),
        lax.psum(shards[1].astype(jnp.bfloat16), "seq").astype(jnp.float32),
        lax.psum(shards[2].astype(jnp.bfloat16), "seq").astype(jnp.float32),
        lax.psum(shards[3].astype(jnp.bfloat16), "seq").astype(jnp.float32),
        lax.psum(shards[4].astype(jnp.bfloat16), "seq").astype(jnp.float32),
        lax.psum(shards[5].astype(jnp.bfloat16), "seq").astype(jnp.float32),
        lax.psum(shards[6].astype(jnp.bfloat16), "seq").astype(jnp.float32),
        lax.psum(shards[7].astype(jnp.bfloat16), "seq").astype(jnp.float32),
        lax.psum(shards[8].astype(jnp.bfloat16), "seq").astype(jnp.float32),
    )
    return (
        result,
        grad_tokens,
        summed[0],
        summed[1],
        summed[2],
        summed[3],
        summed[4],
        summed[5],
        summed[6],
        summed[7],
        summed[8],
    )


def solution(mesh):
    return jax.shard_map(
        body,
        mesh=mesh,
        in_specs=(
            P(("fsdp", "seq"), None),
            P(("fsdp", "seq"), None),
            P("fsdp", None),
            P("fsdp", None),
            P("fsdp", None),
            P("fsdp", None),
            P("fsdp", None),
            P("fsdp", None),
            P(None, "fsdp"),
            P("fsdp"),
            P("fsdp"),
            P("fsdp", "seq", None, None),
            P("fsdp", "seq", None, None),
            P("fsdp", "seq", None, None),
            P("fsdp", "seq", None, None),
        ),
        out_specs=(
            P(("fsdp", "seq"), None),
            P(("fsdp", "seq"), None),
            P("fsdp", None),
            P("fsdp", None),
            P("fsdp", None),
            P("fsdp", None),
            P("fsdp", None),
            P("fsdp", None),
            P(None, "fsdp"),
            P("fsdp"),
            P("fsdp"),
        ),
        check_vma=False,
    )
```

profile of v0, /device:TPU:0, one launch (start us, length us, event | category | flops | bytes accessed | tf_op | source)
XLA Modules:
  0.0 1995.7 jit_solution(10573619585289918737)
XLA Ops:
  18.7 78.8 %all-gather = bf16[8,1,128]{2,1,0:T(2,128)(2,1)S(1)} all-gather(bf16[1,1,128]{2,1,0:T(2,128)(2,1)S(1)} %bitcast.823), channel_id=1, replica_groups=mesh['fsdp'=8,'seq'=4] {'fsdp'}, dimensions={0}, use_global_device_ids=true | all-gather | bytes 2304 | tf_op jit(solution)/shard_map/all_gather | solution.py:129
  105.8 6.1 fusion.362
  112.0 24.4 %all-gather.12.cloned.1.call-done = bf16[1024,1024]{1,0:T(8,128)(2,1)} async-done(((bf16[128,1024]{1,0:T(8,128)(2,1)}), bf16[1024,1024]{1,0:T(8,128)(2,1)}) %all-gather.12.cloned.1.call-update) | async-done | bytes 2097168 | tf_op jit(solution)/shard_map/all_gather | solution.py:122
  152.2 34.1 %all-gather.10.cloned.1.call-done = bf16[1024,1024]{1,0:T(8,128)(2,1)} async-done(((bf16[128,1024]{1,0:T(8,128)(2,1)}), bf16[1024,1024]{1,0:T(8,128)(2,1)}) %all-gather.10.cloned.1.call-update) | async-done | bytes 2097168 | tf_op jit(solution)/shard_map/all_gather | solution.py:124
  203.1 18.0 all-to-all-done
  228.1 80.6 %gather_fusion.1 = bf16[8192,128]{1,0:T(8,128)(2,1)} fusion(bf16[2,4096,128]{2,1,0:T(8,128)(2,1)S(1)} %pad_maximum_fusion.3, s32[8192]{0:T(1024)S(1)} %bitcast.582), kind=kCustom, calls=%fused_computation.1 | custom fusion | bytes 4259840 | tf_op jit(solution)/shard_map/vmap()/gather | solution.py:148
  310.1 80.4 %gather_fusion = bf16[8192,128]{1,0:T(8,128)(2,1)} fusion(bf16[2,4096,128]{2,1,0:T(8,128)(2,1)S(1)} %pad_maximum_fusion.2, s32[8192]{0:T(1024)S(1)} %bitcast.583), kind=kCustom, calls=%fused_computation | custom fusion | bytes 4259840 | tf_op jit(solution)/shard_map/vmap()/gather | solution.py:148
  439.2 5.6 fusion.375
  456.1 6.8 fusion.377
  476.6 8.1 fusion.379
  484.8 5.6 fusion.10
  498.1 7.1 fusion.381
  505.2 6.4 fusion.8
  520.3 10.5 fusion.383
  530.9 7.2 fusion.1
  543.2 11.8 fusion.385
  555.1 8.4 fusion
  583.4 7.0 fusion.225
  590.4 7.8 fusion.227
  603.0 6.3 copy.395
  613.8 17.5 all-gather.1
  655.2 11.5 fusion.387
  666.8 12.1 fusion.388
  678.8 21.9 %multiply_convert_fusion.3 = (bf16[1024,2816]{1,0:T(8,128)(2,1)}, bf16[1024,2816]{1,0:T(8,128)(2,1)}, bf16[1024,2816]{1,0:T(8,128)(2,1)}) fusion(f32[1024,2816]{1,0:T(8,128)} %fusion.387, f32[1024,2816]{1,0:T(8,128)} %fusion.388, bf16[1024,1024]{1,0:T(8,128)(2,1)S(1)} %copy-done.75, bf16[2816,1024]{1,0:T(8,128)(2,1)} %all-gather.22.cloned.1.call-done), kind=kOutput, calls=%fused_computation.27 | convolution fusion | flops 5951717376 | bytes 48234496 | tf_op jit(solution)/shard_map/dot_general | solution.py:48
  700.8 10.0 fusion.389
  710.9 7.2 multiply_reduce_fusion.6
  731.2 6.0 fusion.236
  737.2 16.5 all-to-all-done.4
  776.9 6.9 multiply_reduce_fusion.5
  786.6 6.9 multiply_reduce_fusion.4
  796.3 8.2 multiply_reduce_fusion.3
  806.7 9.2 multiply_reduce_fusion.2
  818.7 10.5 multiply_reduce_fusion.1
  831.9 12.1 multiply_reduce_fusion
  866.5 9.2 multiply_convert_fusion.5
  879.7 7.3 multiply_convert_fusion.2
  889.7 11.6 multiply_convert_fusion.1
  906.7 8.4 multiply_convert_fusion
  922.3 6.2 copy.461
  988.7 6.2 copy.450
  1003.5 7.2 copy.462
  1010.8 13.4 all-to-all-done.5
  1027.6 7.3 copy.451
  1047.4 5.9 fusion.358
  1063.1 5.8 fusion.111
  1078.4 9.8 fusion.90
  1088.1 11.0 fusion.41
  1099.2 6.1 fusion.52
  1105.3 6.2 copy.474
  1111.5 29.5 %all_to_all.120 = bf16[4096,2,128]{2,1,0:T(2,128)(2,1)S(1)} all-to-all(bf16[4096,2,128]{2,1,0:T(2,128)(2,1)} %copy.474), channel_id=1, replica_groups=mesh['fsdp'=8,'seq'=4] {'seq'}, dimensions={0} | all-to-all | bytes 4194304 | tf_op jit(solution)/shard_map/all_to_all | solution.py:300
  1146.7 5.9 fusion.356
  1152.7 11.9 fusion.390
  1164.8 11.8 fusion.391
  1176.7 12.1 fusion.392
  1190.7 11.5 add_convert_fusion
  1206.1 6.7 fusion.393
  1226.2 90.0 %reduce-scatter.12.cloned.1.call-done = f32[128,1024]{1,0:T(8,128)} async-done(((f32[1024,1024]{1,0:T(8,128)}), f32[128,1024]{1,0:T(8,128)}) %reduce-scatter.12.cloned.1.call-update) | async-done | bytes 524304 | tf_op jit(solution)/shard_map/reduce_scatter | solution.py:329
  1318.0 194.1 %reduce-scatter.16.cloned.1.call-done = f32[128,2816]{1,0:T(8,128)} async-done(((f32[1024,2816]{1,0:T(8,128)}), f32[128,2816]{1,0:T(8,128)}) %reduce-scatter.16.cloned.1.call-update) | async-done | bytes 1441808 | tf_op jit(solution)/shard_map/reduce_scatter | solution.py:331
  1514.4 193.1 %reduce-scatter.18.cloned.1.call-done = f32[128,2816]{1,0:T(8,128)} async-done(((f32[1024,2816]{1,0:T(8,128)}), f32[128,2816]{1,0:T(8,128)}) %reduce-scatter.18.cloned.1.call-update) | async-done | bytes 1441808 | tf_op jit(solution)/shard_map/reduce_scatter | solution.py:332
  1709.7 193.4 %reduce-scatter.20.cloned.1.call-done = f32[2816,128]{1,0:T(8,128)} async-done(((f32[2816,1024]{1,0:T(8,128)}), f32[2816,128]{1,0:T(8,128)}) %reduce-scatter.20.cloned.1.call-update) | async-done | bytes 1441808 | tf_op jit(solution)/shard_map/reduce_scatter | solution.py:333
  1905.5 7.9 fusion.59
  1919.8 19.7 all-reduce.4
  1939.6 5.6 all-reduce.5
  1946.3 30.5 %all-reduce.9.cloned.1.call-done = (bf16[128,1024]{1,0:T(8,128)(2,1)}, bf16[128,1024]{1,0:T(8,128)(2,1)}, bf16[128,1024]{1,0:T(8,128)(2,1)}, bf16[128,1024]{1,0:...) async-done(((bf16[128,1024]{1,0:T(8,128)(2,1)}, bf16[128,1024]{1,0:T(8,128)(2,1)}, bf16[128,1024]{1,0:T(8,128)(2,1)}, ...) | async-done | bytes 3211280 | tf_op jit(solution)/shard_map/psum | solution.py:338
  (723 shorter events, 455.6 us)
Async XLA Ops:
  7.2 11.5 copy-start.142
  7.2 98.7 %all-gather.14.cloned.1.call-start = ((), (), s32[]{:S(2)}) async-start(), calls=%async_computation.17 | async-start | bytes 2359296 | tf_op jit(solution)/shard_map/all_gather | solution.py:123
  7.9 128.4 %all-gather.12.cloned.1.call-start = ((), (), s32[]{:S(2)}) async-start(), calls=%async_computation.16 | async-start | bytes 2359296 | tf_op jit(solution)/shard_map/all_gather | solution.py:122
  8.7 177.6 %all-gather.10.cloned.1.call-start = ((), (), s32[]{:S(2)}) async-start(), calls=%async_computation.15 | async-start | bytes 2359296 | tf_op jit(solution)/shard_map/all_gather | solution.py:124
  9.4 637.3 %all-gather.16.cloned.1.call-start = ((), (), s32[]{:S(2)}) async-start(), calls=%async_computation.18 | async-start | bytes 2359296 | tf_op jit(solution)/shard_map/all_gather | solution.py:125
  10.0 643.9 %all-gather.18.cloned.1.call-start = ((), (), s32[]{:S(2)}) async-start(), calls=%async_computation.19 | async-start | bytes 6488064 | tf_op jit(solution)/shard_map/all_gather | solution.py:126
  10.6 656.2 %all-gather.20.cloned.1.call-start = ((), (), s32[]{:S(2)}) async-start(), calls=%async_computation.20 | async-start | bytes 6488064 | tf_op jit(solution)/shard_map/all_gather | solution.py:127
  11.1 667.7 %all-gather.22.cloned.1.call-start = ((), (), s32[]{:S(2)}) async-start(), calls=%async_computation.21 | async-start | bytes 6488064 | tf_op jit(solution)/shard_map/all_gather | solution.py:128
  11.2 215.6 %collective-permute-start.1 = (bf16[1,2,2048,128]{3,2,1,0:T(8,128)(2,1)}, bf16[1,2,2048,128]{3,2,1,0:T(8,128)(2,1)}, u32[]{:S(2)}, u32[]{:S(2)}) collective-permute-start(bf16[1,2,2048,128]{3,2,1,0:T(8,128)(2,1)} %param.63), channel_id=1, source_target_pairs={{0,4},{4,8},{8,12},{12,16},{16,20},{20,24},{24,28},{28,0},{1,5},{5... | collective-permute-start | bytes 3145736 | tf_op jit(solution)/shard_map/ppermute | solution.py:11
  14.2 294.5 %collective-permute-start = (bf16[1,2,2048,128]{3,2,1,0:T(8,128)(2,1)}, bf16[1,2,2048,128]{3,2,1,0:T(8,128)(2,1)}, u32[]{:S(2)}, u32[]{:S(2)}) collective-permute-start(bf16[1,2,2048,128]{3,2,1,0:T(8,128)(2,1)} %param.62), channel_id=1, source_target_pairs={{0,4},{4,8},{8,12},{12,16},{16,20},{20,24},{24,28},{28,0},{1,5},{5... | collective-permute-start | bytes 3145736 | tf_op jit(solution)/shard_map/ppermute | solution.py:11
  15.8 88.2 %copy-start.134 = (s32[1,2,32,128]{3,2,1,0:T(8,128)S(1)}, s32[1,2,32,128]{3,2,1,0:T(8,128)}, u32[]{:S(2)}) copy-start(s32[1,2,32,128]{3,2,1,0:T(8,128)} %param.64) | copy-start | bytes 98308
  15.8 88.2 %copy-start.135 = (s32[1,2,32,128]{3,2,1,0:T(8,128)S(1)}, s32[1,2,32,128]{3,2,1,0:T(8,128)}, u32[]{:S(2)}) copy-start(s32[1,2,32,128]{3,2,1,0:T(8,128)} %param.65) | copy-start | bytes 98308
  18.7 167.6 %copy-start.6 = (bf16[1024,1024]{0,1:T(8,128)(2,1)}, bf16[1024,1024]{0,1:T(8,128)(2,1)S(1)}, u32[]{:S(2)}) copy-start(bf16[1024,1024]{0,1:T(8,128)(2,1)S(1)} %copy.359) | copy-start | bytes 6291460
  97.6 88.7 %copy-start.113 = (f32[8,1,128]{2,1,0:T(1,128)}, f32[8,1,128]{2,1,0:T(1,128)S(1)}, u32[]{:S(2)}) copy-start(f32[8,1,128]{2,1,0:T(1,128)S(1)} %convert_element_type.410) | copy-start | bytes 12292
  98.0 13.9 copy-start.132
  98.1 88.2 %copy-start.119 = (f32[1024]{0:T(1024)}, f32[1024]{0:T(1024)S(1)}, u32[]{:S(2)}) copy-start(f32[1024]{0:T(1024)S(1)} %fusion.295) | copy-start | bytes 12292
  105.8 34.8 %copy-start.65 = (f32[1024,64]{0,1:T(8,128)}, f32[1024,64]{0,1:T(8,128)S(1)}, u32[]{:S(2)}) copy-start(f32[1024,64]{0,1:T(8,128)S(1)} %get-tuple-element.359) | copy-start | bytes 786436
  144.5 47.3 %all-to-all-start.2 = ((bf16[1024,8,128]{0,2,1:T(8,128)(2,1)}), bf16[1024,8,128]{0,2,1:T(8,128)(2,1)}, u32[]{:S(2)}, u32[]{:S(2)}) async-start(bf16[1024,8,128]{0,2,1:T(8,128)(2,1)} %pad_maximum_fusion.1), calls=%async_computation.2 | async-start | bytes 4194304 | tf_op jit(solution)/shard_map/all_to_all | solution.py:143
  191.8 29.3 %all-to-all-start = ((bf16[1024,8,128]{0,2,1:T(8,128)(2,1)}), bf16[1024,8,128]{0,2,1:T(8,128)(2,1)S(1)}, u32[]{:S(2)}, u32[]{:S(2)}) async-start(bf16[1024,8,128]{0,2,1:T(8,128)(2,1)} %bitcast.717), calls=%async_computation | async-start | bytes 4194304 | tf_op jit(solution)/shard_map/all_to_all | solution.py:144
  203.1 23.7 %copy-start.91 = (bf16[1,2,2048,128]{3,2,1,0:T(8,128)(2,1)S(1)}, bf16[1,2,2048,128]{3,2,1,0:T(8,128)(2,1)}, u32[]{:S(2)}) copy-start(bf16[1,2,2048,128]{3,2,1,0:T(8,128)(2,1)} %param.63) | copy-start | bytes 3145732
  221.1 183.4 %all-to-all-start.1 = ((bf16[1024,8,128]{0,2,1:T(8,128)(2,1)}), bf16[1024,8,128]{0,2,1:T(8,128)(2,1)}, u32[]{:S(2)}, u32[]{:S(2)}) async-start(bf16[1024,8,128]{0,2,1:T(8,128)(2,1)} %pad_maximum_fusion), calls=%async_computation.1 | async-start | bytes 4194304 | tf_op jit(solution)/shard_map/all_to_all | solution.py:142
  228.1 80.6 %copy-start.92 = (bf16[1,2,2048,128]{3,2,1,0:T(8,128)(2,1)S(1)}, bf16[1,2,2048,128]{3,2,1,0:T(8,128)(2,1)}, u32[]{:S(2)}) copy-start(bf16[1,2,2048,128]{3,2,1,0:T(8,128)(2,1)} %param.62) | copy-start | bytes 3145732
  414.6 153.6 %copy-start.13 = (f32[2,512,512]{1,2,0:T(8,128)}, f32[2,512,512]{1,2,0:T(8,128)S(1)}, u32[]{:S(2)}) copy-start(f32[2,512,512]{1,2,0:T(8,128)S(1)} %get-tuple-element.361) | copy-start | bytes 6291460
  454.6 14.1 copy-start.41
  476.6 14.5 copy-start.44
  496.3 16.0 copy-start.47
  520.3 18.5 copy-start.50
  543.2 21.0 %copy-start.53 = (f32[2,4,128,128]{2,3,1,0:T(8,128)}, f32[2,4,128,128]{2,3,1,0:T(8,128)S(1)}, u32[]{:S(2)}) copy-start(f32[2,4,128,128]{2,3,1,0:T(8,128)S(1)} %get-tuple-element.391) | copy-start | bytes 1572868
  583.4 14.8 slice-start
  583.4 14.8 slice-start.1
  603.0 28.3 %copy-start.74 = (bf16[1024,1024]{1,0:T(8,128)(2,1)S(1)}, bf16[1024,1024]{1,0:T(8,128)(2,1)}, u32[]{:S(2)}) copy-start(bf16[1024,1024]{1,0:T(8,128)(2,1)} %param.52) | copy-start | bytes 6291460
  609.3 30.2 %all-to-all-start.3 = ((bf16[4096,2,128]{2,1,0:T(2,128)(2,1)}), bf16[4096,2,128]{2,1,0:T(2,128)(2,1)}, u32[]{:S(2)}, u32[]{:S(2)}) async-start(bf16[4096,2,128]{2,1,0:T(2,128)(2,1)} %copy.395), calls=%async_computation.3 | async-start | bytes 4194304 | tf_op jit(solution)/shard_map/all_to_all | solution.py:192
  634.3 12.3 copy-start.7
  666.8 12.1 copy-start.75
  723.4 30.4 %all-to-all-start.4 = ((bf16[1024,8,128]{0,2,1:T(8,128)(2,1)}), bf16[1024,8,128]{0,2,1:T(8,128)(2,1)}, u32[]{:S(2)}, u32[]{:S(2)}) async-start(bf16[1024,8,128]{0,2,1:T(8,128)(2,1)} %bitcast.716), calls=%async_computation.4 | async-start | bytes 4194304 | tf_op jit(solution)/shard_map/all_to_all | solution.py:241
  728.0 489.2 %reduce-scatter.14.cloned.1.call-start = ((), (), s32[]{:S(2)}) async-start(), calls=%async_computation.25 | async-start | bytes 4718592 | tf_op jit(solution)/shard_map/reduce_scatter | solution.py:330
  756.9 75.0 %copy-start.11 = (bf16[1024,4,2,128]{3,0,1,2:T(8,128)(2,1)}, bf16[1024,4,2,128]{3,0,1,2:T(8,128)(2,1)S(1)}, u32[]{:S(2)}) copy-start(bf16[1024,4,2,128]{3,0,1,2:T(8,128)(2,1)S(1)} %copy.402) | copy-start | bytes 6291460
  769.9 77.0 %copy-start.60 = (f32[512,2,128]{0,2,1:T(8,128)}, f32[512,2,128]{0,2,1:T(8,128)S(1)}, u32[]{:S(2)}) copy-start(f32[512,2,128]{0,2,1:T(8,128)S(1)} %fusion.148) | copy-start | bytes 1572868
  806.7 11.9 copy-start.112
  818.7 13.2 copy-start.118
  831.9 12.8 copy-start.54
  831.9 12.8 copy-start.131
  865.2 14.5 slice-start.12
  866.5 13.2 slice-start.13
  866.5 13.2 slice-start.14
  889.7 15.4 slice-start.4
  889.7 15.4 slice-start.5
  889.7 15.4 slice-start.6
  922.3 11.1 copy-start.70
  928.5 66.4 %all-to-all-start.6 = ((bf16[4096,2,128]{2,1,0:T(2,128)(2,1)}), bf16[4096,2,128]{2,1,0:T(2,128)(2,1)}, u32[]{:S(2)}, u32[]{:S(2)}) async-start(bf16[4096,2,128]{2,1,0:T(2,128)(2,1)} %copy.461), calls=%async_computation.6 | async-start | bytes 4194304 | tf_op jit(solution)/shard_map/all_to_all | solution.py:297
  950.4 23.0 %slice-start.40 = ((s8[5242880]{0:T(1024)(128)(4,1)}), s8[1048576]{0:T(1024)(128)(4,1)S(1)}, s32[]{:S(2)}) async-start(s8[5242880]{0:T(1024)(128)(4,1)} %bitcast.614), calls=%async_computation.70 | async-start | bytes 2097152
  957.5 16.0 copy-start.67
  961.9 11.5 slice-start.41
  994.9 29.3 %all-to-all-start.5 = ((bf16[4096,2,128]{2,1,0:T(2,128)(2,1)}), bf16[4096,2,128]{2,1,0:T(2,128)(2,1)S(1)}, u32[]{:S(2)}, u32[]{:S(2)}) async-start(bf16[4096,2,128]{2,1,0:T(2,128)(2,1)} %copy.450), calls=%async_computation.5 | async-start | bytes 4194304 | tf_op jit(solution)/shard_map/all_to_all | solution.py:294
  998.5 220.5 %reduce-scatter.8.cloned.1.call-start = ((), (), s32[]{:S(2)}) async-start(), calls=%async_computation.22 | async-start | bytes 4718592 | tf_op jit(solution)/shard_map/reduce_scatter | solution.py:327
  1047.4 177.0 %reduce-scatter.10.cloned.1.call-start = ((), (), s32[]{:S(2)}) async-start(), calls=%async_computation.23 | async-start | bytes 4718592 | tf_op jit(solution)/shard_map/reduce_scatter | solution.py:328
  1053.4 262.8 %reduce-scatter.12.cloned.1.call-start = ((), (), s32[]{:S(2)}) async-start(), calls=%async_computation.24 | async-start | bytes 4718592 | tf_op jit(solution)/shard_map/reduce_scatter | solution.py:329
  1054.0 14.9 slice-start.28
  1078.4 20.8 %slice-start.8 = ((s8[16777216]{0:T(1024)(128)(4,1)}), s8[4194304]{0:T(1024)(128)(4,1)S(1)}, s32[]{:S(2)}) async-start(s8[16777216]{0:T(1024)(128)(4,1)} %bitcast.588), calls=%async_computation.38 | async-start | bytes 8388608
  1078.4 20.8 %slice-start.9 = ((s8[16777216]{0:T(1024)(128)(4,1)}), s8[4194304]{0:T(1024)(128)(4,1)S(1)}, s32[]{:S(2)}) async-start(s8[16777216]{0:T(1024)(128)(4,1)} %bitcast.588), calls=%async_computation.39 | async-start | bytes 8388608
  1152.7 359.4 %reduce-scatter.16.cloned.1.call-start = ((), (), s32[]{:S(2)}) async-start(), calls=%async_computation.26 | async-start | bytes 12976128 | tf_op jit(solution)/shard_map/reduce_scatter | solution.py:331
  1164.7 542.7 %reduce-scatter.18.cloned.1.call-start = ((), (), s32[]{:S(2)}) async-start(), calls=%async_computation.27 | async-start | bytes 12976128 | tf_op jit(solution)/shard_map/reduce_scatter | solution.py:332
  1176.6 726.5 %reduce-scatter.20.cloned.1.call-start = ((), (), s32[]{:S(2)}) async-start(), calls=%async_computation.28 | async-start | bytes 12976128 | tf_op jit(solution)/shard_map/reduce_scatter | solution.py:333
  1188.8 788.0 %all-reduce.9.cloned.1.call-start = ((), (), s32[]{:S(2)}) async-start(), calls=%async_computation.29 | async-start | bytes 6422528 | tf_op jit(solution)/shard_map/psum | solution.py:338
  (151 other events, 936.5 us)
Sparse Core Ops, SparseCore 0:
  10.1 70.3 all-gather.13
  82.6 53.6 all-gather.11
  138.5 47.7 all-gather.9
  188.3 47.7 all-gather.15
  238.1 91.1 all-gather.17
  331.3 90.8 all-gather.19
  424.2 91.7 all-gather.21
  737.4 87.0 reduce-scatter.13
  1047.5 85.5 reduce-scatter.7
  1136.6 87.7 reduce-scatter.9
  1228.5 87.6 reduce-scatter.11
  1319.6 192.3 reduce-scatter.15
  1515.6 191.7 reduce-scatter.17
  1710.9 192.1 reduce-scatter.19
  1907.0 69.7 all-reduce.8
where the time goes:
time: 2010 us; the launch traced here: 2000 us
  waiting for transfers between devices  820 us (41%)
  matrix products  464 us (23%)
  local copies, waits for them, and re-layouts  332 us (17%)
  other arithmetic  176 us (9%)
  blocking collectives  151 us (8%)
  starting transfers between devices  35.9 us (2%)
    reduce_scatter x1, waiting for transfers between devices, body(): lax.psum_scatter(grad_gate_w, 'fsdp', scatter_dimension=0, tiled=True)  194 us
    reduce_scatter x1, waiting for transfers between devices, body(): lax.psum_scatter(grad_down, 'fsdp', scatter_dimension=1, tiled=True)  193 us
    reduce_scatter x1, waiting for transfers between devices, body(): lax.psum_scatter(grad_up_w, 'fsdp', scatter_dimension=0, tiled=True)  193 us
    gather x2, local copies, waits for them, and re-layouts, body(): picker = jax.vmap(lambda source, chosen: source[chosen])  161 us
    reduce_scatter x1, waiting for transfers between devices, body(): lax.psum_scatter(grad_value_w, 'fsdp', scatter_dimension=0, tiled=True)  90 us
    all_gather x1, blocking collectives, body(): lax.all_gather(attention_gain, 'fsdp', axis=0, tiled=True)  78.8 us
    dot_general x7, matrix products, outer_cols(): lax.dot_general(first_op, second_op, (((1,), (1,)), ((), ())), preferred_...  61.9 us
    dot_general x8, matrix products, body(): jnp.einsum('qhd,khd->hqk', grad_slab, value_heads[:key_end], preferred_el...  60.8 us
  transfers between devices with their start and end apart: 24, of which 12 were waited for; matrix products, arithmetic and copies ran while one was open for 44% of the time, Pallas kernels for 0%

commit v1 on v0

v1 whole, which is shorter than its diff:
```python
import functools

import jax
import jax.numpy as jnp
from jax import lax
from jax.experimental import pallas as pl
from jax.experimental.pallas import tpu as pltpu
from jax.sharding import PartitionSpec as P

epsilon = 1e-06
log2e = 1.4426950408889634
f32 = jnp.float32
bf16 = jnp.bfloat16
VMEM_LIMIT = 60 * 1024 * 1024


def dot(a, b):
    return jnp.dot(a, b, preferred_element_type=f32)


def dot_nt(a, b):
    return lax.dot_general(a, b, (((1,), (1,)), ((), ())), preferred_element_type=f32)


def dot_tn(a, b):
    return lax.dot_general(a, b, (((0,), (0,)), ((), ())), preferred_element_type=f32)


def call(kernel, grid, in_specs, out_specs, out_shape, flops, bytes_accessed, scratch=(), prefetch=0):
    return pl.pallas_call(
        kernel,
        grid_spec=pltpu.PrefetchScalarGridSpec(
            num_scalar_prefetch=prefetch,
            grid=grid,
            in_specs=in_specs,
            out_specs=out_specs,
            scratch_shapes=list(scratch),
        ),
        out_shape=out_shape,
        compiler_params=pltpu.CompilerParams(
            dimension_semantics=("arbitrary",) * len(grid), vmem_limit_bytes=VMEM_LIMIT
        ),
        cost_estimate=pl.CostEstimate(
            flops=int(flops), bytes_accessed=int(bytes_accessed), transcendentals=0
        ),
    )


def resident(shape, index):
    return pl.BlockSpec(shape, lambda *_: index, pipeline_mode=pl.Buffered(1))


def struct(shape, dtype):
    return jax.ShapeDtypeStruct(shape, dtype)


def swap_seq(array, bit):
    count = lax.axis_size("seq")
    return lax.ppermute(array, "seq", [(i, i ^ bit) for i in range(count)])


def spread(array, axis):
    count = lax.axis_size(axis)
    copies = jnp.broadcast_to(array[None], (count,) + array.shape)
    return lax.all_to_all(copies, axis, split_axis=0, concat_axis=0, tiled=True)


def project(order, pieces, weights, gain_row, cosine, sine, head_local, head_dim):
    rows, width = pieces[0].shape
    count = len(pieces)
    block = min(256, rows)
    steps = rows // block
    length = rows * count
    cols = weights.shape[1]
    group = head_local * head_dim

    def kernel(order_ref, *refs):
        xs = refs[:count]
        w_ref, g_ref, c_ref, s_ref, q_ref, k_ref, v_ref, nt_ref = refs[count:]
        slot = pl.program_id(0)

        def run(x_ref):
            x = x_ref[...].astype(f32)
            scale = lax.rsqrt(jnp.mean(x * x, axis=-1, keepdims=True) + epsilon)
            normed = (x * scale * g_ref[...]).astype(bf16)
            nt_ref[...] = normed.T
            lin = dot(normed, w_ref[...])
            cos, sin = c_ref[...], s_ref[...]
            for head in range(head_local):
                for part, out in ((0, q_ref), (1, k_ref)):
                    start = part * group + head * head_dim
                    u = lin[:, start : start + head_dim]
                    out[head] = (u * cos + pltpu.roll(u, head_dim // 2, 1) * sin).astype(bf16)
                start = 2 * group + head * head_dim
                v_ref[head] = lin[:, start : start + head_dim].astype(bf16)

        for k in range(count):
            pl.when(slot == k)(functools.partial(run, xs[k]))

    def piece_spec(k):
        return pl.BlockSpec(
            (block, width),
            lambda slot, i, order_ref: (
                jnp.where(slot == k, i, jnp.where(slot < k, 0, steps - 1)),
                0,
            ),
        )

    def at_rows(slot, i, order_ref):
        return order_ref[slot] * steps + i

    head_spec = pl.BlockSpec((head_local, block, head_dim), lambda *a: (0, at_rows(*a), 0))
    table_spec = pl.BlockSpec((block, head_dim), lambda *a: (at_rows(*a), 0))
    heads = struct((head_local, length, head_dim), bf16)
    return call(
        kernel,
        (count, steps),
        [piece_spec(k) for k in range(count)]
        + [resident((width, cols), (0, 0)), resident((1, width), (0, 0)), table_spec, table_spec],
        [head_spec, head_spec, head_spec, pl.BlockSpec((width, block), lambda *a: (0, at_rows(*a)))],
        [heads, heads, heads, struct((width, length), bf16)],
        2 * length * width * cols,
        4 * length * width + 2 * length * cols + 8 * length * head_dim,
        prefetch=1,
    )(order, *pieces, weights, gain_row, cosine, sine)


def retrieve(chosen, keys, values, base, before=None):
    head_local, rows_cache, head_dim = keys.shape
    blocks, slots = chosen.shape[1:]
    per = min(4, blocks)
    total = blocks * slots

    def kernel(c_ref, k_ref, v_ref, *refs):
        if before is not None:
            bk_ref, bv_ref = refs[:2]
        ok_ref, ov_ref, table, mask = refs[-4:]

        @pl.when(pl.program_id(1) == 0)
        def _():
            table[:, :head_dim] = k_ref[0]
            table[:, head_dim:] = v_ref[0]

        for b in range(per):
            row = c_ref[0, 0, b : b + 1, :] - base
            column = jnp.broadcast_to(row, (slots, slots)).T
            lane = lax.broadcasted_iota(jnp.int32, (slots, slots), 1)
            for start in range(0, rows_cache, slots):
                mask[b * slots : (b + 1) * slots, start : start + slots] = jnp.where(
                    column == lane + start, 1.0, 0.0
                ).astype(bf16)
        picked = dot(mask[...], table[...])
        if before is not None:
            picked_keys = picked[:, :head_dim] + bk_ref[0].astype(f32)
            picked_values = picked[:, head_dim:] + bv_ref[0].astype(f32)
        else:
            picked_keys, picked_values = picked[:, :head_dim], picked[:, head_dim:]
        ok_ref[0] = picked_keys.astype(bf16)
        ov_ref[0] = picked_values.astype(bf16)

    out_spec = pl.BlockSpec((1, per * slots, head_dim), lambda h, i: (h, i, 0))
    table_spec = pl.BlockSpec((1, rows_cache, head_dim), lambda h, i: (h, 0, 0))
    extra = () if before is None else before
    out = struct((head_local, total, head_dim), bf16)
    return call(
        kernel,
        (head_local, blocks // per),
        [pl.BlockSpec((1, 1, per, slots), lambda h, i: (h, i, 0, 0)), table_spec, table_spec]
        + [out_spec] * len(extra),
        [out_spec, out_spec],
        [out, out],
        4 * head_local * total * rows_cache * head_dim,
        8 * head_local * total * head_dim,
        scratch=[
            pltpu.VMEM((rows_cache, 2 * head_dim), bf16),
            pltpu.VMEM((per * slots, rows_cache), bf16),
        ],
    )(chosen.reshape(head_local, blocks // per, per, slots), keys, values, *extra)


def attend(query, key, value, memory_keys, memory_values, mem_block, mem_count):
    head_local, length, head_dim = query.shape
    block = min(512, length)
    count = length // block
    groups = block // mem_block
    factor = head_dim ** (-0.5) * log2e

    def kernel(q_ref, k_ref, v_ref, mk_ref, mv_ref, o_ref, lse_ref):
        index = pl.program_id(0)
        row = lax.broadcasted_iota(jnp.int32, (block, block), 0)
        col = lax.broadcasted_iota(jnp.int32, (block, block), 1)

        def memory(head):
            parts = []
            for g in range(groups):
                q = q_ref[head, g * mem_block : (g + 1) * mem_block, :]
                parts.append(dot_nt(q, mk_ref[head, g * mem_count : (g + 1) * mem_count, :]))
            scores = jnp.concatenate(parts, axis=0) * factor
            top = jnp.max(scores, axis=-1, keepdims=True)
            weight = jnp.exp2(scores - top)
            total = jnp.sum(weight, axis=-1, keepdims=True)
            weight = weight.astype(bf16)
            mixed = jnp.concatenate(
                [
                    dot(
                        weight[g * mem_block : (g + 1) * mem_block],
                        mv_ref[head, g * mem_count : (g + 1) * mem_count, :],
                    )
                    for g in range(groups)
                ],
                axis=0,
            )
            return top, total, mixed

        def step(head, carry, start, masked):
            top, total, mixed = carry
            scores = dot_nt(q_ref[head], k_ref[head, pl.ds(start, block), :]) * factor
            if masked:
                scores = jnp.where(col <= row, scores, -jnp.inf)
            new_top = jnp.maximum(top, jnp.max(scores, axis=-1, keepdims=True))
            decay = jnp.exp2(top - new_top)
            weight = jnp.exp2(scores - new_top)
            total = total * decay + jnp.sum(weight, axis=-1, keepdims=True)
            mixed = mixed * decay + dot(weight.astype(bf16), v_ref[head, pl.ds(start, block), :])
            return new_top, total, mixed

        def both(carries, start, masked):
            return tuple(step(head, carries[head], start, masked) for head in range(head_local))

        carries = tuple(memory(head) for head in range(head_local))
        carries = lax.fori_loop(
            0, index, lambda j, c: both(c, pl.multiple_of(j * block, block), False), carries
        )
        carries = both(carries, pl.multiple_of(index * block, block), True)
        for head, (top, total, mixed) in enumerate(carries):
            o_ref[:, head * head_dim : (head + 1) * head_dim] = (mixed / total).astype(bf16)
            lse = jnp.broadcast_to(top + jnp.log2(total), (block, head_dim))
            lse_ref[0, head : head + 1, :] = lse.T[0:1, :]

    full = resident((head_local, length, head_dim), (0, 0, 0))
    rows = pl.BlockSpec((head_local, block, head_dim), lambda i: (0, i, 0))
    mem_rows = pl.BlockSpec((head_local, groups * mem_count, head_dim), lambda i: (0, i, 0))
    return call(
        kernel,
        (count,),
        [rows, full, full, mem_rows, mem_rows],
        [
            pl.BlockSpec((block, head_local * head_dim), lambda i: (i, 0)),
            pl.BlockSpec((1, 8, block), lambda i: (i, 0, 0)),
        ],
        [struct((length, head_local * head_dim), bf16), struct((count, 8, block), f32)],
        4 * head_local * length * length * head_dim,
        12 * head_local * length * head_dim,
    )(query, key, value, memory_keys, memory_values)


def attend_back(
    query, key, value, memory_keys, memory_values, mem_block, mem_count, grad, attended, lse, cosine, sine
):
    head_local, length, head_dim = query.shape
    count, _, block = lse.shape
    groups = block // mem_block
    scale = head_dim ** (-0.5)
    factor = scale * log2e

    def kernel(
        q_ref, k_ref, v_ref, mk_ref, mv_ref, do_ref, o_ref, lse_ref, c_ref, s_ref,
        dq_ref, dk_ref, dv_ref, dq_acc, delta,
    ):
        index = pl.program_id(0)

        def cols(head):
            return slice(head * head_dim, (head + 1) * head_dim)

        @pl.when(index == 0)
        def _():
            def prepare(i, _):
                start = pl.multiple_of(i * block, block)
                for head in range(head_local):
                    do = do_ref[pl.ds(start, block), cols(head)]
                    o = o_ref[pl.ds(start, block), cols(head)]
                    row = jnp.sum((do.astype(f32) * o.astype(f32)).T, axis=0, keepdims=True)
                    delta[i, head : head + 1, :] = row
                    lse_row = lse_ref[i, head : head + 1, :]
                    q = q_ref[head, pl.ds(start, block), :]
                    mem_start = pl.multiple_of(i * (groups * mem_count), groups * mem_count)
                    for g in range(groups):
                        lanes = slice(g * mem_block, (g + 1) * mem_block)
                        mk = mk_ref[head, pl.ds(mem_start + g * mem_count, mem_count), :]
                        mv = mv_ref[head, pl.ds(mem_start + g * mem_count, mem_count), :]
                        weight = jnp.exp2(dot_nt(mk, q[lanes]) * factor - lse_row[:, lanes])
                        dp = dot_nt(mv, do[lanes])
                        ds = (weight * (dp - row[:, lanes])).astype(bf16)
                        dq_acc[head, pl.ds(start + g * mem_block, mem_block), :] = dot_tn(ds, mk)
                return 0

            lax.fori_loop(0, count, prepare, 0)

        row_id = lax.broadcasted_iota(jnp.int32, (block, block), 0)
        col_id = lax.broadcasted_iota(jnp.int32, (block, block), 1)

        def step(head, carry, i, masked):
            dk, dv = carry
            start = pl.multiple_of(i * block, block)
            q = q_ref[head, pl.ds(start, block), :]
            do = do_ref[pl.ds(start, block), cols(head)]
            k, v = k_ref[head], v_ref[head]
            weight = jnp.exp2(dot_nt(k, q) * factor - lse_ref[i, head : head + 1, :])
            if masked:
                weight = jnp.where(row_id <= col_id, weight, 0.0)
            dp = dot_nt(v, do)
            ds = (weight * (dp - delta[i, head : head + 1, :])).astype(bf16)
            dv = dv + dot(weight.astype(bf16), do)
            dk = dk + dot(ds, q)
            dq_acc[head, pl.ds(start, block), :] += dot_tn(ds, k)
            return dk, dv

        def both(carries, i, masked):
            return tuple(step(head, carries[head], i, masked) for head in range(head_local))

        zero = jnp.zeros((block, head_dim), f32)
        carries = both(tuple((zero, zero) for _ in range(head_local)), index, True)
        carries = lax.fori_loop(index + 1, count, lambda i, c: both(c, i, False), carries)
        cos, sin = c_ref[...], s_ref[...]

        def unrotate(grad_rows):
            u = (grad_rows * scale).astype(bf16).astype(f32)
            return (u * cos - pltpu.roll(u, head_dim // 2, 1) * sin).astype(bf16)

        for head, (dk, dv) in enumerate(carries):
            start = pl.multiple_of(index * block, block)
            dq_ref[:, cols(head)] = unrotate(dq_acc[head, pl.ds(start, block), :])
            dk_ref[:, cols(head)] = unrotate(dk)
            dv_ref[:, cols(head)] = dv.astype(bf16)

    group = head_local * head_dim
    full = resident((head_local, length, head_dim), (0, 0, 0))
    mem_full = resident(memory_keys.shape, (0, 0, 0))
    flat = resident((length, group), (0, 0))
    rows = pl.BlockSpec((head_local, block, head_dim), lambda i: (0, i, 0))
    table = pl.BlockSpec((block, head_dim), lambda i: (i, 0))
    out_rows = pl.BlockSpec((block, group), lambda i: (i, 0))
    out = struct((length, group), bf16)
    return call(
        kernel,
        (count,),
        [full, rows, rows, mem_full, mem_full, flat, flat, resident(lse.shape, (0, 0, 0)), table, table],
        [out_rows, out_rows, out_rows],
        [out, out, out],
        10 * head_local * length * length * head_dim // 2,
        24 * head_local * length * head_dim,
        scratch=[
            pltpu.VMEM((head_local, length, head_dim), f32),
            pltpu.VMEM((count, 8, block), f32),
        ],
    )(query, key, value, memory_keys, memory_values, grad, attended, lse, cosine, sine)


def mix(attended, weights, tokens, gain_row):
    count, rows, group = attended.shape
    width = tokens.shape[1]
    block = min(256, rows)

    def kernel(a_ref, w_ref, x_ref, g_ref, res_ref, n_ref, nt_ref, at_ref):
        total = x_ref[...].astype(f32)
        mixed = dot(a_ref[0], w_ref[0:group, :])
        for k in range(1, count):
            mixed = mixed + dot(a_ref[k], w_ref[k * group : (k + 1) * group, :])
        for k in range(count):
            at_ref[k * group : (k + 1) * group, :] = a_ref[k].T
        residual = total + mixed
        scale = lax.rsqrt(jnp.mean(residual * residual, axis=-1, keepdims=True) + epsilon)
        normed = (residual * scale * g_ref[...]).astype(bf16)
        res_ref[...] = residual
        n_ref[...] = normed
        nt_ref[...] = normed.T

    rows_spec = pl.BlockSpec((block, width), lambda i: (i, 0))
    cols_spec = pl.BlockSpec((width, block), lambda i: (0, i))
    return call(
        kernel,
        (rows // block,),
        [
            pl.BlockSpec((count, block, group), lambda i: (0, i, 0)),
            resident((count * group, width), (0, 0)),
            rows_spec,
            resident((1, width), (0, 0)),
        ],
        [rows_spec, rows_spec, cols_spec, cols_spec],
        [struct((rows, width), f32), struct((rows, width), bf16)]
        + [struct((width, rows), bf16)] * 2,
        2 * rows * width * width,
        16 * rows * width,
    )(attended, weights, tokens, gain_row)


def gated(normed, cotangent, weights, first, hidden_cols):
    rows, width = normed.shape
    block = 256

    def kernel(n_ref, c_ref, wg_ref, wu_ref, wd_ref, h_ref, gg_ref, gu_ref):
        normed_block = n_ref[...]
        gate = dot(normed_block, wg_ref[...])
        up = dot(normed_block, wu_ref[...])
        grad = dot(c_ref[...], wd_ref[...])
        sg = 1.0 / (1.0 + jnp.exp(-gate))
        silu = gate * sg
        h_ref[...] = (silu * up).astype(bf16)
        gg_ref[...] = (grad * up * sg * (1.0 + gate * (1.0 - sg))).astype(bf16)
        gu_ref[...] = (grad * silu).astype(bf16)

    def weight_spec(k):
        offset = (first + k * hidden_cols) // block
        return pl.BlockSpec((width, block), lambda i: (0, i + offset))

    flat = resident((rows, width), (0, 0))
    out_spec = pl.BlockSpec((rows, block), lambda i: (0, i))
    return call(
        kernel,
        (hidden_cols // block,),
        [flat, flat] + [weight_spec(k) for k in range(3)],
        [out_spec] * 3,
        [struct((rows, hidden_cols), bf16)] * 3,
        6 * rows * width * hidden_cols,
        6 * (rows + width) * hidden_cols,
    )(normed, cotangent, weights, weights, weights)


def norm_back(grads, weight_arrays, parts, wo, residual, cotangent, gain_row, count):
    rows, width = residual.shape
    block = min(256, rows)
    steps = width // block
    row_steps = rows // block
    group = width // count
    n_grads = len(grads)

    def kernel(*refs):
        g_refs, w_refs = refs[:n_grads], refs[n_grads : 2 * n_grads]
        wo_ref, r_ref, c_ref, gain_ref, gres_ref, gb_ref, gm_ref, gg_ref, acc = refs[2 * n_grads :]
        step = pl.program_id(0)

        @pl.when(step < steps)
        def _():
            total = dot_nt(g_refs[0][...], w_refs[0][...])
            for k in range(1, n_grads):
                total = total + dot_nt(g_refs[k][...], w_refs[k][...])
            for d in range(steps):
                @pl.when(step == d)
                def _():
                    acc[:, d * block : (d + 1) * block] = total

        @pl.when(step >= steps)
        def _():
            start = pl.multiple_of((step - steps) * block, block)
            grad = acc[pl.ds(start, block), :]
            res = r_ref[...]
            scale = lax.rsqrt(jnp.mean(res * res, axis=-1, keepdims=True) + epsilon)
            unit = res * scale
            scaled = grad * gain_ref[...]
            inner = jnp.mean(scaled * unit, axis=-1, keepdims=True)
            gres = c_ref[...].astype(f32) + scale * (scaled - unit * inner)
            gres_ref[...] = gres
            branch = gres.astype(bf16)
            gb_ref[...] = branch
            for k in range(count):
                gm_ref[k] = dot_nt(branch, wo_ref[k * group : (k + 1) * group, :]).astype(bf16)
            partial = jnp.sum(grad * unit, axis=0, keepdims=True)

            @pl.when(step == steps)
            def _():
                gg_ref[...] = partial

            @pl.when(step > steps)
            def _():
                gg_ref[...] += partial

    def row(i):
        return jnp.maximum(i - steps, 0)

    rows_spec = pl.BlockSpec((block, width), lambda i: (row(i), 0))
    weight_specs = [
        pl.BlockSpec(
            (block, grads[k].shape[1]),
            functools.partial(lambda c, i: (jnp.minimum(i, steps - 1), c), parts[k][1]),
        )
        for k in range(n_grads)
    ]
    hidden_cols = sum(g.shape[1] for g in grads)
    return call(
        kernel,
        (steps + row_steps,),
        [resident(g.shape, (0, 0)) for g in grads]
        + weight_specs
        + [resident((width, width), (0, 0)), rows_spec, rows_spec, resident((1, width), (0, 0))],
        [
            rows_spec,
            rows_spec,
            pl.BlockSpec((count, block, group), lambda i: (0, row(i), 0)),
            pl.BlockSpec((1, width), lambda i: (0, 0)),
        ],
        [
            struct((rows, width), f32),
            struct((rows, width), bf16),
            struct((count, rows, group), bf16),
            struct((1, width), f32),
        ],
        2 * rows * width * hidden_cols + 2 * rows * width * width,
        2 * (rows + width) * hidden_cols + 16 * rows * width,
        scratch=[pltpu.VMEM((rows, width), f32)],
    )(*grads, *[weight_arrays[p[0]] for p in parts], wo, residual, cotangent, gain_row)


def products(lefts, rights, pairs, block=256):
    height = lefts[0].shape[0]
    sizes = [rights[r].shape[1] // block for _, r in pairs]
    firsts = [sum(sizes[:k]) for k in range(len(pairs))]

    def kernel(*refs):
        l_refs, r_refs, out = refs[: len(lefts)], refs[len(lefts) : -1], refs[-1]
        step = pl.program_id(0)
        for k, (l, _) in enumerate(pairs):
            @pl.when((step >= firsts[k]) & (step < firsts[k] + sizes[k]))
            def _():
                out[...] = dot(l_refs[l][...], r_refs[k][...]).astype(bf16)

    def right_spec(k):
        return pl.BlockSpec(
            (rights[pairs[k][1]].shape[0], block),
            lambda i: (0, jnp.clip(i - firsts[k], 0, sizes[k] - 1)),
        )

    width = block * sum(sizes)
    return call(
        kernel,
        (sum(sizes),),
        [resident(a.shape, (0, 0)) for a in lefts] + [right_spec(k) for k in range(len(pairs))],
        pl.BlockSpec((height, block), lambda i: (0, i)),
        struct((height, width), bf16),
        sum(2 * height * lefts[l].shape[1] * rights[r].shape[1] for l, r in pairs),
        2 * height * width,
    )(*lefts, *[rights[r] for _, r in pairs])


def project_back(order, slot, grads, weights):
    length, group = grads[0].shape
    width = weights.shape[0]
    rows = length // order.shape[0]
    block = min(256, rows)
    steps = rows // block

    def kernel(order_ref, a_ref, b_ref, c_ref, w_ref, out_ref):
        total = dot_nt(a_ref[...], w_ref[:, :group])
        total = total + dot_nt(b_ref[...], w_ref[:, group : 2 * group])
        total = total + dot_nt(c_ref[...], w_ref[:, 2 * group :])
        out_ref[...] = total.astype(bf16)

    rows_spec = pl.BlockSpec((block, group), lambda i, order_ref: (order_ref[slot] * steps + i, 0))
    return call(
        kernel,
        (steps,),
        [rows_spec] * 3 + [resident(weights.shape, (0, 0))],
        pl.BlockSpec((block, width), lambda i, order_ref: (i, 0)),
        struct((rows, width), bf16),
        6 * rows * width * group,
        2 * rows * (width + 3 * group),
        prefetch=1,
    )(order, *grads, weights)


def body(
    tokens, cotangent, query_weight, key_weight, value_weight, output_weight, gate_weight, up_weight,
    down_weight, attention_gain, feedforward_gain, cache_keys, cache_values, memory_rows, memory_docs,
):
    seq_count, fsdp_count = lax.axis_size("seq"), lax.axis_size("fsdp")
    here = lax.axis_index("seq")
    tok_rows, width = tokens.shape
    head_local, rows_cache, head_dim = cache_keys.shape[1:]
    group = head_local * head_dim
    length = tok_rows * seq_count
    mem_block = length // memory_rows.shape[2]
    mem_count = memory_rows.shape[3]
    shard = query_weight.shape[0]
    hidden_cols = gate_weight.shape[1]
    order = here ^ jnp.arange(seq_count, dtype=jnp.int32)

    gains = spread(jnp.stack([attention_gain, feedforward_gain]), "fsdp")
    gains = gains.transpose(1, 0, 2).reshape(2, width).astype(f32)
    gain_one, gain_two = gains[0:1], gains[1:2]
    own_cols = [
        lax.dynamic_slice_in_dim(w, here * group, group, axis=1)
        for w in (query_weight, key_weight, value_weight)
    ]
    qkv = spread(jnp.concatenate(own_cols, axis=1), "fsdp").reshape(width, 3 * group)

    pieces = [tokens, swap_seq(tokens, 1), swap_seq(tokens, 2)]
    pieces.append(swap_seq(pieces[2], 1))

    ring = [(i, (i + 1) % fsdp_count) for i in range(fsdp_count)]
    partner_keys = lax.ppermute(cache_keys[0], "fsdp", ring)
    partner_values = lax.ppermute(cache_values[0], "fsdp", ring)

    part = shard // seq_count
    split_a = 1024

    def own_rows(w):
        return lax.dynamic_slice_in_dim(w, here * part, part, axis=0)

    own_wo, own_wg, own_wu = own_rows(output_weight), own_rows(gate_weight), own_rows(up_weight)
    own_wd = lax.dynamic_slice_in_dim(down_weight, here * part, part, axis=1).T
    first_part = jnp.concatenate(
        [own_wo, own_wg[:, :split_a], own_wu[:, :split_a], own_wd[:, :split_a]], axis=1
    )
    second_part = jnp.concatenate(
        [own_wg[:, split_a:], own_wu[:, split_a:], own_wd[:, split_a:]], axis=1
    )
    both_axes = ("fsdp", "seq")
    big_a = lax.all_gather(first_part, both_axes, axis=0, tiled=True)
    big_b = lax.all_gather(second_part, both_axes, axis=0, tiled=True)
    rest = hidden_cols - split_a

    half = head_dim // 2
    frequency = 10000.0 ** (-2.0 * jnp.arange(half, dtype=f32) / head_dim)
    angles = jnp.arange(length, dtype=jnp.int32).astype(f32)[:, None] * frequency[None, :]
    cos_half, sin_half = jnp.cos(angles), jnp.sin(angles)
    cosine = jnp.concatenate([cos_half, cos_half], axis=1)
    sine = jnp.concatenate([-sin_half, sin_half], axis=1)
    cotangent_t = cotangent.T

    chosen = memory_docs[0] * rows_cache + memory_rows[0]
    picked = retrieve(chosen, cache_keys[0], cache_values[0], 0)
    query, key, value, normed_one_t = project(
        order, pieces, qkv, gain_one, cosine, sine, head_local, head_dim
    )
    picked_keys, picked_values = retrieve(chosen, partner_keys, partner_values, rows_cache, picked)
    attended_heads, lse = attend(
        query, key, value, picked_keys, picked_values, mem_block, mem_count
    )
    attended = lax.all_to_all(
        attended_heads.reshape(seq_count, tok_rows, group), "seq", 0, 0, tiled=True
    )
    residual, normed_two, normed_two_t, attended_t = mix(attended, big_a, tokens, gain_two)
    hid_a, gg_a, gu_a = gated(normed_two, cotangent, big_a, width, split_a)
    hid_b, gg_b, gu_b = gated(normed_two, cotangent, big_b, 0, rest)
    offset = width // split_a
    grad_residual, grad_branch, grad_mixed, grad_gain_two = norm_back(
        [gg_a, gu_a, gg_b, gu_b],
        [big_a, big_b],
        [(0, offset), (0, offset + 1), (1, 0), (1, 1)],
        big_a,
        residual,
        cotangent,
        gain_two,
        seq_count,
    )
    grad_heads = lax.all_to_all(grad_mixed, "seq", 0, 0, tiled=True).reshape(length, group)

    gate_up = products([normed_two_t], [gg_a, gg_b, gu_a, gu_b], [(0, 0), (0, 1), (0, 2), (0, 3)])
    down_out = products(
        [cotangent_t, attended_t], [hid_a, hid_b, grad_branch], [(0, 0), (0, 1), (1, 2)]
    )
    gain_cols = jnp.broadcast_to(grad_gain_two.T, (width, 128)).astype(bf16)
    down_out = jnp.concatenate([down_out, gain_cols], axis=1)
    gate_up = lax.psum_scatter(gate_up, both_axes, scatter_dimension=0, tiled=True)
    down_out = lax.psum_scatter(down_out, both_axes, scatter_dimension=0, tiled=True)

    wd_a = big_a[:, width + 2 * split_a :]
    wd_b = big_b[:, 2 * rest :]
    result = (residual + dot_nt(hid_a, wd_a) + dot_nt(hid_b, wd_b)).astype(bf16)

    dq, dk, dv = attend_back(
        query, key, value, picked_keys, picked_values, mem_block, mem_count,
        grad_heads, attended_heads, lse, cosine, sine,
    )
    grads = (dq, dk, dv)
    near = swap_seq(project_back(order, 1, grads, qkv), 1)
    far = swap_seq(project_back(order, 3, grads, qkv), 1)
    across = project_back(order, 2, grads, qkv).astype(f32) + far.astype(f32)
    across = swap_seq(across.astype(bf16), 2)
    own = project_back(order, 0, grads, qkv).astype(f32) + near.astype(f32)
    qkv_grad = products([normed_one_t], list(grads), [(0, 0), (0, 1), (0, 2)])
    grad_normed_one = own + across.astype(f32)

    inputs = tokens.astype(f32)
    scale = lax.rsqrt(jnp.mean(inputs * inputs, axis=-1, keepdims=True) + epsilon)
    unit = inputs * scale
    scaled = grad_normed_one * gain_one
    inner = jnp.mean(scaled * unit, axis=-1, keepdims=True)
    grad_tokens = (grad_residual + scale * (scaled - unit * inner)).astype(bf16)
    grad_gain_one = jnp.sum(grad_normed_one * unit, axis=0)

    def over_fsdp(array):
        moved = lax.all_to_all(
            array.reshape(fsdp_count, shard, array.shape[1]), "fsdp", 0, 0, tiled=True
        )
        return jnp.sum(moved.astype(f32), axis=0)

    qkv_sum = over_fsdp(qkv_grad).astype(bf16)
    qkv_all = spread(qkv_sum, "seq").astype(f32)
    grad_q, grad_k, grad_v = (
        qkv_all[:, :, k * group : (k + 1) * group].transpose(1, 0, 2).reshape(shard, width)
        for k in range(3)
    )
    gain_sum = over_fsdp(jnp.broadcast_to(grad_gain_one[:, None], (width, 128)).astype(bf16))
    gain_one_all = jnp.sum(spread(gain_sum.astype(bf16), "seq").astype(f32), axis=0)[:, 0]

    gate_up = spread(gate_up, "seq").reshape(shard, -1).astype(f32)
    down_out = spread(down_out, "seq").reshape(shard, -1).astype(f32)
    return (
        result,
        grad_tokens,
        grad_q,
        grad_k,
        grad_v,
        down_out[:, hidden_cols : hidden_cols + width],
        gate_up[:, :hidden_cols],
        gate_up[:, hidden_cols:],
        down_out[:, :hidden_cols].T,
        gain_one_all,
        down_out[:, hidden_cols + width],
    )


def solution(mesh):
    tok, row, col, one = P(("fsdp", "seq"), None), P("fsdp", None), P(None, "fsdp"), P("fsdp")
    cache = P("fsdp", "seq", None, None)
    return jax.shard_map(
        body,
        mesh=mesh,
        in_specs=(tok, tok) + (row,) * 6 + (col, one, one) + (cache,) * 4,
        out_specs=(tok, tok) + (row,) * 6 + (col, one, one),
        check_vma=False,
    )
```

time: 2010 us -> 750 us (0.37)
  waiting for transfers between devices: 820 us -> 171 us
  matrix products: 464 us -> 16 us
  Pallas kernels: 0 us -> 340 us
  local copies, waits for them, and re-layouts: 332 us -> 37.9 us
  other arithmetic: 176 us -> 48.7 us
  blocking collectives: 151 us -> 53.9 us
  starting transfers between devices: 35.9 us -> 61.8 us
    reduce_scatter x7 -> x2, waiting for transfers between devices: 674 us -> 0.01 us  [the longest x1 0.01 us: body(): lax.psum_scatter(down_out, both_axes, scatter_dimension=0, tiled=True)]
    dot_general x101 -> x2, matrix products: 464 us -> 16 us  [dot_nt(): lax.dot_general(a, b, (((1,), (1,)), ((), ())), preferred_element_type=f32)]
    pallas_call x0 -> x16, Pallas kernels: none -> 340 us  [the longest x1 83 us: attend_back(): call(kernel, (count,), [full, rows, rows, mem_full, mem_full, flat, flat,...]
    gather x2 -> x0, local copies, waits for them, and re-layouts: 161 us -> none  [body(): picker = jax.vmap(lambda source, chosen: source[chosen])]
    all_gather x2 -> x0, blocking collectives: 96.3 us -> none  [the longest x1 78.8 us: body(): lax.all_gather(attention_gain, 'fsdp', axis=0, tiled=True)]
    ppermute x2 -> x8, waiting for transfers between devices: 0.01 us -> 82.9 us  [the longest x6 82.9 us: swap_seq(): return lax.ppermute(array, 'seq', [(i, i ^ bit) for i in range(count)])]
    convert_element_type x31 -> x7, other arithmetic: 89 us -> 13.8 us  [the longest x1 5.94 us: body(): grad_tokens = (grad_residual + scale * (scaled - unit * inner)).astype(bf16)]
    all_gather x7 -> x2, waiting for transfers between devices: 58.5 us -> 0.01 us  [the longest x1 0.01 us: body(): big_a = lax.all_gather(first_part, both_axes, axis=0, tiled=True)]
  transfers between devices with their start and end apart: 24 -> 21, of which waited for: 12 -> 8; matrix products, arithmetic and copies ran while one was open for 44% -> 11% of each run, Pallas kernels for 0% -> 37%
where the time goes in v1:
time: 750 us; the launch traced here: 743 us
  Pallas kernels  340 us (45%)
  waiting for transfers between devices  171 us (23%)
  starting transfers between devices  61.8 us (8%)
  blocking collectives  53.9 us (7%)
  other arithmetic  48.7 us (6%)
  local copies, waits for them, and re-layouts  37.9 us (5%)
  matrix products  16 us (2%)
  between operations  14.3 us (2%)
    pallas_call x1, Pallas kernels, attend_back(): call(kernel, (count,), [full, rows, rows, mem_full, mem_full, flat, flat,...  83 us
    ppermute x6, waiting for transfers between devices, swap_seq(): return lax.ppermute(array, 'seq', [(i, i ^ bit) for i in range(count)])  82.9 us
    pallas_call x3, Pallas kernels, products(): call(kernel, (sum(sizes),), [resident(a.shape, (0, 0)) for a in lefts] +...  55.6 us
    all_to_all x1, blocking collectives, body(): lax.all_to_all(grad_mixed, 'seq', 0, 0, tiled=True).reshape(length, group)  53.9 us
    pallas_call x1, Pallas kernels, attend(): call(kernel, (count,), [rows, full, full, mem_rows, mem_rows], [pl.BlockS...  53.4 us
    all_to_all x1, waiting for transfers between devices, body(): lax.all_to_all(attended_heads.reshape(seq_count, tok_rows, group), 'seq',...  38.4 us
    all_to_all x6, waiting for transfers between devices, spread(): return lax.all_to_all(copies, axis, split_axis=0, concat_axis=0, tiled=True)  36.5 us
    pallas_call x2, Pallas kernels, retrieve(): call(kernel, (head_local, blocks // per), [pl.BlockSpec((1, 1, per, slots...  35.7 us
  transfers between devices with their start and end apart: 21, of which 8 were waited for; matrix products, arithmetic and copies ran while one was open for 11% of the time, Pallas kernels for 37%

profile of v1, /device:TPU:0, one launch (start us, length us, event | category | flops | bytes accessed | tf_op | source)
XLA Modules:
  0.0 743.4 jit_solution(16646952191671902378)
XLA Ops:
  7.2 1.0 copy-done
  14.0 3.0 collective-permute-start.1
  17.7 5.8 all-to-all-start.1
  23.5 2.0 collective-permute-start.3
  25.5 1.5 collective-permute-start.4
  28.7 9.8 %fusion.16 = (f32[4096,64]{1,0:T(8,128)}, f32[4096,64]{1,0:T(8,128)}, f32[4096,64]{1,0:T(8,128)}) fusion(f32[64]{0:T(128)S(1)} %multiply_power_fusion, f32[4096]{0:T(1024)S(1)} %iota_convert_fusion), kind=kLoop, calls=%fused_computation.27 | loop fusion | flops 524288 | bytes 3162368 | tf_op jit(solution)/shard_map/neg | solution.py:626
  38.6 1.3 broadcast_in_dim.16
  39.8 4.7 all-to-all-start
  45.2 23.4 %collective-permute-done.1.refs_2_ = bf16[1024,1024]{1,0:T(8,128)(2,1)} collective-permute-done((bf16[1024,1024]{1,0:T(8,128)(2,1)}, bf16[1024,1024]{1,0:T(8,128)(2,1)}, u32[]{:S(2)}, u32[]{:S(2)}) %collective-permute-start.1) | collective-permute-done | bytes 2097184 | tf_op jit(solution)/shard_map/ppermute | solution.py:59
  68.7 17.2 %shard_map.231 = (bf16[2,4096,128]{2,1,0:T(8,128)(2,1)}, bf16[2,4096,128]{2,1,0:T(8,128)(2,1)}) custom-call(s32[2,8,4,128]{3,2,1,0:T(4,128)} %bitcast.56, bf16[2,2048,128]{2,1,0:T(8,128)(2,1)} %bitcast.59, bf16[2,2048,128]{2,1,0:T(8,128)(2,1)} %bitcast.7.v_ref), custom_call_target="tpu_custom_call" | custom-call | flops 8589934592 | bytes 8388608 | tf_op jit(solution)/shard_map/pallas_call | solution.py:165
  86.4 6.7 pad_maximum_fusion.1
  93.7 18.5 %shard_map.232 = (bf16[2,4096,128]{2,1,0:T(8,128)(2,1)}, bf16[2,4096,128]{2,1,0:T(8,128)(2,1)}) custom-call(s32[2,8,4,128]{3,2,1,0:T(4,128)} %bitcast.57, bf16[2,2048,128]{2,1,0:T(8,128)(2,1)} %collective-permute-done.3.k_ref, bf16[2,2048,128]{2,1,0:T(8,128)(2,1)} %collective-permute-done.4.v_ref, bf16[2,4096,128]{2,1,0:T(8,128)(2,1)} %get-tuple-element.41.refs_0_, ...), custom_call_target="tpu_custom_call" | custom-call | flops 8589934592 | bytes 8388608 | tf_op jit(solution)/shard_map/pallas_call | solution.py:165
  112.2 1.1 copy-done.2
  113.3 21.3 %shard_map.230 = (bf16[2,4096,128]{2,1,0:T(8,128)(2,1)}, bf16[2,4096,128]{2,1,0:T(8,128)(2,1)}, bf16[2,4096,128]{2,1,0:T(8,128)(2,1)}, bf16[1024,4096]{1,0:T(8,128)(2,1)}) custom-call(s32[4]{0:T(128)} %iota_xor_fusion.order_ref, bf16[1024,1024]{1,0:T(8,128)(2,1)} %x_ref.1, bf16[1024,1024]{1,0:T(8,128)(2,1)} %collective-permute-done.refs_1_, ...), custom_call_target="tpu_custom_call" | custom-call | flops 6442450944 | bytes 27262976 | tf_op jit(solution)/shard_map/pallas_call | solution.py:115
  134.6 53.4 %shard_map.233 = (bf16[4096,256]{1,0:T(8,128)(2,1)}, f32[8,8,512]{2,1,0:T(8,128)}) custom-call(bf16[2,4096,128]{2,1,0:T(8,128)(2,1)} %get-tuple-element.38.q_ref, bf16[2,4096,128]{2,1,0:T(8,128)(2,1)} %get-tuple-element.39.k_ref, bf16[2,4096,128]{2,1,0:T(8,128)(2,1)} %get-tuple-element.40.v_ref, bf16[2,4096,128]{2,1,0:T(8,128)(2,1)} %get-tuple-element.43.mk_ref, ...), custom_call_target="tpu_custom_call" | custom-call | flops 17179869184 | bytes 12582912 | tf_op jit(solution)/shard_map/pallas_call | solution.py:243
  188.1 4.6 all-to-all-start.2
  193.0 2.6 copy.55
  195.6 38.4 %all-to-all-done.2.a_ref = bf16[4,1024,256]{2,1,0:T(8,128)(2,1)} async-done(((bf16[4,1024,256]{2,1,0:T(8,128)(2,1)}), bf16[4,1024,256]{2,1,0:T(8,128)(2,1)}, u32[]{:S(2)}, u32[]{:S(2)}) %all-to-all-start.2) | async-done | bytes 2097184 | tf_op jit(solution)/shard_map/all_to_all | solution.py:638
  233.9 8.8 %shard_map.234 = (f32[1024,1024]{1,0:T(8,128)}, bf16[1024,1024]{1,0:T(8,128)(2,1)}, bf16[1024,1024]{1,0:T(8,128)(2,1)}, bf16[1024,1024]{1,0:T(8,128)(2,1)}) custom-call(bf16[4,1024,256]{2,1,0:T(8,128)(2,1)} %all-to-all-done.2.a_ref, bf16[1024,4096]{1,0:T(8,128)(2,1)} %all-gather.3.cloned.1.call-done.w_ref.wg_ref.wu_ref.wd_ref.refs_4_.refs_5_.refs_8_, ...), custom_call_target="tpu_custom_call" | custom-call | flops 2147483648 | bytes 16777216 | tf_op jit(solution)/shard_map/pallas_call | solution.py:380
  242.7 11.9 %shard_map.235 = (bf16[1024,1024]{1,0:T(8,128)(2,1)}, bf16[1024,1024]{1,0:T(8,128)(2,1)}, bf16[1024,1024]{1,0:T(8,128)(2,1)}) custom-call(bf16[1024,1024]{1,0:T(8,128)(2,1)} %get-tuple-element.47.n_ref, bf16[1024,1024]{1,0:T(8,128)(2,1)} %refs_10_.1, bf16[1024,4096]{1,0:T(8,128)(2,1)} %all-gather.3.cloned.1.call-done.w_ref.wg_ref.wu_ref.wd_ref.refs_4_.refs_5_.refs_8_, ...), custom_call_target="tpu_custom_call" | custom-call | flops 6442450944 | bytes 12582912 | tf_op jit(solution)/shard_map/pallas_call | solution.py:418
  254.5 17.4 %shard_map.236 = (bf16[1024,1792]{1,0:T(8,128)(2,1)}, bf16[1024,1792]{1,0:T(8,128)(2,1)}, bf16[1024,1792]{1,0:T(8,128)(2,1)}) custom-call(bf16[1024,1024]{1,0:T(8,128)(2,1)} %get-tuple-element.47.n_ref, bf16[1024,1024]{1,0:T(8,128)(2,1)} %refs_10_.1, bf16[1024,5376]{1,0:T(8,128)(2,1)} %all-gather.5.cloned.1.call-done.wg_ref.wu_ref.wd_ref.refs_6_.refs_7_, ...), custom_call_target="tpu_custom_call" | custom-call | flops 11274289152 | bytes 22020096 | tf_op jit(solution)/shard_map/pallas_call | solution.py:418
  271.9 27.4 %shard_map.237 = (f32[1024,1024]{1,0:T(8,128)}, bf16[1024,1024]{1,0:T(8,128)(2,1)}, bf16[4,1024,256]{2,1,0:T(8,128)(2,1)}, f32[1,1024]{1,0:T(1,128)}) custom-call(bf16[1024,1024]{1,0:T(8,128)(2,1)} %get-tuple-element.50.refs_0_.refs_1_, bf16[1024,1024]{1,0:T(8,128)(2,1)} %get-tuple-element.51.refs_1_.refs_3_, bf16[1024,1792]{1,0:T(8,128)(2,1)} %get-tuple-element.52.refs_2_, ...), custom_call_target="tpu_custom_call" | custom-call | flops 13958643712 | bytes 39845888 | tf_op jit(solution)/shard_map/pallas_call | solution.py:489
  300.0 17.9 %shard_map.244 = bf16[1024,3840]{1,0:T(8,128)(2,1)} custom-call(bf16[1024,1024]{1,0:T(8,128)(2,1)} %bitcast.46, bf16[1024,1024]{1,0:T(8,128)(2,1)} %get-tuple-element.61.refs_1_, bf16[1024,1024]{1,0:T(8,128)(2,1)} %get-tuple-element.48.refs_2_, bf16[1024,1792]{1,0:T(8,128)(2,1)} %get-tuple-element.49.refs_3_, bf16[1024,1024]{1,0:T(8,128)(2,1)} %get-tuple-element.62.refs_4_), custom_call_target="tpu_custom_call" | custom-call | flops 8053063680 | bytes 7864320 | tf_op jit(solution)/shard_map/pallas_call | solution.py:533
  318.1 7.1 pad_maximum_fusion
  325.7 24.2 %shard_map.245 = bf16[1024,5632]{1,0:T(8,128)(2,1)} custom-call(bf16[1024,1024]{1,0:T(8,128)(2,1)} %get-tuple-element.64.refs_0_, bf16[1024,1024]{1,0:T(8,128)(2,1)} %get-tuple-element.50.refs_0_.refs_1_, bf16[1024,1792]{1,0:T(8,128)(2,1)} %get-tuple-element.52.refs_2_, bf16[1024,1024]{1,0:T(8,128)(2,1)} %get-tuple-element.51.refs_1_.refs_3_, ...), custom_call_target="tpu_custom_call" | custom-call | flops 11811160064 | bytes 11534336 | tf_op jit(solution)/shard_map/pallas_call | solution.py:533
  349.9 1.6 copy-done.5
  351.6 53.9 %all_to_all.50 = bf16[4,1024,256]{2,1,0:T(8,128)(2,1)} all-to-all(bf16[4,1024,256]{2,1,0:T(8,128)(2,1)S(1)} %copy-done.5), channel_id=1, replica_groups=mesh['fsdp'=8,'seq'=4] {'seq'}, dimensions={0} | all-to-all | bytes 4194304 | tf_op jit(solution)/shard_map/all_to_all | solution.py:655
  405.4 83.0 %shard_map.238 = (bf16[4096,256]{1,0:T(8,128)(2,1)}, bf16[4096,256]{1,0:T(8,128)(2,1)}, bf16[4096,256]{1,0:T(8,128)(2,1)}) custom-call(bf16[2,4096,128]{2,1,0:T(8,128)(2,1)} %get-tuple-element.38.q_ref, bf16[2,4096,128]{2,1,0:T(8,128)(2,1)} %get-tuple-element.39.k_ref, bf16[2,4096,128]{2,1,0:T(8,128)(2,1)} %get-tuple-element.40.v_ref, ...), custom_call_target="tpu_custom_call" | custom-call | flops 21474836480 | bytes 25165824 | tf_op jit(solution)/shard_map/pallas_call | solution.py:344
  488.4 6.3 shard_map.242
  494.7 13.4 %shard_map.243 = bf16[1024,768]{1,0:T(8,128)(2,1)} custom-call(bf16[1024,4096]{1,0:T(8,128)(2,1)} %get-tuple-element.60.refs_0_, bf16[4096,256]{1,0:T(8,128)(2,1)} %get-tuple-element.57.a_ref.refs_1_, bf16[4096,256]{1,0:T(8,128)(2,1)} %get-tuple-element.58.b_ref.refs_2_, bf16[4096,256]{1,0:T(8,128)(2,1)} %get-tuple-element.59.c_ref.refs_3_), custom_call_target="tpu_custom_call" | custom-call | flops 6442450944 | bytes 1572864 | tf_op jit(solution)/shard_map/pallas_call | solution.py:533
  508.1 16.8 %all-to-all-start.4 = ((bf16[8,128,768]{2,1,0:T(8,128)(2,1)}), bf16[8,128,768]{2,1,0:T(8,128)(2,1)}, u32[]{:S(2)}, u32[]{:S(2)}) async-start(bf16[8,128,768]{2,1,0:T(8,128)(2,1)} %bitcast.51), calls=%async_computation.4 | async-start | bytes 3145728 | tf_op jit(solution)/shard_map/all_to_all | solution.py:692
  525.0 6.3 shard_map.240
  531.6 6.3 shard_map.241
  537.9 4.0 add_convert_fusion
  541.9 1.0 collective-permute-start.7
  543.0 2.1 fusion.9
  545.1 7.6 %fusion.10 = f32[1024,1024]{1,0:T(8,128)} fusion(bf16[1024,1792]{1,0:T(8,128)(2,1)S(1)} %copy-done.12, bf16[1024,5376]{1,0:T(8,128)(2,1)} %all-gather.5.cloned.1.call-done.wg_ref.wu_ref.wd_ref.refs_6_.refs_7_), kind=kOutput, calls=%fused_computation.16 | convolution fusion | flops 3758096384 | bytes 11534336 | tf_op jit(solution)/shard_map/dot_general | solution.py:22
  552.6 6.3 shard_map.239
  559.0 13.5 %all-to-all-done.4 = bf16[8,128,768]{2,1,0:T(8,128)(2,1)} async-done(((bf16[8,128,768]{2,1,0:T(8,128)(2,1)}), bf16[8,128,768]{2,1,0:T(8,128)(2,1)}, u32[]{:S(2)}, u32[]{:S(2)}) %all-to-all-start.4) | async-done | bytes 1572896 | tf_op jit(solution)/shard_map/all_to_all | solution.py:692
  572.5 1.6 reduce_sum.62
  575.0 4.2 all-to-all-start.5
  579.3 59.4 %collective-permute-done.7 = bf16[1024,1024]{1,0:T(8,128)(2,1)} collective-permute-done((bf16[1024,1024]{1,0:T(8,128)(2,1)}, bf16[1024,1024]{1,0:T(8,128)(2,1)}, u32[]{:S(2)}, u32[]{:S(2)}) %collective-permute-start.7) | collective-permute-done | bytes 2097184 | tf_op jit(solution)/shard_map/ppermute | solution.py:59
  638.7 4.0 fusion.8
  642.7 12.3 %all-to-all-done.5 = bf16[4,128,768]{2,1,0:T(8,128)(2,1)} async-done(((bf16[4,128,768]{2,1,0:T(8,128)(2,1)}), bf16[4,128,768]{2,1,0:T(8,128)(2,1)}, u32[]{:S(2)}, u32[]{:S(2)}) %all-to-all-start.5) | async-done | bytes 786464 | tf_op jit(solution)/shard_map/all_to_all | solution.py:65
  656.0 4.8 all-to-all-start.8
  660.7 8.4 %add_convert_fusion.1 = bf16[1024,1024]{1,0:T(8,128)(2,1)} fusion(f32[1024,1024]{1,0:T(8,128)} %fusion.10, f32[1024,1024]{1,0:T(8,128)} %get-tuple-element.46.refs_9_, bf16[1024,1024]{1,0:T(8,128)(2,1)} %get-tuple-element.48.refs_2_, bf16[1024,4096]{1,0:T(8,128)(2,1)} %all-gather.3.cloned.1.call-done.w_ref.wg_ref.wu_ref.wd_ref.refs_4_.refs_5_.refs_8_), kind=kOutput, calls=%fused_computation.15 | convolution fusion | flops 2150629376 | bytes 14680064 | tf_op jit(solution)/shard_map/dot_general | solution.py:22
  669.2 2.3 copy.54
  671.5 2.0 fusion.18
  673.5 2.0 copy.56
  677.5 1.0 reduce_sum.64
  679.2 3.7 all-to-all-start.9
  682.9 4.7 all-to-all-done.9
  687.6 2.0 broadcast_in_dim.20
  689.5 4.2 all-to-all-start.6
  693.8 5.9 fusion.7
  700.4 7.6 %all-to-all-done.6 = bf16[4,32,3968]{2,1,0:T(8,128)(2,1)} async-done(((bf16[4,32,3968]{2,1,0:T(8,128)(2,1)}), bf16[4,32,3968]{2,1,0:T(8,128)(2,1)}, u32[]{:S(2)}, u32[]{:S(2)}) %all-to-all-start.6) | async-done | bytes 1015840 | tf_op jit(solution)/shard_map/all_to_all | solution.py:65
  708.0 2.2 broadcast_in_dim.21
  710.1 4.3 all-to-all-start.7
  714.5 1.3 bitcast_convert_fusion.1
  716.7 1.2 slice_bitcast_fusion
  717.8 2.9 copy.59
  721.4 11.8 %all-to-all-done.7 = bf16[4,32,5632]{2,1,0:T(8,128)(2,1)} async-done(((bf16[4,32,5632]{2,1,0:T(8,128)(2,1)}), bf16[4,32,5632]{2,1,0:T(8,128)(2,1)}, u32[]{:S(2)}, u32[]{:S(2)}) %all-to-all-start.7) | async-done | bytes 1441824 | tf_op jit(solution)/shard_map/all_to_all | solution.py:65
  733.2 1.7 bitcast_convert_fusion
  734.9 1.8 fusion.17
  (82 shorter events, 18.5 us)
Async XLA Ops:
  7.2 1.1 copy-start
  7.2 226.7 %all-gather.3.cloned.1.call-start = ((), (), s32[]{:S(2)}) async-start(), calls=%async_computation.12 | async-start | bytes 8650752 | tf_op jit(solution)/shard_map/all_gather | solution.py:617
  8.6 8.5 %copy-start.10 = (bf16[128]{0:T(256)(128)(2,1)S(1)}, bf16[128]{0:T(256)(128)(2,1)}, u32[]{:S(2)}) copy-start(bf16[128]{0:T(256)(128)(2,1)} %param.25) | copy-start | bytes 772
  8.6 8.5 %copy-start.11 = (bf16[128]{0:T(256)(128)(2,1)S(1)}, bf16[128]{0:T(256)(128)(2,1)}, u32[]{:S(2)}) copy-start(bf16[128]{0:T(256)(128)(2,1)} %param.24) | copy-start | bytes 772
  8.6 14.9 %copy-start.9 = (bf16[1,2,2048,128]{3,2,1,0:T(8,128)(2,1)S(1)}, bf16[1,2,2048,128]{3,2,1,0:T(8,128)(2,1)}, u32[]{:S(2)}) copy-start(bf16[1,2,2048,128]{3,2,1,0:T(8,128)(2,1)} %param.26) | copy-start | bytes 3145732
  11.4 243.2 %all-gather.5.cloned.1.call-start = ((), (), s32[]{:S(2)}) async-start(), calls=%async_computation.13 | async-start | bytes 11354112 | tf_op jit(solution)/shard_map/all_gather | solution.py:618
  14.0 54.6 %collective-permute-start.1 = (bf16[1024,1024]{1,0:T(8,128)(2,1)}, bf16[1024,1024]{1,0:T(8,128)(2,1)}, u32[]{:S(2)}, u32[]{:S(2)}) collective-permute-start(bf16[1024,1024]{1,0:T(8,128)(2,1)} %x_ref.1), channel_id=1, source_target_pairs={{0,2},{1,3},{2,0},{3,1},{4,6},{5,7},{6,4},{7,5},{8,10},{9,11},{10,... | collective-permute-start | bytes 6291464 | tf_op jit(solution)/shard_map/ppermute | solution.py:59
  17.1 95.1 %collective-permute-start = (bf16[1024,1024]{1,0:T(8,128)(2,1)}, bf16[1024,1024]{1,0:T(8,128)(2,1)}, u32[]{:S(2)}, u32[]{:S(2)}) collective-permute-start(bf16[1024,1024]{1,0:T(8,128)(2,1)} %x_ref.1), channel_id=1, source_target_pairs={{0,1},{1,0},{2,3},{3,2},{4,5},{5,4},{6,7},{7,6},{8,9},{9,8},{10,11... | collective-permute-start | bytes 6291464 | tf_op jit(solution)/shard_map/ppermute | solution.py:59
  17.7 20.9 %all-to-all-start.1 = ((bf16[8,2,128]{2,1,0:T(2,128)(2,1)}), bf16[8,2,128]{2,1,0:T(2,128)(2,1)S(1)}, u32[]{:S(2)}, u32[]{:S(2)}) async-start(bf16[8,2,128]{2,1,0:T(2,128)(2,1)} %broadcast_in_dim.17), calls=%async_computation.1 | async-start | bytes 8192 | tf_op jit(solution)/shard_map/all_to_all | solution.py:65
  23.5 70.2 %collective-permute-start.3 = (bf16[2,2048,128]{2,1,0:T(8,128)(2,1)S(1)}, bf16[2,2048,128]{2,1,0:T(8,128)(2,1)}, u32[]{:S(2)}, u32[]{:S(2)}) collective-permute-start(bf16[2,2048,128]{2,1,0:T(8,128)(2,1)S(1)} %bitcast.60), channel_id=1, source_target_pairs={{0,4},{4,8},{8,12},{12,16},{16,20},{20,24},{24,28},{28,0},{1,5},{5... | collective-permute-start | bytes 3145736 | tf_op jit(solution)/shard_map/ppermute | solution.py:599
  25.5 68.2 %collective-permute-start.4 = (bf16[2,2048,128]{2,1,0:T(8,128)(2,1)}, bf16[2,2048,128]{2,1,0:T(8,128)(2,1)}, u32[]{:S(2)}, u32[]{:S(2)}) collective-permute-start(bf16[2,2048,128]{2,1,0:T(8,128)(2,1)} %bitcast.7.v_ref), channel_id=1, source_target_pairs={{0,4},{4,8},{8,12},{12,16},{16,20},{20,24},{24,28},{28,0},{1,5},{5... | collective-permute-start | bytes 3145736 | tf_op jit(solution)/shard_map/ppermute | solution.py:600
  38.6 6.0 copy-start.7
  38.6 6.0 copy-start.8
  39.8 72.3 %all-to-all-start = ((bf16[8,128,768]{2,1,0:T(8,128)(2,1)}), bf16[8,128,768]{2,1,0:T(8,128)(2,1)S(1)}, u32[]{:S(2)}, u32[]{:S(2)}) async-start(bf16[8,128,768]{2,1,0:T(8,128)(2,1)} %broadcast_in_dim.16), calls=%async_computation | async-start | bytes 3145728 | tf_op jit(solution)/shard_map/all_to_all | solution.py:65
  68.7 43.5 %collective-permute-start.2 = (bf16[1024,1024]{1,0:T(8,128)(2,1)}, bf16[1024,1024]{1,0:T(8,128)(2,1)}, u32[]{:S(2)}, u32[]{:S(2)}) collective-permute-start(bf16[1024,1024]{1,0:T(8,128)(2,1)} %collective-permute-done.1.refs_2_), channel_id=1, source_target_pairs={{0,1},{1,0},{2,3},{3,2},{4,5},{5,4},{6,7},{7,6},{8,9},{9,8},{10,11... | collective-permute-start | bytes 6291464 | tf_op jit(solution)/shard_map/ppermute | solution.py:59
  112.2 1.2 copy-start.2
  188.1 4.9 copy-start.3
  188.1 45.8 %all-to-all-start.2 = ((bf16[4,1024,256]{2,1,0:T(8,128)(2,1)}), bf16[4,1024,256]{2,1,0:T(8,128)(2,1)}, u32[]{:S(2)}, u32[]{:S(2)}) async-start(bf16[4,1024,256]{2,1,0:T(8,128)(2,1)} %bitcast.45), calls=%async_computation.2 | async-start | bytes 4194304 | tf_op jit(solution)/shard_map/all_to_all | solution.py:638
  192.7 494.9 %reduce-scatter.3.cloned.1.call-start = ((), (), s32[]{:S(2)}) async-start(), calls=%async_computation.14 | async-start | bytes 8380416 | tf_op jit(solution)/shard_map/reduce_scatter | solution.py:664
  325.2 382.7 %reduce-scatter.5.cloned.1.call-start = ((), (), s32[]{:S(2)}) async-start(), calls=%async_computation.15 | async-start | bytes 11894784 | tf_op jit(solution)/shard_map/reduce_scatter | solution.py:663
  349.9 1.6 copy-start.5
  494.7 43.2 %collective-permute-start.6 = (bf16[1024,1024]{1,0:T(8,128)(2,1)}, bf16[1024,1024]{1,0:T(8,128)(2,1)S(1)}, u32[]{:S(2)}, u32[]{:S(2)}) collective-permute-start(bf16[1024,1024]{1,0:T(8,128)(2,1)} %shard_map.242), channel_id=1, source_target_pairs={{0,1},{1,0},{2,3},{3,2},{4,5},{5,4},{6,7},{7,6},{8,9},{9,8},{10,11... | collective-permute-start | bytes 6291464 | tf_op jit(solution)/shard_map/ppermute | solution.py:59
  508.1 64.3 %all-to-all-start.4 = ((bf16[8,128,768]{2,1,0:T(8,128)(2,1)}), bf16[8,128,768]{2,1,0:T(8,128)(2,1)}, u32[]{:S(2)}, u32[]{:S(2)}) async-start(bf16[8,128,768]{2,1,0:T(8,128)(2,1)} %bitcast.51), calls=%async_computation.4 | async-start | bytes 3145728 | tf_op jit(solution)/shard_map/all_to_all | solution.py:692
  531.2 48.0 %collective-permute-start.5 = (bf16[1024,1024]{1,0:T(8,128)(2,1)}, bf16[1024,1024]{1,0:T(8,128)(2,1)}, u32[]{:S(2)}, u32[]{:S(2)}) collective-permute-start(bf16[1024,1024]{1,0:T(8,128)(2,1)} %shard_map.240), channel_id=1, source_target_pairs={{0,1},{1,0},{2,3},{3,2},{4,5},{5,4},{6,7},{7,6},{8,9},{9,8},{10,11... | collective-permute-start | bytes 6291464 | tf_op jit(solution)/shard_map/ppermute | solution.py:59
  537.9 7.2 copy-start.12
  541.9 96.8 %collective-permute-start.7 = (bf16[1024,1024]{1,0:T(8,128)(2,1)}, bf16[1024,1024]{1,0:T(8,128)(2,1)}, u32[]{:S(2)}, u32[]{:S(2)}) collective-permute-start(bf16[1024,1024]{1,0:T(8,128)(2,1)} %add_convert_fusion), channel_id=1, source_target_pairs={{0,2},{1,3},{2,0},{3,1},{4,6},{5,7},{6,4},{7,5},{8,10},{9,11},{10,... | collective-permute-start | bytes 6291464 | tf_op jit(solution)/shard_map/ppermute | solution.py:59
  559.0 79.7 %copy-start.4 = (bf16[1024,1024]{1,0:T(8,128)(2,1)S(1)}, bf16[1024,1024]{1,0:T(8,128)(2,1)}, u32[]{:S(2)}) copy-start(bf16[1024,1024]{1,0:T(8,128)(2,1)} %shard_map.239) | copy-start | bytes 6291460
  559.0 79.7 %copy-start.6 = (f32[1,8,128]{2,0,1:T(1,128)S(1)}, f32[1,8,128]{2,0,1:T(1,128)}, u32[]{:S(2)}) copy-start(f32[1,8,128]{2,0,1:T(1,128)} %get-tuple-element.152) | copy-start | bytes 12292
  575.0 80.0 %all-to-all-start.5 = ((bf16[4,128,768]{2,1,0:T(8,128)(2,1)}), bf16[4,128,768]{2,1,0:T(8,128)(2,1)}, u32[]{:S(2)}, u32[]{:S(2)}) async-start(bf16[4,128,768]{2,1,0:T(8,128)(2,1)} %broadcast_in_dim.18), calls=%async_computation.5 | async-start | bytes 1572864 | tf_op jit(solution)/shard_map/all_to_all | solution.py:65
  656.0 21.6 %all-to-all-start.8 = ((bf16[8,128,128]{2,1,0:T(8,128)(2,1)}), bf16[8,128,128]{2,1,0:T(8,128)(2,1)}, u32[]{:S(2)}, u32[]{:S(2)}) async-start(bf16[8,128,128]{2,1,0:T(8,128)(2,1)} %broadcast_in_dim.22), calls=%async_computation.10 | async-start | bytes 524288 | tf_op jit(solution)/shard_map/all_to_all | solution.py:692
  679.2 8.3 %all-to-all-start.9 = ((bf16[4,128,128]{2,1,0:T(8,128)(2,1)}), bf16[4,128,128]{2,1,0:T(8,128)(2,1)S(1)}, u32[]{:S(2)}, u32[]{:S(2)}) async-start(bf16[4,128,128]{2,1,0:T(8,128)(2,1)} %broadcast_in_dim.23), calls=%async_computation.11 | async-start | bytes 262144 | tf_op jit(solution)/shard_map/all_to_all | solution.py:65
  689.5 18.4 %all-to-all-start.6 = ((bf16[4,32,3968]{2,1,0:T(8,128)(2,1)}), bf16[4,32,3968]{2,1,0:T(8,128)(2,1)}, u32[]{:S(2)}, u32[]{:S(2)}) async-start(bf16[4,32,3968]{2,1,0:T(8,128)(2,1)} %broadcast_in_dim.20), calls=%async_computation.7 | async-start | bytes 2031616 | tf_op jit(solution)/shard_map/all_to_all | solution.py:65
  710.1 23.1 %all-to-all-start.7 = ((bf16[4,32,5632]{2,1,0:T(8,128)(2,1)}), bf16[4,32,5632]{2,1,0:T(8,128)(2,1)}, u32[]{:S(2)}, u32[]{:S(2)}) async-start(bf16[4,32,5632]{2,1,0:T(8,128)(2,1)} %broadcast_in_dim.21), calls=%async_computation.9 | async-start | bytes 2883584 | tf_op jit(solution)/shard_map/all_to_all | solution.py:65
  733.2 3.5 copy-start.1
Sparse Core Ops, SparseCore 0:
  11.5 128.2 all-gather.2
  143.3 105.6 all-gather.4
  325.3 163.0 reduce-scatter.2
  490.7 196.3 reduce-scatter.4

commit v2 on v1

v2 whole, which is shorter than its diff:
```python
import functools

import jax
import jax.numpy as jnp
from jax import lax
from jax.experimental import pallas as pl
from jax.experimental.pallas import tpu as pltpu
from jax.sharding import PartitionSpec as P

epsilon = 1e-06
log2e = 1.4426950408889634
f32 = jnp.float32
bf16 = jnp.bfloat16
VMEM_LIMIT = 60 * 1024 * 1024
hint = 0.15


def dot(a, b):
    return jnp.dot(a, b, preferred_element_type=f32)


def dot_nt(a, b):
    return lax.dot_general(a, b, (((1,), (1,)), ((), ())), preferred_element_type=f32)


def dot_tn(a, b):
    return lax.dot_general(a, b, (((0,), (0,)), ((), ())), preferred_element_type=f32)


def call(
    kernel, grid, in_specs, out_specs, out_shape, flops, bytes_accessed, scratch=(), prefetch=0, aliases=None
):
    return pl.pallas_call(
        kernel,
        name=kernel.__qualname__.split(".")[0],
        grid_spec=pltpu.PrefetchScalarGridSpec(
            num_scalar_prefetch=prefetch,
            grid=grid,
            in_specs=in_specs,
            out_specs=out_specs,
            scratch_shapes=list(scratch),
        ),
        out_shape=out_shape,
        input_output_aliases=aliases or {},
        compiler_params=pltpu.CompilerParams(
            dimension_semantics=("arbitrary",) * len(grid), vmem_limit_bytes=VMEM_LIMIT
        ),
        cost_estimate=pl.CostEstimate(
            flops=int(flops * hint), bytes_accessed=int(bytes_accessed * hint), transcendentals=0
        ),
    )


def resident(shape, index):
    return pl.BlockSpec(shape, lambda *_: index, pipeline_mode=pl.Buffered(1))


def column_blocks(height, first, parts):
    return [resident((height, 256), (0, first // 256 + c)) for c in range(parts)]


def struct(shape, dtype):
    return jax.ShapeDtypeStruct(shape, dtype)


def swap_seq(array, bit):
    count = lax.axis_size("seq")
    return lax.ppermute(array, "seq", [(i, i ^ bit) for i in range(count)])


def spread(array, axis):
    count = lax.axis_size(axis)
    copies = jnp.broadcast_to(array[None], (count,) + array.shape)
    return lax.all_to_all(copies, axis, split_axis=0, concat_axis=0, tiled=True)


def project(order, pieces, weights, gain_row, cosine, sine, head_local, head_dim):
    rows, width = pieces[0].shape
    count = len(pieces)
    block = min(512, rows)
    steps = rows // block
    length = rows * count
    cols = weights.shape[1]
    group = head_local * head_dim

    def kernel(order_ref, *refs):
        xs = refs[:count]
        w_ref, g_ref, c_ref, s_ref, q_ref, k_ref, v_ref, vt_ref, nt_ref = refs[count:]
        slot = pl.program_id(0)

        def run(x_ref):
            x = x_ref[...].astype(f32)
            scale = lax.rsqrt(jnp.mean(x * x, axis=-1, keepdims=True) + epsilon)
            normed = (x * scale * g_ref[...]).astype(bf16)
            nt_ref[...] = normed.T
            lin = dot(normed, w_ref[...])
            cos, sin = c_ref[...], s_ref[...]
            for head in range(head_local):
                for part, out in ((0, q_ref), (1, k_ref)):
                    start = part * group + head * head_dim
                    u = lin[:, start : start + head_dim]
                    out[head] = (u * cos + pltpu.roll(u, head_dim // 2, 1) * sin).astype(bf16)
                start = 2 * group + head * head_dim
                v = lin[:, start : start + head_dim].astype(bf16)
                v_ref[head] = v
                vt_ref[head] = v.T

        for k in range(count):
            pl.when(slot == k)(functools.partial(run, xs[k]))

    def piece_spec(k):
        return pl.BlockSpec(
            (block, width),
            lambda slot, i, order_ref: (
                jnp.where(slot == k, i, jnp.where(slot < k, 0, steps - 1)),
                0,
            ),
        )

    def at_rows(slot, i, order_ref):
        return order_ref[slot] * steps + i

    head_spec = pl.BlockSpec((head_local, block, head_dim), lambda *a: (0, at_rows(*a), 0))
    table_spec = pl.BlockSpec((block, head_dim), lambda *a: (at_rows(*a), 0))
    heads = struct((head_local, length, head_dim), bf16)
    return call(
        kernel,
        (count, steps),
        [piece_spec(k) for k in range(count)]
        + [resident((width, cols), (0, 0)), resident((1, width), (0, 0)), table_spec, table_spec],
        [
            head_spec,
            head_spec,
            head_spec,
            pl.BlockSpec((head_local, head_dim, block), lambda *a: (0, 0, at_rows(*a))),
            pl.BlockSpec((width, block), lambda *a: (0, at_rows(*a))),
        ],
        [heads, heads, heads, struct((head_local, head_dim, length), bf16)]
        + [struct((width, length), bf16)],
        2 * length * width * cols,
        4 * length * width + 2 * length * cols + 8 * length * head_dim,
        prefetch=1,
    )(order, *pieces, weights, gain_row, cosine, sine)


def retrieve(chosen, keys, values, base, before=None):
    head_local, rows_cache, head_dim = keys.shape
    blocks, slots = chosen.shape[1:]
    per = min(4, blocks)
    total = blocks * slots

    def kernel(c_ref, k_ref, v_ref, *refs):
        if before is not None:
            bk_ref, bv_ref = refs[:2]
        ok_ref, ov_ref, table, mask = refs[-4:]

        @pl.when(pl.program_id(1) == 0)
        def _():
            table[:, :head_dim] = k_ref[0]
            table[:, head_dim:] = v_ref[0]

        for b in range(per):
            row = c_ref[0, 0, b : b + 1, :] - base
            column = jnp.broadcast_to(row, (slots, slots)).T
            lane = lax.broadcasted_iota(jnp.int32, (slots, slots), 1)
            for start in range(0, rows_cache, slots):
                mask[b * slots : (b + 1) * slots, start : start + slots] = jnp.where(
                    column == lane + start, 1.0, 0.0
                ).astype(bf16)
        picked = dot(mask[...], table[...])
        if before is not None:
            picked_keys = picked[:, :head_dim] + bk_ref[0].astype(f32)
            picked_values = picked[:, head_dim:] + bv_ref[0].astype(f32)
        else:
            picked_keys, picked_values = picked[:, :head_dim], picked[:, head_dim:]
        ok_ref[0] = picked_keys.astype(bf16)
        ov_ref[0] = picked_values.astype(bf16)

    out_spec = pl.BlockSpec((1, per * slots, head_dim), lambda h, i: (h, i, 0))
    table_spec = pl.BlockSpec((1, rows_cache, head_dim), lambda h, i: (h, 0, 0))
    extra = () if before is None else before
    out = struct((head_local, total, head_dim), bf16)
    return call(
        kernel,
        (head_local, blocks // per),
        [pl.BlockSpec((1, 1, per, slots), lambda h, i: (h, i, 0, 0)), table_spec, table_spec]
        + [out_spec] * len(extra),
        [out_spec, out_spec],
        [out, out],
        4 * head_local * total * rows_cache * head_dim,
        8 * head_local * total * head_dim,
        scratch=[
            pltpu.VMEM((rows_cache, 2 * head_dim), bf16),
            pltpu.VMEM((per * slots, rows_cache), bf16),
        ],
    )(chosen.reshape(head_local, blocks // per, per, slots), keys, values, *extra)


def attend(order, query, key, value_t, memory_keys, memory_values, mem_block, mem_count, count):
    head_local, length, head_dim = query.shape
    block = length // count
    half = block // 2
    groups = block // mem_block
    factor = head_dim ** (-0.5) * log2e

    def kernel(order_ref, q_ref, k_ref, vt_ref, mk_ref, mv_ref, *refs):
        o_refs, lse_ref = refs[:count], refs[count]
        index = pl.program_id(0)

        def memory(head):
            parts = []
            for g in range(groups):
                q = q_ref[head, g * mem_block : (g + 1) * mem_block, :]
                parts.append(dot_nt(mk_ref[head, g * mem_count : (g + 1) * mem_count, :], q))
            scores = jnp.concatenate(parts, axis=1) * factor
            top = jnp.max(scores, axis=0, keepdims=True)
            weight = jnp.exp2(scores - top)
            total = jnp.sum(weight, axis=0, keepdims=True)
            weight = weight.astype(bf16)
            values_t = mv_ref[head].T
            mixed = jnp.concatenate(
                [
                    dot(
                        values_t[:, g * mem_count : (g + 1) * mem_count],
                        weight[:, g * mem_block : (g + 1) * mem_block],
                    )
                    for g in range(groups)
                ],
                axis=1,
            )
            return top, total, mixed

        def step(head, carry, start, size, queries, offset):
            top, total, mixed = carry
            keys = k_ref[head, pl.ds(start, size), :]
            scores = dot_nt(keys, q_ref[head, queries, :]) * factor
            if offset is not None:
                row = lax.broadcasted_iota(jnp.int32, scores.shape, 0) + offset
                col = lax.broadcasted_iota(jnp.int32, scores.shape, 1) + (queries.start or 0)
                scores = jnp.where(row <= col, scores, -jnp.inf)
            new_top = jnp.maximum(top, jnp.max(scores, axis=0, keepdims=True))
            decay = jnp.exp2(top - new_top)
            weight = jnp.exp2(scores - new_top)
            total = total * decay + jnp.sum(weight, axis=0, keepdims=True)
            mixed = mixed * decay + dot(vt_ref[head, :, pl.ds(start, size)], weight.astype(bf16))
            return new_top, total, mixed

        every, later = slice(0, block), slice(half, block)
        carries = tuple(memory(head) for head in range(head_local))
        carries = lax.fori_loop(
            0,
            index,
            lambda j, c: tuple(
                step(head, c[head], pl.multiple_of(j * block, block), block, every, None)
                for head in range(head_local)
            ),
            carries,
        )
        start = pl.multiple_of(index * block, block)
        for head in range(head_local):
            carry = step(head, carries[head], start, half, every, 0)
            last = tuple(part[:, half:] for part in carry)
            middle = pl.multiple_of(start + half, half)
            last = step(head, last, middle, half, later, half)
            top, total, mixed = (
                jnp.concatenate([part[:, :half], end], axis=1) for part, end in zip(carry, last)
            )
            columns = slice(head * head_dim, (head + 1) * head_dim)
            mixed = (mixed / total).T.astype(bf16)
            for k in range(count):
                @pl.when(index == order_ref[k])
                def _():
                    o_refs[k][:, columns] = mixed
            lse = top + jnp.log2(total)
            lse_ref[0, head : head + 1, :] = lse[:, :half]
            lse_ref[1, head : head + 1, :] = lse[:, half:]

    full = resident((head_local, length, head_dim), (0, 0, 0))
    full_t = resident((head_local, head_dim, length), (0, 0, 0))
    rows = pl.BlockSpec((head_local, block, head_dim), lambda i, order_ref: (0, i, 0))
    mem_rows = pl.BlockSpec(
        (head_local, groups * mem_count, head_dim), lambda i, order_ref: (0, i, 0)
    )
    return call(
        kernel,
        (count,),
        [rows, full, full_t, mem_rows, mem_rows],
        [pl.BlockSpec((block, head_local * head_dim), lambda i, order_ref: (0, 0))] * count
        + [pl.BlockSpec((2, 8, half), lambda i, order_ref: (i, 0, 0))],
        [struct((block, head_local * head_dim), bf16)] * count
        + [struct((2 * count, 8, half), f32)],
        4 * head_local * length * length * head_dim,
        12 * head_local * length * head_dim,
        prefetch=1,
    )(order, query, key, value_t, memory_keys, memory_values)


def attend_back(
    order, query, key, value, memory_keys, memory_values, mem_block, mem_count, grads, attended, lse,
    cosine, sine, first, last, carried=None,
):
    head_local, length, head_dim = query.shape
    count, _, block = lse.shape
    pieces = len(grads)
    piece = length // pieces
    per = piece // block
    groups = block // mem_block
    scale = head_dim ** (-0.5)
    factor = scale * log2e
    opening, closing = first == 0, last == count

    def kernel(order_ref, q_ref, k_ref, v_ref, mk_ref, mv_ref, *refs):
        g_refs, refs = refs[:pieces], refs[pieces:]
        if opening:
            o_refs, refs = refs[:pieces], refs[pieces:]
        else:
            (part_ref, delta), refs = refs[:2], refs[5:]
        (lse_ref, c_ref, s_ref, dq_ref, dk_ref, dv_ref), refs = refs[:6], refs[6:]
        if opening and not closing:
            (rest_ref, delta), refs = refs[:2], refs[2:]
        elif opening:
            delta, refs = refs[0], refs[1:]
        dq_acc, do_ref = refs
        index = pl.program_id(0) + first

        def cols(head):
            return slice(head * head_dim, (head + 1) * head_dim)

        @pl.when(index == first)
        def _():
            for k in range(pieces):
                start = pl.multiple_of(order_ref[k] * piece, piece)
                do_ref[pl.ds(start, piece), :] = g_refs[k][...]
            if not opening:
                dq_acc[:, :, first * block :] = part_ref[...]
            else:
                for k in range(pieces):
                    for p in range(per):
                        rows = slice(p * block, (p + 1) * block)
                        for head in range(head_local):
                            do = g_refs[k][rows, cols(head)].astype(f32)
                            o = o_refs[k][rows, cols(head)].astype(f32)
                            row = jnp.sum((do * o).T, axis=0, keepdims=True)
                            delta[order_ref[k] * per + p, head : head + 1, :] = row

        row_id = lax.broadcasted_iota(jnp.int32, (block, block), 0)
        col_id = lax.broadcasted_iota(jnp.int32, (block, block), 1)
        keys_t = [k_ref[head].T for head in range(head_local)]

        def memory(head):
            start = pl.multiple_of(index * block, block)
            q = q_ref[head, pl.ds(start, block), :]
            do = do_ref[pl.ds(start, block), cols(head)]
            mk_t = mk_ref[head].T
            parts = []
            for g in range(groups):
                lanes = slice(g * mem_block, (g + 1) * mem_block)
                slots = slice(g * mem_count, (g + 1) * mem_count)
                scores = dot_nt(mk_ref[head, slots, :], q[lanes])
                weight = jnp.exp2(scores * factor - lse_ref[index, head : head + 1, lanes])
                dp = dot_nt(mv_ref[head, slots, :], do[lanes])
                ds = (weight * (dp - delta[index, head : head + 1, lanes])).astype(bf16)
                parts.append(dot(mk_t[:, slots], ds))
            return jnp.concatenate(parts, axis=1)

        def step(head, carry, i, masked):
            dk, dv = carry
            start = pl.multiple_of(i * block, block)
            q = q_ref[head, pl.ds(start, block), :]
            do = do_ref[pl.ds(start, block), cols(head)]
            k, v = k_ref[head], v_ref[head]
            weight = jnp.exp2(dot_nt(k, q) * factor - lse_ref[i, head : head + 1, :])
            if masked:
                weight = jnp.where(row_id <= col_id, weight, 0.0)
            dp = dot_nt(v, do)
            ds = (weight * (dp - delta[i, head : head + 1, :])).astype(bf16)
            dv = dv + dot(weight.astype(bf16), do)
            dk = dk + dot(ds, q)
            so_far = dq_acc[head, :, pl.ds(start, block)]
            if opening:
                so_far = jnp.where(index == 0, 0.0, so_far)
            total = so_far + dot(keys_t[head], ds)
            if masked:
                return dk, dv, total
            dq_acc[head, :, pl.ds(start, block)] = total
            return dk, dv

        cos, sin = c_ref[...], s_ref[...]

        def unrotate(grad_rows):
            u = (grad_rows * scale).astype(bf16).astype(f32)
            return (u * cos - pltpu.roll(u, head_dim // 2, 1) * sin).astype(bf16)

        zero = jnp.zeros((block, head_dim), f32)
        carries = []
        for head in range(head_local):
            dk, dv, dq = step(head, (zero, zero), index, True)
            dq_ref[:, cols(head)] = unrotate((dq + memory(head)).T)
            carries.append((dk, dv))
        carries = lax.fori_loop(
            index + 1,
            count,
            lambda i, c: tuple(step(head, c[head], i, False) for head in range(head_local)),
            tuple(carries),
        )
        for head, (dk, dv) in enumerate(carries):
            dk_ref[:, cols(head)] = unrotate(dk)
            dv_ref[:, cols(head)] = dv.astype(bf16)
        if opening and not closing:
            @pl.when(index == last - 1)
            def _():
                rest_ref[...] = dq_acc[:, :, last * block :]

    group = head_local * head_dim
    full = resident((head_local, length, head_dim), (0, 0, 0))
    flat = resident((piece, group), (0, 0))
    rows = pl.BlockSpec((head_local, block, head_dim), lambda i, o: (0, i + first, 0))
    mem_rows = pl.BlockSpec(
        (head_local, groups * mem_count, head_dim), lambda i, o: (0, i + first, 0)
    )
    table = pl.BlockSpec((block, head_dim), lambda i, o: (i + first, 0))
    out_rows = pl.BlockSpec((block, group), lambda i, o: (i + first, 0))
    out = struct((length, group), bf16)
    aliases = {}
    small = resident(lse.shape, (0, 0, 0))
    in_specs = [full, rows, rows, mem_rows, mem_rows] + [flat] * pieces
    inputs = [query, key, value, memory_keys, memory_values, *grads]
    out_specs, out_shape, scratch = [out_rows] * 3, [out] * 3, []
    if opening:
        in_specs += [flat] * pieces
        inputs += list(attended)
        if closing:
            scratch.append(pltpu.VMEM(lse.shape, f32))
        else:
            rest = (head_local, head_dim, length - last * block)
            out_specs += [pl.BlockSpec(rest, lambda i, o: (0, 0, 0)), pl.BlockSpec(lse.shape, lambda i, o: (0, 0, 0))]
            out_shape += [struct(rest, f32), struct(lse.shape, f32)]
    else:
        in_specs += [resident(carried[0].shape, (0, 0, 0)), small]
        in_specs += [pl.BlockSpec(memory_space=pl.ANY)] * 3
        aliases = {1 + len(inputs) + 2 + k: k for k in range(3)}
        inputs += list(carried)
    done = sum(count - j for j in range(first, last)) / (count * (count + 1) / 2)
    return call(
        kernel,
        (last - first,),
        in_specs + [small, table, table],
        out_specs,
        out_shape,
        done * 10 * head_local * length * length * head_dim // 2,
        24 * head_local * length * head_dim,
        scratch=scratch
        + [pltpu.VMEM((head_local, head_dim, length), f32), pltpu.VMEM((length, group), bf16)],
        prefetch=1,
        aliases=aliases,
    )(order, *inputs, lse, cosine, sine)


def mix(order, attended, weights, first, tokens, gain_row):
    count = len(attended)
    rows, group = attended[0].shape
    width = tokens.shape[1]
    block = min(256, rows)
    parts = width // 256

    def kernel(order_ref, *refs):
        a_refs = refs[:count]
        w_refs, refs = refs[count : count + parts], refs[count + parts :]
        x_ref, g_ref, res_ref, n_ref, nt_ref, at_ref = refs
        residual = x_ref[...].astype(f32)
        mixed = [None] * parts
        for k in range(count):
            start = pl.multiple_of(order_ref[k] * group, group)
            for c in range(parts):
                part = dot(a_refs[k][...], w_refs[c][pl.ds(start, group), :])
                mixed[c] = part if mixed[c] is None else mixed[c] + part
            at_ref[pl.ds(start, group), :] = a_refs[k][...].T
        residual = residual + jnp.concatenate(mixed, axis=1)
        scale = lax.rsqrt(jnp.mean(residual * residual, axis=-1, keepdims=True) + epsilon)
        normed = (residual * scale * g_ref[...]).astype(bf16)
        res_ref[...] = residual
        n_ref[...] = normed
        nt_ref[...] = normed.T

    rows_spec = pl.BlockSpec((block, width), lambda i, o: (i, 0))
    cols_spec = pl.BlockSpec((width, block), lambda i, o: (0, i))
    return call(
        kernel,
        (rows // block,),
        [pl.BlockSpec((block, group), lambda i, o: (i, 0))] * count
        + column_blocks(width, first, parts)
        + [rows_spec, resident((1, width), (0, 0))],
        [rows_spec, rows_spec, cols_spec, cols_spec],
        [struct((rows, width), f32), struct((rows, width), bf16)]
        + [struct((width, rows), bf16)] * 2,
        2 * rows * width * width,
        16 * rows * width,
        prefetch=1,
    )(order, *attended, *[weights] * parts, tokens, gain_row)


def gated(normed, cotangent, weights, first, hidden_cols):
    rows, width = normed.shape
    block = 256

    def kernel(n_ref, c_ref, wg_ref, wu_ref, wd_ref, h_ref, gg_ref, gu_ref):
        normed_block = n_ref[...]
        gate = dot(normed_block, wg_ref[...])
        up = dot(normed_block, wu_ref[...])
        grad = dot(c_ref[...], wd_ref[...])
        sg = 1.0 / (1.0 + jnp.exp(-gate))
        silu = gate * sg
        h_ref[...] = (silu * up).astype(bf16)
        gg_ref[...] = (grad * up * sg * (1.0 + gate * (1.0 - sg))).astype(bf16)
        gu_ref[...] = (grad * silu).astype(bf16)

    def weight_spec(k):
        offset = (first + k * hidden_cols) // block
        return pl.BlockSpec((width, block), lambda i: (0, i + offset))

    flat = resident((rows, width), (0, 0))
    out_spec = pl.BlockSpec((rows, block), lambda i: (0, i))
    return call(
        kernel,
        (hidden_cols // block,),
        [flat, flat] + [weight_spec(k) for k in range(3)],
        [out_spec] * 3,
        [struct((rows, hidden_cols), bf16)] * 3,
        6 * rows * width * hidden_cols,
        6 * (rows + width) * hidden_cols,
    )(normed, cotangent, weights, weights, weights)


def norm_back(order, grads, weights, first, residual, cotangent, gain_row):
    rows, width = residual.shape
    count = order.shape[0]
    block = min(256, rows)
    steps = width // block
    row_steps = rows // block
    group = width // count
    parts = width // 256
    n_grads = len(grads)

    def kernel(order_ref, *refs):
        g_refs, w_refs = refs[:n_grads], refs[n_grads : 2 * n_grads]
        wo_refs, refs = refs[2 * n_grads : 2 * n_grads + parts], refs[2 * n_grads + parts :]
        r_ref, c_ref, gain_ref, gres_ref, gb_ref = refs[:5]
        gm_refs, acc = refs[5 : 5 + count], refs[5 + count]
        step = pl.program_id(0)

        @pl.when(step < steps)
        def _():
            total = dot_nt(g_refs[0][...], w_refs[0][...])
            for k in range(1, n_grads):
                total = total + dot_nt(g_refs[k][...], w_refs[k][...])
            for d in range(steps):
                @pl.when(step == d)
                def _():
                    acc[:, d * block : (d + 1) * block] = total

        @pl.when(step >= steps)
        def _():
            start = pl.multiple_of((step - steps) * block, block)
            grad = acc[pl.ds(start, block), :]
            res = r_ref[...]
            scale = lax.rsqrt(jnp.mean(res * res, axis=-1, keepdims=True) + epsilon)
            unit = res * scale
            scaled = grad * gain_ref[...]
            inner = jnp.mean(scaled * unit, axis=-1, keepdims=True)
            gres = c_ref[...].astype(f32) + scale * (scaled - unit * inner)
            gres_ref[...] = gres
            branch = gres.astype(bf16)
            gb_ref[...] = branch
            for k in range(count):
                start_k = pl.multiple_of(order_ref[k] * group, group)
                mixed = None
                for c in range(parts):
                    part = dot_nt(
                        branch[:, c * 256 : (c + 1) * 256], wo_refs[c][pl.ds(start_k, group), :]
                    )
                    mixed = part if mixed is None else mixed + part
                gm_refs[k][...] = mixed.astype(bf16)

    def row(i):
        return jnp.maximum(i - steps, 0)

    rows_spec = pl.BlockSpec((block, width), lambda i, o: (row(i), 0))
    weight_specs = [
        pl.BlockSpec(
            (block, grads[k].shape[1]),
            functools.partial(lambda c, i, o: (jnp.minimum(i, steps - 1), c), k),
        )
        for k in range(n_grads)
    ]
    hidden_cols = sum(g.shape[1] for g in grads)
    return call(
        kernel,
        (steps + row_steps,),
        [resident(g.shape, (0, 0)) for g in grads]
        + weight_specs
        + column_blocks(width, first, parts)
        + [rows_spec, rows_spec, resident((1, width), (0, 0))],
        [
            rows_spec,
            rows_spec,
        ]
        + [pl.BlockSpec((block, group), lambda i, o: (row(i), 0))] * count,
        [
            struct((rows, width), f32),
            struct((rows, width), bf16),
        ]
        + [struct((rows, group), bf16)] * count,
        2 * rows * width * hidden_cols + 2 * rows * width * width,
        2 * (rows + width) * hidden_cols + 16 * rows * width,
        scratch=[pltpu.VMEM((rows, width), f32)],
        prefetch=1,
    )(order, *grads, *[weights] * (n_grads + parts), residual, cotangent, gain_row)


def products(select, lefts, rights, parts, added=None, joined=False):
    height = lefts[0].shape[0]
    block = min(256, height)
    n = len(rights)
    sizes = [r.shape[1] // p for r, p in zip(rights, parts)]
    added = added or []
    distinct = []
    for left in lefts:
        if not any(left is d for d in distinct):
            distinct.append(left)
    which = [next(i for i, d in enumerate(distinct) if d is left) for left in lefts]
    n_left, n_add = len(distinct), len(added)

    def kernel(select_ref, *refs):
        l_refs, r_refs, outs = refs[:n_left], refs[n_left : n_left + n], refs[n_left + n + n_add :]
        for k in range(n):
            total = dot(l_refs[which[k]][...], r_refs[k][...])
            if k < n_add:
                total = total + refs[n_left + n + k][...].astype(f32)
            if joined:
                start = sum(sizes[:k])
                outs[0][:, start : start + sizes[k]] = total.astype(bf16)
            else:
                outs[k][...] = total.astype(bf16)

    def right_spec(k):
        return pl.BlockSpec(
            (rights[k].shape[0], sizes[k]),
            lambda i, s: (0, s[0] if parts[k] > 1 else 0),
            pipeline_mode=pl.Buffered(1),
        )

    out_sizes = [sum(sizes)] if joined else sizes
    out_specs = [pl.BlockSpec((block, size), lambda i, s: (i, 0)) for size in out_sizes]
    return call(
        kernel,
        (height // block,),
        [pl.BlockSpec((block, d.shape[1]), lambda i, s: (i, 0)) for d in distinct]
        + [right_spec(k) for k in range(n)]
        + out_specs[:n_add],
        out_specs,
        [struct((height, size), bf16) for size in out_sizes],
        sum(2 * height * r.shape[0] * size for r, size in zip(rights, sizes)),
        2 * height * sum(sizes) + sum(2 * r.shape[0] * size for r, size in zip(rights, sizes)),
        prefetch=1,
    )(select, *distinct, *rights, *added)


def finish(residual, hidden, weights, first):
    rows, width = residual.shape
    block = min(256, rows)
    hidden_cols = hidden.shape[1]

    def kernel(r_ref, h_ref, w_ref, out_ref):
        out_ref[...] = (r_ref[...] + dot_nt(h_ref[...], w_ref[...])).astype(bf16)

    rows_spec = pl.BlockSpec((block, width), lambda i: (i, 0))
    return call(
        kernel,
        (rows // block,),
        [
            rows_spec,
            pl.BlockSpec((block, hidden_cols), lambda i: (i, 0)),
            resident((width, hidden_cols), (0, first)),
        ],
        rows_spec,
        struct((rows, width), bf16),
        2 * rows * width * hidden_cols,
        6 * rows * width + 2 * (rows + width) * hidden_cols,
    )(residual, hidden, weights)


def project_back(order, slot, grads, weights, added=(), part=(0, 1), last=None, into=None):
    length, group = grads[0].shape
    width = weights.shape[0]
    piece = length // order.shape[0]
    rows = piece // part[1]
    block = min(512 if last is None else 256, rows)
    steps = rows // block
    before = part[0] * steps
    n = len(added)

    def kernel(order_ref, a_ref, b_ref, c_ref, w_ref, *refs):
        total = dot_nt(a_ref[...], w_ref[:, :group])
        total = total + dot_nt(b_ref[...], w_ref[:, group : 2 * group])
        total = total + dot_nt(c_ref[...], w_ref[:, 2 * group :])
        for ref in refs[:n]:
            total = total + ref[...].astype(f32)
        if last is not None:
            x_ref, gain_ref, g_ref = refs[n : n + 3]
            x = x_ref[...].astype(f32)
            scale = lax.rsqrt(jnp.mean(x * x, axis=-1, keepdims=True) + epsilon)
            unit = x * scale
            scaled = total * gain_ref[...]
            inner = jnp.mean(scaled * unit, axis=-1, keepdims=True)
            total = g_ref[...] + scale * (scaled - unit * inner)
        refs[-1][...] = total.astype(bf16)

    def rows_of(array):
        first = before if array.shape[0] == piece else 0
        return pl.BlockSpec((block, width), lambda i, order_ref: (i + first, 0))

    def grad_rows(i, order_ref):
        return (order_ref[slot] * (piece // block) + before + i, 0)

    inputs = [*grads, weights, *added]
    in_specs = [pl.BlockSpec((block, group), grad_rows)] * 3 + [resident(weights.shape, (0, 0))]
    in_specs += [rows_of(a) for a in added]
    aliases = {}
    out = struct((rows, width), bf16)
    if last is not None:
        out = struct((piece, width), bf16)
        inputs += last
        in_specs += [rows_of(last[0]), resident((1, width), (0, 0)), rows_of(last[2])]
        if into is not None:
            aliases = {1 + len(inputs): 0}
            inputs.append(into)
            in_specs.append(pl.BlockSpec(memory_space=pl.ANY))
    return call(
        kernel,
        (steps,),
        in_specs,
        rows_of(out),
        out,
        6 * rows * width * group,
        2 * rows * (2 * width + 3 * group),
        prefetch=1,
        aliases=aliases,
    )(order, *inputs)


def pair_add(a, b):
    return (a.astype(f32) + b.astype(f32)).astype(bf16)


def axis_bits(axis, first=1):
    bits = []
    while first < lax.axis_size(axis):
        bits.append(first)
        first *= 2
    return bits


def trade(array, dim, axis, bit):
    count = lax.axis_size(axis)
    mine = (lax.axis_index(axis) // bit) % 2
    keep = lax.dynamic_index_in_dim(array, mine, axis=dim, keepdims=False)
    give = lax.dynamic_index_in_dim(array, 1 - mine, axis=dim, keepdims=False)
    return keep, lax.ppermute(give, axis, [(i, i ^ bit) for i in range(count)])


def scatter_start(array, turn, halve_seq):
    count = lax.axis_size("fsdp")
    bits = axis_bits("fsdp")
    bits = bits[turn % len(bits) :] + bits[: turn % len(bits)]
    left = axis_bits("fsdp")[::-1]
    array = array.reshape((2,) * len(bits) + (array.shape[0] // count, array.shape[1]))
    todo = [("fsdp", bit) for bit in bits]
    seq = [("seq", bit) for bit in axis_bits("seq", 2)]
    if halve_seq is not None:
        todo = seq + todo if halve_seq else todo + seq
    return exchange((array, None, todo, left, halve_seq))


def exchange(state):
    array, _, todo, left, halve_seq = state
    if not todo:
        return state
    axis, bit = todo[0]
    if axis == "fsdp":
        pair = trade(array, left.index(bit), axis, bit)
        left = [b for b in left if b != bit]
    elif halve_seq:
        rows, n = array.shape[-2:]
        array = array.reshape(array.shape[:-2] + (2, rows // 2, n))
        pair = trade(array, array.ndim - 3, axis, bit)
    else:
        pair = array, swap_seq(array, bit)
    return (*pair, todo[1:], left, halve_seq)


def settle(states, done, ahead):
    keeps, done = lax.optimization_barrier(([state[0] for state in states], done))
    arrays = [
        keep if state[1] is None else pair_add(keep, state[1])
        for keep, state in zip(keeps, states)
    ]
    arrays, ahead = lax.optimization_barrier((arrays, ahead))
    return [(a, None) + state[2:] for a, state in zip(arrays, states)], done, ahead


def rows_whole(state):
    array = state[0].reshape(state[0].shape[-2:])
    if state[4]:
        for bit in axis_bits("seq", 2)[::-1]:
            first = (lax.axis_index("seq") // bit) % 2 == 0
            array = both_ways(array, swap_seq(array, bit), first).reshape(-1, array.shape[1])
    return array


def both_ways(own, other, first):
    return jnp.stack([jnp.where(first, own, other), jnp.where(first, other, own)])


def join_halves(own):
    other = swap_seq(own, 1)
    first = lax.axis_index("seq") % 2 == 0
    own, other = own.astype(f32), other.astype(f32)
    return jnp.where(first, own, other), jnp.where(first, other, own)


def body(
    tokens, cotangent, query_weight, key_weight, value_weight, output_weight, gate_weight, up_weight,
    down_weight, attention_gain, feedforward_gain, cache_keys, cache_values, memory_rows, memory_docs,
):
    seq_count, fsdp_count = lax.axis_size("seq"), lax.axis_size("fsdp")
    here = lax.axis_index("seq")
    tok_rows, width = tokens.shape
    head_local, rows_cache, head_dim = cache_keys.shape[1:]
    group = head_local * head_dim
    length = tok_rows * seq_count
    mem_block = length // memory_rows.shape[2]
    mem_count = memory_rows.shape[3]
    shard = query_weight.shape[0]
    hidden_cols = gate_weight.shape[1]
    order = here ^ jnp.arange(seq_count, dtype=jnp.int32)

    gains = spread(jnp.stack([attention_gain, feedforward_gain]), "fsdp")
    gains = gains.transpose(1, 0, 2).reshape(2, width).astype(f32)
    gain_one, gain_two = gains[0:1], gains[1:2]
    own_cols = [
        lax.dynamic_slice_in_dim(w, here * group, group, axis=1)
        for w in (query_weight, key_weight, value_weight)
    ]
    qkv = spread(jnp.concatenate(own_cols, axis=1), "fsdp").reshape(width, 3 * group)

    pieces = [tokens, swap_seq(tokens, 1), swap_seq(tokens, 2)]
    pieces.append(swap_seq(pieces[2], 1))

    ring = [(i, (i + 1) % fsdp_count) for i in range(fsdp_count)]
    partner_keys = lax.ppermute(cache_keys[0], "fsdp", ring)
    partner_values = lax.ppermute(cache_values[0], "fsdp", ring)

    part = shard // seq_count

    def own_rows(w):
        return lax.dynamic_slice_in_dim(w, here * part, part, axis=0)

    own_wd = lax.dynamic_slice_in_dim(down_weight, here * part, part, axis=1).T
    own_part = jnp.concatenate(
        [own_rows(gate_weight), own_rows(up_weight), own_wd, own_rows(output_weight)], axis=1
    )
    big = lax.all_gather(own_part, ("fsdp", "seq"), axis=0, tiled=True)

    half = head_dim // 2
    frequency = 10000.0 ** (-2.0 * jnp.arange(half, dtype=f32) / head_dim)
    angles = jnp.arange(length, dtype=jnp.int32).astype(f32)[:, None] * frequency[None, :]
    cos_half, sin_half = jnp.cos(angles), jnp.sin(angles)
    cosine = jnp.concatenate([cos_half, cos_half], axis=1)
    sine = jnp.concatenate([-sin_half, sin_half], axis=1)
    cotangent_t = cotangent.T

    chosen = memory_docs[0] * rows_cache + memory_rows[0]
    picked = retrieve(chosen, cache_keys[0], cache_values[0], 0)
    query, key, value, value_t, normed_one_t = project(
        order, pieces, qkv, gain_one, cosine, sine, head_local, head_dim
    )
    picked_keys, picked_values = retrieve(chosen, partner_keys, partner_values, rows_cache, picked)
    *attended_heads, lse = attend(
        order, query, key, value_t, picked_keys, picked_values, mem_block, mem_count, seq_count
    )

    def by_distance(stack):
        return [stack[0]] + [swap_seq(stack[k], k) for k in range(1, seq_count)]

    attended = by_distance(attended_heads)
    residual, normed_two, normed_two_t, attended_t = mix(
        order, attended, big, 3 * hidden_cols, tokens, gain_two
    )
    hid, gg, gu = gated(normed_two, cotangent, big, 0, hidden_cols)
    own_half, other_half = (here % 2)[None].astype(jnp.int32), (1 - here % 2)[None].astype(jnp.int32)
    lefts, rights = [cotangent_t, normed_two_t, normed_two_t], [hid, gg, gu]
    given = products(other_half, lefts, rights, (2, 2, 2))
    given, gg_later = lax.optimization_barrier((given, gg))
    got = [swap_seq(g, 1) for g in given]
    grad_residual, grad_branch, *grad_mixed = norm_back(
        order, [gg_later, gu], big, 3 * hidden_cols, residual, cotangent, gain_two
    )
    grad_heads = by_distance(grad_mixed)
    own = products(own_half, [*lefts, attended_t], [*rights, grad_branch], (2, 2, 2, 1), got)
    grad_heads, own = lax.optimization_barrier((grad_heads, own))
    halved = (True, False, False, False)
    sums = [scatter_start(g, turn, h) for g, turn, h in zip(own, (0, 0, 1, 2), halved)]

    blocks = lse.shape[0]
    middle = 3 * blocks // 8
    attention = (order, query, key, value, picked_keys, picked_values, mem_block, mem_count)
    *grads, rest, delta = attend_back(
        *attention, grad_heads, attended_heads, lse, cosine, sine, 0, middle
    )
    sums, _, (rest, delta) = settle(sums, (), (rest, delta))
    sums = [exchange(g) for g in sums]
    grads = attend_back(
        *attention, grad_heads, None, lse, cosine, sine, middle, blocks, (rest, delta, *grads)
    )

    zero = jnp.zeros((1,), jnp.int32)
    (qkv_grad,) = products(zero, [normed_one_t] * 3, list(grads), (1, 1, 1), joined=True)
    sums, _, (qkv_grad, grads) = settle(sums, (), (qkv_grad, grads))
    qkv_state = scatter_start(qkv_grad, 0, None)
    sums = [exchange(g) for g in sums]
    far = project_back(order, 3, grads, qkv)
    far, grads = lax.optimization_barrier((far, grads))
    near = project_back(order, 1, grads, qkv)
    far = swap_seq(far, 1)
    near, far, grads = lax.optimization_barrier((near, far, grads))
    near = swap_seq(near, 1)
    across = project_back(order, 2, grads, qkv, [far])
    (qkv_state, *sums), _, (across, hid) = settle([qkv_state, *sums], across, (across, hid))
    across = [swap_seq(half, 2) for half in jnp.split(across, 2)]
    qkv_state, *sums = [exchange(g) for g in [qkv_state, *sums]]
    result = finish(residual, hid, big, 2)
    (qkv_state, *sums), result, (near, across[0]) = settle(
        [qkv_state, *sums], result, (near, across[0])
    )
    qkv_state, *sums = [exchange(g) for g in [qkv_state, *sums]]
    last = (tokens, gain_one, grad_residual)
    grad_tokens = project_back(order, 0, grads, qkv, [near, across[0]], (0, 2), last)
    (qkv_state, *sums), _, (grad_tokens, across[1]) = settle(
        [qkv_state, *sums], grad_tokens, (grad_tokens, across[1])
    )
    while any(state[2] for state in sums):
        sums = settle([exchange(g) for g in sums], (), ())[0]
    while qkv_state[2]:
        qkv_state = settle([exchange(qkv_state)], (), ())[0][0]
    qkv_sum = qkv_state[0].reshape(qkv_state[0].shape[-2:])
    by_piece = lambda a, other, bit: both_ways(a, other, (here // bit) % 2 == 0)
    pair = by_piece(qkv_sum, swap_seq(qkv_sum, 2), 2)
    qkv_all = by_piece(pair, swap_seq(pair, 1), 1)
    sums = [rows_whole(g) for g in sums]
    grad_down, grad_gate, grad_up = (jnp.concatenate(join_halves(g), axis=1) for g in sums[:3])
    grad_out = sums[3].astype(f32) + swap_seq(sums[3], 1).astype(f32)
    grad_tokens = project_back(
        order, 0, grads, qkv, [near, across[1]], (1, 2), last, grad_tokens
    )
    qkv_all = qkv_all.swapaxes(0, 1).reshape(seq_count, shard, 3 * group).astype(f32)
    grad_q, grad_k, grad_v = (
        qkv_all[:, :, k * group : (k + 1) * group].transpose(1, 0, 2).reshape(shard, width)
        for k in range(3)
    )

    def gain_grad(gain, pairs):
        total = sum(jnp.sum(w.astype(f32) * g, axis=1) for w, g in pairs)
        return total / gain.astype(f32)

    grad_gain_one = gain_grad(
        attention_gain, [(query_weight, grad_q), (key_weight, grad_k), (value_weight, grad_v)]
    )
    grad_gain_two = gain_grad(
        feedforward_gain, [(gate_weight, grad_gate), (up_weight, grad_up)]
    )
    grad_down = grad_down.T
    return (
        result,
        grad_tokens,
        grad_q,
        grad_k,
        grad_v,
        grad_out,
        grad_gate,
        grad_up,
        grad_down,
        grad_gain_one,
        grad_gain_two,
    )


def solution(mesh):
    tok, row, col, one = P(("fsdp", "seq"), None), P("fsdp", None), P(None, "fsdp"), P("fsdp")
    cache = P("fsdp", "seq", None, None)
    return jax.shard_map(
        body,
        mesh=mesh,
        in_specs=(tok, tok) + (row,) * 6 + (col, one, one) + (cache,) * 4,
        out_specs=(tok, tok) + (row,) * 6 + (col, one, one),
        check_vma=False,
    )
```

time: 750 us -> 614 us (0.82)
  blocking collectives: 53.9 us -> 0 us
  waiting for transfers between devices: 171 us -> 122 us
  matrix products: 16 us -> 0 us
  Pallas kernels: 340 us -> 325 us
  local copies, waits for them, and re-layouts: 37.9 us -> 46.7 us
  other arithmetic: 48.7 us -> 40.9 us
    all_to_all x1 -> x0, blocking collectives: 53.9 us -> none  [body(): lax.all_to_all(grad_mixed, 'seq', 0, 0, tiled=True).reshape(length, group)]
    all_to_all x3 -> x0, waiting for transfers between devices: 51.9 us -> none  [the longest x1 38.4 us: body(): lax.all_to_all(attended_heads.reshape(seq_count, tok_rows, group), 'seq',...]
    all_to_all x6 -> x2, waiting for transfers between devices: 36.5 us -> 5 us  [spread(): return lax.all_to_all(copies, axis, split_axis=0, concat_axis=0, tiled=True)]
    ppermute x0 -> x16, starting transfers between devices: none -> 26.3 us  [trade(): lax.ppermute(give, axis, [(i, i ^ bit) for i in range(count)])]
    all_to_all x3 -> x0, starting transfers between devices: 26.2 us -> none  [the longest x2 21.6 us: over_fsdp(): lax.all_to_all(array.reshape(fsdp_count, shard, array.shape[1]), 'fsdp',...]
    ppermute x0 -> x16, waiting for transfers between devices: none -> 17.8 us  [trade(): lax.ppermute(give, axis, [(i, i ^ bit) for i in range(count)])]
    all_to_all x6 -> x2, starting transfers between devices: 26.9 us -> 9.39 us  [spread(): return lax.all_to_all(copies, axis, split_axis=0, concat_axis=0, tiled=True)]
    dot_general x2 -> x0, matrix products: 16 us -> none  [dot_nt(): lax.dot_general(a, b, (((1,), (1,)), ((), ())), preferred_element_type=f32)]
  transfers between devices with their start and end apart: 21 -> 47, of which waited for: 8 -> 15; matrix products, arithmetic and copies ran while one was open for 11% -> 11% of each run, Pallas kernels for 37% -> 45%
where the time goes in v2:
time: 614 us; the launch traced here: 605 us
  Pallas kernels  325 us (53%)
  waiting for transfers between devices  122 us (20%)
  starting transfers between devices  55.6 us (9%)
  local copies, waits for them, and re-layouts  46.7 us (8%)
  other arithmetic  40.9 us (7%)
  between operations  15.2 us (2%)
    pallas_call x2, Pallas kernels, attend_back(): call(kernel, (last - first,), in_specs + [small, table, table], out_specs...  81.9 us
    ppermute x26, waiting for transfers between devices, swap_seq(): return lax.ppermute(array, 'seq', [(i, i ^ bit) for i in range(count)])  80.8 us
    pallas_call x3, Pallas kernels, products(): call(kernel, (height // block,), [pl.BlockSpec((block, d.shape[1]), lambd...  46.1 us
    pallas_call x1, Pallas kernels, attend(): call(kernel, (count,), [rows, full, full_t, mem_rows, mem_rows], [pl.Bloc...  39.7 us
    pallas_call x2, Pallas kernels, retrieve(): call(kernel, (head_local, blocks // per), [pl.BlockSpec((1, 1, per, slots...  35.5 us
    pallas_call x5, Pallas kernels, project_back(): call(kernel, (steps,), in_specs, rows_of(out), out, 6 * rows * width * gr...  28.9 us
    pallas_call x1, Pallas kernels, norm_back(): call(kernel, (steps + row_steps,), [resident(g.shape, (0, 0)) for g in gr...  27.6 us
    ppermute x16, starting transfers between devices, trade(): lax.ppermute(give, axis, [(i, i ^ bit) for i in range(count)])  26.3 us
  transfers between devices with their start and end apart: 47, of which 15 were waited for; matrix products, arithmetic and copies ran while one was open for 11% of the time, Pallas kernels for 45%

profile of v2, /device:TPU:0, one launch (start us, length us, event | category | flops | bytes accessed | tf_op | source)
XLA Modules:
  0.0 604.8 jit_solution(17115980250527917841)
XLA Ops:
  11.6 3.0 collective-permute-start.1
  15.3 5.8 all-to-all-start.1
  21.1 2.0 collective-permute-start.3
  23.1 1.5 collective-permute-start.4
  27.5 1.3 broadcast_in_dim.9
  28.8 3.6 all-to-all-start
  33.1 17.2 %retrieve.2 = (bf16[2,4096,128]{2,1,0:T(8,128)(2,1)}, bf16[2,4096,128]{2,1,0:T(8,128)(2,1)}) custom-call(s32[2,8,4,128]{3,2,1,0:T(4,128)} %bitcast.139, bf16[2,2048,128]{2,1,0:T(8,128)(2,1)} %bitcast.8.k_ref, bf16[2,2048,128]{2,1,0:T(8,128)(2,1)} %bitcast.9.v_ref), custom_call_target="tpu_custom_call" | custom-call | flops 1288490240 | bytes 1258291 | tf_op jit(solution)/shard_map/retrieve/pallas_call | solution.py:183
  50.3 14.6 %collective-permute-done.1.refs_2_ = bf16[1024,1024]{1,0:T(8,128)(2,1)} collective-permute-done((bf16[1024,1024]{1,0:T(8,128)(2,1)}, bf16[1024,1024]{1,0:T(8,128)(2,1)}, u32[]{:S(2)}, u32[]{:S(2)}) %collective-permute-start.1) | collective-permute-done | bytes 2097184 | tf_op jit(solution)/shard_map/ppermute | solution.py:68
  64.9 7.5 %fusion = (f32[4096,64]{1,0:T(8,128)S(1)}, f32[4096,64]{1,0:T(8,128)S(1)}, f32[4096,64]{1,0:T(8,128)S(1)}) fusion(f32[64]{0:T(128)S(1)} %multiply_power_fusion, f32[4096]{0:T(1024)S(1)} %iota_convert_fusion), kind=kLoop, calls=%fused_computation.47 | loop fusion | flops 524288 | bytes 3162368 | tf_op jit(solution)/shard_map/neg | solution.py:879
  72.9 3.2 pad_maximum_fusion
  76.7 9.1 %collective-permute-done.4.v_ref = bf16[2,2048,128]{2,1,0:T(8,128)(2,1)} collective-permute-done((bf16[2,2048,128]{2,1,0:T(8,128)(2,1)}, bf16[2,2048,128]{2,1,0:T(8,128)(2,1)}, u32[]{:S(2)}, u32[]{:S(2)}) %collective-permute-start.4) | collective-permute-done | bytes 1048608 | tf_op jit(solution)/shard_map/ppermute | solution.py:861
  85.8 18.3 %retrieve.3 = (bf16[2,4096,128]{2,1,0:T(8,128)(2,1)}, bf16[2,4096,128]{2,1,0:T(8,128)(2,1)}) custom-call(s32[2,8,4,128]{3,2,1,0:T(4,128)} %bitcast.140, bf16[2,2048,128]{2,1,0:T(8,128)(2,1)} %copy-done.20, bf16[2,2048,128]{2,1,0:T(8,128)(2,1)} %collective-permute-done.4.v_ref, bf16[2,4096,128]{2,1,0:T(8,128)(2,1)} %get-tuple-element.136.refs_0_, ...), custom_call_target="tpu_custom_call" | custom-call | flops 1288490240 | bytes 1258291 | tf_op jit(solution)/shard_map/retrieve/pallas_call | solution.py:183
  104.1 3.8 all-to-all-done
  109.0 18.8 %project.1 = (bf16[2,4096,128]{2,1,0:T(8,128)(2,1)}, bf16[2,4096,128]{2,1,0:T(8,128)(2,1)}, bf16[2,4096,128]{2,1,0:T(8,128)(2,1)}, bf16[2,128,4096]{2,1,0:T(8,128)(2,1)}, bf16[1024,4096]{1,0:T(8,128)(2,1)}) custom-call(s32[4]{0:T(128)} %iota_xor_fusion.order_ref, bf16[1024,1024]{1,0:T(8,128)(2,1)} %refs_2_.3, ...), custom_call_target="tpu_custom_call" | custom-call | flops 966367616 | bytes 4089446 | tf_op jit(solution)/shard_map/project/pallas_call | solution.py:126
  127.8 39.7 %attend.1 = (bf16[1024,256]{1,0:T(8,128)(2,1)}, bf16[1024,256]{1,0:T(8,128)(2,1)}, bf16[1024,256]{1,0:T(8,128)(2,1)}, bf16[1024,256]{1,0:T(8,128)(2,1)}, f32[8,8,512]{2,1,0:T(8,128)}) custom-call(s32[4]{0:T(128)} %iota_xor_fusion.order_ref, bf16[2,4096,128]{2,1,0:T(8,128)(2,1)} %get-tuple-element.133.q_ref, bf16[2,4096,128]{2,1,0:T(8,128)(2,1)} %get-tuple-element.134.k_ref, ...), custom_call_target="tpu_custom_call" | custom-call | flops 2576980480 | bytes 1887436 | tf_op jit(solution)/shard_map/attend/pallas_call | solution.py:284
  167.6 1.8 collective-permute-start.7
  169.4 3.0 copy.70
  172.4 21.4 %collective-permute-done.6.refs_2_ = bf16[1024,256]{1,0:T(8,128)(2,1)S(1)} collective-permute-done((bf16[1024,256]{1,0:T(8,128)(2,1)}, bf16[1024,256]{1,0:T(8,128)(2,1)S(1)}, u32[]{:S(2)}, u32[]{:S(2)}) %collective-permute-start.6) | collective-permute-done | bytes 524320 | tf_op jit(solution)/shard_map/ppermute | solution.py:68
  193.8 13.0 %collective-permute-done.7.refs_3_ = bf16[1024,256]{1,0:T(8,128)(2,1)} collective-permute-done((bf16[1024,256]{1,0:T(8,128)(2,1)}, bf16[1024,256]{1,0:T(8,128)(2,1)}, u32[]{:S(2)}, u32[]{:S(2)}) %collective-permute-start.7) | collective-permute-done | bytes 524320 | tf_op jit(solution)/shard_map/ppermute | solution.py:68
  206.8 9.1 %all-gather.2.cloned.1.call-done.refs_4_.refs_5_.refs_6_.refs_7_.wg_ref.wu_ref.wd_ref.refs_2_.refs_3_.w_ref = bf16[1024,9472]{1,0:T(8,128)(2,1)} async-done(((bf16[32,9472]{1,0:T(8,128)(2,1)}), bf16[1024,9472]{1,0:T(8,128)(2,1)}) %all-gather.2.cloned.1.call-update) | async-done | bytes 19398672 | tf_op jit(solution)/shard_map/all_gather | solution.py:872
  215.9 9.6 %mix.1 = (f32[1024,1024]{1,0:T(8,128)}, bf16[1024,1024]{1,0:T(8,128)(2,1)}, bf16[1024,1024]{1,0:T(8,128)(2,1)}, bf16[1024,1024]{1,0:T(8,128)(2,1)}) custom-call(s32[4]{0:T(128)} %iota_xor_fusion.order_ref, bf16[1024,256]{1,0:T(8,128)(2,1)} %get-tuple-element.140.refs_0_.refs_4_, bf16[1024,256]{1,0:T(8,128)(2,1)} %copy-done.21, bf16[1024,256]{1,0:T(8,128)(2,1)} %copy-done.22, ...), custom_call_target="tpu_custom_call" | custom-call | flops 322122560 | bytes 2516582 | tf_op jit(solution)/shard_map/mix/pallas_call | solution.py:487
  225.5 24.9 %gated.1 = (bf16[1024,2816]{1,0:T(8,128)(2,1)}, bf16[1024,2816]{1,0:T(8,128)(2,1)}, bf16[1024,2816]{1,0:T(8,128)(2,1)}) custom-call(bf16[1024,1024]{1,0:T(8,128)(2,1)} %get-tuple-element.145.n_ref, bf16[1024,1024]{1,0:T(8,128)(2,1)} %refs_9_.1, ...), custom_call_target="tpu_custom_call" | custom-call | flops 2657510912 | bytes 5190451 | tf_op jit(solution)/shard_map/gated/pallas_call | solution.py:523
  250.4 15.3 %products.3 = (bf16[1024,1408]{1,0:T(8,128)(2,1)}, bf16[1024,1408]{1,0:T(8,128)(2,1)}, bf16[1024,1408]{1,0:T(8,128)(2,1)}) custom-call(s32[1]{0:T(128)} %bitcast.select_ref, bf16[1024,1024]{1,0:T(8,128)(2,1)} %bitcast.125, bf16[1024,1024]{1,0:T(8,128)(2,1)} %get-tuple-element.144.refs_1_, bf16[1024,2816]{1,0:T(8,128)(2,1)} %get-tuple-element.226.refs_2_.refs_3_.h_ref, ...), custom_call_target="tpu_custom_call" | custom-call | flops 1328755456 | bytes 2595225 | tf_op jit(solution)/shard_map/products/pallas_call | solution.py:654
  266.3 27.6 %norm_back.1 = (f32[1024,1024]{1,0:T(8,128)}, bf16[1024,1024]{1,0:T(8,128)(2,1)}, bf16[1024,256]{1,0:T(8,128)(2,1)}, bf16[1024,256]{1,0:T(8,128)(2,1)}, bf16[102...) custom-call(s32[4]{0:T(128)} %iota_xor_fusion.order_ref, bf16[1024,2816]{1,0:T(8,128)(2,1)} %get-tuple-element.152.refs_3_.refs_0_.refs_4_, ...), custom_call_target="tpu_custom_call" | custom-call | flops 2093796608 | bytes 5976883 | tf_op jit(solution)/shard_map/norm_back/pallas_call | solution.py:596
  296.1 19.4 %products.4 = (bf16[1024,1408]{1,0:T(8,128)(2,1)}, bf16[1024,1408]{1,0:T(8,128)(2,1)}, bf16[1024,1408]{1,0:T(8,128)(2,1)}, bf16[1024,1024]{1,0:T(8,128)(2,1)}) custom-call(s32[1]{0:T(128)} %bitcast.12.select_ref, bf16[1024,1024]{1,0:T(8,128)(2,1)} %bitcast.126, bf16[1024,1024]{1,0:T(8,128)(2,1)} %get-tuple-element.144.refs_1_, ...), custom_call_target="tpu_custom_call" | custom-call | flops 1650878080 | bytes 3224371 | tf_op jit(solution)/shard_map/products/pallas_call | solution.py:654
  315.6 4.1 collective-permute-done.9.refs_2_
  319.7 3.4 dynamic-slice_bitcast_fusion
  323.1 6.2 %collective-permute-start.16 = (bf16[2,2,128,1408]{3,2,1,0:T(8,128)(2,1)}, bf16[2,2,128,1408]{3,2,1,0:T(8,128)(2,1)}, u32[]{:S(2)}, u32[]{:S(2)}) collective-permute-start(bf16[2,2,128,1408]{3,2,1,0:T(8,128)(2,1)} %get-tuple-element.314), channel_id=1, source_target_pairs={{0,8},{4,12},{8,0},{12,4},{16,24},{20,28},{24,16},{28,20},{1,9},{5... | collective-permute-start | bytes 4325384 | tf_op jit(solution)/shard_map/ppermute | solution.py:768
  329.3 1.5 dynamic-slice_bitcast_fusion.4
  331.8 3.6 dynamic-slice_bitcast_fusion.1
  335.5 6.9 %collective-permute-start.15 = (bf16[2,2,128,1408]{3,2,1,0:T(8,128)(2,1)}, bf16[2,2,128,1408]{3,2,1,0:T(8,128)(2,1)}, u32[]{:S(2)}, u32[]{:S(2)}) collective-permute-start(bf16[2,2,128,1408]{3,2,1,0:T(8,128)(2,1)} %get-tuple-element.316), channel_id=1, source_target_pairs={{0,4},{4,0},{8,12},{12,8},{16,20},{20,16},{24,28},{28,24},{1,5},{5... | collective-permute-start | bytes 4325384 | tf_op jit(solution)/shard_map/ppermute | solution.py:768
  342.4 2.1 constant_dynamic-slice_fusion.1
  346.2 44.5 %attend_back.2 = (bf16[4096,256]{1,0:T(8,128)(2,1)}, bf16[4096,256]{1,0:T(8,128)(2,1)}, bf16[4096,256]{1,0:T(8,128)(2,1)}, f32[2,128,2560]{2,1,0:T(8,128)}, f32[8,8,512]{2,1,0:T(8,128)}) custom-call(s32[4]{0:T(128)} %iota_xor_fusion.order_ref, bf16[2,4096,128]{2,1,0:T(8,128)(2,1)} %get-tuple-element.133.q_ref, ...), custom_call_target="tpu_custom_call" | custom-call | flops 1879048192 | bytes 3774873 | tf_op jit(solution)/shard_map/attend_back/pallas_call | solution.py:444
  390.7 1.9 add_convert_fusion.3
  392.6 1.8 add_convert_fusion
  394.5 1.7 add_convert_fusion.1
  396.2 1.7 add_convert_fusion.2
  401.6 2.0 collective-permute-start.18
  403.6 37.5 %attend_back.3 = (bf16[4096,256]{1,0:T(8,128)(2,1)}, bf16[4096,256]{1,0:T(8,128)(2,1)}, bf16[4096,256]{1,0:T(8,128)(2,1)}) custom-call(s32[4]{0:T(128)} %iota_xor_fusion.order_ref, bf16[2,4096,128]{2,1,0:T(8,128)(2,1)} %get-tuple-element.133.q_ref, ...), custom_call_target="tpu_custom_call", output_to_operand_aliasing={{0}: (12, {}), {1}: (13, {}), {2}: (14, {})} | custom-call | flops 1342177280 | bytes 3774873 | tf_op jit(solution)/shard_map/attend_back/pallas_call | solution.py:444
  441.0 11.5 %products.5 = bf16[1024,768]{1,0:T(8,128)(2,1)} custom-call(s32[1]{0:T(128)} %constant.268.clone.1.select_ref, bf16[1024,4096]{1,0:T(8,128)(2,1)} %get-tuple-element.191.refs_0_, bf16[4096,256]{1,0:T(8,128)(2,1)} %get-tuple-element.212.refs_1_.a_ref, bf16[4096,256]{1,0:T(8,128)(2,1)} %get-tuple-element.213.refs_2_.b_ref, ...), custom_call_target="tpu_custom_call" | custom-call | flops 966367616 | bytes 1179648 | tf_op jit(solution)/shard_map/products/pallas_call | solution.py:654
  457.6 5.5 project_back.5
  466.5 2.7 collective-permute-start.25
  470.9 5.5 project_back.6
  478.6 5.8 project_back.7
  487.2 1.7 add_convert_fusion.16
  490.0 6.4 %collective-permute-done.23 = bf16[2,2,128,768]{3,2,1,0:T(8,128)(2,1)S(1)} collective-permute-done((bf16[2,2,128,768]{3,2,1,0:T(8,128)(2,1)}, bf16[2,2,128,768]{3,2,1,0:T(8,128)(2,1)S(1)}, u32[]{:S(2)}, u32[]{:S(2)}) %collective-permute-start.23) | collective-permute-done | bytes 786464 | tf_op jit(solution)/shard_map/ppermute | solution.py:768
  497.5 1.4 collective-permute-start.32
  499.5 1.4 collective-permute-start.30
  500.9 11.4 %finish.1 = bf16[1024,1024]{1,0:T(8,128)(2,1)} custom-call(f32[1024,1024]{1,0:T(8,128)} %get-tuple-element.153.refs_8_.r_ref, bf16[1024,2816]{1,0:T(8,128)(2,1)} %get-tuple-element.226.refs_2_.refs_3_.h_ref, bf16[1024,9472]{1,0:T(8,128)(2,1)} %all-gather.2.cloned.1.call-done.refs_4_.refs_5_.refs_6_.refs_7_.wg_ref.wu_ref.wd_ref.refs_2_.refs_3_.w_ref), custom_call_target="tpu_custom_call" | custom-call | flops 885836992 | bytes 2673868 | tf_op jit(solution)/shard_map/finish/pallas_call | solution.py:677
  513.2 2.7 fusion.1
  515.9 6.0 collective-permute-done.29
  524.1 1.8 collective-permute-start.36
  528.0 4.1 collective-permute-done.28
  532.2 16.6 %collective-permute-done.34.refs_1_ = bf16[512,1024]{1,0:T(8,128)(2,1)S(1)} collective-permute-done((bf16[512,1024]{1,0:T(8,128)(2,1)S(1)}, bf16[512,1024]{1,0:T(8,128)(2,1)S(1)}, u32[]{:S(2)}, u32[]{:S(2)}) %collective-permute-start.34) | collective-permute-done | bytes 1048608 | tf_op jit(solution)/shard_map/ppermute | solution.py:68
  549.7 1.9 collective-permute-start.35
  551.6 6.1 %project_back.8.refs_5_ = bf16[1024,1024]{1,0:T(8,128)(2,1)} custom-call(s32[4]{0:T(128)} %iota_xor_fusion.order_ref, bf16[4096,256]{1,0:T(8,128)(2,1)} %get-tuple-element.212.refs_1_.a_ref, bf16[4096,256]{1,0:T(8,128)(2,1)} %get-tuple-element.213.refs_2_.b_ref, bf16[4096,256]{1,0:T(8,128)(2,1)} %get-tuple-element.214.refs_3_.c_ref, ...), custom_call_target="tpu_custom_call" | custom-call | flops 120795952 | bytes 432537 | tf_op jit(solution)/shard_map/project_back/pallas_call | solution.py:738
  558.4 11.0 %collective-permute-done.36.refs_1_ = bf16[512,1024]{1,0:T(8,128)(2,1)} collective-permute-done((bf16[512,1024]{1,0:T(8,128)(2,1)}, bf16[512,1024]{1,0:T(8,128)(2,1)}, u32[]{:S(2)}, u32[]{:S(2)}) %collective-permute-start.36) | collective-permute-done | bytes 1048608 | tf_op jit(solution)/shard_map/ppermute | solution.py:68
  569.8 1.8 copy.80
  571.6 1.8 copy.79
  573.4 1.8 copy.78
  575.7 1.7 collective-permute-start.37
  577.4 6.1 %project_back.9 = bf16[1024,1024]{1,0:T(8,128)(2,1)} custom-call(s32[4]{0:T(128)} %iota_xor_fusion.order_ref, bf16[4096,256]{1,0:T(8,128)(2,1)} %get-tuple-element.212.refs_1_.a_ref, bf16[4096,256]{1,0:T(8,128)(2,1)} %get-tuple-element.213.refs_2_.b_ref, bf16[4096,256]{1,0:T(8,128)(2,1)} %get-tuple-element.214.refs_3_.c_ref, ...), custom_call_target="tpu_custom_call", output_to_operand_aliasing={{}: (10, {})} | custom-call | flops 120795952 | bytes 432537 | tf_op jit(solution)/shard_map/project_back/pallas_call | solution.py:738
  586.1 1.3 multiply_reduce_fusion
  589.5 1.5 copy.84
  (199 shorter events, 56.8 us)
Async XLA Ops:
  7.2 208.7 %all-gather.2.cloned.1.call-start = ((), (), s32[]{:S(2)}) async-start(), calls=%async_computation.2 | async-start | bytes 20004864 | tf_op jit(solution)/shard_map/all_gather | solution.py:872
  8.6 6.1 %copy-start.27 = (bf16[128]{0:T(256)(128)(2,1)S(1)}, bf16[128]{0:T(256)(128)(2,1)}, u32[]{:S(2)}) copy-start(bf16[128]{0:T(256)(128)(2,1)} %param.24) | copy-start | bytes 772
  8.6 6.1 %copy-start.29 = (bf16[128]{0:T(256)(128)(2,1)S(1)}, bf16[128]{0:T(256)(128)(2,1)}, u32[]{:S(2)}) copy-start(bf16[128]{0:T(256)(128)(2,1)} %param.25) | copy-start | bytes 772
  11.6 53.3 %collective-permute-start.1 = (bf16[1024,1024]{1,0:T(8,128)(2,1)}, bf16[1024,1024]{1,0:T(8,128)(2,1)}, u32[]{:S(2)}, u32[]{:S(2)}) collective-permute-start(bf16[1024,1024]{1,0:T(8,128)(2,1)} %refs_2_.3), channel_id=1, source_target_pairs={{0,2},{1,3},{2,0},{3,1},{4,6},{5,7},{6,4},{7,5},{8,10},{9,11},{10,... | collective-permute-start | bytes 6291464 | tf_op jit(solution)/shard_map/ppermute | solution.py:68
  14.6 89.4 %collective-permute-start = (bf16[1024,1024]{1,0:T(8,128)(2,1)}, bf16[1024,1024]{1,0:T(8,128)(2,1)}, u32[]{:S(2)}, u32[]{:S(2)}) collective-permute-start(bf16[1024,1024]{1,0:T(8,128)(2,1)} %refs_2_.3), channel_id=1, source_target_pairs={{0,1},{1,0},{2,3},{3,2},{4,5},{5,4},{6,7},{7,6},{8,9},{9,8},{10,11... | collective-permute-start | bytes 6291464 | tf_op jit(solution)/shard_map/ppermute | solution.py:68
  15.3 12.3 %all-to-all-start.1 = ((bf16[8,2,128]{2,1,0:T(2,128)(2,1)}), bf16[8,2,128]{2,1,0:T(2,128)(2,1)S(1)}, u32[]{:S(2)}, u32[]{:S(2)}) async-start(bf16[8,2,128]{2,1,0:T(2,128)(2,1)} %broadcast_in_dim.10), calls=%async_computation.1 | async-start | bytes 8192 | tf_op jit(solution)/shard_map/all_to_all | solution.py:74
  21.1 55.6 %collective-permute-start.3 = (bf16[2,2048,128]{2,1,0:T(8,128)(2,1)}, bf16[2,2048,128]{2,1,0:T(8,128)(2,1)S(1)}, u32[]{:S(2)}, u32[]{:S(2)}) collective-permute-start(bf16[2,2048,128]{2,1,0:T(8,128)(2,1)} %bitcast.8.k_ref), channel_id=1, source_target_pairs={{0,4},{4,8},{8,12},{12,16},{16,20},{20,24},{24,28},{28,0},{1,5},{5... | collective-permute-start | bytes 3145736 | tf_op jit(solution)/shard_map/ppermute | solution.py:860
  23.1 62.7 %collective-permute-start.4 = (bf16[2,2048,128]{2,1,0:T(8,128)(2,1)}, bf16[2,2048,128]{2,1,0:T(8,128)(2,1)}, u32[]{:S(2)}, u32[]{:S(2)}) collective-permute-start(bf16[2,2048,128]{2,1,0:T(8,128)(2,1)} %bitcast.9.v_ref), channel_id=1, source_target_pairs={{0,4},{4,8},{8,12},{12,16},{16,20},{20,24},{24,28},{28,0},{1,5},{5... | collective-permute-start | bytes 3145736 | tf_op jit(solution)/shard_map/ppermute | solution.py:861
  26.3 6.2 %copy-start.25 = (s32[1,2,32,128]{3,2,1,0:T(8,128)S(1)}, s32[1,2,32,128]{3,2,1,0:T(8,128)}, u32[]{:S(2)}) copy-start(s32[1,2,32,128]{3,2,1,0:T(8,128)} %param.28) | copy-start | bytes 98308
  26.3 6.2 %copy-start.26 = (s32[1,2,32,128]{3,2,1,0:T(8,128)S(1)}, s32[1,2,32,128]{3,2,1,0:T(8,128)}, u32[]{:S(2)}) copy-start(s32[1,2,32,128]{3,2,1,0:T(8,128)} %param.29) | copy-start | bytes 98308
  28.8 79.0 %all-to-all-start = ((bf16[8,128,768]{2,1,0:T(8,128)(2,1)}), bf16[8,128,768]{2,1,0:T(8,128)(2,1)S(1)}, u32[]{:S(2)}, u32[]{:S(2)}) async-start(bf16[8,128,768]{2,1,0:T(8,128)(2,1)} %broadcast_in_dim.9), calls=%async_computation | async-start | bytes 3145728 | tf_op jit(solution)/shard_map/all_to_all | solution.py:74
  64.9 43.0 %collective-permute-start.2 = (bf16[1024,1024]{1,0:T(8,128)(2,1)}, bf16[1024,1024]{1,0:T(8,128)(2,1)}, u32[]{:S(2)}, u32[]{:S(2)}) collective-permute-start(bf16[1024,1024]{1,0:T(8,128)(2,1)} %collective-permute-done.1.refs_2_), channel_id=1, source_target_pairs={{0,1},{1,0},{2,3},{3,2},{4,5},{5,4},{6,7},{7,6},{8,9},{9,8},{10,11... | collective-permute-start | bytes 6291464 | tf_op jit(solution)/shard_map/ppermute | solution.py:68
  76.7 9.1 %copy-start.20 = (bf16[2,2048,128]{2,1,0:T(8,128)(2,1)}, bf16[2,2048,128]{2,1,0:T(8,128)(2,1)S(1)}, u32[]{:S(2)}) copy-start(bf16[2,2048,128]{2,1,0:T(8,128)(2,1)S(1)} %collective-permute-done.3.k_ref) | copy-start | bytes 3145732
  127.8 41.6 %copy-start.3 = (bf16[1024,1024]{1,0:T(8,128)(2,1)S(1)}, bf16[1024,1024]{1,0:T(8,128)(2,1)}, u32[]{:S(2)}) copy-start(bf16[1024,1024]{1,0:T(8,128)(2,1)} %refs_9_.1) | copy-start | bytes 6291460
  167.5 4.9 collective-permute-start.5
  167.5 26.3 %collective-permute-start.6 = (bf16[1024,256]{1,0:T(8,128)(2,1)}, bf16[1024,256]{1,0:T(8,128)(2,1)S(1)}, u32[]{:S(2)}, u32[]{:S(2)}) collective-permute-start(bf16[1024,256]{1,0:T(8,128)(2,1)} %get-tuple-element.142.refs_6_), channel_id=1, source_target_pairs={{0,2},{1,3},{2,0},{3,1},{4,6},{5,7},{6,4},{7,5},{8,10},{9,11},{10,... | collective-permute-start | bytes 1572872 | tf_op jit(solution)/shard_map/ppermute | solution.py:68
  167.6 39.2 %collective-permute-start.7 = (bf16[1024,256]{1,0:T(8,128)(2,1)}, bf16[1024,256]{1,0:T(8,128)(2,1)}, u32[]{:S(2)}, u32[]{:S(2)}) collective-permute-start(bf16[1024,256]{1,0:T(8,128)(2,1)} %get-tuple-element.143.refs_7_), channel_id=1, source_target_pairs={{0,3},{1,2},{2,1},{3,0},{4,7},{5,6},{6,5},{7,4},{8,11},{9,10},{10,... | collective-permute-start | bytes 1572872 | tf_op jit(solution)/shard_map/ppermute | solution.py:68
  172.4 43.5 %copy-start.21 = (bf16[1024,256]{1,0:T(8,128)(2,1)}, bf16[1024,256]{1,0:T(8,128)(2,1)S(1)}, u32[]{:S(2)}) copy-start(bf16[1024,256]{1,0:T(8,128)(2,1)S(1)} %collective-permute-done.5.refs_1_) | copy-start | bytes 1572868
  193.8 22.1 %copy-start.22 = (bf16[1024,256]{1,0:T(8,128)(2,1)}, bf16[1024,256]{1,0:T(8,128)(2,1)S(1)}, u32[]{:S(2)}) copy-start(bf16[1024,256]{1,0:T(8,128)(2,1)S(1)} %collective-permute-done.6.refs_2_) | copy-start | bytes 1572868
  265.8 29.1 %collective-permute-start.11 = (bf16[1024,1408]{1,0:T(8,128)(2,1)}, bf16[1024,1408]{1,0:T(8,128)(2,1)}, u32[]{:S(2)}, u32[]{:S(2)}) collective-permute-start(bf16[1024,1408]{1,0:T(8,128)(2,1)} %get-tuple-element.160), channel_id=1, source_target_pairs={{0,1},{1,0},{2,3},{3,2},{4,5},{5,4},{6,7},{7,6},{8,9},{9,8},{10,11... | collective-permute-start | bytes 8650760 | tf_op jit(solution)/shard_map/ppermute | solution.py:68
  265.8 30.4 %collective-permute-start.12 = (bf16[1024,1408]{1,0:T(8,128)(2,1)}, bf16[1024,1408]{1,0:T(8,128)(2,1)}, u32[]{:S(2)}, u32[]{:S(2)}) collective-permute-start(bf16[1024,1408]{1,0:T(8,128)(2,1)} %get-tuple-element.161), channel_id=1, source_target_pairs={{0,1},{1,0},{2,3},{3,2},{4,5},{5,4},{6,7},{7,6},{8,9},{9,8},{10,11... | collective-permute-start | bytes 8650760 | tf_op jit(solution)/shard_map/ppermute | solution.py:68
  266.3 29.9 %collective-permute-start.13 = (bf16[1024,1408]{1,0:T(8,128)(2,1)}, bf16[1024,1408]{1,0:T(8,128)(2,1)}, u32[]{:S(2)}, u32[]{:S(2)}) collective-permute-start(bf16[1024,1408]{1,0:T(8,128)(2,1)} %get-tuple-element.162), channel_id=1, source_target_pairs={{0,1},{1,0},{2,3},{3,2},{4,5},{5,4},{6,7},{7,6},{8,9},{9,8},{10,11... | collective-permute-start | bytes 8650760 | tf_op jit(solution)/shard_map/ppermute | solution.py:68
  293.9 21.6 %collective-permute-start.10 = (bf16[1024,256]{1,0:T(8,128)(2,1)}, bf16[1024,256]{1,0:T(8,128)(2,1)S(1)}, u32[]{:S(2)}, u32[]{:S(2)}) collective-permute-start(bf16[1024,256]{1,0:T(8,128)(2,1)} %get-tuple-element.157), channel_id=1, source_target_pairs={{0,3},{1,2},{2,1},{3,0},{4,7},{5,6},{6,5},{7,4},{8,11},{9,10},{10,... | collective-permute-start | bytes 1572872 | tf_op jit(solution)/shard_map/ppermute | solution.py:68
  294.8 20.7 %collective-permute-start.8 = (bf16[1024,256]{1,0:T(8,128)(2,1)}, bf16[1024,256]{1,0:T(8,128)(2,1)S(1)}, u32[]{:S(2)}, u32[]{:S(2)}) collective-permute-start(bf16[1024,256]{1,0:T(8,128)(2,1)} %get-tuple-element.155), channel_id=1, source_target_pairs={{0,1},{1,0},{2,3},{3,2},{4,5},{5,4},{6,7},{7,6},{8,9},{9,8},{10,11... | collective-permute-start | bytes 1572872 | tf_op jit(solution)/shard_map/ppermute | solution.py:68
  294.9 24.8 %collective-permute-start.9 = (bf16[1024,256]{1,0:T(8,128)(2,1)}, bf16[1024,256]{1,0:T(8,128)(2,1)S(1)}, u32[]{:S(2)}, u32[]{:S(2)}) collective-permute-start(bf16[1024,256]{1,0:T(8,128)(2,1)} %get-tuple-element.156), channel_id=1, source_target_pairs={{0,2},{1,3},{2,0},{3,1},{4,6},{5,7},{6,4},{7,5},{8,10},{9,11},{10,... | collective-permute-start | bytes 1572872 | tf_op jit(solution)/shard_map/ppermute | solution.py:68
  315.5 7.6 %copy-start.7 = (bf16[1024,256]{1,0:T(8,128)(2,1)}, bf16[1024,256]{1,0:T(8,128)(2,1)S(1)}, u32[]{:S(2)}) copy-start(bf16[1024,256]{1,0:T(8,128)(2,1)S(1)} %collective-permute-done.10.refs_3_) | copy-start | bytes 1572868
  315.5 7.5 %copy-start.8 = (bf16[1024,256]{1,0:T(8,128)(2,1)}, bf16[1024,256]{1,0:T(8,128)(2,1)S(1)}, u32[]{:S(2)}) copy-start(bf16[1024,256]{1,0:T(8,128)(2,1)S(1)} %collective-permute-done.8.refs_1_) | copy-start | bytes 1572868
  319.7 3.4 copy-start.9
  319.7 9.7 %copy-start.10 = (bf16[1024,1024]{1,0:T(8,128)(2,1)S(1)}, bf16[1024,1024]{1,0:T(8,128)(2,1)}, u32[]{:S(2)}) copy-start(bf16[1024,1024]{1,0:T(8,128)(2,1)} %get-tuple-element.170) | copy-start | bytes 6291460
  323.1 69.5 %collective-permute-start.16 = (bf16[2,2,128,1408]{3,2,1,0:T(8,128)(2,1)}, bf16[2,2,128,1408]{3,2,1,0:T(8,128)(2,1)}, u32[]{:S(2)}, u32[]{:S(2)}) collective-permute-start(bf16[2,2,128,1408]{3,2,1,0:T(8,128)(2,1)} %get-tuple-element.314), channel_id=1, source_target_pairs={{0,8},{4,12},{8,0},{12,4},{16,24},{20,28},{24,16},{28,20},{1,9},{5... | collective-permute-start | bytes 4325384 | tf_op jit(solution)/shard_map/ppermute | solution.py:768
  330.9 59.8 %collective-permute-start.17 = (bf16[2,2,128,1024]{3,2,1,0:T(8,128)(2,1)}, bf16[2,2,128,1024]{3,2,1,0:T(8,128)(2,1)}, u32[]{:S(2)}, u32[]{:S(2)}) collective-permute-start(bf16[2,2,128,1024]{3,2,1,0:T(8,128)(2,1)} %get-tuple-element.322), channel_id=1, source_target_pairs={{0,16},{4,20},{8,24},{12,28},{16,0},{20,4},{24,8},{28,12},{1,17},{... | collective-permute-start | bytes 3145736 | tf_op jit(solution)/shard_map/ppermute | solution.py:768
  335.5 59.0 %collective-permute-start.15 = (bf16[2,2,128,1408]{3,2,1,0:T(8,128)(2,1)}, bf16[2,2,128,1408]{3,2,1,0:T(8,128)(2,1)}, u32[]{:S(2)}, u32[]{:S(2)}) collective-permute-start(bf16[2,2,128,1408]{3,2,1,0:T(8,128)(2,1)} %get-tuple-element.316), channel_id=1, source_target_pairs={{0,4},{4,0},{8,12},{12,8},{16,20},{20,16},{24,28},{28,24},{1,5},{5... | collective-permute-start | bytes 4325384 | tf_op jit(solution)/shard_map/ppermute | solution.py:768
  345.9 50.3 %collective-permute-start.14 = (bf16[2,2,2,64,1408]{4,3,1,0,2:T(8,128)(2,1)}, bf16[2,2,2,64,1408]{4,3,1,0,2:T(8,128)(2,1)}, u32[]{:S(2)}, u32[]{:S(2)}) collective-permute-start(bf16[2,2,2,64,1408]{4,3,1,0,2:T(8,128)(2,1)} %bitcast.117), channel_id=1, source_target_pairs={{0,2},{1,3},{2,0},{3,1},{4,6},{5,7},{6,4},{7,5},{8,10},{9,11},{10,... | collective-permute-start | bytes 4325384 | tf_op jit(solution)/shard_map/ppermute | solution.py:768
  398.1 54.4 %collective-permute-start.21 = (bf16[2,128,1024]{2,1,0:T(8,128)(2,1)S(1)}, bf16[2,128,1024]{2,1,0:T(8,128)(2,1)}, u32[]{:S(2)}, u32[]{:S(2)}) collective-permute-start(bf16[2,128,1024]{2,1,0:T(8,128)(2,1)S(1)} %get-tuple-element.335), channel_id=1, source_target_pairs={{0,4},{4,0},{8,12},{12,8},{16,20},{20,16},{24,28},{28,24},{1,5},{5... | collective-permute-start | bytes 1572872 | tf_op jit(solution)/shard_map/ppermute | solution.py:768
  399.2 54.6 %collective-permute-start.20 = (bf16[2,128,1408]{2,1,0:T(8,128)(2,1)S(1)}, bf16[2,128,1408]{2,1,0:T(8,128)(2,1)}, u32[]{:S(2)}, u32[]{:S(2)}) collective-permute-start(bf16[2,128,1408]{2,1,0:T(8,128)(2,1)S(1)} %get-tuple-element.329), channel_id=1, source_target_pairs={{0,16},{4,20},{8,24},{12,28},{16,0},{20,4},{24,8},{28,12},{1,17},{... | collective-permute-start | bytes 2162696 | tf_op jit(solution)/shard_map/ppermute | solution.py:768
  400.4 54.6 %collective-permute-start.19 = (bf16[2,128,1408]{2,1,0:T(8,128)(2,1)}, bf16[2,128,1408]{2,1,0:T(8,128)(2,1)}, u32[]{:S(2)}, u32[]{:S(2)}) collective-permute-start(bf16[2,128,1408]{2,1,0:T(8,128)(2,1)} %get-tuple-element.331), channel_id=1, source_target_pairs={{0,8},{4,12},{8,0},{12,4},{16,24},{20,28},{24,16},{28,20},{1,9},{5... | collective-permute-start | bytes 2162696 | tf_op jit(solution)/shard_map/ppermute | solution.py:768
  401.6 54.8 %collective-permute-start.18 = (bf16[2,2,64,1408]{3,2,1,0:T(8,128)(2,1)}, bf16[2,2,64,1408]{3,2,1,0:T(8,128)(2,1)}, u32[]{:S(2)}, u32[]{:S(2)}) collective-permute-start(bf16[2,2,64,1408]{3,2,1,0:T(8,128)(2,1)} %get-tuple-element.334), channel_id=1, source_target_pairs={{0,4},{4,0},{8,12},{12,8},{16,20},{20,16},{24,28},{28,24},{1,5},{5... | collective-permute-start | bytes 2162696 | tf_op jit(solution)/shard_map/ppermute | solution.py:768
  463.1 14.2 %collective-permute-start.22 = (bf16[1024,1024]{1,0:T(8,128)(2,1)}, bf16[1024,1024]{1,0:T(8,128)(2,1)}, u32[]{:S(2)}, u32[]{:S(2)}) collective-permute-start(bf16[1024,1024]{1,0:T(8,128)(2,1)} %project_back.5), channel_id=1, source_target_pairs={{0,1},{1,0},{2,3},{3,2},{4,5},{5,4},{6,7},{7,6},{8,9},{9,8},{10,11... | collective-permute-start | bytes 6291464 | tf_op jit(solution)/shard_map/ppermute | solution.py:68
  463.9 23.3 %collective-permute-start.27 = (bf16[128,1024]{1,0:T(8,128)(2,1)}, bf16[128,1024]{1,0:T(8,128)(2,1)}, u32[]{:S(2)}, u32[]{:S(2)}) collective-permute-start(bf16[128,1024]{1,0:T(8,128)(2,1)} %get-tuple-element.353), channel_id=1, source_target_pairs={{0,8},{4,12},{8,0},{12,4},{16,24},{20,28},{24,16},{28,20},{1,9},{5... | collective-permute-start | bytes 786440 | tf_op jit(solution)/shard_map/ppermute | solution.py:768
  465.3 19.1 %collective-permute-start.26 = (bf16[128,1408]{1,0:T(8,128)(2,1)S(1)}, bf16[128,1408]{1,0:T(8,128)(2,1)}, u32[]{:S(2)}, u32[]{:S(2)}) collective-permute-start(bf16[128,1408]{1,0:T(8,128)(2,1)S(1)} %get-tuple-element.347), channel_id=1, source_target_pairs={{0,4},{4,0},{8,12},{12,8},{16,20},{20,16},{24,28},{28,24},{1,5},{5... | collective-permute-start | bytes 1081352 | tf_op jit(solution)/shard_map/ppermute | solution.py:768
  466.5 19.6 %collective-permute-start.25 = (bf16[128,1408]{1,0:T(8,128)(2,1)}, bf16[128,1408]{1,0:T(8,128)(2,1)}, u32[]{:S(2)}, u32[]{:S(2)}) collective-permute-start(bf16[128,1408]{1,0:T(8,128)(2,1)} %get-tuple-element.349), channel_id=1, source_target_pairs={{0,16},{4,20},{8,24},{12,28},{16,0},{20,4},{24,8},{28,12},{1,17},{... | collective-permute-start | bytes 1081352 | tf_op jit(solution)/shard_map/ppermute | solution.py:768
  470.0 6.4 %copy-start.5 = (bf16[1024,768]{1,0:T(8,128)(2,1)S(1)}, bf16[1024,768]{1,0:T(8,128)(2,1)}, u32[]{:S(2)}) copy-start(bf16[1024,768]{1,0:T(8,128)(2,1)} %products.5) | copy-start | bytes 4718596
  470.0 19.0 %collective-permute-start.24 = (bf16[2,64,1408]{2,1,0:T(8,128)(2,1)}, bf16[2,64,1408]{2,1,0:T(8,128)(2,1)}, u32[]{:S(2)}, u32[]{:S(2)}) collective-permute-start(bf16[2,64,1408]{2,1,0:T(8,128)(2,1)} %get-tuple-element.351), channel_id=1, source_target_pairs={{0,8},{4,12},{8,0},{12,4},{16,24},{20,28},{24,16},{28,20},{1,9},{5... | collective-permute-start | bytes 1081352 | tf_op jit(solution)/shard_map/ppermute | solution.py:768
  477.3 7.1 %copy-start.11 = (bf16[128,1408]{1,0:T(8,128)(2,1)S(1)}, bf16[128,1408]{1,0:T(8,128)(2,1)}, u32[]{:S(2)}) copy-start(bf16[128,1408]{1,0:T(8,128)(2,1)} %get-tuple-element.219) | copy-start | bytes 1081348
  477.3 8.8 %copy-start.12 = (bf16[128,1408]{1,0:T(8,128)(2,1)S(1)}, bf16[128,1408]{1,0:T(8,128)(2,1)}, u32[]{:S(2)}) copy-start(bf16[128,1408]{1,0:T(8,128)(2,1)} %get-tuple-element.218) | copy-start | bytes 1081348
  477.3 19.2 %collective-permute-start.23 = (bf16[2,2,128,768]{3,2,1,0:T(8,128)(2,1)}, bf16[2,2,128,768]{3,2,1,0:T(8,128)(2,1)S(1)}, u32[]{:S(2)}, u32[]{:S(2)}) collective-permute-start(bf16[2,2,128,768]{3,2,1,0:T(8,128)(2,1)} %get-tuple-element.328), channel_id=1, source_target_pairs={{0,4},{4,0},{8,12},{12,8},{16,20},{20,16},{24,28},{28,24},{1,5},{5... | collective-permute-start | bytes 2359304 | tf_op jit(solution)/shard_map/ppermute | solution.py:768
  497.5 24.4 %collective-permute-start.32 = (bf16[128,1024]{1,0:T(8,128)(2,1)}, bf16[128,1024]{1,0:T(8,128)(2,1)S(1)}, u32[]{:S(2)}, u32[]{:S(2)}) collective-permute-start(bf16[128,1024]{1,0:T(8,128)(2,1)} %add_convert_fusion.16), channel_id=1, source_target_pairs={{0,2},{1,3},{2,0},{3,1},{4,6},{5,7},{6,4},{7,5},{8,10},{9,11},{10,... | collective-permute-start | bytes 786440 | tf_op jit(solution)/shard_map/ppermute | solution.py:68
  498.9 25.2 %collective-permute-start.31 = (bf16[128,1408]{1,0:T(8,128)(2,1)S(1)}, bf16[128,1408]{1,0:T(8,128)(2,1)}, u32[]{:S(2)}, u32[]{:S(2)}) collective-permute-start(bf16[128,1408]{1,0:T(8,128)(2,1)S(1)} %add_convert_fusion.12), channel_id=1, source_target_pairs={{0,2},{1,3},{2,0},{3,1},{4,6},{5,7},{6,4},{7,5},{8,10},{9,11},{10,... | collective-permute-start | bytes 1081352 | tf_op jit(solution)/shard_map/ppermute | solution.py:68
  499.5 27.4 %collective-permute-start.30 = (bf16[128,1408]{1,0:T(8,128)(2,1)S(1)}, bf16[128,1408]{1,0:T(8,128)(2,1)}, u32[]{:S(2)}, u32[]{:S(2)}) collective-permute-start(bf16[128,1408]{1,0:T(8,128)(2,1)S(1)} %add_convert_fusion.13), channel_id=1, source_target_pairs={{0,2},{1,3},{2,0},{3,1},{4,6},{5,7},{6,4},{7,5},{8,10},{9,11},{10,... | collective-permute-start | bytes 1081352 | tf_op jit(solution)/shard_map/ppermute | solution.py:68
  512.4 9.5 %copy-start.23 = (bf16[2,128,768]{2,1,0:T(8,128)(2,1)S(1)}, bf16[2,128,768]{2,1,0:T(8,128)(2,1)}, u32[]{:S(2)}) copy-start(bf16[2,128,768]{2,1,0:T(8,128)(2,1)} %get-tuple-element.339) | copy-start | bytes 1179652
  512.4 9.5 %collective-permute-start.29 = (bf16[64,1408]{1,0:T(8,128)(2,1)S(1)}, bf16[64,1408]{1,0:T(8,128)(2,1)S(1)}, u32[]{:S(2)}, u32[]{:S(2)}) collective-permute-start(bf16[64,1408]{1,0:T(8,128)(2,1)S(1)} %get-tuple-element.361), channel_id=1, source_target_pairs={{0,16},{4,20},{8,24},{12,28},{16,0},{20,4},{24,8},{28,12},{1,17},{... | collective-permute-start | bytes 540680 | tf_op jit(solution)/shard_map/ppermute | solution.py:768
  513.2 35.6 %collective-permute-start.33 = (bf16[1024,1024]{1,0:T(8,128)(2,1)}, bf16[1024,1024]{1,0:T(8,128)(2,1)S(1)}, u32[]{:S(2)}, u32[]{:S(2)}) collective-permute-start(bf16[1024,1024]{1,0:T(8,128)(2,1)} %project_back.6), channel_id=1, source_target_pairs={{0,1},{1,0},{2,3},{3,2},{4,5},{5,4},{6,7},{7,6},{8,9},{9,8},{10,11... | collective-permute-start | bytes 6291464 | tf_op jit(solution)/shard_map/ppermute | solution.py:68
  521.9 10.2 %collective-permute-start.28 = (bf16[2,128,768]{2,1,0:T(8,128)(2,1)S(1)}, bf16[2,128,768]{2,1,0:T(8,128)(2,1)S(1)}, u32[]{:S(2)}, u32[]{:S(2)}) collective-permute-start(bf16[2,128,768]{2,1,0:T(8,128)(2,1)S(1)} %copy-done.23), channel_id=1, source_target_pairs={{0,8},{4,12},{8,0},{12,4},{16,24},{20,28},{24,16},{28,20},{1,9},{5... | collective-permute-start | bytes 1179656 | tf_op jit(solution)/shard_map/ppermute | solution.py:768
  522.6 26.1 %collective-permute-start.34 = (bf16[512,1024]{1,0:T(8,128)(2,1)S(1)}, bf16[512,1024]{1,0:T(8,128)(2,1)S(1)}, u32[]{:S(2)}, u32[]{:S(2)}) collective-permute-start(bf16[512,1024]{1,0:T(8,128)(2,1)S(1)} %get-tuple-element.321), channel_id=1, source_target_pairs={{0,2},{1,3},{2,0},{3,1},{4,6},{5,7},{6,4},{7,5},{8,10},{9,11},{10,... | collective-permute-start | bytes 3145736 | tf_op jit(solution)/shard_map/ppermute | solution.py:68
  524.1 45.4 %collective-permute-start.36 = (bf16[512,1024]{1,0:T(8,128)(2,1)}, bf16[512,1024]{1,0:T(8,128)(2,1)}, u32[]{:S(2)}, u32[]{:S(2)}) collective-permute-start(bf16[512,1024]{1,0:T(8,128)(2,1)} %get-tuple-element.320), channel_id=1, source_target_pairs={{0,2},{1,3},{2,0},{3,1},{4,6},{5,7},{6,4},{7,5},{8,10},{9,11},{10,... | collective-permute-start | bytes 3145736 | tf_op jit(solution)/shard_map/ppermute | solution.py:68
  549.7 8.7 %collective-permute-start.35 = (bf16[128,768]{1,0:T(8,128)(2,1)S(1)}, bf16[128,768]{1,0:T(8,128)(2,1)S(1)}, u32[]{:S(2)}, u32[]{:S(2)}) collective-permute-start(bf16[128,768]{1,0:T(8,128)(2,1)S(1)} %get-tuple-element.358), channel_id=1, source_target_pairs={{0,16},{4,20},{8,24},{12,28},{16,0},{20,4},{24,8},{28,12},{1,17},{... | collective-permute-start | bytes 589832 | tf_op jit(solution)/shard_map/ppermute | solution.py:768
  569.5 14.1 %collective-permute-start.42 = (bf16[64,1408]{1,0:T(8,128)(2,1)S(1)}, bf16[64,1408]{1,0:T(8,128)(2,1)S(1)}, u32[]{:S(2)}, u32[]{:S(2)}) collective-permute-start(bf16[64,1408]{1,0:T(8,128)(2,1)S(1)} %add_convert_fusion.18), channel_id=1, source_target_pairs={{0,2},{1,3},{2,0},{3,1},{4,6},{5,7},{6,4},{7,5},{8,10},{9,11},{10,... | collective-permute-start | bytes 540680 | tf_op jit(solution)/shard_map/ppermute | solution.py:68
  575.2 10.8 %collective-permute-start.41 = (bf16[128,1408]{1,0:T(8,128)(2,1)S(1)}, bf16[128,1408]{1,0:T(8,128)(2,1)S(1)}, u32[]{:S(2)}, u32[]{:S(2)}) collective-permute-start(bf16[128,1408]{1,0:T(8,128)(2,1)S(1)} %add_convert_fusion.10), channel_id=1, source_target_pairs={{0,1},{1,0},{2,3},{3,2},{4,5},{5,4},{6,7},{7,6},{8,9},{9,8},{10,11... | collective-permute-start | bytes 1081352 | tf_op jit(solution)/shard_map/ppermute | solution.py:68
  575.2 12.2 %collective-permute-start.40 = (bf16[128,1408]{1,0:T(8,128)(2,1)S(1)}, bf16[128,1408]{1,0:T(8,128)(2,1)S(1)}, u32[]{:S(2)}, u32[]{:S(2)}) collective-permute-start(bf16[128,1408]{1,0:T(8,128)(2,1)S(1)} %add_convert_fusion.11), channel_id=1, source_target_pairs={{0,1},{1,0},{2,3},{3,2},{4,5},{5,4},{6,7},{7,6},{8,9},{9,8},{10,11... | collective-permute-start | bytes 1081352 | tf_op jit(solution)/shard_map/ppermute | solution.py:68
  575.7 8.5 %collective-permute-start.37 = (bf16[128,768]{1,0:T(8,128)(2,1)S(1)}, bf16[128,768]{1,0:T(8,128)(2,1)S(1)}, u32[]{:S(2)}, u32[]{:S(2)}) collective-permute-start(bf16[128,768]{1,0:T(8,128)(2,1)S(1)} %add_convert_fusion.17), channel_id=1, source_target_pairs={{0,2},{1,3},{2,0},{3,1},{4,6},{5,7},{6,4},{7,5},{8,10},{9,11},{10,... | collective-permute-start | bytes 589832 | tf_op jit(solution)/shard_map/ppermute | solution.py:68
  577.4 7.6 %collective-permute-start.39 = (bf16[128,1024]{1,0:T(8,128)(2,1)S(1)}, bf16[128,1024]{1,0:T(8,128)(2,1)S(1)}, u32[]{:S(2)}, u32[]{:S(2)}) collective-permute-start(bf16[128,1024]{1,0:T(8,128)(2,1)S(1)} %add_convert_fusion.15), channel_id=1, source_target_pairs={{0,1},{1,0},{2,3},{3,2},{4,5},{5,4},{6,7},{7,6},{8,9},{9,8},{10,11... | collective-permute-start | bytes 786440 | tf_op jit(solution)/shard_map/ppermute | solution.py:68
  583.6 5.7 collective-permute-start.43
  585.0 6.0 collective-permute-start.38
  593.7 3.8 copy-start.1
  (14 other events, 23.5 us)
Sparse Core Ops, SparseCore 0:
  11.7 204.1 all-gather.1

commit v3 on v2

--- a/solution.py
+++ b/solution.py
@@ -85,7 +85,7 @@
 
     def kernel(order_ref, *refs):
         xs = refs[:count]
-        w_ref, g_ref, c_ref, s_ref, q_ref, k_ref, v_ref, vt_ref, nt_ref = refs[count:]
+        w_ref, g_ref, c_ref, s_ref, q_ref, k_ref, v_ref, vt_ref, nt_ref, x_block = refs[count:]
         slot = pl.program_id(0)
 
         def run(x_ref):
@@ -106,7 +106,11 @@
                 vt_ref[head] = v.T
 
         for k in range(count):
-            pl.when(slot == k)(functools.partial(run, xs[k]))
+            @pl.when(slot == k)
+            def _():
+                x_block[...] = xs[k][...]
+
+        run(x_block)
 
     def piece_spec(k):
         return pl.BlockSpec(
@@ -139,6 +143,7 @@
         + [struct((width, length), bf16)],
         2 * length * width * cols,
         4 * length * width + 2 * length * cols + 8 * length * head_dim,
+        scratch=[pltpu.VMEM((block, width), bf16)],
         prefetch=1,
     )(order, *pieces, weights, gain_row, cosine, sine)
 
@@ -456,7 +461,7 @@
     )(order, *inputs, lse, cosine, sine)
 
 
-def mix(order, attended, weights, first, tokens, gain_row):
+def mix(order, attended, weights, first, tokens, gain_row, places):
     count = len(attended)
     rows, group = attended[0].shape
     width = tokens.shape[1]
@@ -480,7 +485,10 @@
         normed = (residual * scale * g_ref[...]).astype(bf16)
         res_ref[...] = residual
         n_ref[...] = normed
-        nt_ref[...] = normed.T
+        normed_t = normed.T
+        size = width // len(places)
+        for source, place in enumerate(places):
+            nt_ref[place * size : (place + 1) * size, :] = normed_t[source * size : (source + 1) * size]
 
     rows_spec = pl.BlockSpec((block, width), lambda i, o: (i, 0))
     cols_spec = pl.BlockSpec((width, block), lambda i, o: (0, i))
@@ -617,9 +625,9 @@
     )(order, *grads, *[weights] * (n_grads + parts), residual, cotangent, gain_row)
 
 
-def products(select, lefts, rights, parts, added=None, joined=False):
+def products(select, lefts, rights, parts, added=None, joined=False, halves=None):
     height = lefts[0].shape[0]
-    block = min(256, height)
+    block = min(256, height) if halves is None else height // 4
     n = len(rights)
     sizes = [r.shape[1] // p for r, p in zip(rights, parts)]
     added = added or []
@@ -636,7 +644,14 @@
             total = dot(l_refs[which[k]][...], r_refs[k][...])
             if k < n_add:
                 total = total + refs[n_left + n + k][...].astype(f32)
-            if joined:
+            if halves is not None:
+                step, mine = pl.program_id(0), select_ref[1 + k]
+                keep = (step // 2 if halves[k] == 0 else step % 2) == mine
+                for cond, out in ((keep, outs[k]), (jnp.logical_not(keep), outs[n + k])):
+                    @pl.when(cond)
+                    def _():
+                        out[...] = total.astype(bf16)
+            elif joined:
                 start = sum(sizes[:k])
                 outs[0][:, start : start + sizes[k]] = total.astype(bf16)
             else:
@@ -651,14 +666,27 @@
 
     out_sizes = [sum(sizes)] if joined else sizes
     out_specs = [pl.BlockSpec((block, size), lambda i, s: (i, 0)) for size in out_sizes]
+    add_specs = out_specs[:n_add]
+    out_shape = [struct((height, size), bf16) for size in out_sizes]
+    if halves is not None:
+
+        def half_spec(k, kept):
+            def index(i, s):
+                value = s[1 + k] if kept else 1 - s[1 + k]
+                return (jnp.clip(i - 2 * value, 0, 1) if halves[k] == 0 else i // 2, 0)
+
+            return pl.BlockSpec((block, sizes[k]), index)
+
+        out_specs = [half_spec(k, kept) for kept in (True, False) for k in range(n)]
+        out_shape = [struct((height // 2, size), bf16) for size in sizes] * 2
     return call(
         kernel,
         (height // block,),
         [pl.BlockSpec((block, d.shape[1]), lambda i, s: (i, 0)) for d in distinct]
         + [right_spec(k) for k in range(n)]
-        + out_specs[:n_add],
+        + add_specs,
         out_specs,
-        [struct((height, size), bf16) for size in out_sizes],
+        out_shape,
         sum(2 * height * r.shape[0] * size for r, size in zip(rights, sizes)),
         2 * height * sum(sizes) + sum(2 * r.shape[0] * size for r, size in zip(rights, sizes)),
         prefetch=1,
@@ -768,34 +796,38 @@
     return keep, lax.ppermute(give, axis, [(i, i ^ bit) for i in range(count)])
 
 
-def scatter_start(array, turn, halve_seq):
+def scatter_start(array, turn, halve_at):
     count = lax.axis_size("fsdp")
     bits = axis_bits("fsdp")
     bits = bits[turn % len(bits) :] + bits[: turn % len(bits)]
     left = axis_bits("fsdp")[::-1]
     array = array.reshape((2,) * len(bits) + (array.shape[0] // count, array.shape[1]))
     todo = [("fsdp", bit) for bit in bits]
-    seq = [("seq", bit) for bit in axis_bits("seq", 2)]
-    if halve_seq is not None:
-        todo = seq + todo if halve_seq else todo + seq
-    return exchange((array, None, todo, left, halve_seq))
+    if halve_at is not None:
+        todo[halve_at:halve_at] = [("seq", bit) for bit in axis_bits("seq", 2)]
+    return exchange((array, None, todo, left))
+
+
+def scatter_from(keep, give, axis, bit, left, todo, rows):
+    count = lax.axis_size(axis)
+    got = lax.ppermute(give, axis, [(i, i ^ bit) for i in range(count)])
+    shape = (2,) * len(left) + (rows, keep.shape[1])
+    return keep.reshape(shape), got.reshape(shape), todo, left
 
 
 def exchange(state):
-    array, _, todo, left, halve_seq = state
+    array, _, todo, left = state
     if not todo:
         return state
     axis, bit = todo[0]
     if axis == "fsdp":
         pair = trade(array, left.index(bit), axis, bit)
         left = [b for b in left if b != bit]
-    elif halve_seq:
+    else:
         rows, n = array.shape[-2:]
         array = array.reshape(array.shape[:-2] + (2, rows // 2, n))
         pair = trade(array, array.ndim - 3, axis, bit)
-    else:
-        pair = array, swap_seq(array, bit)
-    return (*pair, todo[1:], left, halve_seq)
+    return (*pair, todo[1:], left)
 
 
 def settle(states, done, ahead):
@@ -808,24 +840,91 @@
     return [(a, None) + state[2:] for a, state in zip(arrays, states)], done, ahead
 
 
-def rows_whole(state):
-    array = state[0].reshape(state[0].shape[-2:])
-    if state[4]:
-        for bit in axis_bits("seq", 2)[::-1]:
-            first = (lax.axis_index("seq") // bit) % 2 == 0
-            array = both_ways(array, swap_seq(array, bit), first).reshape(-1, array.shape[1])
-    return array
+def rows_whole(array, other):
+    first = (lax.axis_index("seq") // 2) % 2 == 0
+    return both_ways(array, other, first).reshape(-1, array.shape[1])
+
+
+def last_rows(state):
+    return state[0].reshape(state[0].shape[-2:])
 
 
 def both_ways(own, other, first):
     return jnp.stack([jnp.where(first, own, other), jnp.where(first, other, own)])
 
 
-def join_halves(own):
-    other = swap_seq(own, 1)
-    first = lax.axis_index("seq") % 2 == 0
-    own, other = own.astype(f32), other.astype(f32)
-    return jnp.where(first, own, other), jnp.where(first, other, own)
+def feedforward_ends(half, joined, other, gate_weight, up_weight, gain):
+    rows, hidden_cols = gate_weight.shape
+    width = joined.shape[1] - 3 * (hidden_cols // 2)
+    size = hidden_cols // 2
+
+    def kernel(half_ref, j_ref, o_ref, wg_ref, wu_ref, gain_ref, g_ref, u_ref, d_ref, out_ref, gg_ref):
+        def both(k):
+            columns = slice(k * size, (k + 1) * size)
+            own, far = j_ref[:, columns].astype(f32), o_ref[:, columns].astype(f32)
+            lower = half_ref[0] == 0
+            return jnp.concatenate(
+                [jnp.where(lower, own, far), jnp.where(lower, far, own)], axis=1
+            )
+
+        down, gate, up = both(0), both(1), both(2)
+        g_ref[...] = gate
+        u_ref[...] = up
+        d_ref[...] = down.T
+        out_ref[...] = j_ref[:, 3 * size :].astype(f32) + o_ref[:, 3 * size :].astype(f32)
+        total = jnp.sum(
+            wg_ref[...].astype(f32) * gate + wu_ref[...].astype(f32) * up, axis=1, keepdims=True
+        )
+        gg_ref[...] = total / gain_ref[...]
+
+    whole = lambda shape: pl.BlockSpec(shape, lambda i, h: (0, 0))
+    shapes = [(rows, hidden_cols)] * 2 + [(hidden_cols, rows), (rows, width), (rows, 1)]
+    *ends, gain_grad = call(
+        kernel,
+        (1,),
+        [whole(joined.shape)] * 2 + [whole(gate_weight.shape)] * 2 + [whole((rows, 1))],
+        [whole(shape) for shape in shapes],
+        [struct(shape, f32) for shape in shapes],
+        4 * rows * hidden_cols,
+        20 * rows * hidden_cols,
+        prefetch=1,
+    )(half, joined, other, gate_weight, up_weight, gain.astype(f32)[:, None])
+    return *ends, gain_grad[:, 0]
+
+
+def projection_ends(order, pieces, weights, gain):
+    rows, width = weights[0].shape
+    count = len(pieces)
+    group = width // count
+
+    def kernel(order_ref, *refs):
+        p_refs, refs = refs[:count], refs[count:]
+        w_refs, gain_ref, outs, gg_ref = refs[:3], refs[3], refs[4:7], refs[7]
+        for k in range(count):
+            start = pl.multiple_of(order_ref[k] * group, group)
+            for j in range(3):
+                outs[j][:, pl.ds(start, group)] = p_refs[k][
+                    :, j * group : (j + 1) * group
+                ].astype(f32)
+        total = None
+        for j in range(3):
+            part = jnp.sum(w_refs[j][...].astype(f32) * outs[j][...], axis=1, keepdims=True)
+            total = part if total is None else total + part
+        gg_ref[...] = total / gain_ref[...]
+
+    whole = lambda shape: pl.BlockSpec(shape, lambda i, o: (0, 0))
+    shapes = [(rows, width)] * 3 + [(rows, 1)]
+    *ends, gain_grad = call(
+        kernel,
+        (1,),
+        [whole(pieces[0].shape)] * count + [whole((rows, width))] * 3 + [whole((rows, 1))],
+        [whole(shape) for shape in shapes],
+        [struct(shape, f32) for shape in shapes],
+        6 * rows * width,
+        24 * rows * width,
+        prefetch=1,
+    )(order, *pieces, *weights, gain.astype(f32)[:, None])
+    return *ends, gain_grad[:, 0]
 
 
 def body(
@@ -877,7 +976,11 @@
     cos_half, sin_half = jnp.cos(angles), jnp.sin(angles)
     cosine = jnp.concatenate([cos_half, cos_half], axis=1)
     sine = jnp.concatenate([-sin_half, sin_half], axis=1)
-    cotangent_t = cotangent.T
+    cotangent_t = cotangent.T.reshape(fsdp_count, 2, shard // 2, tok_rows)
+    cotangent_t = cotangent_t.swapaxes(0, 1).reshape(width, tok_rows)
+    places = [
+        (f % 4 // 2 + f % 2 * 2) * (fsdp_count // 4) + f // 4 for f in range(fsdp_count)
+    ]
 
     chosen = memory_docs[0] * rows_cache + memory_rows[0]
     picked = retrieve(chosen, cache_keys[0], cache_values[0], 0)
@@ -894,7 +997,7 @@
 
     attended = by_distance(attended_heads)
     residual, normed_two, normed_two_t, attended_t = mix(
-        order, attended, big, 3 * hidden_cols, tokens, gain_two
+        order, attended, big, 3 * hidden_cols, tokens, gain_two, places
     )
     hid, gg, gu = gated(normed_two, cotangent, big, 0, hidden_cols)
     own_half, other_half = (here % 2)[None].astype(jnp.int32), (1 - here % 2)[None].astype(jnp.int32)
@@ -906,10 +1009,32 @@
         order, [gg_later, gu], big, 3 * hidden_cols, residual, cotangent, gain_two
     )
     grad_heads = by_distance(grad_mixed)
-    own = products(own_half, [*lefts, attended_t], [*rights, grad_branch], (2, 2, 2, 1), got)
+    bits, upper = axis_bits("fsdp"), axis_bits("seq", 2)
+    firsts = (("seq", upper[0]), ("fsdp", bits[0]), ("fsdp", bits[1]), ("fsdp", bits[-1]))
+    mine = [(lax.axis_index(axis) // bit) % 2 for axis, bit in firsts]
+    select = jnp.stack([here % 2, *mine]).astype(jnp.int32)
+    own = products(
+        select, [*lefts, attended_t], [*rights, grad_branch], (2, 2, 2, 1), got, halves=(0, 0, 1, 0)
+    )
     grad_heads, own = lax.optimization_barrier((grad_heads, own))
-    halved = (True, False, False, False)
-    sums = [scatter_start(g, turn, h) for g, turn, h in zip(own, (0, 0, 1, 2), halved)]
+    down = bits[::-1]
+    over = lambda *picks: [("fsdp", b) if b else ("seq", upper[0]) for b in picks]
+    sums = [
+        scatter_from(keep, give, axis, bit, left, todo, rows)
+        for keep, give, (axis, bit), left, todo, rows in zip(
+            own[:4],
+            own[4:],
+            firsts,
+            (down, [bits[1], *down[: -2]], [bits[0], *down[: -2]], down[1:]),
+            (
+                over(*bits),
+                over(0, *bits[1:]),
+                over(0, bits[0], *bits[2:]),
+                over(*bits[:-1], 0),
+            ),
+            (shard // 2, shard, shard, shard),
+        )
+    ]
 
     blocks = lse.shape[0]
     middle = 3 * blocks // 8
@@ -924,61 +1049,55 @@
     )
 
     zero = jnp.zeros((1,), jnp.int32)
+    sums, _, grads = settle(sums, (), grads)
+    sums = [exchange(g) for g in sums]
+    far_part = project_back(order, 3, grads, qkv)
+    far = swap_seq(far_part, 1)
+    far_part, grads = lax.optimization_barrier((far_part, grads))
+    near_part = project_back(order, 1, grads, qkv)
+    near = swap_seq(near_part, 1)
+    far, near_part, grads = lax.optimization_barrier((far, near_part, grads))
+    half = project_back(order, 2, grads, qkv, [far], (0, 2))
+    across = [swap_seq(half, 2)]
+    half, grads = lax.optimization_barrier((half, grads))
+    half = project_back(order, 2, grads, qkv, [far], (1, 2))
+    across.append(swap_seq(half, 2))
+    half, grads = lax.optimization_barrier((half, grads))
     (qkv_grad,) = products(zero, [normed_one_t] * 3, list(grads), (1, 1, 1), joined=True)
-    sums, _, (qkv_grad, grads) = settle(sums, (), (qkv_grad, grads))
     qkv_state = scatter_start(qkv_grad, 0, None)
+    across[0], qkv_grad, grads = lax.optimization_barrier((across[0], qkv_grad, grads))
+    sums, across[0], near = settle(sums, across[0], near)
     sums = [exchange(g) for g in sums]
-    far = project_back(order, 3, grads, qkv)
-    far, grads = lax.optimization_barrier((far, grads))
-    near = project_back(order, 1, grads, qkv)
-    far = swap_seq(far, 1)
-    near, far, grads = lax.optimization_barrier((near, far, grads))
-    near = swap_seq(near, 1)
-    across = project_back(order, 2, grads, qkv, [far])
-    (qkv_state, *sums), _, (across, hid) = settle([qkv_state, *sums], across, (across, hid))
-    across = [swap_seq(half, 2) for half in jnp.split(across, 2)]
-    qkv_state, *sums = [exchange(g) for g in [qkv_state, *sums]]
-    result = finish(residual, hid, big, 2)
-    (qkv_state, *sums), result, (near, across[0]) = settle(
-        [qkv_state, *sums], result, (near, across[0])
-    )
-    qkv_state, *sums = [exchange(g) for g in [qkv_state, *sums]]
+    (qkv_state, *sums), _, near = settle([qkv_state, *sums], (), near)
+    while any(state[2] for state in sums):
+        sums = settle([exchange(g) for g in sums], (), ())[0]
+    qkv_state = exchange(qkv_state)
+    joined = jnp.concatenate([last_rows(state) for state in sums], axis=1)
+    lower = swap_seq(joined, upper[0])
     last = (tokens, gain_one, grad_residual)
     grad_tokens = project_back(order, 0, grads, qkv, [near, across[0]], (0, 2), last)
-    (qkv_state, *sums), _, (grad_tokens, across[1]) = settle(
-        [qkv_state, *sums], grad_tokens, (grad_tokens, across[1])
-    )
-    while any(state[2] for state in sums):
-        sums = settle([exchange(g) for g in sums], (), ())[0]
+    (qkv_state,), grad_tokens, (hid, across[1]) = settle(
+        [qkv_state], grad_tokens, (hid, across[1])
+    )
+    qkv_state = exchange(qkv_state)
+    result = finish(residual, hid, big, 2)
+    grad_tokens = project_back(
+        order, 0, grads, qkv, [near, across[1]], (1, 2), last, grad_tokens
+    )
+    joined, grad_tokens = lax.optimization_barrier((joined, grad_tokens))
+    joined = rows_whole(joined, lower)
+    other = swap_seq(joined, 1)
+    (qkv_state,), _, _ = settle([qkv_state], (result, grad_tokens), ())
     while qkv_state[2]:
         qkv_state = settle([exchange(qkv_state)], (), ())[0][0]
-    qkv_sum = qkv_state[0].reshape(qkv_state[0].shape[-2:])
-    by_piece = lambda a, other, bit: both_ways(a, other, (here // bit) % 2 == 0)
-    pair = by_piece(qkv_sum, swap_seq(qkv_sum, 2), 2)
-    qkv_all = by_piece(pair, swap_seq(pair, 1), 1)
-    sums = [rows_whole(g) for g in sums]
-    grad_down, grad_gate, grad_up = (jnp.concatenate(join_halves(g), axis=1) for g in sums[:3])
-    grad_out = sums[3].astype(f32) + swap_seq(sums[3], 1).astype(f32)
-    grad_tokens = project_back(
-        order, 0, grads, qkv, [near, across[1]], (1, 2), last, grad_tokens
-    )
-    qkv_all = qkv_all.swapaxes(0, 1).reshape(seq_count, shard, 3 * group).astype(f32)
-    grad_q, grad_k, grad_v = (
-        qkv_all[:, :, k * group : (k + 1) * group].transpose(1, 0, 2).reshape(shard, width)
-        for k in range(3)
-    )
-
-    def gain_grad(gain, pairs):
-        total = sum(jnp.sum(w.astype(f32) * g, axis=1) for w, g in pairs)
-        return total / gain.astype(f32)
-
-    grad_gain_one = gain_grad(
-        attention_gain, [(query_weight, grad_q), (key_weight, grad_k), (value_weight, grad_v)]
-    )
-    grad_gain_two = gain_grad(
-        feedforward_gain, [(gate_weight, grad_gate), (up_weight, grad_up)]
-    )
-    grad_down = grad_down.T
+    qkv_pieces = by_distance([last_rows(qkv_state)] * seq_count)
+    grad_gate, grad_up, grad_down, grad_out, grad_gain_two = feedforward_ends(
+        own_half, joined, other, gate_weight, up_weight, feedforward_gain
+    )
+    qkv_pieces[0], grad_out = lax.optimization_barrier((qkv_pieces[0], grad_out))
+    grad_q, grad_k, grad_v, grad_gain_one = projection_ends(
+        order, qkv_pieces, (query_weight, key_weight, value_weight), attention_gain
+    )
     return (
         result,
         grad_tokens,

time: 614 us -> 587 us (0.956)
  waiting for transfers between devices: 122 us -> 101 us
  local copies, waits for them, and re-layouts: 46.7 us -> 28.1 us
  Pallas kernels: 325 us -> 343 us
  other arithmetic: 40.9 us -> 28.2 us
    ppermute x26 -> x21, waiting for transfers between devices: 80.8 us -> 48.4 us  [swap_seq(): return lax.ppermute(array, 'seq', [(i, i ^ bit) for i in range(count)])]
    ppermute x0 -> x4, starting transfers between devices: none -> 15.1 us  [scatter_from(): got = lax.ppermute(give, axis, [(i, i ^ bit) for i in range(count)])]
    ppermute x16 -> x15, waiting for transfers between devices: 17.8 us -> 29.7 us  [trade(): lax.ppermute(give, axis, [(i, i ^ bit) for i in range(count)])]
    unnamed x71 -> x57, local copies, waits for them, and re-layouts: 17.4 us -> 7.05 us
    squeeze x12 -> x10, local copies, waits for them, and re-layouts: 13.9 us -> 4.91 us  [trade(): give = lax.dynamic_index_in_dim(array, 1 - mine, axis=dim, keepdims=False)]
    convert_element_type x19, other arithmetic: 20.8 us -> 12.3 us  [pair_add(): return (a.astype(f32) + b.astype(f32)).astype(bf16)]
    pallas_call x0 -> x2, Pallas kernels: none -> 8.33 us  [the longest x1 5.06 us: feedforward_ends(): call(kernel, (1,), [whole(joined.shape)] * 2 + [whole(gate_weight.shape)]...]
    pallas_call x3, Pallas kernels: 46.1 us -> 52.4 us  [products(): call(kernel, (height // block,), [pl.BlockSpec((block, d.shape[1]), lambd...]
  transfers between devices with their start and end apart: 47 -> 45, of which waited for: 15 -> 15; matrix products, arithmetic and copies ran while one was open for 11% -> 7% of each run, Pallas kernels for 45% -> 49%
where the time goes in v3:
time: 587 us; the launch traced here: 577 us
  Pallas kernels  343 us (58%)
  waiting for transfers between devices  101 us (17%)
  starting transfers between devices  61.2 us (10%)
  other arithmetic  28.2 us (5%)
  local copies, waits for them, and re-layouts  28.1 us (5%)
  between operations  15.2 us (3%)
    pallas_call x2, Pallas kernels, attend_back(): call(kernel, (last - first,), in_specs + [small, table, table], out_specs...  82.2 us
    pallas_call x3, Pallas kernels, products(): call(kernel, (height // block,), [pl.BlockSpec((block, d.shape[1]), lambd...  52.4 us
    ppermute x21, waiting for transfers between devices, swap_seq(): return lax.ppermute(array, 'seq', [(i, i ^ bit) for i in range(count)])  48.4 us
    pallas_call x1, Pallas kernels, attend(): call(kernel, (count,), [rows, full, full_t, mem_rows, mem_rows], [pl.Bloc...  39.8 us
    pallas_call x2, Pallas kernels, retrieve(): call(kernel, (head_local, blocks // per), [pl.BlockSpec((1, 1, per, slots...  35.5 us
    pallas_call x6, Pallas kernels, project_back(): call(kernel, (steps,), in_specs, rows_of(out), out, 6 * rows * width * gr...  32.3 us
    ppermute x15, waiting for transfers between devices, trade(): lax.ppermute(give, axis, [(i, i ^ bit) for i in range(count)])  29.7 us
    pallas_call x1, Pallas kernels, norm_back(): call(kernel, (steps + row_steps,), [resident(g.shape, (0, 0)) for g in gr...  27.7 us
  transfers between devices with their start and end apart: 45, of which 15 were waited for; matrix products, arithmetic and copies ran while one was open for 7% of the time, Pallas kernels for 49%

profile of v3, /device:TPU:0, one launch (start us, length us, event | category | flops | bytes accessed | tf_op | source)
XLA Modules:
  0.0 576.7 jit_solution(4403050864299918557)
XLA Ops:
  11.6 3.0 collective-permute-start.1
  15.3 5.8 %all-to-all-start.1 = ((bf16[8,2,128]{2,1,0:T(2,128)(2,1)}), bf16[8,2,128]{2,1,0:T(2,128)(2,1)S(1)}, u32[]{:S(2)}, u32[]{:S(2)}) async-start(bf16[8,2,128]{2,1,0:T(2,128)(2,1)} %broadcast_in_dim.29), calls=%async_computation.1 | async-start | bytes 8192 | tf_op jit(solution)/shard_map/all_to_all | solution.py:74
  21.1 2.0 collective-permute-start.3
  23.1 1.5 collective-permute-start.4
  27.5 1.3 broadcast_in_dim.28
  28.9 3.6 all-to-all-start
  33.1 17.2 %retrieve.2 = (bf16[2,4096,128]{2,1,0:T(8,128)(2,1)}, bf16[2,4096,128]{2,1,0:T(8,128)(2,1)}) custom-call(s32[2,8,4,128]{3,2,1,0:T(4,128)} %bitcast.138, bf16[2,2048,128]{2,1,0:T(8,128)(2,1)} %bitcast.6.k_ref, bf16[2,2048,128]{2,1,0:T(8,128)(2,1)} %bitcast.7.v_ref), custom_call_target="tpu_custom_call" | custom-call | flops 1288490240 | bytes 1258291 | tf_op jit(solution)/shard_map/retrieve/pallas_call | solution.py:188
  50.3 14.6 %collective-permute-done.1.refs_2_ = bf16[1024,1024]{1,0:T(8,128)(2,1)} collective-permute-done((bf16[1024,1024]{1,0:T(8,128)(2,1)}, bf16[1024,1024]{1,0:T(8,128)(2,1)}, u32[]{:S(2)}, u32[]{:S(2)}) %collective-permute-start.1) | collective-permute-done | bytes 2097184 | tf_op jit(solution)/shard_map/ppermute | solution.py:68
  64.9 7.5 %fusion.4 = (f32[4096,64]{1,0:T(8,128)S(1)}, f32[4096,64]{1,0:T(8,128)S(1)}, f32[4096,64]{1,0:T(8,128)S(1)}) fusion(f32[64]{0:T(128)S(1)} %multiply_power_fusion, f32[4096]{0:T(1024)S(1)} %iota_convert_fusion), kind=kLoop, calls=%fused_computation.32 | loop fusion | flops 524288 | bytes 3162368 | tf_op jit(solution)/shard_map/neg | solution.py:978
  72.9 3.2 pad_maximum_fusion
  76.7 9.1 %collective-permute-done.4.v_ref = bf16[2,2048,128]{2,1,0:T(8,128)(2,1)} collective-permute-done((bf16[2,2048,128]{2,1,0:T(8,128)(2,1)}, bf16[2,2048,128]{2,1,0:T(8,128)(2,1)}, u32[]{:S(2)}, u32[]{:S(2)}) %collective-permute-start.4) | collective-permute-done | bytes 1048608 | tf_op jit(solution)/shard_map/ppermute | solution.py:960
  85.8 18.3 %retrieve.3 = (bf16[2,4096,128]{2,1,0:T(8,128)(2,1)}, bf16[2,4096,128]{2,1,0:T(8,128)(2,1)}) custom-call(s32[2,8,4,128]{3,2,1,0:T(4,128)} %bitcast.139, bf16[2,2048,128]{2,1,0:T(8,128)(2,1)} %copy-done.16, bf16[2,2048,128]{2,1,0:T(8,128)(2,1)} %collective-permute-done.4.v_ref, bf16[2,4096,128]{2,1,0:T(8,128)(2,1)} %get-tuple-element.154.refs_0_, ...), custom_call_target="tpu_custom_call" | custom-call | flops 1288490240 | bytes 1258291 | tf_op jit(solution)/shard_map/retrieve/pallas_call | solution.py:188
  104.1 3.8 all-to-all-done
  109.1 19.0 %project.1 = (bf16[2,4096,128]{2,1,0:T(8,128)(2,1)}, bf16[2,4096,128]{2,1,0:T(8,128)(2,1)}, bf16[2,4096,128]{2,1,0:T(8,128)(2,1)}, bf16[2,128,4096]{2,1,0:T(8,128)(2,1)}, bf16[1024,4096]{1,0:T(8,128)(2,1)}) custom-call(s32[4]{0:T(128)} %iota_xor_fusion.order_ref, bf16[1024,1024]{1,0:T(8,128)(2,1)} %refs_2_.3, ...), custom_call_target="tpu_custom_call" | custom-call | flops 966367616 | bytes 4089446 | tf_op jit(solution)/shard_map/project/pallas_call | solution.py:130
  128.1 39.8 %attend.1 = (bf16[1024,256]{1,0:T(8,128)(2,1)}, bf16[1024,256]{1,0:T(8,128)(2,1)}, bf16[1024,256]{1,0:T(8,128)(2,1)}, bf16[1024,256]{1,0:T(8,128)(2,1)}, f32[8,8,512]{2,1,0:T(8,128)}) custom-call(s32[4]{0:T(128)} %iota_xor_fusion.order_ref, bf16[2,4096,128]{2,1,0:T(8,128)(2,1)} %get-tuple-element.151.q_ref, bf16[2,4096,128]{2,1,0:T(8,128)(2,1)} %get-tuple-element.152.k_ref, ...), custom_call_target="tpu_custom_call" | custom-call | flops 2576980480 | bytes 1887436 | tf_op jit(solution)/shard_map/attend/pallas_call | solution.py:289
  168.0 1.8 collective-permute-start.7
  169.8 2.6 copy.42
  172.4 3.2 copy.43
  175.5 18.7 %collective-permute-done.6.refs_2_ = bf16[1024,256]{1,0:T(8,128)(2,1)S(1)} collective-permute-done((bf16[1024,256]{1,0:T(8,128)(2,1)}, bf16[1024,256]{1,0:T(8,128)(2,1)S(1)}, u32[]{:S(2)}, u32[]{:S(2)}) %collective-permute-start.6) | collective-permute-done | bytes 524320 | tf_op jit(solution)/shard_map/ppermute | solution.py:68
  194.2 12.6 %collective-permute-done.7.refs_3_ = bf16[1024,256]{1,0:T(8,128)(2,1)} collective-permute-done((bf16[1024,256]{1,0:T(8,128)(2,1)}, bf16[1024,256]{1,0:T(8,128)(2,1)}, u32[]{:S(2)}, u32[]{:S(2)}) %collective-permute-start.7) | collective-permute-done | bytes 524320 | tf_op jit(solution)/shard_map/ppermute | solution.py:68
  206.8 8.7 %all-gather.2.cloned.1.call-done.refs_4_.refs_5_.refs_6_.refs_7_.wg_ref.wu_ref.wd_ref.refs_2_.refs_3_.w_ref = bf16[1024,9472]{1,0:T(8,128)(2,1)} async-done(((bf16[32,9472]{1,0:T(8,128)(2,1)}), bf16[1024,9472]{1,0:T(8,128)(2,1)}) %all-gather.2.cloned.1.call-update) | async-done | bytes 19398672 | tf_op jit(solution)/shard_map/all_gather | solution.py:971
  215.5 9.6 %mix.1 = (f32[1024,1024]{1,0:T(8,128)}, bf16[1024,1024]{1,0:T(8,128)(2,1)}, bf16[1024,1024]{1,0:T(8,128)(2,1)}, bf16[1024,1024]{1,0:T(8,128)(2,1)}) custom-call(s32[4]{0:T(128)} %iota_xor_fusion.order_ref, bf16[1024,256]{1,0:T(8,128)(2,1)} %get-tuple-element.158.refs_0_.refs_4_, bf16[1024,256]{1,0:T(8,128)(2,1)} %copy-done.17, bf16[1024,256]{1,0:T(8,128)(2,1)} %copy-done.18, ...), custom_call_target="tpu_custom_call" | custom-call | flops 322122560 | bytes 2516582 | tf_op jit(solution)/shard_map/mix/pallas_call | solution.py:495
  225.1 24.9 %gated.1 = (bf16[1024,2816]{1,0:T(8,128)(2,1)}, bf16[1024,2816]{1,0:T(8,128)(2,1)}, bf16[1024,2816]{1,0:T(8,128)(2,1)}) custom-call(bf16[1024,1024]{1,0:T(8,128)(2,1)} %get-tuple-element.165.n_ref, bf16[1024,1024]{1,0:T(8,128)(2,1)} %refs_9_.1, ...), custom_call_target="tpu_custom_call" | custom-call | flops 2657510912 | bytes 5190451 | tf_op jit(solution)/shard_map/gated/pallas_call | solution.py:531
  250.1 15.7 %products.3 = (bf16[1024,1408]{1,0:T(8,128)(2,1)}, bf16[1024,1408]{1,0:T(8,128)(2,1)}, bf16[1024,1408]{1,0:T(8,128)(2,1)}) custom-call(s32[1]{0:T(128)} %bitcast.10.select_ref, bf16[1024,1024]{1,0:T(8,128)(2,1)} %bitcast.123, bf16[1024,1024]{1,0:T(8,128)(2,1)} %get-tuple-element.164.refs_1_, bf16[1024,2816]{1,0:T(8,128)(2,1)} %get-tuple-element.269.refs_2_.refs_3_.h_ref, ...), custom_call_target="tpu_custom_call" | custom-call | flops 1328755456 | bytes 2595225 | tf_op jit(solution)/shard_map/products/pallas_call | solution.py:682
  266.4 27.7 %norm_back.1 = (f32[1024,1024]{1,0:T(8,128)}, bf16[1024,1024]{1,0:T(8,128)(2,1)}, bf16[1024,256]{1,0:T(8,128)(2,1)}, bf16[1024,256]{1,0:T(8,128)(2,1)}, bf16[102...) custom-call(s32[4]{0:T(128)} %iota_xor_fusion.order_ref, bf16[1024,2816]{1,0:T(8,128)(2,1)} %get-tuple-element.172.refs_3_.refs_0_.refs_4_, ...), custom_call_target="tpu_custom_call" | custom-call | flops 2093796608 | bytes 5976883 | tf_op jit(solution)/shard_map/norm_back/pallas_call | solution.py:604
  297.0 25.0 %products.4 = (bf16[512,1408]{1,0:T(8,128)(2,1)}, bf16[512,1408]{1,0:T(8,128)(2,1)}, bf16[512,1408]{1,0:T(8,128)(2,1)}, bf16[512,1024]{1,0:T(8,128)(2,1)}, bf16[...) custom-call(s32[5]{0:T(128)} %stack.44.select_ref, ...), custom_call_target="tpu_custom_call" | custom-call | flops 1650878080 | bytes 3224371 | tf_op jit(solution)/shard_map/products/pallas_call | solution.py:682
  322.1 6.2 %collective-permute-start.16 = (bf16[512,1408]{1,0:T(8,128)(2,1)}, bf16[512,1408]{1,0:T(8,128)(2,1)}, u32[]{:S(2)}, u32[]{:S(2)}) collective-permute-start(bf16[512,1408]{1,0:T(8,128)(2,1)} %get-tuple-element.199), channel_id=1, source_target_pairs={{0,8},{4,12},{8,0},{12,4},{16,24},{20,28},{24,16},{28,20},{1,9},{5... | collective-permute-start | bytes 4325384 | tf_op jit(solution)/shard_map/ppermute | solution.py:813
  329.3 7.5 %collective-permute-start.15 = (bf16[512,1408]{1,0:T(8,128)(2,1)}, bf16[512,1408]{1,0:T(8,128)(2,1)}, u32[]{:S(2)}, u32[]{:S(2)}) collective-permute-start(bf16[512,1408]{1,0:T(8,128)(2,1)} %get-tuple-element.197), channel_id=1, source_target_pairs={{0,4},{4,0},{8,12},{12,8},{16,20},{20,16},{24,28},{28,24},{1,5},{5... | collective-permute-start | bytes 4325384 | tf_op jit(solution)/shard_map/ppermute | solution.py:813
  337.1 44.8 %attend_back.2 = (bf16[4096,256]{1,0:T(8,128)(2,1)}, bf16[4096,256]{1,0:T(8,128)(2,1)}, bf16[4096,256]{1,0:T(8,128)(2,1)}, f32[2,128,2560]{2,1,0:T(8,128)}, f32[8,8,512]{2,1,0:T(8,128)}) custom-call(s32[4]{0:T(128)} %iota_xor_fusion.order_ref, bf16[2,4096,128]{2,1,0:T(8,128)(2,1)} %get-tuple-element.151.q_ref, ...), custom_call_target="tpu_custom_call" | custom-call | flops 1879048192 | bytes 3774873 | tf_op jit(solution)/shard_map/attend_back/pallas_call | solution.py:449
  382.0 2.0 fusion.3
  384.0 1.8 fusion
  385.9 1.8 fusion.1
  388.2 5.2 collective-permute-start.21
  397.0 1.6 collective-permute-start.19
  398.6 37.5 %attend_back.3 = (bf16[4096,256]{1,0:T(8,128)(2,1)}, bf16[4096,256]{1,0:T(8,128)(2,1)}, bf16[4096,256]{1,0:T(8,128)(2,1)}) custom-call(s32[4]{0:T(128)} %iota_xor_fusion.order_ref, bf16[2,4096,128]{2,1,0:T(8,128)(2,1)} %get-tuple-element.151.q_ref, ...), custom_call_target="tpu_custom_call", output_to_operand_aliasing={{0}: (12, {}), {1}: (13, {}), {2}: (14, {})} | custom-call | flops 1342177280 | bytes 3774873 | tf_op jit(solution)/shard_map/attend_back/pallas_call | solution.py:449
  438.5 2.1 add_convert_fusion.3
  440.7 5.5 project_back.6
  446.1 5.5 project_back.7
  452.1 4.6 project_back.8
  458.0 1.9 dynamic-slice_bitcast_fusion.17
  460.7 2.0 collective-permute-start.26
  463.5 4.0 collective-permute-start.27
  467.5 4.6 project_back.9
  472.1 11.7 %products.5 = bf16[1024,768]{1,0:T(8,128)(2,1)} custom-call(s32[1]{0:T(128)} %constant.240.clone.1.select_ref, bf16[1024,4096]{1,0:T(8,128)(2,1)} %get-tuple-element.163.refs_0_, bf16[4096,256]{1,0:T(8,128)(2,1)} %get-tuple-element.262.a_ref.refs_1_, bf16[4096,256]{1,0:T(8,128)(2,1)} %get-tuple-element.263.b_ref.refs_2_, ...), custom_call_target="tpu_custom_call" | custom-call | flops 966367616 | bytes 1179648 | tf_op jit(solution)/shard_map/products/pallas_call | solution.py:682
  483.8 1.6 dynamic-slice_bitcast_fusion.1
  485.4 2.1 collective-permute-start.24
  487.5 1.6 collective-permute-start.35
  490.4 4.6 collective-permute-done.24
  495.1 1.6 collective-permute-start.33
  498.1 1.8 collective-permute-start.31
  499.9 7.1 %collective-permute-done.29 = bf16[2,2,128,768]{3,2,1,0:T(8,128)(2,1)S(1)} collective-permute-done((bf16[2,2,128,768]{3,2,1,0:T(8,128)(2,1)S(1)}, bf16[2,2,128,768]{3,2,1,0:T(8,128)(2,1)S(1)}, u32[]{:S(2)}, u32[]{:S(2)}) %collective-permute-start.29) | collective-permute-done | bytes 786464 | tf_op jit(solution)/shard_map/ppermute | solution.py:796
  507.2 7.0 %collective-permute-done.33 = bf16[64,1024]{1,0:T(8,128)(2,1)S(1)} collective-permute-done((bf16[64,1024]{1,0:T(8,128)(2,1)S(1)}, bf16[64,1024]{1,0:T(8,128)(2,1)S(1)}, u32[]{:S(2)}, u32[]{:S(2)}) %collective-permute-start.33) | collective-permute-done | bytes 131104 | tf_op jit(solution)/shard_map/ppermute | solution.py:796
  515.0 3.8 collective-permute-done.31
  518.9 2.8 collective-permute-done.30
  522.5 6.1 %project_back.10.refs_5_ = bf16[1024,1024]{1,0:T(8,128)(2,1)} custom-call(s32[4]{0:T(128)} %iota_xor_fusion.order_ref, bf16[4096,256]{1,0:T(8,128)(2,1)} %get-tuple-element.262.a_ref.refs_1_, bf16[4096,256]{1,0:T(8,128)(2,1)} %get-tuple-element.263.b_ref.refs_2_, bf16[4096,256]{1,0:T(8,128)(2,1)} %get-tuple-element.264.c_ref.refs_3_, ...), custom_call_target="tpu_custom_call" | custom-call | flops 120795952 | bytes 432537 | tf_op jit(solution)/shard_map/project_back/pallas_call | solution.py:766
  528.6 3.7 collective-permute-done.34
  532.4 6.1 %project_back.11 = bf16[1024,1024]{1,0:T(8,128)(2,1)} custom-call(s32[4]{0:T(128)} %iota_xor_fusion.order_ref, bf16[4096,256]{1,0:T(8,128)(2,1)} %get-tuple-element.262.a_ref.refs_1_, bf16[4096,256]{1,0:T(8,128)(2,1)} %get-tuple-element.263.b_ref.refs_2_, bf16[4096,256]{1,0:T(8,128)(2,1)} %get-tuple-element.264.c_ref.refs_3_, ...), custom_call_target="tpu_custom_call", output_to_operand_aliasing={{}: (10, {})} | custom-call | flops 120795952 | bytes 432537 | tf_op jit(solution)/shard_map/project_back/pallas_call | solution.py:766
  540.1 11.2 %finish.1 = bf16[1024,1024]{1,0:T(8,128)(2,1)} custom-call(f32[1024,1024]{1,0:T(8,128)} %get-tuple-element.162.refs_8_.r_ref, bf16[1024,2816]{1,0:T(8,128)(2,1)} %get-tuple-element.269.refs_2_.refs_3_.h_ref, bf16[1024,9472]{1,0:T(8,128)(2,1)} %all-gather.2.cloned.1.call-done.refs_4_.refs_5_.refs_6_.refs_7_.wg_ref.wu_ref.wd_ref.refs_2_.refs_3_.w_ref), custom_call_target="tpu_custom_call" | custom-call | flops 885836992 | bytes 2673868 | tf_op jit(solution)/shard_map/finish/pallas_call | solution.py:705
  552.2 1.6 collective-permute-start.40
  555.7 5.1 feedforward_ends.1
  560.8 2.5 collective-permute-done.41.refs_3_
  563.2 3.3 projection_ends.1
  566.5 1.5 reduce
  568.0 1.5 reduce.1
  (168 shorter events, 34.9 us)
Async XLA Ops:
  7.2 208.3 %all-gather.2.cloned.1.call-start = ((), (), s32[]{:S(2)}) async-start(), calls=%async_computation.2 | async-start | bytes 20004864 | tf_op jit(solution)/shard_map/all_gather | solution.py:971
  8.6 6.1 %copy-start.22 = (bf16[128]{0:T(256)(128)(2,1)S(1)}, bf16[128]{0:T(256)(128)(2,1)}, u32[]{:S(2)}) copy-start(bf16[128]{0:T(256)(128)(2,1)} %param.25) | copy-start | bytes 772
  8.6 6.1 %copy-start.24 = (bf16[128]{0:T(256)(128)(2,1)S(1)}, bf16[128]{0:T(256)(128)(2,1)}, u32[]{:S(2)}) copy-start(bf16[128]{0:T(256)(128)(2,1)} %param.24) | copy-start | bytes 772
  11.6 53.3 %collective-permute-start.1 = (bf16[1024,1024]{1,0:T(8,128)(2,1)}, bf16[1024,1024]{1,0:T(8,128)(2,1)}, u32[]{:S(2)}, u32[]{:S(2)}) collective-permute-start(bf16[1024,1024]{1,0:T(8,128)(2,1)} %refs_2_.3), channel_id=1, source_target_pairs={{0,2},{1,3},{2,0},{3,1},{4,6},{5,7},{6,4},{7,5},{8,10},{9,11},{10,... | collective-permute-start | bytes 6291464 | tf_op jit(solution)/shard_map/ppermute | solution.py:68
  14.6 89.4 %collective-permute-start = (bf16[1024,1024]{1,0:T(8,128)(2,1)}, bf16[1024,1024]{1,0:T(8,128)(2,1)}, u32[]{:S(2)}, u32[]{:S(2)}) collective-permute-start(bf16[1024,1024]{1,0:T(8,128)(2,1)} %refs_2_.3), channel_id=1, source_target_pairs={{0,1},{1,0},{2,3},{3,2},{4,5},{5,4},{6,7},{7,6},{8,9},{9,8},{10,11... | collective-permute-start | bytes 6291464 | tf_op jit(solution)/shard_map/ppermute | solution.py:68
  15.3 12.3 %all-to-all-start.1 = ((bf16[8,2,128]{2,1,0:T(2,128)(2,1)}), bf16[8,2,128]{2,1,0:T(2,128)(2,1)S(1)}, u32[]{:S(2)}, u32[]{:S(2)}) async-start(bf16[8,2,128]{2,1,0:T(2,128)(2,1)} %broadcast_in_dim.29), calls=%async_computation.1 | async-start | bytes 8192 | tf_op jit(solution)/shard_map/all_to_all | solution.py:74
  21.1 55.6 %collective-permute-start.3 = (bf16[2,2048,128]{2,1,0:T(8,128)(2,1)}, bf16[2,2048,128]{2,1,0:T(8,128)(2,1)S(1)}, u32[]{:S(2)}, u32[]{:S(2)}) collective-permute-start(bf16[2,2048,128]{2,1,0:T(8,128)(2,1)} %bitcast.6.k_ref), channel_id=1, source_target_pairs={{0,4},{4,8},{8,12},{12,16},{16,20},{20,24},{24,28},{28,0},{1,5},{5... | collective-permute-start | bytes 3145736 | tf_op jit(solution)/shard_map/ppermute | solution.py:959
  23.1 62.7 %collective-permute-start.4 = (bf16[2,2048,128]{2,1,0:T(8,128)(2,1)}, bf16[2,2048,128]{2,1,0:T(8,128)(2,1)}, u32[]{:S(2)}, u32[]{:S(2)}) collective-permute-start(bf16[2,2048,128]{2,1,0:T(8,128)(2,1)} %bitcast.7.v_ref), channel_id=1, source_target_pairs={{0,4},{4,8},{8,12},{12,16},{16,20},{20,24},{24,28},{28,0},{1,5},{5... | collective-permute-start | bytes 3145736 | tf_op jit(solution)/shard_map/ppermute | solution.py:960
  26.3 6.2 %copy-start.20 = (s32[1,2,32,128]{3,2,1,0:T(8,128)S(1)}, s32[1,2,32,128]{3,2,1,0:T(8,128)}, u32[]{:S(2)}) copy-start(s32[1,2,32,128]{3,2,1,0:T(8,128)} %param.28) | copy-start | bytes 98308
  26.3 6.2 %copy-start.21 = (s32[1,2,32,128]{3,2,1,0:T(8,128)S(1)}, s32[1,2,32,128]{3,2,1,0:T(8,128)}, u32[]{:S(2)}) copy-start(s32[1,2,32,128]{3,2,1,0:T(8,128)} %param.29) | copy-start | bytes 98308
  28.9 79.0 %all-to-all-start = ((bf16[8,128,768]{2,1,0:T(8,128)(2,1)}), bf16[8,128,768]{2,1,0:T(8,128)(2,1)S(1)}, u32[]{:S(2)}, u32[]{:S(2)}) async-start(bf16[8,128,768]{2,1,0:T(8,128)(2,1)} %broadcast_in_dim.28), calls=%async_computation | async-start | bytes 3145728 | tf_op jit(solution)/shard_map/all_to_all | solution.py:74
  64.9 43.0 %collective-permute-start.2 = (bf16[1024,1024]{1,0:T(8,128)(2,1)}, bf16[1024,1024]{1,0:T(8,128)(2,1)}, u32[]{:S(2)}, u32[]{:S(2)}) collective-permute-start(bf16[1024,1024]{1,0:T(8,128)(2,1)} %collective-permute-done.1.refs_2_), channel_id=1, source_target_pairs={{0,1},{1,0},{2,3},{3,2},{4,5},{5,4},{6,7},{7,6},{8,9},{9,8},{10,11... | collective-permute-start | bytes 6291464 | tf_op jit(solution)/shard_map/ppermute | solution.py:68
  76.7 9.1 %copy-start.16 = (bf16[2,2048,128]{2,1,0:T(8,128)(2,1)}, bf16[2,2048,128]{2,1,0:T(8,128)(2,1)S(1)}, u32[]{:S(2)}) copy-start(bf16[2,2048,128]{2,1,0:T(8,128)(2,1)S(1)} %collective-permute-done.3.k_ref) | copy-start | bytes 3145732
  128.1 41.7 %copy-start.3 = (bf16[1024,1024]{1,0:T(8,128)(2,1)S(1)}, bf16[1024,1024]{1,0:T(8,128)(2,1)}, u32[]{:S(2)}) copy-start(bf16[1024,1024]{1,0:T(8,128)(2,1)} %refs_9_.1) | copy-start | bytes 6291460
  167.9 7.6 %collective-permute-start.5 = (bf16[1024,256]{1,0:T(8,128)(2,1)}, bf16[1024,256]{1,0:T(8,128)(2,1)S(1)}, u32[]{:S(2)}, u32[]{:S(2)}) collective-permute-start(bf16[1024,256]{1,0:T(8,128)(2,1)} %get-tuple-element.159.refs_5_), channel_id=1, source_target_pairs={{0,1},{1,0},{2,3},{3,2},{4,5},{5,4},{6,7},{7,6},{8,9},{9,8},{10,11... | collective-permute-start | bytes 1572872 | tf_op jit(solution)/shard_map/ppermute | solution.py:68
  167.9 26.3 %collective-permute-start.6 = (bf16[1024,256]{1,0:T(8,128)(2,1)}, bf16[1024,256]{1,0:T(8,128)(2,1)S(1)}, u32[]{:S(2)}, u32[]{:S(2)}) collective-permute-start(bf16[1024,256]{1,0:T(8,128)(2,1)} %get-tuple-element.160.refs_6_), channel_id=1, source_target_pairs={{0,2},{1,3},{2,0},{3,1},{4,6},{5,7},{6,4},{7,5},{8,10},{9,11},{10,... | collective-permute-start | bytes 1572872 | tf_op jit(solution)/shard_map/ppermute | solution.py:68
  168.0 38.8 %collective-permute-start.7 = (bf16[1024,256]{1,0:T(8,128)(2,1)}, bf16[1024,256]{1,0:T(8,128)(2,1)}, u32[]{:S(2)}, u32[]{:S(2)}) collective-permute-start(bf16[1024,256]{1,0:T(8,128)(2,1)} %get-tuple-element.161.refs_7_), channel_id=1, source_target_pairs={{0,3},{1,2},{2,1},{3,0},{4,7},{5,6},{6,5},{7,4},{8,11},{9,10},{10,... | collective-permute-start | bytes 1572872 | tf_op jit(solution)/shard_map/ppermute | solution.py:68
  175.5 40.0 %copy-start.17 = (bf16[1024,256]{1,0:T(8,128)(2,1)}, bf16[1024,256]{1,0:T(8,128)(2,1)S(1)}, u32[]{:S(2)}) copy-start(bf16[1024,256]{1,0:T(8,128)(2,1)S(1)} %collective-permute-done.5.refs_1_) | copy-start | bytes 1572868
  194.2 21.4 %copy-start.18 = (bf16[1024,256]{1,0:T(8,128)(2,1)}, bf16[1024,256]{1,0:T(8,128)(2,1)S(1)}, u32[]{:S(2)}) copy-start(bf16[1024,256]{1,0:T(8,128)(2,1)S(1)} %collective-permute-done.6.refs_2_) | copy-start | bytes 1572868
  265.8 29.2 %collective-permute-start.11 = (bf16[1024,1408]{1,0:T(8,128)(2,1)}, bf16[1024,1408]{1,0:T(8,128)(2,1)}, u32[]{:S(2)}, u32[]{:S(2)}) collective-permute-start(bf16[1024,1408]{1,0:T(8,128)(2,1)} %get-tuple-element.179), channel_id=1, source_target_pairs={{0,1},{1,0},{2,3},{3,2},{4,5},{5,4},{6,7},{7,6},{8,9},{9,8},{10,11... | collective-permute-start | bytes 8650760 | tf_op jit(solution)/shard_map/ppermute | solution.py:68
  265.8 31.2 %collective-permute-start.12 = (bf16[1024,1408]{1,0:T(8,128)(2,1)}, bf16[1024,1408]{1,0:T(8,128)(2,1)}, u32[]{:S(2)}, u32[]{:S(2)}) collective-permute-start(bf16[1024,1408]{1,0:T(8,128)(2,1)} %get-tuple-element.180), channel_id=1, source_target_pairs={{0,1},{1,0},{2,3},{3,2},{4,5},{5,4},{6,7},{7,6},{8,9},{9,8},{10,11... | collective-permute-start | bytes 8650760 | tf_op jit(solution)/shard_map/ppermute | solution.py:68
  266.3 30.7 %collective-permute-start.13 = (bf16[1024,1408]{1,0:T(8,128)(2,1)}, bf16[1024,1408]{1,0:T(8,128)(2,1)}, u32[]{:S(2)}, u32[]{:S(2)}) collective-permute-start(bf16[1024,1408]{1,0:T(8,128)(2,1)} %get-tuple-element.181), channel_id=1, source_target_pairs={{0,1},{1,0},{2,3},{3,2},{4,5},{5,4},{6,7},{7,6},{8,9},{9,8},{10,11... | collective-permute-start | bytes 8650760 | tf_op jit(solution)/shard_map/ppermute | solution.py:68
  294.1 27.9 %collective-permute-start.10 = (bf16[1024,256]{1,0:T(8,128)(2,1)}, bf16[1024,256]{1,0:T(8,128)(2,1)S(1)}, u32[]{:S(2)}, u32[]{:S(2)}) collective-permute-start(bf16[1024,256]{1,0:T(8,128)(2,1)} %get-tuple-element.176), channel_id=1, source_target_pairs={{0,3},{1,2},{2,1},{3,0},{4,7},{5,6},{6,5},{7,4},{8,11},{9,10},{10,... | collective-permute-start | bytes 1572872 | tf_op jit(solution)/shard_map/ppermute | solution.py:68
  295.0 27.0 %collective-permute-start.8 = (bf16[1024,256]{1,0:T(8,128)(2,1)}, bf16[1024,256]{1,0:T(8,128)(2,1)S(1)}, u32[]{:S(2)}, u32[]{:S(2)}) collective-permute-start(bf16[1024,256]{1,0:T(8,128)(2,1)} %get-tuple-element.174), channel_id=1, source_target_pairs={{0,1},{1,0},{2,3},{3,2},{4,5},{5,4},{6,7},{7,6},{8,9},{9,8},{10,11... | collective-permute-start | bytes 1572872 | tf_op jit(solution)/shard_map/ppermute | solution.py:68
  295.0 27.0 %collective-permute-start.9 = (bf16[1024,256]{1,0:T(8,128)(2,1)}, bf16[1024,256]{1,0:T(8,128)(2,1)S(1)}, u32[]{:S(2)}, u32[]{:S(2)}) collective-permute-start(bf16[1024,256]{1,0:T(8,128)(2,1)} %get-tuple-element.175), channel_id=1, source_target_pairs={{0,2},{1,3},{2,0},{3,1},{4,6},{5,7},{6,4},{7,5},{8,10},{9,11},{10,... | collective-permute-start | bytes 1572872 | tf_op jit(solution)/shard_map/ppermute | solution.py:68
  322.0 15.1 %copy-start.7 = (bf16[1024,256]{1,0:T(8,128)(2,1)}, bf16[1024,256]{1,0:T(8,128)(2,1)S(1)}, u32[]{:S(2)}) copy-start(bf16[1024,256]{1,0:T(8,128)(2,1)S(1)} %collective-permute-done.10.refs_3_) | copy-start | bytes 1572868
  322.0 15.1 %copy-start.8 = (bf16[1024,256]{1,0:T(8,128)(2,1)}, bf16[1024,256]{1,0:T(8,128)(2,1)S(1)}, u32[]{:S(2)}) copy-start(bf16[1024,256]{1,0:T(8,128)(2,1)S(1)} %collective-permute-done.8.refs_1_) | copy-start | bytes 1572868
  322.0 15.1 %copy-start.9 = (bf16[1024,256]{1,0:T(8,128)(2,1)}, bf16[1024,256]{1,0:T(8,128)(2,1)S(1)}, u32[]{:S(2)}) copy-start(bf16[1024,256]{1,0:T(8,128)(2,1)S(1)} %collective-permute-done.9.refs_2_) | copy-start | bytes 1572868
  322.1 62.0 %collective-permute-start.16 = (bf16[512,1408]{1,0:T(8,128)(2,1)}, bf16[512,1408]{1,0:T(8,128)(2,1)}, u32[]{:S(2)}, u32[]{:S(2)}) collective-permute-start(bf16[512,1408]{1,0:T(8,128)(2,1)} %get-tuple-element.199), channel_id=1, source_target_pairs={{0,8},{4,12},{8,0},{12,4},{16,24},{20,28},{24,16},{28,20},{1,9},{5... | collective-permute-start | bytes 4325384 | tf_op jit(solution)/shard_map/ppermute | solution.py:813
  328.3 53.7 %collective-permute-start.17 = (bf16[512,1024]{1,0:T(8,128)(2,1)}, bf16[512,1024]{1,0:T(8,128)(2,1)}, u32[]{:S(2)}, u32[]{:S(2)}) collective-permute-start(bf16[512,1024]{1,0:T(8,128)(2,1)} %get-tuple-element.201), channel_id=1, source_target_pairs={{0,16},{4,20},{8,24},{12,28},{16,0},{20,4},{24,8},{28,12},{1,17},{... | collective-permute-start | bytes 3145736 | tf_op jit(solution)/shard_map/ppermute | solution.py:813
  329.3 56.6 %collective-permute-start.15 = (bf16[512,1408]{1,0:T(8,128)(2,1)}, bf16[512,1408]{1,0:T(8,128)(2,1)}, u32[]{:S(2)}, u32[]{:S(2)}) collective-permute-start(bf16[512,1408]{1,0:T(8,128)(2,1)} %get-tuple-element.197), channel_id=1, source_target_pairs={{0,4},{4,0},{8,12},{12,8},{16,20},{20,16},{24,28},{28,24},{1,5},{5... | collective-permute-start | bytes 4325384 | tf_op jit(solution)/shard_map/ppermute | solution.py:813
  336.8 50.9 %collective-permute-start.14 = (bf16[512,1408]{1,0:T(8,128)(2,1)}, bf16[512,1408]{1,0:T(8,128)(2,1)S(1)}, u32[]{:S(2)}, u32[]{:S(2)}) collective-permute-start(bf16[512,1408]{1,0:T(8,128)(2,1)} %get-tuple-element.195), channel_id=1, source_target_pairs={{0,2},{1,3},{2,0},{3,1},{4,6},{5,7},{6,4},{7,5},{8,10},{9,11},{10,... | collective-permute-start | bytes 4325384 | tf_op jit(solution)/shard_map/ppermute | solution.py:813
  381.9 2.1 copy-start.12
  384.0 1.9 copy-start.11
  388.2 47.9 %collective-permute-start.21 = (bf16[2,128,1024]{2,1,0:T(8,128)(2,1)S(1)}, bf16[2,128,1024]{2,1,0:T(8,128)(2,1)S(1)}, u32[]{:S(2)}, u32[]{:S(2)}) collective-permute-start(bf16[2,128,1024]{2,1,0:T(8,128)(2,1)S(1)} %get-tuple-element.301), channel_id=1, source_target_pairs={{0,4},{4,0},{8,12},{12,8},{16,20},{20,16},{24,28},{28,24},{1,5},{5... | collective-permute-start | bytes 1572872 | tf_op jit(solution)/shard_map/ppermute | solution.py:796
  394.4 41.9 %collective-permute-start.20 = (bf16[2,2,64,1408]{3,2,1,0:T(8,128)(2,1)}, bf16[2,2,64,1408]{3,2,1,0:T(8,128)(2,1)S(1)}, u32[]{:S(2)}, u32[]{:S(2)}) collective-permute-start(bf16[2,2,64,1408]{3,2,1,0:T(8,128)(2,1)} %get-tuple-element.293), channel_id=1, source_target_pairs={{0,2},{1,3},{2,0},{3,1},{4,6},{5,7},{6,4},{7,5},{8,10},{9,11},{10,... | collective-permute-start | bytes 2162696 | tf_op jit(solution)/shard_map/ppermute | solution.py:796
  397.0 39.5 %collective-permute-start.19 = (bf16[2,2,64,1408]{3,2,1,0:T(8,128)(2,1)}, bf16[2,2,64,1408]{3,2,1,0:T(8,128)(2,1)}, u32[]{:S(2)}, u32[]{:S(2)}) collective-permute-start(bf16[2,2,64,1408]{3,2,1,0:T(8,128)(2,1)} %get-tuple-element.295), channel_id=1, source_target_pairs={{0,2},{1,3},{2,0},{3,1},{4,6},{5,7},{6,4},{7,5},{8,10},{9,11},{10,... | collective-permute-start | bytes 2162696 | tf_op jit(solution)/shard_map/ppermute | solution.py:796
  398.6 39.9 %collective-permute-start.18 = (bf16[2,2,64,1408]{3,2,1,0:T(8,128)(2,1)}, bf16[2,2,64,1408]{3,2,1,0:T(8,128)(2,1)}, u32[]{:S(2)}, u32[]{:S(2)}) collective-permute-start(bf16[2,2,64,1408]{3,2,1,0:T(8,128)(2,1)} %get-tuple-element.298), channel_id=1, source_target_pairs={{0,4},{4,0},{8,12},{12,8},{16,20},{20,16},{24,28},{28,24},{1,5},{5... | collective-permute-start | bytes 2162696 | tf_op jit(solution)/shard_map/ppermute | solution.py:796
  446.1 6.0 %collective-permute-start.22 = (bf16[1024,1024]{1,0:T(8,128)(2,1)}, bf16[1024,1024]{1,0:T(8,128)(2,1)}, u32[]{:S(2)}, u32[]{:S(2)}) collective-permute-start(bf16[1024,1024]{1,0:T(8,128)(2,1)} %project_back.6), channel_id=1, source_target_pairs={{0,1},{1,0},{2,3},{3,2},{4,5},{5,4},{6,7},{7,6},{8,9},{9,8},{10,11... | collective-permute-start | bytes 6291464 | tf_op jit(solution)/shard_map/ppermute | solution.py:68
  451.6 43.5 %collective-permute-start.28 = (bf16[1024,1024]{1,0:T(8,128)(2,1)}, bf16[1024,1024]{1,0:T(8,128)(2,1)S(1)}, u32[]{:S(2)}, u32[]{:S(2)}) collective-permute-start(bf16[1024,1024]{1,0:T(8,128)(2,1)} %project_back.7), channel_id=1, source_target_pairs={{0,1},{1,0},{2,3},{3,2},{4,5},{5,4},{6,7},{7,6},{8,9},{9,8},{10,11... | collective-permute-start | bytes 6291464 | tf_op jit(solution)/shard_map/ppermute | solution.py:68
  456.7 28.7 %collective-permute-start.23 = (bf16[512,1024]{1,0:T(8,128)(2,1)}, bf16[512,1024]{1,0:T(8,128)(2,1)}, u32[]{:S(2)}, u32[]{:S(2)}) collective-permute-start(bf16[512,1024]{1,0:T(8,128)(2,1)} %project_back.8), channel_id=1, source_target_pairs={{0,2},{1,3},{2,0},{3,1},{4,6},{5,7},{6,4},{7,5},{8,10},{9,11},{10,... | collective-permute-start | bytes 3145736 | tf_op jit(solution)/shard_map/ppermute | solution.py:68
  460.7 26.8 %collective-permute-start.26 = (bf16[2,64,1408]{2,1,0:T(8,128)(2,1)}, bf16[2,64,1408]{2,1,0:T(8,128)(2,1)S(1)}, u32[]{:S(2)}, u32[]{:S(2)}) collective-permute-start(bf16[2,64,1408]{2,1,0:T(8,128)(2,1)} %get-tuple-element.305), channel_id=1, source_target_pairs={{0,4},{4,0},{8,12},{12,8},{16,20},{20,16},{24,28},{28,24},{1,5},{5... | collective-permute-start | bytes 1081352 | tf_op jit(solution)/shard_map/ppermute | solution.py:796
  463.5 25.8 %collective-permute-start.27 = (bf16[128,1024]{1,0:T(8,128)(2,1)}, bf16[128,1024]{1,0:T(8,128)(2,1)}, u32[]{:S(2)}, u32[]{:S(2)}) collective-permute-start(bf16[128,1024]{1,0:T(8,128)(2,1)} %get-tuple-element.311), channel_id=1, source_target_pairs={{0,8},{4,12},{8,0},{12,4},{16,24},{20,28},{24,16},{28,20},{1,9},{5... | collective-permute-start | bytes 786440 | tf_op jit(solution)/shard_map/ppermute | solution.py:796
  467.5 21.6 %collective-permute-start.25 = (bf16[2,64,1408]{2,1,0:T(8,128)(2,1)}, bf16[2,64,1408]{2,1,0:T(8,128)(2,1)S(1)}, u32[]{:S(2)}, u32[]{:S(2)}) collective-permute-start(bf16[2,64,1408]{2,1,0:T(8,128)(2,1)} %get-tuple-element.307), channel_id=1, source_target_pairs={{0,8},{4,12},{8,0},{12,4},{16,24},{20,28},{24,16},{28,20},{1,9},{5... | collective-permute-start | bytes 1081352 | tf_op jit(solution)/shard_map/ppermute | solution.py:796
  483.8 5.4 copy-start.13
  483.8 5.5 copy-start.15
  485.4 9.6 %collective-permute-start.24 = (bf16[2,64,1408]{2,1,0:T(8,128)(2,1)S(1)}, bf16[2,64,1408]{2,1,0:T(8,128)(2,1)S(1)}, u32[]{:S(2)}, u32[]{:S(2)}) collective-permute-start(bf16[2,64,1408]{2,1,0:T(8,128)(2,1)S(1)} %copy-done.19), channel_id=1, source_target_pairs={{0,8},{4,12},{8,0},{12,4},{16,24},{20,28},{24,16},{28,20},{1,9},{5... | collective-permute-start | bytes 1081352 | tf_op jit(solution)/shard_map/ppermute | solution.py:796
  487.5 44.9 %collective-permute-start.35 = (bf16[512,1024]{1,0:T(8,128)(2,1)}, bf16[512,1024]{1,0:T(8,128)(2,1)}, u32[]{:S(2)}, u32[]{:S(2)}) collective-permute-start(bf16[512,1024]{1,0:T(8,128)(2,1)} %project_back.9), channel_id=1, source_target_pairs={{0,2},{1,3},{2,0},{3,1},{4,6},{5,7},{6,4},{7,5},{8,10},{9,11},{10,... | collective-permute-start | bytes 3145736 | tf_op jit(solution)/shard_map/ppermute | solution.py:68
  489.1 17.8 %collective-permute-start.29 = (bf16[2,2,128,768]{3,2,1,0:T(8,128)(2,1)S(1)}, bf16[2,2,128,768]{3,2,1,0:T(8,128)(2,1)S(1)}, u32[]{:S(2)}, u32[]{:S(2)}) collective-permute-start(bf16[2,2,128,768]{3,2,1,0:T(8,128)(2,1)S(1)} %get-tuple-element.292), channel_id=1, source_target_pairs={{0,4},{4,0},{8,12},{12,8},{16,20},{20,16},{24,28},{28,24},{1,5},{5... | collective-permute-start | bytes 2359304 | tf_op jit(solution)/shard_map/ppermute | solution.py:796
  495.1 12.1 %copy-start.4 = (bf16[1024,1024]{1,0:T(8,128)(2,1)}, bf16[1024,1024]{1,0:T(8,128)(2,1)S(1)}, u32[]{:S(2)}) copy-start(bf16[1024,1024]{1,0:T(8,128)(2,1)S(1)} %collective-permute-done.28.refs_0_) | copy-start | bytes 6291460
  495.1 19.0 %collective-permute-start.33 = (bf16[64,1024]{1,0:T(8,128)(2,1)S(1)}, bf16[64,1024]{1,0:T(8,128)(2,1)S(1)}, u32[]{:S(2)}, u32[]{:S(2)}) collective-permute-start(bf16[64,1024]{1,0:T(8,128)(2,1)S(1)} %get-tuple-element.321), channel_id=1, source_target_pairs={{0,2},{1,3},{2,0},{3,1},{4,6},{5,7},{6,4},{7,5},{8,10},{9,11},{10,... | collective-permute-start | bytes 393224 | tf_op jit(solution)/shard_map/ppermute | solution.py:796
  496.9 18.1 %collective-permute-start.32 = (bf16[64,1408]{1,0:T(8,128)(2,1)S(1)}, bf16[64,1408]{1,0:T(8,128)(2,1)S(1)}, u32[]{:S(2)}, u32[]{:S(2)}) collective-permute-start(bf16[64,1408]{1,0:T(8,128)(2,1)S(1)} %get-tuple-element.315), channel_id=1, source_target_pairs={{0,16},{4,20},{8,24},{12,28},{16,0},{20,4},{24,8},{28,12},{1,17},{... | collective-permute-start | bytes 540680 | tf_op jit(solution)/shard_map/ppermute | solution.py:796
  498.1 20.8 %collective-permute-start.31 = (bf16[64,1408]{1,0:T(8,128)(2,1)S(1)}, bf16[64,1408]{1,0:T(8,128)(2,1)S(1)}, u32[]{:S(2)}, u32[]{:S(2)}) collective-permute-start(bf16[64,1408]{1,0:T(8,128)(2,1)S(1)} %get-tuple-element.317), channel_id=1, source_target_pairs={{0,16},{4,20},{8,24},{12,28},{16,0},{20,4},{24,8},{28,12},{1,17},{... | collective-permute-start | bytes 540680 | tf_op jit(solution)/shard_map/ppermute | solution.py:796
  507.0 14.7 %collective-permute-start.30 = (bf16[64,1408]{1,0:T(8,128)(2,1)S(1)}, bf16[64,1408]{1,0:T(8,128)(2,1)S(1)}, u32[]{:S(2)}, u32[]{:S(2)}) collective-permute-start(bf16[64,1408]{1,0:T(8,128)(2,1)S(1)} %get-tuple-element.319), channel_id=1, source_target_pairs={{0,16},{4,20},{8,24},{12,28},{16,0},{20,4},{24,8},{28,12},{1,17},{... | collective-permute-start | bytes 540680 | tf_op jit(solution)/shard_map/ppermute | solution.py:796
  521.8 16.7 %collective-permute-start.37 = (bf16[64,5248]{1,0:T(8,128)(2,1)S(1)}, bf16[64,5248]{1,0:T(8,128)(2,1)S(1)}, u32[]{:S(2)}, u32[]{:S(2)}) collective-permute-start(bf16[64,5248]{1,0:T(8,128)(2,1)S(1)} %constant_dynamic-update-slice_fusion), channel_id=1, source_target_pairs={{0,2},{1,3},{2,0},{3,1},{4,6},{5,7},{6,4},{7,5},{8,10},{9,11},{10,... | collective-permute-start | bytes 2015240 | tf_op jit(solution)/shard_map/ppermute | solution.py:68
  522.4 9.9 %collective-permute-start.34 = (bf16[2,128,768]{2,1,0:T(8,128)(2,1)S(1)}, bf16[2,128,768]{2,1,0:T(8,128)(2,1)S(1)}, u32[]{:S(2)}, u32[]{:S(2)}) collective-permute-start(bf16[2,128,768]{2,1,0:T(8,128)(2,1)S(1)} %get-tuple-element.304), channel_id=1, source_target_pairs={{0,8},{4,12},{8,0},{12,4},{16,24},{20,28},{24,16},{28,20},{1,9},{5... | collective-permute-start | bytes 1179656 | tf_op jit(solution)/shard_map/ppermute | solution.py:796
  538.8 12.5 %copy-start.5 = (bf16[2,64,5248]{2,1,0:T(8,128)(2,1)}, bf16[2,64,5248]{2,1,0:T(8,128)(2,1)S(1)}, u32[]{:S(2)}) copy-start(bf16[2,64,5248]{2,1,0:T(8,128)(2,1)S(1)} %pad_maximum_fusion.2) | copy-start | bytes 4030468
  538.8 15.8 %collective-permute-start.38 = (bf16[128,5248]{1,0:T(8,128)(2,1)S(1)}, bf16[128,5248]{1,0:T(8,128)(2,1)S(1)}, u32[]{:S(2)}, u32[]{:S(2)}) collective-permute-start(bf16[128,5248]{1,0:T(8,128)(2,1)S(1)} %bitcast.129), channel_id=1, source_target_pairs={{0,1},{1,0},{2,3},{3,2},{4,5},{5,4},{6,7},{7,6},{8,9},{9,8},{10,11... | collective-permute-start | bytes 4030472 | tf_op jit(solution)/shard_map/ppermute | solution.py:68
  538.9 12.3 %collective-permute-start.36 = (bf16[128,768]{1,0:T(8,128)(2,1)S(1)}, bf16[128,768]{1,0:T(8,128)(2,1)S(1)}, u32[]{:S(2)}, u32[]{:S(2)}) collective-permute-start(bf16[128,768]{1,0:T(8,128)(2,1)S(1)} %get-tuple-element.314), channel_id=1, source_target_pairs={{0,16},{4,20},{8,24},{12,28},{16,0},{20,4},{24,8},{28,12},{1,17},{... | collective-permute-start | bytes 589832 | tf_op jit(solution)/shard_map/ppermute | solution.py:796
  540.1 13.8 %copy-start.25 = (bf16[128]{0:T(256)(128)(2,1)S(1)}, bf16[128]{0:T(256)(128)(2,1)}, u32[]{:S(2)}) copy-start(bf16[128]{0:T(256)(128)(2,1)} %param.24) | copy-start | bytes 772
  552.0 8.7 %collective-permute-start.39 = (bf16[128,768]{1,0:T(8,128)(2,1)}, bf16[128,768]{1,0:T(8,128)(2,1)}, u32[]{:S(2)}, u32[]{:S(2)}) collective-permute-start(bf16[128,768]{1,0:T(8,128)(2,1)} %add_convert_fusion.10.refs_0_), channel_id=1, source_target_pairs={{0,1},{1,0},{2,3},{3,2},{4,5},{5,4},{6,7},{7,6},{8,9},{9,8},{10,11... | collective-permute-start | bytes 589832 | tf_op jit(solution)/shard_map/ppermute | solution.py:68
  552.2 8.5 %collective-permute-start.40 = (bf16[128,768]{1,0:T(8,128)(2,1)}, bf16[128,768]{1,0:T(8,128)(2,1)}, u32[]{:S(2)}, u32[]{:S(2)}) collective-permute-start(bf16[128,768]{1,0:T(8,128)(2,1)} %add_convert_fusion.10.refs_0_), channel_id=1, source_target_pairs={{0,2},{1,3},{2,0},{3,1},{4,6},{5,7},{6,4},{7,5},{8,10},{9,11},{10,... | collective-permute-start | bytes 589832 | tf_op jit(solution)/shard_map/ppermute | solution.py:68
  553.8 9.4 %collective-permute-start.41 = (bf16[128,768]{1,0:T(8,128)(2,1)}, bf16[128,768]{1,0:T(8,128)(2,1)}, u32[]{:S(2)}, u32[]{:S(2)}) collective-permute-start(bf16[128,768]{1,0:T(8,128)(2,1)} %add_convert_fusion.10.refs_0_), channel_id=1, source_target_pairs={{0,3},{1,2},{2,1},{3,0},{4,7},{5,6},{6,5},{7,4},{8,11},{9,10},{10,... | collective-permute-start | bytes 589832 | tf_op jit(solution)/shard_map/ppermute | solution.py:68
  553.9 15.6 %copy-start.1 = (bf16[2816,128]{1,0:T(8,128)(2,1)S(1)}, bf16[2816,128]{1,0:T(8,128)(2,1)}, u32[]{:S(2)}) copy-start(bf16[2816,128]{1,0:T(8,128)(2,1)} %param.23) | copy-start | bytes 2162692
  (7 other events, 8.6 us)
Sparse Core Ops, SparseCore 0:
  11.7 203.7 all-gather.1

commit v4 on v3

--- a/solution.py
+++ b/solution.py
@@ -561,10 +561,7 @@
             total = dot_nt(g_refs[0][...], w_refs[0][...])
             for k in range(1, n_grads):
                 total = total + dot_nt(g_refs[k][...], w_refs[k][...])
-            for d in range(steps):
-                @pl.when(step == d)
-                def _():
-                    acc[:, d * block : (d + 1) * block] = total
+            acc[:, pl.ds(pl.multiple_of(step * block, block), block)] = total
 
         @pl.when(step >= steps)
         def _():
@@ -640,22 +637,25 @@
 
     def kernel(select_ref, *refs):
         l_refs, r_refs, outs = refs[:n_left], refs[n_left : n_left + n], refs[n_left + n + n_add :]
-        for k in range(n):
+        def product(k):
             total = dot(l_refs[which[k]][...], r_refs[k][...])
             if k < n_add:
                 total = total + refs[n_left + n + k][...].astype(f32)
+            return total.astype(bf16)
+
+        for k in range(n):
             if halves is not None:
                 step, mine = pl.program_id(0), select_ref[1 + k]
                 keep = (step // 2 if halves[k] == 0 else step % 2) == mine
                 for cond, out in ((keep, outs[k]), (jnp.logical_not(keep), outs[n + k])):
                     @pl.when(cond)
                     def _():
-                        out[...] = total.astype(bf16)
+                        out[...] = product(k)
             elif joined:
                 start = sum(sizes[:k])
-                outs[0][:, start : start + sizes[k]] = total.astype(bf16)
+                outs[0][:, start : start + sizes[k]] = product(k)
             else:
-                outs[k][...] = total.astype(bf16)
+                outs[k][...] = product(k)
 
     def right_spec(k):
         return pl.BlockSpec(
@@ -972,8 +972,15 @@
 
     half = head_dim // 2
     frequency = 10000.0 ** (-2.0 * jnp.arange(half, dtype=f32) / head_dim)
-    angles = jnp.arange(length, dtype=jnp.int32).astype(f32)[:, None] * frequency[None, :]
-    cos_half, sin_half = jnp.cos(angles), jnp.sin(angles)
+    near_count = 64
+    near_angles = jnp.arange(near_count, dtype=f32)[:, None] * frequency[None, :]
+    far_angles = jnp.arange(0, length, near_count).astype(f32)[:, None] * frequency[None, :]
+    near_angles, far_angles = near_angles[None], far_angles[:, None]
+    near_cos, near_sin, far_cos, far_sin = lax.optimization_barrier(
+        (jnp.cos(near_angles), jnp.sin(near_angles), jnp.cos(far_angles), jnp.sin(far_angles))
+    )
+    cos_half = (far_cos * near_cos - far_sin * near_sin).reshape(length, half)
+    sin_half = (far_sin * near_cos + far_cos * near_sin).reshape(length, half)
     cosine = jnp.concatenate([cos_half, cos_half], axis=1)
     sine = jnp.concatenate([-sin_half, sin_half], axis=1)
     cotangent_t = cotangent.T.reshape(fsdp_count, 2, shard // 2, tok_rows)
@@ -1029,8 +1036,8 @@
             (
                 over(*bits),
                 over(0, *bits[1:]),
-                over(0, bits[0], *bits[2:]),
-                over(*bits[:-1], 0),
+                over(0, *bits[2:], bits[0]),
+                over(bits[0], 0, *bits[1:-1]),
             ),
             (shard // 2, shard, shard, shard),
         )

time: 587 us -> 578 us (0.985)
  starting transfers between devices: 61.2 us -> 68.6 us
  other arithmetic: 28.2 us -> 21.8 us
  waiting for transfers between devices: 101 us -> 94.7 us
    ppermute x15, waiting for transfers between devices: 29.7 us -> 18.8 us  [trade(): lax.ppermute(give, axis, [(i, i ^ bit) for i in range(count)])]
    ppermute x1, waiting for transfers between devices: 9.08 us -> 16.4 us  [body(): partner_values = lax.ppermute(cache_values[0], 'fsdp', ring)]
    neg x1, other arithmetic: 7.46 us -> 0.14 us  [body(): sine = jnp.concatenate([-sin_half, sin_half], axis=1)]
  transfers between devices with their start and end apart: 45 -> 45, of which waited for: 15 -> 12; matrix products, arithmetic and copies ran while one was open for 7% -> 6% of each run, Pallas kernels for 49% -> 50%
where the time goes in v4:
time: 578 us; the launch traced here: 570 us
  Pallas kernels  342 us (59%)
  waiting for transfers between devices  94.7 us (16%)
  starting transfers between devices  68.6 us (12%)
  local copies, waits for them, and re-layouts  28.1 us (5%)
  other arithmetic  21.8 us (4%)
  between operations  15 us (3%)
    pallas_call x2, Pallas kernels, attend_back(): call(kernel, (last - first,), in_specs + [small, table, table], out_specs...  82.4 us
    pallas_call x3, Pallas kernels, products(): call(kernel, (height // block,), [pl.BlockSpec((block, d.shape[1]), lambd...  51.1 us
    ppermute x21, waiting for transfers between devices, swap_seq(): return lax.ppermute(array, 'seq', [(i, i ^ bit) for i in range(count)])  46.9 us
    pallas_call x1, Pallas kernels, attend(): call(kernel, (count,), [rows, full, full_t, mem_rows, mem_rows], [pl.Bloc...  40.1 us
    pallas_call x2, Pallas kernels, retrieve(): call(kernel, (head_local, blocks // per), [pl.BlockSpec((1, 1, per, slots...  35.7 us
    pallas_call x6, Pallas kernels, project_back(): call(kernel, (steps,), in_specs, rows_of(out), out, 6 * rows * width * gr...  32.3 us
    pallas_call x1, Pallas kernels, norm_back(): call(kernel, (steps + row_steps,), [resident(g.shape, (0, 0)) for g in gr...  27.3 us
    ppermute x15, starting transfers between devices, trade(): lax.ppermute(give, axis, [(i, i ^ bit) for i in range(count)])  25.8 us
  transfers between devices with their start and end apart: 45, of which 12 were waited for; matrix products, arithmetic and copies ran while one was open for 6% of the time, Pallas kernels for 50%

profile of v4, /device:TPU:0, one launch (start us, length us, event | category | flops | bytes accessed | tf_op | source)
XLA Modules:
  0.0 570.0 jit_solution(17674252708765084362)
XLA Ops:
  11.6 3.0 collective-permute-start.1
  15.3 5.8 %all-to-all-start.1 = ((bf16[8,2,128]{2,1,0:T(2,128)(2,1)}), bf16[8,2,128]{2,1,0:T(2,128)(2,1)S(1)}, u32[]{:S(2)}, u32[]{:S(2)}) async-start(bf16[8,2,128]{2,1,0:T(2,128)(2,1)} %broadcast_in_dim.15), calls=%async_computation.1 | async-start | bytes 8192 | tf_op jit(solution)/shard_map/all_to_all | solution.py:74
  21.1 2.0 collective-permute-start.3
  23.1 1.5 collective-permute-start.4
  27.6 1.3 broadcast_in_dim.14
  28.9 4.2 all-to-all-start
  33.2 17.2 %retrieve.2 = (bf16[2,4096,128]{2,1,0:T(8,128)(2,1)}, bf16[2,4096,128]{2,1,0:T(8,128)(2,1)}) custom-call(s32[2,8,4,128]{3,2,1,0:T(4,128)} %bitcast.147, bf16[2,2048,128]{2,1,0:T(8,128)(2,1)} %bitcast.12.k_ref, bf16[2,2048,128]{2,1,0:T(8,128)(2,1)} %bitcast.13.v_ref), custom_call_target="tpu_custom_call" | custom-call | flops 1288490240 | bytes 1258291 | tf_op jit(solution)/shard_map/retrieve/pallas_call | solution.py:188
  51.1 13.9 %collective-permute-done.1.refs_2_ = bf16[1024,1024]{1,0:T(8,128)(2,1)} collective-permute-done((bf16[1024,1024]{1,0:T(8,128)(2,1)}, bf16[1024,1024]{1,0:T(8,128)(2,1)}, u32[]{:S(2)}, u32[]{:S(2)}) %collective-permute-start.1) | collective-permute-done | bytes 2097184 | tf_op jit(solution)/shard_map/ppermute | solution.py:68
  65.6 3.2 pad_maximum_fusion
  69.4 16.4 %collective-permute-done.4.v_ref = bf16[2,2048,128]{2,1,0:T(8,128)(2,1)} collective-permute-done((bf16[2,2048,128]{2,1,0:T(8,128)(2,1)}, bf16[2,2048,128]{2,1,0:T(8,128)(2,1)}, u32[]{:S(2)}, u32[]{:S(2)}) %collective-permute-start.4) | collective-permute-done | bytes 1048608 | tf_op jit(solution)/shard_map/ppermute | solution.py:960
  85.8 18.4 %retrieve.3 = (bf16[2,4096,128]{2,1,0:T(8,128)(2,1)}, bf16[2,4096,128]{2,1,0:T(8,128)(2,1)}) custom-call(s32[2,8,4,128]{3,2,1,0:T(4,128)} %bitcast.148, bf16[2,2048,128]{2,1,0:T(8,128)(2,1)} %copy-done.16, bf16[2,2048,128]{2,1,0:T(8,128)(2,1)} %collective-permute-done.4.v_ref, bf16[2,4096,128]{2,1,0:T(8,128)(2,1)} %get-tuple-element.162.refs_0_, ...), custom_call_target="tpu_custom_call" | custom-call | flops 1288490240 | bytes 1258291 | tf_op jit(solution)/shard_map/retrieve/pallas_call | solution.py:188
  104.2 4.3 all-to-all-done
  109.7 18.9 %project.1 = (bf16[2,4096,128]{2,1,0:T(8,128)(2,1)}, bf16[2,4096,128]{2,1,0:T(8,128)(2,1)}, bf16[2,4096,128]{2,1,0:T(8,128)(2,1)}, bf16[2,128,4096]{2,1,0:T(8,128)(2,1)}, bf16[1024,4096]{1,0:T(8,128)(2,1)}) custom-call(s32[4]{0:T(128)} %iota_xor_fusion.order_ref, bf16[1024,1024]{1,0:T(8,128)(2,1)} %refs_2_.3, ...), custom_call_target="tpu_custom_call" | custom-call | flops 966367616 | bytes 4089446 | tf_op jit(solution)/shard_map/project/pallas_call | solution.py:130
  128.6 40.1 %attend.1 = (bf16[1024,256]{1,0:T(8,128)(2,1)}, bf16[1024,256]{1,0:T(8,128)(2,1)}, bf16[1024,256]{1,0:T(8,128)(2,1)}, bf16[1024,256]{1,0:T(8,128)(2,1)}, f32[8,8,512]{2,1,0:T(8,128)}) custom-call(s32[4]{0:T(128)} %iota_xor_fusion.order_ref, bf16[2,4096,128]{2,1,0:T(8,128)(2,1)} %get-tuple-element.159.q_ref, bf16[2,4096,128]{2,1,0:T(8,128)(2,1)} %get-tuple-element.160.k_ref, ...), custom_call_target="tpu_custom_call" | custom-call | flops 2576980480 | bytes 1887436 | tf_op jit(solution)/shard_map/attend/pallas_call | solution.py:289
  168.8 1.8 collective-permute-start.7
  170.6 2.6 copy.49
  173.2 3.1 copy.50
  176.3 18.7 %collective-permute-done.6.refs_2_ = bf16[1024,256]{1,0:T(8,128)(2,1)S(1)} collective-permute-done((bf16[1024,256]{1,0:T(8,128)(2,1)}, bf16[1024,256]{1,0:T(8,128)(2,1)S(1)}, u32[]{:S(2)}, u32[]{:S(2)}) %collective-permute-start.6) | collective-permute-done | bytes 524320 | tf_op jit(solution)/shard_map/ppermute | solution.py:68
  195.0 11.8 %collective-permute-done.7.refs_3_ = bf16[1024,256]{1,0:T(8,128)(2,1)} collective-permute-done((bf16[1024,256]{1,0:T(8,128)(2,1)}, bf16[1024,256]{1,0:T(8,128)(2,1)}, u32[]{:S(2)}, u32[]{:S(2)}) %collective-permute-start.7) | collective-permute-done | bytes 524320 | tf_op jit(solution)/shard_map/ppermute | solution.py:68
  206.8 7.9 %all-gather.2.cloned.1.call-done.refs_4_.refs_5_.refs_6_.refs_7_.wg_ref.wu_ref.wd_ref.refs_2_.refs_3_.w_ref = bf16[1024,9472]{1,0:T(8,128)(2,1)} async-done(((bf16[32,9472]{1,0:T(8,128)(2,1)}), bf16[1024,9472]{1,0:T(8,128)(2,1)}) %all-gather.2.cloned.1.call-update) | async-done | bytes 19398672 | tf_op jit(solution)/shard_map/all_gather | solution.py:971
  214.7 9.6 %mix.1 = (f32[1024,1024]{1,0:T(8,128)}, bf16[1024,1024]{1,0:T(8,128)(2,1)}, bf16[1024,1024]{1,0:T(8,128)(2,1)}, bf16[1024,1024]{1,0:T(8,128)(2,1)}) custom-call(s32[4]{0:T(128)} %iota_xor_fusion.order_ref, bf16[1024,256]{1,0:T(8,128)(2,1)} %get-tuple-element.166.refs_0_.refs_4_, bf16[1024,256]{1,0:T(8,128)(2,1)} %copy-done.17, bf16[1024,256]{1,0:T(8,128)(2,1)} %copy-done.18, ...), custom_call_target="tpu_custom_call" | custom-call | flops 322122560 | bytes 2516582 | tf_op jit(solution)/shard_map/mix/pallas_call | solution.py:495
  224.3 24.9 %gated.1 = (bf16[1024,2816]{1,0:T(8,128)(2,1)}, bf16[1024,2816]{1,0:T(8,128)(2,1)}, bf16[1024,2816]{1,0:T(8,128)(2,1)}) custom-call(bf16[1024,1024]{1,0:T(8,128)(2,1)} %get-tuple-element.173.n_ref, bf16[1024,1024]{1,0:T(8,128)(2,1)} %refs_9_.1, ...), custom_call_target="tpu_custom_call" | custom-call | flops 2657510912 | bytes 5190451 | tf_op jit(solution)/shard_map/gated/pallas_call | solution.py:531
  249.3 15.5 %products.3 = (bf16[1024,1408]{1,0:T(8,128)(2,1)}, bf16[1024,1408]{1,0:T(8,128)(2,1)}, bf16[1024,1408]{1,0:T(8,128)(2,1)}) custom-call(s32[1]{0:T(128)} %bitcast.16.select_ref, bf16[1024,1024]{1,0:T(8,128)(2,1)} %bitcast.130, bf16[1024,1024]{1,0:T(8,128)(2,1)} %get-tuple-element.172.refs_1_, bf16[1024,2816]{1,0:T(8,128)(2,1)} %get-tuple-element.277.refs_2_.refs_3_.h_ref, ...), custom_call_target="tpu_custom_call" | custom-call | flops 1328755456 | bytes 2595225 | tf_op jit(solution)/shard_map/products/pallas_call | solution.py:682
  265.3 27.3 %norm_back.1 = (f32[1024,1024]{1,0:T(8,128)}, bf16[1024,1024]{1,0:T(8,128)(2,1)}, bf16[1024,256]{1,0:T(8,128)(2,1)}, bf16[1024,256]{1,0:T(8,128)(2,1)}, bf16[102...) custom-call(s32[4]{0:T(128)} %iota_xor_fusion.order_ref, bf16[1024,2816]{1,0:T(8,128)(2,1)} %get-tuple-element.180.refs_3_.refs_0_.refs_4_, ...), custom_call_target="tpu_custom_call" | custom-call | flops 2093796608 | bytes 5976883 | tf_op jit(solution)/shard_map/norm_back/pallas_call | solution.py:601
  295.5 24.1 %products.4 = (bf16[512,1408]{1,0:T(8,128)(2,1)}, bf16[512,1408]{1,0:T(8,128)(2,1)}, bf16[512,1408]{1,0:T(8,128)(2,1)}, bf16[512,1024]{1,0:T(8,128)(2,1)}, bf16[...) custom-call(s32[5]{0:T(128)} %stack.44.select_ref, ...), custom_call_target="tpu_custom_call" | custom-call | flops 1650878080 | bytes 3224371 | tf_op jit(solution)/shard_map/products/pallas_call | solution.py:682
  319.6 5.8 %collective-permute-start.16 = (bf16[512,1408]{1,0:T(8,128)(2,1)}, bf16[512,1408]{1,0:T(8,128)(2,1)}, u32[]{:S(2)}, u32[]{:S(2)}) collective-permute-start(bf16[512,1408]{1,0:T(8,128)(2,1)} %get-tuple-element.207), channel_id=1, source_target_pairs={{0,8},{4,12},{8,0},{12,4},{16,24},{20,28},{24,16},{28,20},{1,9},{5... | collective-permute-start | bytes 4325384 | tf_op jit(solution)/shard_map/ppermute | solution.py:813
  326.5 9.5 %collective-permute-start.15 = (bf16[512,1408]{1,0:T(8,128)(2,1)}, bf16[512,1408]{1,0:T(8,128)(2,1)}, u32[]{:S(2)}, u32[]{:S(2)}) collective-permute-start(bf16[512,1408]{1,0:T(8,128)(2,1)} %get-tuple-element.205), channel_id=1, source_target_pairs={{0,4},{4,0},{8,12},{12,8},{16,20},{20,16},{24,28},{28,24},{1,5},{5... | collective-permute-start | bytes 4325384 | tf_op jit(solution)/shard_map/ppermute | solution.py:813
  336.2 44.7 %attend_back.2 = (bf16[4096,256]{1,0:T(8,128)(2,1)}, bf16[4096,256]{1,0:T(8,128)(2,1)}, bf16[4096,256]{1,0:T(8,128)(2,1)}, f32[2,128,2560]{2,1,0:T(8,128)}, f32[8,8,512]{2,1,0:T(8,128)}) custom-call(s32[4]{0:T(128)} %iota_xor_fusion.order_ref, bf16[2,4096,128]{2,1,0:T(8,128)(2,1)} %get-tuple-element.159.q_ref, ...), custom_call_target="tpu_custom_call" | custom-call | flops 1879048192 | bytes 3774873 | tf_op jit(solution)/shard_map/attend_back/pallas_call | solution.py:449
  381.0 2.0 fusion.3
  383.1 1.8 fusion
  385.0 1.8 fusion.1
  387.2 5.5 collective-permute-start.21
  396.3 1.5 collective-permute-start.19
  397.9 37.7 %attend_back.3 = (bf16[4096,256]{1,0:T(8,128)(2,1)}, bf16[4096,256]{1,0:T(8,128)(2,1)}, bf16[4096,256]{1,0:T(8,128)(2,1)}) custom-call(s32[4]{0:T(128)} %iota_xor_fusion.order_ref, bf16[2,4096,128]{2,1,0:T(8,128)(2,1)} %get-tuple-element.159.q_ref, ...), custom_call_target="tpu_custom_call", output_to_operand_aliasing={{0}: (12, {}), {1}: (13, {}), {2}: (14, {})} | custom-call | flops 1342177280 | bytes 3774873 | tf_op jit(solution)/shard_map/attend_back/pallas_call | solution.py:449
  436.7 1.3 add_convert_fusion.2
  438.0 2.1 add_convert_fusion.3
  440.1 5.5 project_back.6
  445.6 5.5 project_back.7
  451.5 4.6 project_back.8
  457.5 1.9 dynamic-slice_bitcast_fusion.17
  460.2 3.4 collective-permute-start.26
  464.4 1.5 collective-permute-start.27
  466.5 4.6 project_back.9
  471.1 11.6 %products.5 = bf16[1024,768]{1,0:T(8,128)(2,1)} custom-call(s32[1]{0:T(128)} %constant.242.clone.1.select_ref, bf16[1024,4096]{1,0:T(8,128)(2,1)} %get-tuple-element.171.refs_0_, bf16[4096,256]{1,0:T(8,128)(2,1)} %get-tuple-element.270.a_ref.refs_1_, bf16[4096,256]{1,0:T(8,128)(2,1)} %get-tuple-element.271.b_ref.refs_2_, ...), custom_call_target="tpu_custom_call" | custom-call | flops 966367616 | bytes 1179648 | tf_op jit(solution)/shard_map/products/pallas_call | solution.py:682
  482.7 1.6 dynamic-slice_bitcast_fusion.1
  484.3 2.1 collective-permute-start.24
  487.0 2.1 collective-permute-start.29
  490.2 3.7 collective-permute-done.24
  495.4 2.1 collective-permute-start.32
  497.4 1.7 collective-permute-start.31
  499.2 7.3 %collective-permute-done.29 = bf16[2,2,128,768]{3,2,1,0:T(8,128)(2,1)S(1)} collective-permute-done((bf16[2,2,128,768]{3,2,1,0:T(8,128)(2,1)S(1)}, bf16[2,2,128,768]{3,2,1,0:T(8,128)(2,1)S(1)}, u32[]{:S(2)}, u32[]{:S(2)}) %collective-permute-start.29) | collective-permute-done | bytes 786464 | tf_op jit(solution)/shard_map/ppermute | solution.py:796
  506.4 1.8 collective-permute-start.30
  508.7 6.2 %collective-permute-done.30 = bf16[64,1408]{1,0:T(8,128)(2,1)S(1)} collective-permute-done((bf16[64,1408]{1,0:T(8,128)(2,1)S(1)}, bf16[64,1408]{1,0:T(8,128)(2,1)S(1)}, u32[]{:S(2)}, u32[]{:S(2)}) %collective-permute-start.30) | collective-permute-done | bytes 180256 | tf_op jit(solution)/shard_map/ppermute | solution.py:796
  515.0 1.6 collective-permute-start.37
  516.8 6.1 %project_back.10.refs_5_ = bf16[1024,1024]{1,0:T(8,128)(2,1)} custom-call(s32[4]{0:T(128)} %iota_xor_fusion.order_ref, bf16[4096,256]{1,0:T(8,128)(2,1)} %get-tuple-element.270.a_ref.refs_1_, bf16[4096,256]{1,0:T(8,128)(2,1)} %get-tuple-element.271.b_ref.refs_2_, bf16[4096,256]{1,0:T(8,128)(2,1)} %get-tuple-element.272.c_ref.refs_3_, ...), custom_call_target="tpu_custom_call" | custom-call | flops 120795952 | bytes 432537 | tf_op jit(solution)/shard_map/project_back/pallas_call | solution.py:766
  522.9 1.7 collective-permute-done.34
  524.6 6.1 %project_back.11 = bf16[1024,1024]{1,0:T(8,128)(2,1)} custom-call(s32[4]{0:T(128)} %iota_xor_fusion.order_ref, bf16[4096,256]{1,0:T(8,128)(2,1)} %get-tuple-element.270.a_ref.refs_1_, bf16[4096,256]{1,0:T(8,128)(2,1)} %get-tuple-element.271.b_ref.refs_2_, bf16[4096,256]{1,0:T(8,128)(2,1)} %get-tuple-element.272.c_ref.refs_3_, ...), custom_call_target="tpu_custom_call", output_to_operand_aliasing={{}: (10, {})} | custom-call | flops 120795952 | bytes 432537 | tf_op jit(solution)/shard_map/project_back/pallas_call | solution.py:766
  531.2 1.7 collective-permute-start.36
  533.6 11.2 %finish.1 = bf16[1024,1024]{1,0:T(8,128)(2,1)} custom-call(f32[1024,1024]{1,0:T(8,128)} %get-tuple-element.170.refs_8_.r_ref, bf16[1024,2816]{1,0:T(8,128)(2,1)} %get-tuple-element.277.refs_2_.refs_3_.h_ref, bf16[1024,9472]{1,0:T(8,128)(2,1)} %all-gather.2.cloned.1.call-done.refs_4_.refs_5_.refs_6_.refs_7_.wg_ref.wu_ref.wd_ref.refs_2_.refs_3_.w_ref), custom_call_target="tpu_custom_call" | custom-call | flops 885836992 | bytes 2673868 | tf_op jit(solution)/shard_map/finish/pallas_call | solution.py:705
  549.3 5.1 feedforward_ends.1
  554.3 2.5 collective-permute-done.41.refs_3_
  556.8 3.3 projection_ends.1
  560.1 1.5 reduce
  561.5 1.5 reduce.1
  (171 shorter events, 34.7 us)
Async XLA Ops:
  7.2 207.5 %all-gather.2.cloned.1.call-start = ((), (), s32[]{:S(2)}) async-start(), calls=%async_computation.2 | async-start | bytes 20004864 | tf_op jit(solution)/shard_map/all_gather | solution.py:971
  8.6 6.1 %copy-start.22 = (bf16[128]{0:T(256)(128)(2,1)S(1)}, bf16[128]{0:T(256)(128)(2,1)}, u32[]{:S(2)}) copy-start(bf16[128]{0:T(256)(128)(2,1)} %param.25) | copy-start | bytes 772
  8.6 6.1 %copy-start.24 = (bf16[128]{0:T(256)(128)(2,1)S(1)}, bf16[128]{0:T(256)(128)(2,1)}, u32[]{:S(2)}) copy-start(bf16[128]{0:T(256)(128)(2,1)} %param.24) | copy-start | bytes 772
  8.6 17.9 %copy-start.20 = (s32[1,2,32,128]{3,2,1,0:T(8,128)S(1)}, s32[1,2,32,128]{3,2,1,0:T(8,128)}, u32[]{:S(2)}) copy-start(s32[1,2,32,128]{3,2,1,0:T(8,128)} %param.28) | copy-start | bytes 98308
  8.6 17.9 %copy-start.21 = (s32[1,2,32,128]{3,2,1,0:T(8,128)S(1)}, s32[1,2,32,128]{3,2,1,0:T(8,128)}, u32[]{:S(2)}) copy-start(s32[1,2,32,128]{3,2,1,0:T(8,128)} %param.29) | copy-start | bytes 98308
  11.6 53.3 %collective-permute-start.1 = (bf16[1024,1024]{1,0:T(8,128)(2,1)}, bf16[1024,1024]{1,0:T(8,128)(2,1)}, u32[]{:S(2)}, u32[]{:S(2)}) collective-permute-start(bf16[1024,1024]{1,0:T(8,128)(2,1)} %refs_2_.3), channel_id=1, source_target_pairs={{0,2},{1,3},{2,0},{3,1},{4,6},{5,7},{6,4},{7,5},{8,10},{9,11},{10,... | collective-permute-start | bytes 6291464 | tf_op jit(solution)/shard_map/ppermute | solution.py:68
  14.7 89.5 %collective-permute-start = (bf16[1024,1024]{1,0:T(8,128)(2,1)}, bf16[1024,1024]{1,0:T(8,128)(2,1)}, u32[]{:S(2)}, u32[]{:S(2)}) collective-permute-start(bf16[1024,1024]{1,0:T(8,128)(2,1)} %refs_2_.3), channel_id=1, source_target_pairs={{0,1},{1,0},{2,3},{3,2},{4,5},{5,4},{6,7},{7,6},{8,9},{9,8},{10,11... | collective-permute-start | bytes 6291464 | tf_op jit(solution)/shard_map/ppermute | solution.py:68
  15.3 12.3 %all-to-all-start.1 = ((bf16[8,2,128]{2,1,0:T(2,128)(2,1)}), bf16[8,2,128]{2,1,0:T(2,128)(2,1)S(1)}, u32[]{:S(2)}, u32[]{:S(2)}) async-start(bf16[8,2,128]{2,1,0:T(2,128)(2,1)} %broadcast_in_dim.15), calls=%async_computation.1 | async-start | bytes 8192 | tf_op jit(solution)/shard_map/all_to_all | solution.py:74
  21.1 48.3 %collective-permute-start.3 = (bf16[2,2048,128]{2,1,0:T(8,128)(2,1)}, bf16[2,2048,128]{2,1,0:T(8,128)(2,1)S(1)}, u32[]{:S(2)}, u32[]{:S(2)}) collective-permute-start(bf16[2,2048,128]{2,1,0:T(8,128)(2,1)} %bitcast.12.k_ref), channel_id=1, source_target_pairs={{0,4},{4,8},{8,12},{12,16},{16,20},{20,24},{24,28},{28,0},{1,5},{5... | collective-permute-start | bytes 3145736 | tf_op jit(solution)/shard_map/ppermute | solution.py:959
  23.1 62.7 %collective-permute-start.4 = (bf16[2,2048,128]{2,1,0:T(8,128)(2,1)}, bf16[2,2048,128]{2,1,0:T(8,128)(2,1)}, u32[]{:S(2)}, u32[]{:S(2)}) collective-permute-start(bf16[2,2048,128]{2,1,0:T(8,128)(2,1)} %bitcast.13.v_ref), channel_id=1, source_target_pairs={{0,4},{4,8},{8,12},{12,16},{16,20},{20,24},{24,28},{28,0},{1,5},{5... | collective-permute-start | bytes 3145736 | tf_op jit(solution)/shard_map/ppermute | solution.py:960
  28.9 79.6 %all-to-all-start = ((bf16[8,128,768]{2,1,0:T(8,128)(2,1)}), bf16[8,128,768]{2,1,0:T(8,128)(2,1)S(1)}, u32[]{:S(2)}, u32[]{:S(2)}) async-start(bf16[8,128,768]{2,1,0:T(8,128)(2,1)} %broadcast_in_dim.14), calls=%async_computation | async-start | bytes 3145728 | tf_op jit(solution)/shard_map/all_to_all | solution.py:74
  64.9 43.6 %collective-permute-start.2 = (bf16[1024,1024]{1,0:T(8,128)(2,1)}, bf16[1024,1024]{1,0:T(8,128)(2,1)}, u32[]{:S(2)}, u32[]{:S(2)}) collective-permute-start(bf16[1024,1024]{1,0:T(8,128)(2,1)} %collective-permute-done.1.refs_2_), channel_id=1, source_target_pairs={{0,1},{1,0},{2,3},{3,2},{4,5},{5,4},{6,7},{7,6},{8,9},{9,8},{10,11... | collective-permute-start | bytes 6291464 | tf_op jit(solution)/shard_map/ppermute | solution.py:68
  69.4 16.4 %copy-start.16 = (bf16[2,2048,128]{2,1,0:T(8,128)(2,1)}, bf16[2,2048,128]{2,1,0:T(8,128)(2,1)S(1)}, u32[]{:S(2)}) copy-start(bf16[2,2048,128]{2,1,0:T(8,128)(2,1)S(1)} %collective-permute-done.3.k_ref) | copy-start | bytes 3145732
  128.6 42.0 %copy-start.3 = (bf16[1024,1024]{1,0:T(8,128)(2,1)S(1)}, bf16[1024,1024]{1,0:T(8,128)(2,1)}, u32[]{:S(2)}) copy-start(bf16[1024,1024]{1,0:T(8,128)(2,1)} %refs_9_.1) | copy-start | bytes 6291460
  168.7 7.6 %collective-permute-start.5 = (bf16[1024,256]{1,0:T(8,128)(2,1)}, bf16[1024,256]{1,0:T(8,128)(2,1)S(1)}, u32[]{:S(2)}, u32[]{:S(2)}) collective-permute-start(bf16[1024,256]{1,0:T(8,128)(2,1)} %get-tuple-element.167.refs_5_), channel_id=1, source_target_pairs={{0,1},{1,0},{2,3},{3,2},{4,5},{5,4},{6,7},{7,6},{8,9},{9,8},{10,11... | collective-permute-start | bytes 1572872 | tf_op jit(solution)/shard_map/ppermute | solution.py:68
  168.7 26.3 %collective-permute-start.6 = (bf16[1024,256]{1,0:T(8,128)(2,1)}, bf16[1024,256]{1,0:T(8,128)(2,1)S(1)}, u32[]{:S(2)}, u32[]{:S(2)}) collective-permute-start(bf16[1024,256]{1,0:T(8,128)(2,1)} %get-tuple-element.168.refs_6_), channel_id=1, source_target_pairs={{0,2},{1,3},{2,0},{3,1},{4,6},{5,7},{6,4},{7,5},{8,10},{9,11},{10,... | collective-permute-start | bytes 1572872 | tf_op jit(solution)/shard_map/ppermute | solution.py:68
  168.8 38.0 %collective-permute-start.7 = (bf16[1024,256]{1,0:T(8,128)(2,1)}, bf16[1024,256]{1,0:T(8,128)(2,1)}, u32[]{:S(2)}, u32[]{:S(2)}) collective-permute-start(bf16[1024,256]{1,0:T(8,128)(2,1)} %get-tuple-element.169.refs_7_), channel_id=1, source_target_pairs={{0,3},{1,2},{2,1},{3,0},{4,7},{5,6},{6,5},{7,4},{8,11},{9,10},{10,... | collective-permute-start | bytes 1572872 | tf_op jit(solution)/shard_map/ppermute | solution.py:68
  176.3 38.4 %copy-start.17 = (bf16[1024,256]{1,0:T(8,128)(2,1)}, bf16[1024,256]{1,0:T(8,128)(2,1)S(1)}, u32[]{:S(2)}) copy-start(bf16[1024,256]{1,0:T(8,128)(2,1)S(1)} %collective-permute-done.5.refs_1_) | copy-start | bytes 1572868
  195.0 19.7 %copy-start.18 = (bf16[1024,256]{1,0:T(8,128)(2,1)}, bf16[1024,256]{1,0:T(8,128)(2,1)S(1)}, u32[]{:S(2)}) copy-start(bf16[1024,256]{1,0:T(8,128)(2,1)S(1)} %collective-permute-done.6.refs_2_) | copy-start | bytes 1572868
  264.8 28.8 %collective-permute-start.11 = (bf16[1024,1408]{1,0:T(8,128)(2,1)}, bf16[1024,1408]{1,0:T(8,128)(2,1)}, u32[]{:S(2)}, u32[]{:S(2)}) collective-permute-start(bf16[1024,1408]{1,0:T(8,128)(2,1)} %get-tuple-element.187), channel_id=1, source_target_pairs={{0,1},{1,0},{2,3},{3,2},{4,5},{5,4},{6,7},{7,6},{8,9},{9,8},{10,11... | collective-permute-start | bytes 8650760 | tf_op jit(solution)/shard_map/ppermute | solution.py:68
  264.8 30.7 %collective-permute-start.12 = (bf16[1024,1408]{1,0:T(8,128)(2,1)}, bf16[1024,1408]{1,0:T(8,128)(2,1)}, u32[]{:S(2)}, u32[]{:S(2)}) collective-permute-start(bf16[1024,1408]{1,0:T(8,128)(2,1)} %get-tuple-element.188), channel_id=1, source_target_pairs={{0,1},{1,0},{2,3},{3,2},{4,5},{5,4},{6,7},{7,6},{8,9},{9,8},{10,11... | collective-permute-start | bytes 8650760 | tf_op jit(solution)/shard_map/ppermute | solution.py:68
  265.3 30.2 %collective-permute-start.13 = (bf16[1024,1408]{1,0:T(8,128)(2,1)}, bf16[1024,1408]{1,0:T(8,128)(2,1)}, u32[]{:S(2)}, u32[]{:S(2)}) collective-permute-start(bf16[1024,1408]{1,0:T(8,128)(2,1)} %get-tuple-element.189), channel_id=1, source_target_pairs={{0,1},{1,0},{2,3},{3,2},{4,5},{5,4},{6,7},{7,6},{8,9},{9,8},{10,11... | collective-permute-start | bytes 8650760 | tf_op jit(solution)/shard_map/ppermute | solution.py:68
  292.6 27.0 %collective-permute-start.10 = (bf16[1024,256]{1,0:T(8,128)(2,1)}, bf16[1024,256]{1,0:T(8,128)(2,1)S(1)}, u32[]{:S(2)}, u32[]{:S(2)}) collective-permute-start(bf16[1024,256]{1,0:T(8,128)(2,1)} %get-tuple-element.184), channel_id=1, source_target_pairs={{0,3},{1,2},{2,1},{3,0},{4,7},{5,6},{6,5},{7,4},{8,11},{9,10},{10,... | collective-permute-start | bytes 1572872 | tf_op jit(solution)/shard_map/ppermute | solution.py:68
  293.5 26.1 %collective-permute-start.8 = (bf16[1024,256]{1,0:T(8,128)(2,1)}, bf16[1024,256]{1,0:T(8,128)(2,1)S(1)}, u32[]{:S(2)}, u32[]{:S(2)}) collective-permute-start(bf16[1024,256]{1,0:T(8,128)(2,1)} %get-tuple-element.182), channel_id=1, source_target_pairs={{0,1},{1,0},{2,3},{3,2},{4,5},{5,4},{6,7},{7,6},{8,9},{9,8},{10,11... | collective-permute-start | bytes 1572872 | tf_op jit(solution)/shard_map/ppermute | solution.py:68
  293.5 26.1 %collective-permute-start.9 = (bf16[1024,256]{1,0:T(8,128)(2,1)}, bf16[1024,256]{1,0:T(8,128)(2,1)S(1)}, u32[]{:S(2)}, u32[]{:S(2)}) collective-permute-start(bf16[1024,256]{1,0:T(8,128)(2,1)} %get-tuple-element.183), channel_id=1, source_target_pairs={{0,2},{1,3},{2,0},{3,1},{4,6},{5,7},{6,4},{7,5},{8,10},{9,11},{10,... | collective-permute-start | bytes 1572872 | tf_op jit(solution)/shard_map/ppermute | solution.py:68
  319.6 16.7 %copy-start.7 = (bf16[1024,256]{1,0:T(8,128)(2,1)}, bf16[1024,256]{1,0:T(8,128)(2,1)S(1)}, u32[]{:S(2)}) copy-start(bf16[1024,256]{1,0:T(8,128)(2,1)S(1)} %collective-permute-done.10.refs_3_) | copy-start | bytes 1572868
  319.6 16.6 %copy-start.8 = (bf16[1024,256]{1,0:T(8,128)(2,1)}, bf16[1024,256]{1,0:T(8,128)(2,1)S(1)}, u32[]{:S(2)}) copy-start(bf16[1024,256]{1,0:T(8,128)(2,1)S(1)} %collective-permute-done.8.refs_1_) | copy-start | bytes 1572868
  319.6 16.6 %copy-start.9 = (bf16[1024,256]{1,0:T(8,128)(2,1)}, bf16[1024,256]{1,0:T(8,128)(2,1)S(1)}, u32[]{:S(2)}) copy-start(bf16[1024,256]{1,0:T(8,128)(2,1)S(1)} %collective-permute-done.9.refs_2_) | copy-start | bytes 1572868
  319.6 63.4 %collective-permute-start.16 = (bf16[512,1408]{1,0:T(8,128)(2,1)}, bf16[512,1408]{1,0:T(8,128)(2,1)}, u32[]{:S(2)}, u32[]{:S(2)}) collective-permute-start(bf16[512,1408]{1,0:T(8,128)(2,1)} %get-tuple-element.207), channel_id=1, source_target_pairs={{0,8},{4,12},{8,0},{12,4},{16,24},{20,28},{24,16},{28,20},{1,9},{5... | collective-permute-start | bytes 4325384 | tf_op jit(solution)/shard_map/ppermute | solution.py:813
  325.4 55.6 %collective-permute-start.17 = (bf16[512,1024]{1,0:T(8,128)(2,1)}, bf16[512,1024]{1,0:T(8,128)(2,1)}, u32[]{:S(2)}, u32[]{:S(2)}) collective-permute-start(bf16[512,1024]{1,0:T(8,128)(2,1)} %get-tuple-element.209), channel_id=1, source_target_pairs={{0,16},{4,20},{8,24},{12,28},{16,0},{20,4},{24,8},{28,12},{1,17},{... | collective-permute-start | bytes 3145736 | tf_op jit(solution)/shard_map/ppermute | solution.py:813
  326.5 58.5 %collective-permute-start.15 = (bf16[512,1408]{1,0:T(8,128)(2,1)}, bf16[512,1408]{1,0:T(8,128)(2,1)}, u32[]{:S(2)}, u32[]{:S(2)}) collective-permute-start(bf16[512,1408]{1,0:T(8,128)(2,1)} %get-tuple-element.205), channel_id=1, source_target_pairs={{0,4},{4,0},{8,12},{12,8},{16,20},{20,16},{24,28},{28,24},{1,5},{5... | collective-permute-start | bytes 4325384 | tf_op jit(solution)/shard_map/ppermute | solution.py:813
  336.0 50.8 %collective-permute-start.14 = (bf16[512,1408]{1,0:T(8,128)(2,1)}, bf16[512,1408]{1,0:T(8,128)(2,1)S(1)}, u32[]{:S(2)}, u32[]{:S(2)}) collective-permute-start(bf16[512,1408]{1,0:T(8,128)(2,1)} %get-tuple-element.203), channel_id=1, source_target_pairs={{0,2},{1,3},{2,0},{3,1},{4,6},{5,7},{6,4},{7,5},{8,10},{9,11},{10,... | collective-permute-start | bytes 4325384 | tf_op jit(solution)/shard_map/ppermute | solution.py:813
  381.0 2.1 copy-start.12
  387.2 48.3 %collective-permute-start.21 = (bf16[2,128,1024]{2,1,0:T(8,128)(2,1)S(1)}, bf16[2,128,1024]{2,1,0:T(8,128)(2,1)S(1)}, u32[]{:S(2)}, u32[]{:S(2)}) collective-permute-start(bf16[2,128,1024]{2,1,0:T(8,128)(2,1)S(1)} %get-tuple-element.309), channel_id=1, source_target_pairs={{0,4},{4,0},{8,12},{12,8},{16,20},{20,16},{24,28},{28,24},{1,5},{5... | collective-permute-start | bytes 1572872 | tf_op jit(solution)/shard_map/ppermute | solution.py:796
  393.7 42.1 %collective-permute-start.20 = (bf16[2,2,64,1408]{3,2,1,0:T(8,128)(2,1)}, bf16[2,2,64,1408]{3,2,1,0:T(8,128)(2,1)S(1)}, u32[]{:S(2)}, u32[]{:S(2)}) collective-permute-start(bf16[2,2,64,1408]{3,2,1,0:T(8,128)(2,1)} %get-tuple-element.301), channel_id=1, source_target_pairs={{0,2},{1,3},{2,0},{3,1},{4,6},{5,7},{6,4},{7,5},{8,10},{9,11},{10,... | collective-permute-start | bytes 2162696 | tf_op jit(solution)/shard_map/ppermute | solution.py:796
  396.3 39.7 %collective-permute-start.19 = (bf16[2,2,64,1408]{3,2,1,0:T(8,128)(2,1)}, bf16[2,2,64,1408]{3,2,1,0:T(8,128)(2,1)}, u32[]{:S(2)}, u32[]{:S(2)}) collective-permute-start(bf16[2,2,64,1408]{3,2,1,0:T(8,128)(2,1)} %get-tuple-element.303), channel_id=1, source_target_pairs={{0,2},{1,3},{2,0},{3,1},{4,6},{5,7},{6,4},{7,5},{8,10},{9,11},{10,... | collective-permute-start | bytes 2162696 | tf_op jit(solution)/shard_map/ppermute | solution.py:796
  397.9 40.1 %collective-permute-start.18 = (bf16[2,2,64,1408]{3,2,1,0:T(8,128)(2,1)}, bf16[2,2,64,1408]{3,2,1,0:T(8,128)(2,1)}, u32[]{:S(2)}, u32[]{:S(2)}) collective-permute-start(bf16[2,2,64,1408]{3,2,1,0:T(8,128)(2,1)} %get-tuple-element.306), channel_id=1, source_target_pairs={{0,4},{4,0},{8,12},{12,8},{16,20},{20,16},{24,28},{28,24},{1,5},{5... | collective-permute-start | bytes 2162696 | tf_op jit(solution)/shard_map/ppermute | solution.py:796
  445.6 6.0 %collective-permute-start.22 = (bf16[1024,1024]{1,0:T(8,128)(2,1)}, bf16[1024,1024]{1,0:T(8,128)(2,1)}, u32[]{:S(2)}, u32[]{:S(2)}) collective-permute-start(bf16[1024,1024]{1,0:T(8,128)(2,1)} %project_back.6), channel_id=1, source_target_pairs={{0,1},{1,0},{2,3},{3,2},{4,5},{5,4},{6,7},{7,6},{8,9},{9,8},{10,11... | collective-permute-start | bytes 6291464 | tf_op jit(solution)/shard_map/ppermute | solution.py:68
  451.0 42.9 %collective-permute-start.28 = (bf16[1024,1024]{1,0:T(8,128)(2,1)}, bf16[1024,1024]{1,0:T(8,128)(2,1)S(1)}, u32[]{:S(2)}, u32[]{:S(2)}) collective-permute-start(bf16[1024,1024]{1,0:T(8,128)(2,1)} %project_back.7), channel_id=1, source_target_pairs={{0,1},{1,0},{2,3},{3,2},{4,5},{5,4},{6,7},{7,6},{8,9},{9,8},{10,11... | collective-permute-start | bytes 6291464 | tf_op jit(solution)/shard_map/ppermute | solution.py:68
  456.1 28.2 %collective-permute-start.23 = (bf16[512,1024]{1,0:T(8,128)(2,1)}, bf16[512,1024]{1,0:T(8,128)(2,1)}, u32[]{:S(2)}, u32[]{:S(2)}) collective-permute-start(bf16[512,1024]{1,0:T(8,128)(2,1)} %project_back.8), channel_id=1, source_target_pairs={{0,2},{1,3},{2,0},{3,1},{4,6},{5,7},{6,4},{7,5},{8,10},{9,11},{10,... | collective-permute-start | bytes 3145736 | tf_op jit(solution)/shard_map/ppermute | solution.py:68
  460.2 26.2 %collective-permute-start.26 = (bf16[2,64,1408]{2,1,0:T(8,128)(2,1)}, bf16[2,64,1408]{2,1,0:T(8,128)(2,1)S(1)}, u32[]{:S(2)}, u32[]{:S(2)}) collective-permute-start(bf16[2,64,1408]{2,1,0:T(8,128)(2,1)} %get-tuple-element.313), channel_id=1, source_target_pairs={{0,16},{4,20},{8,24},{12,28},{16,0},{20,4},{24,8},{28,12},{1,17},{... | collective-permute-start | bytes 1081352 | tf_op jit(solution)/shard_map/ppermute | solution.py:796
  464.4 24.8 %collective-permute-start.27 = (bf16[2,64,1024]{2,1,0:T(8,128)(2,1)}, bf16[2,64,1024]{2,1,0:T(8,128)(2,1)}, u32[]{:S(2)}, u32[]{:S(2)}) collective-permute-start(bf16[2,64,1024]{2,1,0:T(8,128)(2,1)} %get-tuple-element.319), channel_id=1, source_target_pairs={{0,2},{1,3},{2,0},{3,1},{4,6},{5,7},{6,4},{7,5},{8,10},{9,11},{10,... | collective-permute-start | bytes 786440 | tf_op jit(solution)/shard_map/ppermute | solution.py:796
  465.9 21.0 %collective-permute-start.25 = (bf16[2,64,1408]{2,1,0:T(8,128)(2,1)}, bf16[2,64,1408]{2,1,0:T(8,128)(2,1)S(1)}, u32[]{:S(2)}, u32[]{:S(2)}) collective-permute-start(bf16[2,64,1408]{2,1,0:T(8,128)(2,1)} %get-tuple-element.315), channel_id=1, source_target_pairs={{0,8},{4,12},{8,0},{12,4},{16,24},{20,28},{24,16},{28,20},{1,9},{5... | collective-permute-start | bytes 1081352 | tf_op jit(solution)/shard_map/ppermute | solution.py:796
  482.7 6.4 %copy-start.13 = (bf16[2,64,1408]{2,1,0:T(8,128)(2,1)S(1)}, bf16[2,64,1408]{2,1,0:T(8,128)(2,1)}, u32[]{:S(2)}) copy-start(bf16[2,64,1408]{2,1,0:T(8,128)(2,1)} %get-tuple-element.256) | copy-start | bytes 1081348
  482.7 6.5 %copy-start.15 = (bf16[2,64,1024]{2,1,0:T(8,128)(2,1)S(1)}, bf16[2,64,1024]{2,1,0:T(8,128)(2,1)}, u32[]{:S(2)}) copy-start(bf16[2,64,1024]{2,1,0:T(8,128)(2,1)} %get-tuple-element.258) | copy-start | bytes 786436
  484.3 9.6 %collective-permute-start.24 = (bf16[2,64,1408]{2,1,0:T(8,128)(2,1)S(1)}, bf16[2,64,1408]{2,1,0:T(8,128)(2,1)S(1)}, u32[]{:S(2)}, u32[]{:S(2)}) collective-permute-start(bf16[2,64,1408]{2,1,0:T(8,128)(2,1)S(1)} %copy-done.19), channel_id=1, source_target_pairs={{0,8},{4,12},{8,0},{12,4},{16,24},{20,28},{24,16},{28,20},{1,9},{5... | collective-permute-start | bytes 1081352 | tf_op jit(solution)/shard_map/ppermute | solution.py:796
  486.4 38.2 %collective-permute-start.35 = (bf16[512,1024]{1,0:T(8,128)(2,1)}, bf16[512,1024]{1,0:T(8,128)(2,1)}, u32[]{:S(2)}, u32[]{:S(2)}) collective-permute-start(bf16[512,1024]{1,0:T(8,128)(2,1)} %project_back.9), channel_id=1, source_target_pairs={{0,2},{1,3},{2,0},{3,1},{4,6},{5,7},{6,4},{7,5},{8,10},{9,11},{10,... | collective-permute-start | bytes 3145736 | tf_op jit(solution)/shard_map/ppermute | solution.py:68
  487.0 19.5 %collective-permute-start.29 = (bf16[2,2,128,768]{3,2,1,0:T(8,128)(2,1)S(1)}, bf16[2,2,128,768]{3,2,1,0:T(8,128)(2,1)S(1)}, u32[]{:S(2)}, u32[]{:S(2)}) collective-permute-start(bf16[2,2,128,768]{3,2,1,0:T(8,128)(2,1)S(1)} %get-tuple-element.300), channel_id=1, source_target_pairs={{0,4},{4,0},{8,12},{12,8},{16,20},{20,16},{24,28},{28,24},{1,5},{5... | collective-permute-start | bytes 2359304 | tf_op jit(solution)/shard_map/ppermute | solution.py:796
  494.0 14.5 %copy-start.4 = (bf16[1024,1024]{1,0:T(8,128)(2,1)}, bf16[1024,1024]{1,0:T(8,128)(2,1)S(1)}, u32[]{:S(2)}) copy-start(bf16[1024,1024]{1,0:T(8,128)(2,1)S(1)} %collective-permute-done.28.refs_0_) | copy-start | bytes 6291460
  494.0 14.5 %collective-permute-start.33 = (bf16[64,1024]{1,0:T(8,128)(2,1)S(1)}, bf16[64,1024]{1,0:T(8,128)(2,1)S(1)}, u32[]{:S(2)}, u32[]{:S(2)}) collective-permute-start(bf16[64,1024]{1,0:T(8,128)(2,1)S(1)} %get-tuple-element.329), channel_id=1, source_target_pairs={{0,8},{4,12},{8,0},{12,4},{16,24},{20,28},{24,16},{28,20},{1,9},{5... | collective-permute-start | bytes 393224 | tf_op jit(solution)/shard_map/ppermute | solution.py:796
  495.4 13.2 %collective-permute-start.32 = (bf16[64,1408]{1,0:T(8,128)(2,1)S(1)}, bf16[64,1408]{1,0:T(8,128)(2,1)S(1)}, u32[]{:S(2)}, u32[]{:S(2)}) collective-permute-start(bf16[64,1408]{1,0:T(8,128)(2,1)S(1)} %get-tuple-element.323), channel_id=1, source_target_pairs={{0,4},{4,0},{8,12},{12,8},{16,20},{20,16},{24,28},{28,24},{1,5},{5... | collective-permute-start | bytes 540680 | tf_op jit(solution)/shard_map/ppermute | solution.py:796
  497.4 11.2 %collective-permute-start.31 = (bf16[64,1408]{1,0:T(8,128)(2,1)S(1)}, bf16[64,1408]{1,0:T(8,128)(2,1)S(1)}, u32[]{:S(2)}, u32[]{:S(2)}) collective-permute-start(bf16[64,1408]{1,0:T(8,128)(2,1)S(1)} %get-tuple-element.325), channel_id=1, source_target_pairs={{0,16},{4,20},{8,24},{12,28},{16,0},{20,4},{24,8},{28,12},{1,17},{... | collective-permute-start | bytes 540680 | tf_op jit(solution)/shard_map/ppermute | solution.py:796
  506.4 8.4 %collective-permute-start.30 = (bf16[64,1408]{1,0:T(8,128)(2,1)S(1)}, bf16[64,1408]{1,0:T(8,128)(2,1)S(1)}, u32[]{:S(2)}, u32[]{:S(2)}) collective-permute-start(bf16[64,1408]{1,0:T(8,128)(2,1)S(1)} %get-tuple-element.327), channel_id=1, source_target_pairs={{0,16},{4,20},{8,24},{12,28},{16,0},{20,4},{24,8},{28,12},{1,17},{... | collective-permute-start | bytes 540680 | tf_op jit(solution)/shard_map/ppermute | solution.py:796
  515.0 15.7 %collective-permute-start.37 = (bf16[64,5248]{1,0:T(8,128)(2,1)S(1)}, bf16[64,5248]{1,0:T(8,128)(2,1)S(1)}, u32[]{:S(2)}, u32[]{:S(2)}) collective-permute-start(bf16[64,5248]{1,0:T(8,128)(2,1)S(1)} %constant_dynamic-update-slice_fusion), channel_id=1, source_target_pairs={{0,2},{1,3},{2,0},{3,1},{4,6},{5,7},{6,4},{7,5},{8,10},{9,11},{10,... | collective-permute-start | bytes 2015240 | tf_op jit(solution)/shard_map/ppermute | solution.py:68
  516.7 7.8 %collective-permute-start.34 = (bf16[2,128,768]{2,1,0:T(8,128)(2,1)S(1)}, bf16[2,128,768]{2,1,0:T(8,128)(2,1)S(1)}, u32[]{:S(2)}, u32[]{:S(2)}) collective-permute-start(bf16[2,128,768]{2,1,0:T(8,128)(2,1)S(1)} %get-tuple-element.312), channel_id=1, source_target_pairs={{0,8},{4,12},{8,0},{12,4},{16,24},{20,28},{24,16},{28,20},{1,9},{5... | collective-permute-start | bytes 1179656 | tf_op jit(solution)/shard_map/ppermute | solution.py:796
  530.9 2.0 copy-start.23
  531.1 13.8 %copy-start.5 = (bf16[2,64,5248]{2,1,0:T(8,128)(2,1)}, bf16[2,64,5248]{2,1,0:T(8,128)(2,1)S(1)}, u32[]{:S(2)}) copy-start(bf16[2,64,5248]{2,1,0:T(8,128)(2,1)S(1)} %pad_maximum_fusion.2) | copy-start | bytes 4030468
  531.1 17.1 %collective-permute-start.38 = (bf16[128,5248]{1,0:T(8,128)(2,1)S(1)}, bf16[128,5248]{1,0:T(8,128)(2,1)S(1)}, u32[]{:S(2)}, u32[]{:S(2)}) collective-permute-start(bf16[128,5248]{1,0:T(8,128)(2,1)S(1)} %bitcast.138), channel_id=1, source_target_pairs={{0,1},{1,0},{2,3},{3,2},{4,5},{5,4},{6,7},{7,6},{8,9},{9,8},{10,11... | collective-permute-start | bytes 4030472 | tf_op jit(solution)/shard_map/ppermute | solution.py:68
  531.2 13.6 %collective-permute-start.36 = (bf16[128,768]{1,0:T(8,128)(2,1)S(1)}, bf16[128,768]{1,0:T(8,128)(2,1)S(1)}, u32[]{:S(2)}, u32[]{:S(2)}) collective-permute-start(bf16[128,768]{1,0:T(8,128)(2,1)S(1)} %get-tuple-element.322), channel_id=1, source_target_pairs={{0,16},{4,20},{8,24},{12,28},{16,0},{20,4},{24,8},{28,12},{1,17},{... | collective-permute-start | bytes 589832 | tf_op jit(solution)/shard_map/ppermute | solution.py:796
  533.6 13.8 %copy-start.25 = (bf16[128]{0:T(256)(128)(2,1)S(1)}, bf16[128]{0:T(256)(128)(2,1)}, u32[]{:S(2)}) copy-start(bf16[128]{0:T(256)(128)(2,1)} %param.24) | copy-start | bytes 772
  545.6 8.7 %collective-permute-start.39 = (bf16[128,768]{1,0:T(8,128)(2,1)}, bf16[128,768]{1,0:T(8,128)(2,1)}, u32[]{:S(2)}, u32[]{:S(2)}) collective-permute-start(bf16[128,768]{1,0:T(8,128)(2,1)} %add_convert_fusion.10.refs_0_), channel_id=1, source_target_pairs={{0,1},{1,0},{2,3},{3,2},{4,5},{5,4},{6,7},{7,6},{8,9},{9,8},{10,11... | collective-permute-start | bytes 589832 | tf_op jit(solution)/shard_map/ppermute | solution.py:68
  545.8 8.5 %collective-permute-start.40 = (bf16[128,768]{1,0:T(8,128)(2,1)}, bf16[128,768]{1,0:T(8,128)(2,1)}, u32[]{:S(2)}, u32[]{:S(2)}) collective-permute-start(bf16[128,768]{1,0:T(8,128)(2,1)} %add_convert_fusion.10.refs_0_), channel_id=1, source_target_pairs={{0,2},{1,3},{2,0},{3,1},{4,6},{5,7},{6,4},{7,5},{8,10},{9,11},{10,... | collective-permute-start | bytes 589832 | tf_op jit(solution)/shard_map/ppermute | solution.py:68
  546.2 10.6 %collective-permute-start.41 = (bf16[128,768]{1,0:T(8,128)(2,1)}, bf16[128,768]{1,0:T(8,128)(2,1)}, u32[]{:S(2)}, u32[]{:S(2)}) collective-permute-start(bf16[128,768]{1,0:T(8,128)(2,1)} %add_convert_fusion.10.refs_0_), channel_id=1, source_target_pairs={{0,3},{1,2},{2,1},{3,0},{4,7},{5,6},{6,5},{7,4},{8,11},{9,10},{10,... | collective-permute-start | bytes 589832 | tf_op jit(solution)/shard_map/ppermute | solution.py:68
  547.4 15.6 %copy-start.1 = (bf16[2816,128]{1,0:T(8,128)(2,1)S(1)}, bf16[2816,128]{1,0:T(8,128)(2,1)}, u32[]{:S(2)}) copy-start(bf16[2816,128]{1,0:T(8,128)(2,1)} %param.23) | copy-start | bytes 2162692
  (7 other events, 9.8 us)
Sparse Core Ops, SparseCore 0:
  11.8 202.9 all-gather.1

commit v5 on v4

--- a/solution.py
+++ b/solution.py
@@ -356,17 +356,13 @@
             start = pl.multiple_of(index * block, block)
             q = q_ref[head, pl.ds(start, block), :]
             do = do_ref[pl.ds(start, block), cols(head)]
-            mk_t = mk_ref[head].T
-            parts = []
-            for g in range(groups):
-                lanes = slice(g * mem_block, (g + 1) * mem_block)
-                slots = slice(g * mem_count, (g + 1) * mem_count)
-                scores = dot_nt(mk_ref[head, slots, :], q[lanes])
-                weight = jnp.exp2(scores * factor - lse_ref[index, head : head + 1, lanes])
-                dp = dot_nt(mv_ref[head, slots, :], do[lanes])
-                ds = (weight * (dp - delta[index, head : head + 1, lanes])).astype(bf16)
-                parts.append(dot(mk_t[:, slots], ds))
-            return jnp.concatenate(parts, axis=1)
+            scores = dot_nt(mk_ref[head], q)
+            weight = jnp.exp2(scores * factor - lse_ref[index, head : head + 1, :])
+            slot = lax.broadcasted_iota(jnp.int32, scores.shape, 0) // mem_count
+            own = slot == lax.broadcasted_iota(jnp.int32, scores.shape, 1) // mem_block
+            dp = dot_nt(mv_ref[head], do)
+            ds = jnp.where(own, weight * (dp - delta[index, head : head + 1, :]), 0.0)
+            return dot(mk_ref[head].T, ds.astype(bf16))
 
         def step(head, carry, i, masked):
             dk, dv = carry
@@ -875,10 +871,10 @@
         total = jnp.sum(
             wg_ref[...].astype(f32) * gate + wu_ref[...].astype(f32) * up, axis=1, keepdims=True
         )
-        gg_ref[...] = total / gain_ref[...]
+        gg_ref[...] = jnp.broadcast_to(total / gain_ref[...], (rows, 128)).T[0:1, :]
 
     whole = lambda shape: pl.BlockSpec(shape, lambda i, h: (0, 0))
-    shapes = [(rows, hidden_cols)] * 2 + [(hidden_cols, rows), (rows, width), (rows, 1)]
+    shapes = [(rows, hidden_cols)] * 2 + [(hidden_cols, rows), (rows, width), (1, rows)]
     *ends, gain_grad = call(
         kernel,
         (1,),
@@ -889,7 +885,7 @@
         20 * rows * hidden_cols,
         prefetch=1,
     )(half, joined, other, gate_weight, up_weight, gain.astype(f32)[:, None])
-    return *ends, gain_grad[:, 0]
+    return *ends, gain_grad[0]
 
 
 def projection_ends(order, pieces, weights, gain):
@@ -910,10 +906,10 @@
         for j in range(3):
             part = jnp.sum(w_refs[j][...].astype(f32) * outs[j][...], axis=1, keepdims=True)
             total = part if total is None else total + part
-        gg_ref[...] = total / gain_ref[...]
+        gg_ref[...] = jnp.broadcast_to(total / gain_ref[...], (rows, 128)).T[0:1, :]
 
     whole = lambda shape: pl.BlockSpec(shape, lambda i, o: (0, 0))
-    shapes = [(rows, width)] * 3 + [(rows, 1)]
+    shapes = [(rows, width)] * 3 + [(1, rows)]
     *ends, gain_grad = call(
         kernel,
         (1,),
@@ -924,7 +920,7 @@
         24 * rows * width,
         prefetch=1,
     )(order, *pieces, *weights, gain.astype(f32)[:, None])
-    return *ends, gain_grad[:, 0]
+    return *ends, gain_grad[0]
 
 
 def body(

time: 578 us -> 573 us (level)
  transfers between devices with their start and end apart: 45 -> 45, of which waited for: 12 -> 12; matrix products, arithmetic and copies ran while one was open for 6% -> 7% of each run, Pallas kernels for 50% -> 50%
where the time goes in v5:
time: 573 us; the launch traced here: 565 us
  Pallas kernels  339 us (59%)
  waiting for transfers between devices  94.3 us (16%)
  starting transfers between devices  70.4 us (12%)
  local copies, waits for them, and re-layouts  28.1 us (5%)
  other arithmetic  18.9 us (3%)
  between operations  15 us (3%)
    pallas_call x2, Pallas kernels, attend_back(): call(kernel, (last - first,), in_specs + [small, table, table], out_specs...  79.2 us
    pallas_call x3, Pallas kernels, products(): call(kernel, (height // block,), [pl.BlockSpec((block, d.shape[1]), lambd...  51.2 us
    ppermute x21, waiting for transfers between devices, swap_seq(): return lax.ppermute(array, 'seq', [(i, i ^ bit) for i in range(count)])  46.7 us
    pallas_call x1, Pallas kernels, attend(): call(kernel, (count,), [rows, full, full_t, mem_rows, mem_rows], [pl.Bloc...  40.3 us
    pallas_call x2, Pallas kernels, retrieve(): call(kernel, (head_local, blocks // per), [pl.BlockSpec((1, 1, per, slots...  35.7 us
    pallas_call x6, Pallas kernels, project_back(): call(kernel, (steps,), in_specs, rows_of(out), out, 6 * rows * width * gr...  32.3 us
    pallas_call x1, Pallas kernels, norm_back(): call(kernel, (steps + row_steps,), [resident(g.shape, (0, 0)) for g in gr...  27.3 us
    ppermute x15, starting transfers between devices, trade(): lax.ppermute(give, axis, [(i, i ^ bit) for i in range(count)])  27.2 us
  transfers between devices with their start and end apart: 45, of which 12 were waited for; matrix products, arithmetic and copies ran while one was open for 7% of the time, Pallas kernels for 50%

profile of v5, /device:TPU:0, one launch (start us, length us, event | category | flops | bytes accessed | tf_op | source)
XLA Modules:
  0.0 565.5 jit_solution(3561092275417529441)
XLA Ops:
  11.6 3.0 collective-permute-start.1
  15.3 5.8 %all-to-all-start.1 = ((bf16[8,2,128]{2,1,0:T(2,128)(2,1)}), bf16[8,2,128]{2,1,0:T(2,128)(2,1)S(1)}, u32[]{:S(2)}, u32[]{:S(2)}) async-start(bf16[8,2,128]{2,1,0:T(2,128)(2,1)} %broadcast_in_dim.15), calls=%async_computation.1 | async-start | bytes 8192 | tf_op jit(solution)/shard_map/all_to_all | solution.py:74
  21.1 2.0 collective-permute-start.3
  23.1 1.5 collective-permute-start.4
  27.6 1.3 broadcast_in_dim.14
  28.9 4.2 all-to-all-start
  33.2 17.3 %retrieve.2 = (bf16[2,4096,128]{2,1,0:T(8,128)(2,1)}, bf16[2,4096,128]{2,1,0:T(8,128)(2,1)}) custom-call(s32[2,8,4,128]{3,2,1,0:T(4,128)} %bitcast.149, bf16[2,2048,128]{2,1,0:T(8,128)(2,1)} %bitcast.12.k_ref, bf16[2,2048,128]{2,1,0:T(8,128)(2,1)} %bitcast.13.v_ref), custom_call_target="tpu_custom_call" | custom-call | flops 1288490240 | bytes 1258291 | tf_op jit(solution)/shard_map/retrieve/pallas_call | solution.py:188
  51.1 13.8 %collective-permute-done.1.refs_2_ = bf16[1024,1024]{1,0:T(8,128)(2,1)} collective-permute-done((bf16[1024,1024]{1,0:T(8,128)(2,1)}, bf16[1024,1024]{1,0:T(8,128)(2,1)}, u32[]{:S(2)}, u32[]{:S(2)}) %collective-permute-start.1) | collective-permute-done | bytes 2097184 | tf_op jit(solution)/shard_map/ppermute | solution.py:68
  65.7 3.2 pad_maximum_fusion
  69.4 16.3 %collective-permute-done.4.v_ref = bf16[2,2048,128]{2,1,0:T(8,128)(2,1)} collective-permute-done((bf16[2,2048,128]{2,1,0:T(8,128)(2,1)}, bf16[2,2048,128]{2,1,0:T(8,128)(2,1)}, u32[]{:S(2)}, u32[]{:S(2)}) %collective-permute-start.4) | collective-permute-done | bytes 1048608 | tf_op jit(solution)/shard_map/ppermute | solution.py:956
  85.8 18.4 %retrieve.3 = (bf16[2,4096,128]{2,1,0:T(8,128)(2,1)}, bf16[2,4096,128]{2,1,0:T(8,128)(2,1)}) custom-call(s32[2,8,4,128]{3,2,1,0:T(4,128)} %bitcast.150, bf16[2,2048,128]{2,1,0:T(8,128)(2,1)} %copy-done.16, bf16[2,2048,128]{2,1,0:T(8,128)(2,1)} %collective-permute-done.4.v_ref, bf16[2,4096,128]{2,1,0:T(8,128)(2,1)} %get-tuple-element.162.refs_0_, ...), custom_call_target="tpu_custom_call" | custom-call | flops 1288490240 | bytes 1258291 | tf_op jit(solution)/shard_map/retrieve/pallas_call | solution.py:188
  104.2 4.3 all-to-all-done
  109.7 18.9 %project.1 = (bf16[2,4096,128]{2,1,0:T(8,128)(2,1)}, bf16[2,4096,128]{2,1,0:T(8,128)(2,1)}, bf16[2,4096,128]{2,1,0:T(8,128)(2,1)}, bf16[2,128,4096]{2,1,0:T(8,128)(2,1)}, bf16[1024,4096]{1,0:T(8,128)(2,1)}) custom-call(s32[4]{0:T(128)} %iota_xor_fusion.order_ref, bf16[1024,1024]{1,0:T(8,128)(2,1)} %refs_2_.3, ...), custom_call_target="tpu_custom_call" | custom-call | flops 966367616 | bytes 4089446 | tf_op jit(solution)/shard_map/project/pallas_call | solution.py:130
  128.6 40.3 %attend.1 = (bf16[1024,256]{1,0:T(8,128)(2,1)}, bf16[1024,256]{1,0:T(8,128)(2,1)}, bf16[1024,256]{1,0:T(8,128)(2,1)}, bf16[1024,256]{1,0:T(8,128)(2,1)}, f32[8,8,512]{2,1,0:T(8,128)}) custom-call(s32[4]{0:T(128)} %iota_xor_fusion.order_ref, bf16[2,4096,128]{2,1,0:T(8,128)(2,1)} %get-tuple-element.159.q_ref, bf16[2,4096,128]{2,1,0:T(8,128)(2,1)} %get-tuple-element.160.k_ref, ...), custom_call_target="tpu_custom_call" | custom-call | flops 2576980480 | bytes 1887436 | tf_op jit(solution)/shard_map/attend/pallas_call | solution.py:289
  169.0 1.8 collective-permute-start.7
  170.8 2.6 copy.49
  173.4 3.2 copy.50
  176.5 18.6 %collective-permute-done.6.refs_2_ = bf16[1024,256]{1,0:T(8,128)(2,1)S(1)} collective-permute-done((bf16[1024,256]{1,0:T(8,128)(2,1)}, bf16[1024,256]{1,0:T(8,128)(2,1)S(1)}, u32[]{:S(2)}, u32[]{:S(2)}) %collective-permute-start.6) | collective-permute-done | bytes 524320 | tf_op jit(solution)/shard_map/ppermute | solution.py:68
  195.2 11.7 %collective-permute-done.7.refs_3_ = bf16[1024,256]{1,0:T(8,128)(2,1)} collective-permute-done((bf16[1024,256]{1,0:T(8,128)(2,1)}, bf16[1024,256]{1,0:T(8,128)(2,1)}, u32[]{:S(2)}, u32[]{:S(2)}) %collective-permute-start.7) | collective-permute-done | bytes 524320 | tf_op jit(solution)/shard_map/ppermute | solution.py:68
  206.8 7.7 %all-gather.2.cloned.1.call-done.refs_4_.refs_5_.refs_6_.refs_7_.wg_ref.wu_ref.wd_ref.refs_2_.refs_3_.w_ref = bf16[1024,9472]{1,0:T(8,128)(2,1)} async-done(((bf16[32,9472]{1,0:T(8,128)(2,1)}), bf16[1024,9472]{1,0:T(8,128)(2,1)}) %all-gather.2.cloned.1.call-update) | async-done | bytes 19398672 | tf_op jit(solution)/shard_map/all_gather | solution.py:967
  214.6 9.6 %mix.1 = (f32[1024,1024]{1,0:T(8,128)}, bf16[1024,1024]{1,0:T(8,128)(2,1)}, bf16[1024,1024]{1,0:T(8,128)(2,1)}, bf16[1024,1024]{1,0:T(8,128)(2,1)}) custom-call(s32[4]{0:T(128)} %iota_xor_fusion.order_ref, bf16[1024,256]{1,0:T(8,128)(2,1)} %get-tuple-element.166.refs_0_.refs_4_, bf16[1024,256]{1,0:T(8,128)(2,1)} %copy-done.17, bf16[1024,256]{1,0:T(8,128)(2,1)} %copy-done.18, ...), custom_call_target="tpu_custom_call" | custom-call | flops 322122560 | bytes 2516582 | tf_op jit(solution)/shard_map/mix/pallas_call | solution.py:491
  224.2 24.9 %gated.1 = (bf16[1024,2816]{1,0:T(8,128)(2,1)}, bf16[1024,2816]{1,0:T(8,128)(2,1)}, bf16[1024,2816]{1,0:T(8,128)(2,1)}) custom-call(bf16[1024,1024]{1,0:T(8,128)(2,1)} %get-tuple-element.173.n_ref, bf16[1024,1024]{1,0:T(8,128)(2,1)} %refs_9_.1, ...), custom_call_target="tpu_custom_call" | custom-call | flops 2657510912 | bytes 5190451 | tf_op jit(solution)/shard_map/gated/pallas_call | solution.py:527
  249.1 15.5 %products.3 = (bf16[1024,1408]{1,0:T(8,128)(2,1)}, bf16[1024,1408]{1,0:T(8,128)(2,1)}, bf16[1024,1408]{1,0:T(8,128)(2,1)}) custom-call(s32[1]{0:T(128)} %bitcast.16.select_ref, bf16[1024,1024]{1,0:T(8,128)(2,1)} %bitcast.132, bf16[1024,1024]{1,0:T(8,128)(2,1)} %get-tuple-element.172.refs_1_, bf16[1024,2816]{1,0:T(8,128)(2,1)} %get-tuple-element.277.refs_2_.refs_3_.h_ref, ...), custom_call_target="tpu_custom_call" | custom-call | flops 1328755456 | bytes 2595225 | tf_op jit(solution)/shard_map/products/pallas_call | solution.py:678
  265.2 27.3 %norm_back.1 = (f32[1024,1024]{1,0:T(8,128)}, bf16[1024,1024]{1,0:T(8,128)(2,1)}, bf16[1024,256]{1,0:T(8,128)(2,1)}, bf16[1024,256]{1,0:T(8,128)(2,1)}, bf16[102...) custom-call(s32[4]{0:T(128)} %iota_xor_fusion.order_ref, bf16[1024,2816]{1,0:T(8,128)(2,1)} %get-tuple-element.180.refs_3_.refs_0_.refs_4_, ...), custom_call_target="tpu_custom_call" | custom-call | flops 2093796608 | bytes 5976883 | tf_op jit(solution)/shard_map/norm_back/pallas_call | solution.py:597
  293.4 1.2 collective-permute-start.9
  295.3 24.1 %products.4 = (bf16[512,1408]{1,0:T(8,128)(2,1)}, bf16[512,1408]{1,0:T(8,128)(2,1)}, bf16[512,1408]{1,0:T(8,128)(2,1)}, bf16[512,1024]{1,0:T(8,128)(2,1)}, bf16[...) custom-call(s32[5]{0:T(128)} %stack.44.select_ref, ...), custom_call_target="tpu_custom_call" | custom-call | flops 1650878080 | bytes 3224371 | tf_op jit(solution)/shard_map/products/pallas_call | solution.py:678
  319.4 5.8 %collective-permute-start.16 = (bf16[512,1408]{1,0:T(8,128)(2,1)}, bf16[512,1408]{1,0:T(8,128)(2,1)}, u32[]{:S(2)}, u32[]{:S(2)}) collective-permute-start(bf16[512,1408]{1,0:T(8,128)(2,1)} %get-tuple-element.207), channel_id=1, source_target_pairs={{0,8},{4,12},{8,0},{12,4},{16,24},{20,28},{24,16},{28,20},{1,9},{5... | collective-permute-start | bytes 4325384 | tf_op jit(solution)/shard_map/ppermute | solution.py:809
  326.3 9.8 %collective-permute-start.15 = (bf16[512,1408]{1,0:T(8,128)(2,1)}, bf16[512,1408]{1,0:T(8,128)(2,1)}, u32[]{:S(2)}, u32[]{:S(2)}) collective-permute-start(bf16[512,1408]{1,0:T(8,128)(2,1)} %get-tuple-element.205), channel_id=1, source_target_pairs={{0,4},{4,0},{8,12},{12,8},{16,20},{20,16},{24,28},{28,24},{1,5},{5... | collective-permute-start | bytes 4325384 | tf_op jit(solution)/shard_map/ppermute | solution.py:809
  336.4 43.5 %attend_back.2 = (bf16[4096,256]{1,0:T(8,128)(2,1)}, bf16[4096,256]{1,0:T(8,128)(2,1)}, bf16[4096,256]{1,0:T(8,128)(2,1)}, f32[2,128,2560]{2,1,0:T(8,128)}, f32[8,8,512]{2,1,0:T(8,128)}) custom-call(s32[4]{0:T(128)} %iota_xor_fusion.order_ref, bf16[2,4096,128]{2,1,0:T(8,128)(2,1)} %get-tuple-element.159.q_ref, ...), custom_call_target="tpu_custom_call" | custom-call | flops 1879048192 | bytes 3774873 | tf_op jit(solution)/shard_map/attend_back/pallas_call | solution.py:445
  379.9 2.0 fusion.3
  382.0 1.8 fusion
  383.9 1.8 fusion.1
  386.1 6.8 %collective-permute-start.21 = (bf16[2,128,1024]{2,1,0:T(8,128)(2,1)S(1)}, bf16[2,128,1024]{2,1,0:T(8,128)(2,1)S(1)}, u32[]{:S(2)}, u32[]{:S(2)}) collective-permute-start(bf16[2,128,1024]{2,1,0:T(8,128)(2,1)S(1)} %get-tuple-element.309), channel_id=1, source_target_pairs={{0,4},{4,0},{8,12},{12,8},{16,20},{20,16},{24,28},{28,24},{1,5},{5... | collective-permute-start | bytes 1572872 | tf_op jit(solution)/shard_map/ppermute | solution.py:792
  396.6 1.5 collective-permute-start.19
  398.2 35.7 %attend_back.3 = (bf16[4096,256]{1,0:T(8,128)(2,1)}, bf16[4096,256]{1,0:T(8,128)(2,1)}, bf16[4096,256]{1,0:T(8,128)(2,1)}) custom-call(s32[4]{0:T(128)} %iota_xor_fusion.order_ref, bf16[2,4096,128]{2,1,0:T(8,128)(2,1)} %get-tuple-element.159.q_ref, ...), custom_call_target="tpu_custom_call", output_to_operand_aliasing={{0}: (12, {}), {1}: (13, {}), {2}: (14, {})} | custom-call | flops 1342177280 | bytes 3774873 | tf_op jit(solution)/shard_map/attend_back/pallas_call | solution.py:445
  435.0 1.3 add_convert_fusion.2
  436.3 2.1 add_convert_fusion.3
  438.4 5.5 project_back.6
  443.9 5.5 project_back.7
  449.9 4.6 project_back.8
  455.9 1.9 dynamic-slice_bitcast_fusion.17
  458.5 3.4 collective-permute-start.26
  462.7 1.5 collective-permute-start.27
  464.8 4.6 project_back.9
  469.4 11.6 %products.5 = bf16[1024,768]{1,0:T(8,128)(2,1)} custom-call(s32[1]{0:T(128)} %constant.242.clone.1.select_ref, bf16[1024,4096]{1,0:T(8,128)(2,1)} %get-tuple-element.171.refs_0_, bf16[4096,256]{1,0:T(8,128)(2,1)} %get-tuple-element.270.a_ref.refs_1_, bf16[4096,256]{1,0:T(8,128)(2,1)} %get-tuple-element.271.b_ref.refs_2_, ...), custom_call_target="tpu_custom_call" | custom-call | flops 966367616 | bytes 1179648 | tf_op jit(solution)/shard_map/products/pallas_call | solution.py:678
  481.0 1.6 dynamic-slice_bitcast_fusion.1
  482.6 2.1 collective-permute-start.24
  485.3 2.1 collective-permute-start.29
  488.5 3.7 collective-permute-done.24
  492.3 1.2 collective-permute-start.33
  493.7 2.1 collective-permute-start.32
  495.8 1.8 collective-permute-start.31
  497.5 7.2 %collective-permute-done.29 = bf16[2,2,128,768]{3,2,1,0:T(8,128)(2,1)S(1)} collective-permute-done((bf16[2,2,128,768]{3,2,1,0:T(8,128)(2,1)S(1)}, bf16[2,2,128,768]{3,2,1,0:T(8,128)(2,1)S(1)}, u32[]{:S(2)}, u32[]{:S(2)}) %collective-permute-start.29) | collective-permute-done | bytes 786464 | tf_op jit(solution)/shard_map/ppermute | solution.py:792
  504.8 1.8 collective-permute-start.30
  507.0 6.2 %collective-permute-done.30 = bf16[64,1408]{1,0:T(8,128)(2,1)S(1)} collective-permute-done((bf16[64,1408]{1,0:T(8,128)(2,1)S(1)}, bf16[64,1408]{1,0:T(8,128)(2,1)S(1)}, u32[]{:S(2)}, u32[]{:S(2)}) %collective-permute-start.30) | collective-permute-done | bytes 180256 | tf_op jit(solution)/shard_map/ppermute | solution.py:792
  513.3 1.6 collective-permute-start.37
  515.1 6.1 %project_back.10.refs_5_ = bf16[1024,1024]{1,0:T(8,128)(2,1)} custom-call(s32[4]{0:T(128)} %iota_xor_fusion.order_ref, bf16[4096,256]{1,0:T(8,128)(2,1)} %get-tuple-element.270.a_ref.refs_1_, bf16[4096,256]{1,0:T(8,128)(2,1)} %get-tuple-element.271.b_ref.refs_2_, bf16[4096,256]{1,0:T(8,128)(2,1)} %get-tuple-element.272.c_ref.refs_3_, ...), custom_call_target="tpu_custom_call" | custom-call | flops 120795952 | bytes 432537 | tf_op jit(solution)/shard_map/project_back/pallas_call | solution.py:762
  521.2 1.7 collective-permute-done.34
  523.0 6.1 %project_back.11 = bf16[1024,1024]{1,0:T(8,128)(2,1)} custom-call(s32[4]{0:T(128)} %iota_xor_fusion.order_ref, bf16[4096,256]{1,0:T(8,128)(2,1)} %get-tuple-element.270.a_ref.refs_1_, bf16[4096,256]{1,0:T(8,128)(2,1)} %get-tuple-element.271.b_ref.refs_2_, bf16[4096,256]{1,0:T(8,128)(2,1)} %get-tuple-element.272.c_ref.refs_3_, ...), custom_call_target="tpu_custom_call", output_to_operand_aliasing={{}: (10, {})} | custom-call | flops 120795952 | bytes 432537 | tf_op jit(solution)/shard_map/project_back/pallas_call | solution.py:762
  529.5 1.7 collective-permute-start.36
  532.0 11.2 %finish.1 = bf16[1024,1024]{1,0:T(8,128)(2,1)} custom-call(f32[1024,1024]{1,0:T(8,128)} %get-tuple-element.170.refs_8_.r_ref, bf16[1024,2816]{1,0:T(8,128)(2,1)} %get-tuple-element.277.refs_2_.refs_3_.h_ref, bf16[1024,9472]{1,0:T(8,128)(2,1)} %all-gather.2.cloned.1.call-done.refs_4_.refs_5_.refs_6_.refs_7_.wg_ref.wu_ref.wd_ref.refs_2_.refs_3_.w_ref), custom_call_target="tpu_custom_call" | custom-call | flops 885836992 | bytes 2673868 | tf_op jit(solution)/shard_map/finish/pallas_call | solution.py:701
  547.6 5.0 feedforward_ends.1
  552.6 2.5 collective-permute-done.41.refs_3_
  555.2 3.3 projection_ends.1
  (169 shorter events, 32.3 us)
Async XLA Ops:
  7.2 207.4 %all-gather.2.cloned.1.call-start = ((), (), s32[]{:S(2)}) async-start(), calls=%async_computation.2 | async-start | bytes 20004864 | tf_op jit(solution)/shard_map/all_gather | solution.py:967
  8.6 6.1 %copy-start.22 = (bf16[128]{0:T(256)(128)(2,1)S(1)}, bf16[128]{0:T(256)(128)(2,1)}, u32[]{:S(2)}) copy-start(bf16[128]{0:T(256)(128)(2,1)} %param.25) | copy-start | bytes 772
  8.6 6.1 %copy-start.24 = (bf16[128]{0:T(256)(128)(2,1)S(1)}, bf16[128]{0:T(256)(128)(2,1)}, u32[]{:S(2)}) copy-start(bf16[128]{0:T(256)(128)(2,1)} %param.24) | copy-start | bytes 772
  8.6 17.9 %copy-start.20 = (s32[1,2,32,128]{3,2,1,0:T(8,128)S(1)}, s32[1,2,32,128]{3,2,1,0:T(8,128)}, u32[]{:S(2)}) copy-start(s32[1,2,32,128]{3,2,1,0:T(8,128)} %param.28) | copy-start | bytes 98308
  8.6 17.9 %copy-start.21 = (s32[1,2,32,128]{3,2,1,0:T(8,128)S(1)}, s32[1,2,32,128]{3,2,1,0:T(8,128)}, u32[]{:S(2)}) copy-start(s32[1,2,32,128]{3,2,1,0:T(8,128)} %param.29) | copy-start | bytes 98308
  11.6 53.3 %collective-permute-start.1 = (bf16[1024,1024]{1,0:T(8,128)(2,1)}, bf16[1024,1024]{1,0:T(8,128)(2,1)}, u32[]{:S(2)}, u32[]{:S(2)}) collective-permute-start(bf16[1024,1024]{1,0:T(8,128)(2,1)} %refs_2_.3), channel_id=1, source_target_pairs={{0,2},{1,3},{2,0},{3,1},{4,6},{5,7},{6,4},{7,5},{8,10},{9,11},{10,... | collective-permute-start | bytes 6291464 | tf_op jit(solution)/shard_map/ppermute | solution.py:68
  14.7 89.5 %collective-permute-start = (bf16[1024,1024]{1,0:T(8,128)(2,1)}, bf16[1024,1024]{1,0:T(8,128)(2,1)}, u32[]{:S(2)}, u32[]{:S(2)}) collective-permute-start(bf16[1024,1024]{1,0:T(8,128)(2,1)} %refs_2_.3), channel_id=1, source_target_pairs={{0,1},{1,0},{2,3},{3,2},{4,5},{5,4},{6,7},{7,6},{8,9},{9,8},{10,11... | collective-permute-start | bytes 6291464 | tf_op jit(solution)/shard_map/ppermute | solution.py:68
  15.3 12.3 %all-to-all-start.1 = ((bf16[8,2,128]{2,1,0:T(2,128)(2,1)}), bf16[8,2,128]{2,1,0:T(2,128)(2,1)S(1)}, u32[]{:S(2)}, u32[]{:S(2)}) async-start(bf16[8,2,128]{2,1,0:T(2,128)(2,1)} %broadcast_in_dim.15), calls=%async_computation.1 | async-start | bytes 8192 | tf_op jit(solution)/shard_map/all_to_all | solution.py:74
  21.1 48.3 %collective-permute-start.3 = (bf16[2,2048,128]{2,1,0:T(8,128)(2,1)}, bf16[2,2048,128]{2,1,0:T(8,128)(2,1)S(1)}, u32[]{:S(2)}, u32[]{:S(2)}) collective-permute-start(bf16[2,2048,128]{2,1,0:T(8,128)(2,1)} %bitcast.12.k_ref), channel_id=1, source_target_pairs={{0,4},{4,8},{8,12},{12,16},{16,20},{20,24},{24,28},{28,0},{1,5},{5... | collective-permute-start | bytes 3145736 | tf_op jit(solution)/shard_map/ppermute | solution.py:955
  23.1 62.7 %collective-permute-start.4 = (bf16[2,2048,128]{2,1,0:T(8,128)(2,1)}, bf16[2,2048,128]{2,1,0:T(8,128)(2,1)}, u32[]{:S(2)}, u32[]{:S(2)}) collective-permute-start(bf16[2,2048,128]{2,1,0:T(8,128)(2,1)} %bitcast.13.v_ref), channel_id=1, source_target_pairs={{0,4},{4,8},{8,12},{12,16},{16,20},{20,24},{24,28},{28,0},{1,5},{5... | collective-permute-start | bytes 3145736 | tf_op jit(solution)/shard_map/ppermute | solution.py:956
  28.9 79.6 %all-to-all-start = ((bf16[8,128,768]{2,1,0:T(8,128)(2,1)}), bf16[8,128,768]{2,1,0:T(8,128)(2,1)S(1)}, u32[]{:S(2)}, u32[]{:S(2)}) async-start(bf16[8,128,768]{2,1,0:T(8,128)(2,1)} %broadcast_in_dim.14), calls=%async_computation | async-start | bytes 3145728 | tf_op jit(solution)/shard_map/all_to_all | solution.py:74
  64.9 43.6 %collective-permute-start.2 = (bf16[1024,1024]{1,0:T(8,128)(2,1)}, bf16[1024,1024]{1,0:T(8,128)(2,1)}, u32[]{:S(2)}, u32[]{:S(2)}) collective-permute-start(bf16[1024,1024]{1,0:T(8,128)(2,1)} %collective-permute-done.1.refs_2_), channel_id=1, source_target_pairs={{0,1},{1,0},{2,3},{3,2},{4,5},{5,4},{6,7},{7,6},{8,9},{9,8},{10,11... | collective-permute-start | bytes 6291464 | tf_op jit(solution)/shard_map/ppermute | solution.py:68
  69.4 16.3 %copy-start.16 = (bf16[2,2048,128]{2,1,0:T(8,128)(2,1)}, bf16[2,2048,128]{2,1,0:T(8,128)(2,1)S(1)}, u32[]{:S(2)}) copy-start(bf16[2,2048,128]{2,1,0:T(8,128)(2,1)S(1)} %collective-permute-done.3.k_ref) | copy-start | bytes 3145732
  128.6 42.2 %copy-start.3 = (bf16[1024,1024]{1,0:T(8,128)(2,1)S(1)}, bf16[1024,1024]{1,0:T(8,128)(2,1)}, u32[]{:S(2)}) copy-start(bf16[1024,1024]{1,0:T(8,128)(2,1)} %refs_9_.1) | copy-start | bytes 6291460
  168.9 7.7 %collective-permute-start.5 = (bf16[1024,256]{1,0:T(8,128)(2,1)}, bf16[1024,256]{1,0:T(8,128)(2,1)S(1)}, u32[]{:S(2)}, u32[]{:S(2)}) collective-permute-start(bf16[1024,256]{1,0:T(8,128)(2,1)} %get-tuple-element.167.refs_5_), channel_id=1, source_target_pairs={{0,1},{1,0},{2,3},{3,2},{4,5},{5,4},{6,7},{7,6},{8,9},{9,8},{10,11... | collective-permute-start | bytes 1572872 | tf_op jit(solution)/shard_map/ppermute | solution.py:68
  168.9 26.3 %collective-permute-start.6 = (bf16[1024,256]{1,0:T(8,128)(2,1)}, bf16[1024,256]{1,0:T(8,128)(2,1)S(1)}, u32[]{:S(2)}, u32[]{:S(2)}) collective-permute-start(bf16[1024,256]{1,0:T(8,128)(2,1)} %get-tuple-element.168.refs_6_), channel_id=1, source_target_pairs={{0,2},{1,3},{2,0},{3,1},{4,6},{5,7},{6,4},{7,5},{8,10},{9,11},{10,... | collective-permute-start | bytes 1572872 | tf_op jit(solution)/shard_map/ppermute | solution.py:68
  169.0 37.9 %collective-permute-start.7 = (bf16[1024,256]{1,0:T(8,128)(2,1)}, bf16[1024,256]{1,0:T(8,128)(2,1)}, u32[]{:S(2)}, u32[]{:S(2)}) collective-permute-start(bf16[1024,256]{1,0:T(8,128)(2,1)} %get-tuple-element.169.refs_7_), channel_id=1, source_target_pairs={{0,3},{1,2},{2,1},{3,0},{4,7},{5,6},{6,5},{7,4},{8,11},{9,10},{10,... | collective-permute-start | bytes 1572872 | tf_op jit(solution)/shard_map/ppermute | solution.py:68
  176.5 38.0 %copy-start.17 = (bf16[1024,256]{1,0:T(8,128)(2,1)}, bf16[1024,256]{1,0:T(8,128)(2,1)S(1)}, u32[]{:S(2)}) copy-start(bf16[1024,256]{1,0:T(8,128)(2,1)S(1)} %collective-permute-done.5.refs_1_) | copy-start | bytes 1572868
  195.2 19.4 %copy-start.18 = (bf16[1024,256]{1,0:T(8,128)(2,1)}, bf16[1024,256]{1,0:T(8,128)(2,1)S(1)}, u32[]{:S(2)}) copy-start(bf16[1024,256]{1,0:T(8,128)(2,1)S(1)} %collective-permute-done.6.refs_2_) | copy-start | bytes 1572868
  264.6 28.9 %collective-permute-start.11 = (bf16[1024,1408]{1,0:T(8,128)(2,1)}, bf16[1024,1408]{1,0:T(8,128)(2,1)}, u32[]{:S(2)}, u32[]{:S(2)}) collective-permute-start(bf16[1024,1408]{1,0:T(8,128)(2,1)} %get-tuple-element.187), channel_id=1, source_target_pairs={{0,1},{1,0},{2,3},{3,2},{4,5},{5,4},{6,7},{7,6},{8,9},{9,8},{10,11... | collective-permute-start | bytes 8650760 | tf_op jit(solution)/shard_map/ppermute | solution.py:68
  264.6 30.7 %collective-permute-start.12 = (bf16[1024,1408]{1,0:T(8,128)(2,1)}, bf16[1024,1408]{1,0:T(8,128)(2,1)}, u32[]{:S(2)}, u32[]{:S(2)}) collective-permute-start(bf16[1024,1408]{1,0:T(8,128)(2,1)} %get-tuple-element.188), channel_id=1, source_target_pairs={{0,1},{1,0},{2,3},{3,2},{4,5},{5,4},{6,7},{7,6},{8,9},{9,8},{10,11... | collective-permute-start | bytes 8650760 | tf_op jit(solution)/shard_map/ppermute | solution.py:68
  265.1 30.2 %collective-permute-start.13 = (bf16[1024,1408]{1,0:T(8,128)(2,1)}, bf16[1024,1408]{1,0:T(8,128)(2,1)}, u32[]{:S(2)}, u32[]{:S(2)}) collective-permute-start(bf16[1024,1408]{1,0:T(8,128)(2,1)} %get-tuple-element.189), channel_id=1, source_target_pairs={{0,1},{1,0},{2,3},{3,2},{4,5},{5,4},{6,7},{7,6},{8,9},{9,8},{10,11... | collective-permute-start | bytes 8650760 | tf_op jit(solution)/shard_map/ppermute | solution.py:68
  292.5 26.9 %collective-permute-start.10 = (bf16[1024,256]{1,0:T(8,128)(2,1)}, bf16[1024,256]{1,0:T(8,128)(2,1)S(1)}, u32[]{:S(2)}, u32[]{:S(2)}) collective-permute-start(bf16[1024,256]{1,0:T(8,128)(2,1)} %get-tuple-element.184), channel_id=1, source_target_pairs={{0,3},{1,2},{2,1},{3,0},{4,7},{5,6},{6,5},{7,4},{8,11},{9,10},{10,... | collective-permute-start | bytes 1572872 | tf_op jit(solution)/shard_map/ppermute | solution.py:68
  293.4 26.0 %collective-permute-start.8 = (bf16[1024,256]{1,0:T(8,128)(2,1)}, bf16[1024,256]{1,0:T(8,128)(2,1)S(1)}, u32[]{:S(2)}, u32[]{:S(2)}) collective-permute-start(bf16[1024,256]{1,0:T(8,128)(2,1)} %get-tuple-element.182), channel_id=1, source_target_pairs={{0,1},{1,0},{2,3},{3,2},{4,5},{5,4},{6,7},{7,6},{8,9},{9,8},{10,11... | collective-permute-start | bytes 1572872 | tf_op jit(solution)/shard_map/ppermute | solution.py:68
  293.4 26.0 %collective-permute-start.9 = (bf16[1024,256]{1,0:T(8,128)(2,1)}, bf16[1024,256]{1,0:T(8,128)(2,1)S(1)}, u32[]{:S(2)}, u32[]{:S(2)}) collective-permute-start(bf16[1024,256]{1,0:T(8,128)(2,1)} %get-tuple-element.183), channel_id=1, source_target_pairs={{0,2},{1,3},{2,0},{3,1},{4,6},{5,7},{6,4},{7,5},{8,10},{9,11},{10,... | collective-permute-start | bytes 1572872 | tf_op jit(solution)/shard_map/ppermute | solution.py:68
  319.4 17.0 %copy-start.7 = (bf16[1024,256]{1,0:T(8,128)(2,1)}, bf16[1024,256]{1,0:T(8,128)(2,1)S(1)}, u32[]{:S(2)}) copy-start(bf16[1024,256]{1,0:T(8,128)(2,1)S(1)} %collective-permute-done.10.refs_3_) | copy-start | bytes 1572868
  319.4 17.0 %copy-start.8 = (bf16[1024,256]{1,0:T(8,128)(2,1)}, bf16[1024,256]{1,0:T(8,128)(2,1)S(1)}, u32[]{:S(2)}) copy-start(bf16[1024,256]{1,0:T(8,128)(2,1)S(1)} %collective-permute-done.8.refs_1_) | copy-start | bytes 1572868
  319.4 17.0 %copy-start.9 = (bf16[1024,256]{1,0:T(8,128)(2,1)}, bf16[1024,256]{1,0:T(8,128)(2,1)S(1)}, u32[]{:S(2)}) copy-start(bf16[1024,256]{1,0:T(8,128)(2,1)S(1)} %collective-permute-done.9.refs_2_) | copy-start | bytes 1572868
  319.4 62.5 %collective-permute-start.16 = (bf16[512,1408]{1,0:T(8,128)(2,1)}, bf16[512,1408]{1,0:T(8,128)(2,1)}, u32[]{:S(2)}, u32[]{:S(2)}) collective-permute-start(bf16[512,1408]{1,0:T(8,128)(2,1)} %get-tuple-element.207), channel_id=1, source_target_pairs={{0,8},{4,12},{8,0},{12,4},{16,24},{20,28},{24,16},{28,20},{1,9},{5... | collective-permute-start | bytes 4325384 | tf_op jit(solution)/shard_map/ppermute | solution.py:809
  325.3 54.7 %collective-permute-start.17 = (bf16[512,1024]{1,0:T(8,128)(2,1)}, bf16[512,1024]{1,0:T(8,128)(2,1)}, u32[]{:S(2)}, u32[]{:S(2)}) collective-permute-start(bf16[512,1024]{1,0:T(8,128)(2,1)} %get-tuple-element.209), channel_id=1, source_target_pairs={{0,16},{4,20},{8,24},{12,28},{16,0},{20,4},{24,8},{28,12},{1,17},{... | collective-permute-start | bytes 3145736 | tf_op jit(solution)/shard_map/ppermute | solution.py:809
  326.3 57.6 %collective-permute-start.15 = (bf16[512,1408]{1,0:T(8,128)(2,1)}, bf16[512,1408]{1,0:T(8,128)(2,1)}, u32[]{:S(2)}, u32[]{:S(2)}) collective-permute-start(bf16[512,1408]{1,0:T(8,128)(2,1)} %get-tuple-element.205), channel_id=1, source_target_pairs={{0,4},{4,0},{8,12},{12,8},{16,20},{20,16},{24,28},{28,24},{1,5},{5... | collective-permute-start | bytes 4325384 | tf_op jit(solution)/shard_map/ppermute | solution.py:809
  336.1 49.6 %collective-permute-start.14 = (bf16[512,1408]{1,0:T(8,128)(2,1)}, bf16[512,1408]{1,0:T(8,128)(2,1)S(1)}, u32[]{:S(2)}, u32[]{:S(2)}) collective-permute-start(bf16[512,1408]{1,0:T(8,128)(2,1)} %get-tuple-element.203), channel_id=1, source_target_pairs={{0,2},{1,3},{2,0},{3,1},{4,6},{5,7},{6,4},{7,5},{8,10},{9,11},{10,... | collective-permute-start | bytes 4325384 | tf_op jit(solution)/shard_map/ppermute | solution.py:809
  379.9 2.1 copy-start.12
  386.1 47.8 %collective-permute-start.21 = (bf16[2,128,1024]{2,1,0:T(8,128)(2,1)S(1)}, bf16[2,128,1024]{2,1,0:T(8,128)(2,1)S(1)}, u32[]{:S(2)}, u32[]{:S(2)}) collective-permute-start(bf16[2,128,1024]{2,1,0:T(8,128)(2,1)S(1)} %get-tuple-element.309), channel_id=1, source_target_pairs={{0,4},{4,0},{8,12},{12,8},{16,20},{20,16},{24,28},{28,24},{1,5},{5... | collective-permute-start | bytes 1572872 | tf_op jit(solution)/shard_map/ppermute | solution.py:792
  394.0 40.2 %collective-permute-start.20 = (bf16[2,2,64,1408]{3,2,1,0:T(8,128)(2,1)}, bf16[2,2,64,1408]{3,2,1,0:T(8,128)(2,1)S(1)}, u32[]{:S(2)}, u32[]{:S(2)}) collective-permute-start(bf16[2,2,64,1408]{3,2,1,0:T(8,128)(2,1)} %get-tuple-element.301), channel_id=1, source_target_pairs={{0,2},{1,3},{2,0},{3,1},{4,6},{5,7},{6,4},{7,5},{8,10},{9,11},{10,... | collective-permute-start | bytes 2162696 | tf_op jit(solution)/shard_map/ppermute | solution.py:792
  396.6 37.7 %collective-permute-start.19 = (bf16[2,2,64,1408]{3,2,1,0:T(8,128)(2,1)}, bf16[2,2,64,1408]{3,2,1,0:T(8,128)(2,1)}, u32[]{:S(2)}, u32[]{:S(2)}) collective-permute-start(bf16[2,2,64,1408]{3,2,1,0:T(8,128)(2,1)} %get-tuple-element.303), channel_id=1, source_target_pairs={{0,2},{1,3},{2,0},{3,1},{4,6},{5,7},{6,4},{7,5},{8,10},{9,11},{10,... | collective-permute-start | bytes 2162696 | tf_op jit(solution)/shard_map/ppermute | solution.py:792
  398.2 38.1 %collective-permute-start.18 = (bf16[2,2,64,1408]{3,2,1,0:T(8,128)(2,1)}, bf16[2,2,64,1408]{3,2,1,0:T(8,128)(2,1)}, u32[]{:S(2)}, u32[]{:S(2)}) collective-permute-start(bf16[2,2,64,1408]{3,2,1,0:T(8,128)(2,1)} %get-tuple-element.306), channel_id=1, source_target_pairs={{0,4},{4,0},{8,12},{12,8},{16,20},{20,16},{24,28},{28,24},{1,5},{5... | collective-permute-start | bytes 2162696 | tf_op jit(solution)/shard_map/ppermute | solution.py:792
  443.9 6.0 %collective-permute-start.22 = (bf16[1024,1024]{1,0:T(8,128)(2,1)}, bf16[1024,1024]{1,0:T(8,128)(2,1)}, u32[]{:S(2)}, u32[]{:S(2)}) collective-permute-start(bf16[1024,1024]{1,0:T(8,128)(2,1)} %project_back.6), channel_id=1, source_target_pairs={{0,1},{1,0},{2,3},{3,2},{4,5},{5,4},{6,7},{7,6},{8,9},{9,8},{10,11... | collective-permute-start | bytes 6291464 | tf_op jit(solution)/shard_map/ppermute | solution.py:68
  449.4 42.9 %collective-permute-start.28 = (bf16[1024,1024]{1,0:T(8,128)(2,1)}, bf16[1024,1024]{1,0:T(8,128)(2,1)S(1)}, u32[]{:S(2)}, u32[]{:S(2)}) collective-permute-start(bf16[1024,1024]{1,0:T(8,128)(2,1)} %project_back.7), channel_id=1, source_target_pairs={{0,1},{1,0},{2,3},{3,2},{4,5},{5,4},{6,7},{7,6},{8,9},{9,8},{10,11... | collective-permute-start | bytes 6291464 | tf_op jit(solution)/shard_map/ppermute | solution.py:68
  454.4 28.2 %collective-permute-start.23 = (bf16[512,1024]{1,0:T(8,128)(2,1)}, bf16[512,1024]{1,0:T(8,128)(2,1)}, u32[]{:S(2)}, u32[]{:S(2)}) collective-permute-start(bf16[512,1024]{1,0:T(8,128)(2,1)} %project_back.8), channel_id=1, source_target_pairs={{0,2},{1,3},{2,0},{3,1},{4,6},{5,7},{6,4},{7,5},{8,10},{9,11},{10,... | collective-permute-start | bytes 3145736 | tf_op jit(solution)/shard_map/ppermute | solution.py:68
  458.5 26.2 %collective-permute-start.26 = (bf16[2,64,1408]{2,1,0:T(8,128)(2,1)}, bf16[2,64,1408]{2,1,0:T(8,128)(2,1)S(1)}, u32[]{:S(2)}, u32[]{:S(2)}) collective-permute-start(bf16[2,64,1408]{2,1,0:T(8,128)(2,1)} %get-tuple-element.313), channel_id=1, source_target_pairs={{0,16},{4,20},{8,24},{12,28},{16,0},{20,4},{24,8},{28,12},{1,17},{... | collective-permute-start | bytes 1081352 | tf_op jit(solution)/shard_map/ppermute | solution.py:792
  462.7 24.8 %collective-permute-start.27 = (bf16[2,64,1024]{2,1,0:T(8,128)(2,1)}, bf16[2,64,1024]{2,1,0:T(8,128)(2,1)}, u32[]{:S(2)}, u32[]{:S(2)}) collective-permute-start(bf16[2,64,1024]{2,1,0:T(8,128)(2,1)} %get-tuple-element.319), channel_id=1, source_target_pairs={{0,2},{1,3},{2,0},{3,1},{4,6},{5,7},{6,4},{7,5},{8,10},{9,11},{10,... | collective-permute-start | bytes 786440 | tf_op jit(solution)/shard_map/ppermute | solution.py:792
  464.3 21.1 %collective-permute-start.25 = (bf16[2,64,1408]{2,1,0:T(8,128)(2,1)}, bf16[2,64,1408]{2,1,0:T(8,128)(2,1)S(1)}, u32[]{:S(2)}, u32[]{:S(2)}) collective-permute-start(bf16[2,64,1408]{2,1,0:T(8,128)(2,1)} %get-tuple-element.315), channel_id=1, source_target_pairs={{0,8},{4,12},{8,0},{12,4},{16,24},{20,28},{24,16},{28,20},{1,9},{5... | collective-permute-start | bytes 1081352 | tf_op jit(solution)/shard_map/ppermute | solution.py:792
  481.0 6.4 %copy-start.13 = (bf16[2,64,1408]{2,1,0:T(8,128)(2,1)S(1)}, bf16[2,64,1408]{2,1,0:T(8,128)(2,1)}, u32[]{:S(2)}) copy-start(bf16[2,64,1408]{2,1,0:T(8,128)(2,1)} %get-tuple-element.256) | copy-start | bytes 1081348
  481.0 6.5 %copy-start.15 = (bf16[2,64,1024]{2,1,0:T(8,128)(2,1)S(1)}, bf16[2,64,1024]{2,1,0:T(8,128)(2,1)}, u32[]{:S(2)}) copy-start(bf16[2,64,1024]{2,1,0:T(8,128)(2,1)} %get-tuple-element.258) | copy-start | bytes 786436
  482.6 9.6 %collective-permute-start.24 = (bf16[2,64,1408]{2,1,0:T(8,128)(2,1)S(1)}, bf16[2,64,1408]{2,1,0:T(8,128)(2,1)S(1)}, u32[]{:S(2)}, u32[]{:S(2)}) collective-permute-start(bf16[2,64,1408]{2,1,0:T(8,128)(2,1)S(1)} %copy-done.19), channel_id=1, source_target_pairs={{0,8},{4,12},{8,0},{12,4},{16,24},{20,28},{24,16},{28,20},{1,9},{5... | collective-permute-start | bytes 1081352 | tf_op jit(solution)/shard_map/ppermute | solution.py:792
  484.7 38.2 %collective-permute-start.35 = (bf16[512,1024]{1,0:T(8,128)(2,1)}, bf16[512,1024]{1,0:T(8,128)(2,1)}, u32[]{:S(2)}, u32[]{:S(2)}) collective-permute-start(bf16[512,1024]{1,0:T(8,128)(2,1)} %project_back.9), channel_id=1, source_target_pairs={{0,2},{1,3},{2,0},{3,1},{4,6},{5,7},{6,4},{7,5},{8,10},{9,11},{10,... | collective-permute-start | bytes 3145736 | tf_op jit(solution)/shard_map/ppermute | solution.py:68
  485.3 19.4 %collective-permute-start.29 = (bf16[2,2,128,768]{3,2,1,0:T(8,128)(2,1)S(1)}, bf16[2,2,128,768]{3,2,1,0:T(8,128)(2,1)S(1)}, u32[]{:S(2)}, u32[]{:S(2)}) collective-permute-start(bf16[2,2,128,768]{3,2,1,0:T(8,128)(2,1)S(1)} %get-tuple-element.300), channel_id=1, source_target_pairs={{0,4},{4,0},{8,12},{12,8},{16,20},{20,16},{24,28},{28,24},{1,5},{5... | collective-permute-start | bytes 2359304 | tf_op jit(solution)/shard_map/ppermute | solution.py:792
  492.3 14.5 %copy-start.4 = (bf16[1024,1024]{1,0:T(8,128)(2,1)}, bf16[1024,1024]{1,0:T(8,128)(2,1)S(1)}, u32[]{:S(2)}) copy-start(bf16[1024,1024]{1,0:T(8,128)(2,1)S(1)} %collective-permute-done.28.refs_0_) | copy-start | bytes 6291460
  492.3 14.5 %collective-permute-start.33 = (bf16[64,1024]{1,0:T(8,128)(2,1)S(1)}, bf16[64,1024]{1,0:T(8,128)(2,1)S(1)}, u32[]{:S(2)}, u32[]{:S(2)}) collective-permute-start(bf16[64,1024]{1,0:T(8,128)(2,1)S(1)} %get-tuple-element.329), channel_id=1, source_target_pairs={{0,8},{4,12},{8,0},{12,4},{16,24},{20,28},{24,16},{28,20},{1,9},{5... | collective-permute-start | bytes 393224 | tf_op jit(solution)/shard_map/ppermute | solution.py:792
  493.7 13.2 %collective-permute-start.32 = (bf16[64,1408]{1,0:T(8,128)(2,1)S(1)}, bf16[64,1408]{1,0:T(8,128)(2,1)S(1)}, u32[]{:S(2)}, u32[]{:S(2)}) collective-permute-start(bf16[64,1408]{1,0:T(8,128)(2,1)S(1)} %get-tuple-element.323), channel_id=1, source_target_pairs={{0,4},{4,0},{8,12},{12,8},{16,20},{20,16},{24,28},{28,24},{1,5},{5... | collective-permute-start | bytes 540680 | tf_op jit(solution)/shard_map/ppermute | solution.py:792
  495.8 11.2 %collective-permute-start.31 = (bf16[64,1408]{1,0:T(8,128)(2,1)S(1)}, bf16[64,1408]{1,0:T(8,128)(2,1)S(1)}, u32[]{:S(2)}, u32[]{:S(2)}) collective-permute-start(bf16[64,1408]{1,0:T(8,128)(2,1)S(1)} %get-tuple-element.325), channel_id=1, source_target_pairs={{0,16},{4,20},{8,24},{12,28},{16,0},{20,4},{24,8},{28,12},{1,17},{... | collective-permute-start | bytes 540680 | tf_op jit(solution)/shard_map/ppermute | solution.py:792
  504.8 8.4 %collective-permute-start.30 = (bf16[64,1408]{1,0:T(8,128)(2,1)S(1)}, bf16[64,1408]{1,0:T(8,128)(2,1)S(1)}, u32[]{:S(2)}, u32[]{:S(2)}) collective-permute-start(bf16[64,1408]{1,0:T(8,128)(2,1)S(1)} %get-tuple-element.327), channel_id=1, source_target_pairs={{0,16},{4,20},{8,24},{12,28},{16,0},{20,4},{24,8},{28,12},{1,17},{... | collective-permute-start | bytes 540680 | tf_op jit(solution)/shard_map/ppermute | solution.py:792
  513.3 15.7 %collective-permute-start.37 = (bf16[64,5248]{1,0:T(8,128)(2,1)S(1)}, bf16[64,5248]{1,0:T(8,128)(2,1)S(1)}, u32[]{:S(2)}, u32[]{:S(2)}) collective-permute-start(bf16[64,5248]{1,0:T(8,128)(2,1)S(1)} %constant_dynamic-update-slice_fusion), channel_id=1, source_target_pairs={{0,2},{1,3},{2,0},{3,1},{4,6},{5,7},{6,4},{7,5},{8,10},{9,11},{10,... | collective-permute-start | bytes 2015240 | tf_op jit(solution)/shard_map/ppermute | solution.py:68
  515.0 7.8 %collective-permute-start.34 = (bf16[2,128,768]{2,1,0:T(8,128)(2,1)S(1)}, bf16[2,128,768]{2,1,0:T(8,128)(2,1)S(1)}, u32[]{:S(2)}, u32[]{:S(2)}) collective-permute-start(bf16[2,128,768]{2,1,0:T(8,128)(2,1)S(1)} %get-tuple-element.312), channel_id=1, source_target_pairs={{0,8},{4,12},{8,0},{12,4},{16,24},{20,28},{24,16},{28,20},{1,9},{5... | collective-permute-start | bytes 1179656 | tf_op jit(solution)/shard_map/ppermute | solution.py:792
  529.2 2.0 copy-start.23
  529.4 13.8 %copy-start.5 = (bf16[2,64,5248]{2,1,0:T(8,128)(2,1)}, bf16[2,64,5248]{2,1,0:T(8,128)(2,1)S(1)}, u32[]{:S(2)}) copy-start(bf16[2,64,5248]{2,1,0:T(8,128)(2,1)S(1)} %pad_maximum_fusion.2) | copy-start | bytes 4030468
  529.4 17.1 %collective-permute-start.38 = (bf16[128,5248]{1,0:T(8,128)(2,1)S(1)}, bf16[128,5248]{1,0:T(8,128)(2,1)S(1)}, u32[]{:S(2)}, u32[]{:S(2)}) collective-permute-start(bf16[128,5248]{1,0:T(8,128)(2,1)S(1)} %bitcast.140), channel_id=1, source_target_pairs={{0,1},{1,0},{2,3},{3,2},{4,5},{5,4},{6,7},{7,6},{8,9},{9,8},{10,11... | collective-permute-start | bytes 4030472 | tf_op jit(solution)/shard_map/ppermute | solution.py:68
  529.5 13.7 %collective-permute-start.36 = (bf16[128,768]{1,0:T(8,128)(2,1)S(1)}, bf16[128,768]{1,0:T(8,128)(2,1)S(1)}, u32[]{:S(2)}, u32[]{:S(2)}) collective-permute-start(bf16[128,768]{1,0:T(8,128)(2,1)S(1)} %get-tuple-element.322), channel_id=1, source_target_pairs={{0,16},{4,20},{8,24},{12,28},{16,0},{20,4},{24,8},{28,12},{1,17},{... | collective-permute-start | bytes 589832 | tf_op jit(solution)/shard_map/ppermute | solution.py:792
  532.0 13.8 %copy-start.25 = (bf16[128]{0:T(256)(128)(2,1)S(1)}, bf16[128]{0:T(256)(128)(2,1)}, u32[]{:S(2)}) copy-start(bf16[128]{0:T(256)(128)(2,1)} %param.24) | copy-start | bytes 772
  543.9 8.7 %collective-permute-start.39 = (bf16[128,768]{1,0:T(8,128)(2,1)}, bf16[128,768]{1,0:T(8,128)(2,1)}, u32[]{:S(2)}, u32[]{:S(2)}) collective-permute-start(bf16[128,768]{1,0:T(8,128)(2,1)} %add_convert_fusion.10.refs_0_), channel_id=1, source_target_pairs={{0,1},{1,0},{2,3},{3,2},{4,5},{5,4},{6,7},{7,6},{8,9},{9,8},{10,11... | collective-permute-start | bytes 589832 | tf_op jit(solution)/shard_map/ppermute | solution.py:68
  544.1 8.5 %collective-permute-start.40 = (bf16[128,768]{1,0:T(8,128)(2,1)}, bf16[128,768]{1,0:T(8,128)(2,1)}, u32[]{:S(2)}, u32[]{:S(2)}) collective-permute-start(bf16[128,768]{1,0:T(8,128)(2,1)} %add_convert_fusion.10.refs_0_), channel_id=1, source_target_pairs={{0,2},{1,3},{2,0},{3,1},{4,6},{5,7},{6,4},{7,5},{8,10},{9,11},{10,... | collective-permute-start | bytes 589832 | tf_op jit(solution)/shard_map/ppermute | solution.py:68
  544.6 10.6 %collective-permute-start.41 = (bf16[128,768]{1,0:T(8,128)(2,1)}, bf16[128,768]{1,0:T(8,128)(2,1)}, u32[]{:S(2)}, u32[]{:S(2)}) collective-permute-start(bf16[128,768]{1,0:T(8,128)(2,1)} %add_convert_fusion.10.refs_0_), channel_id=1, source_target_pairs={{0,3},{1,2},{2,1},{3,0},{4,7},{5,6},{6,5},{7,4},{8,11},{9,10},{10,... | collective-permute-start | bytes 589832 | tf_op jit(solution)/shard_map/ppermute | solution.py:68
  545.8 12.6 %copy-start.1 = (bf16[2816,128]{1,0:T(8,128)(2,1)S(1)}, bf16[2816,128]{1,0:T(8,128)(2,1)}, u32[]{:S(2)}) copy-start(bf16[2816,128]{1,0:T(8,128)(2,1)} %param.23) | copy-start | bytes 2162692
  (7 other events, 9.8 us)
Sparse Core Ops, SparseCore 0:
  11.8 202.7 all-gather.1

commit v6 on v5

--- a/solution.py
+++ b/solution.py
@@ -1063,12 +1063,12 @@
     half = project_back(order, 2, grads, qkv, [far], (0, 2))
     across = [swap_seq(half, 2)]
     half, grads = lax.optimization_barrier((half, grads))
+    (qkv_grad,) = products(zero, [normed_one_t] * 3, list(grads), (1, 1, 1), joined=True)
+    qkv_state = scatter_start(qkv_grad, 0, None)
+    qkv_grad, grads = lax.optimization_barrier((qkv_grad, grads))
     half = project_back(order, 2, grads, qkv, [far], (1, 2))
     across.append(swap_seq(half, 2))
-    half, grads = lax.optimization_barrier((half, grads))
-    (qkv_grad,) = products(zero, [normed_one_t] * 3, list(grads), (1, 1, 1), joined=True)
-    qkv_state = scatter_start(qkv_grad, 0, None)
-    across[0], qkv_grad, grads = lax.optimization_barrier((across[0], qkv_grad, grads))
+    across[0], half, grads = lax.optimization_barrier((across[0], half, grads))
     sums, across[0], near = settle(sums, across[0], near)
     sums = [exchange(g) for g in sums]
     (qkv_state, *sums), _, near = settle([qkv_state, *sums], (), near)

time: 573 us -> 573 us (level)
  no operation moved by 1% of the time
where the time goes in v6:
time: 573 us; the launch traced here: 565 us
  Pallas kernels  339 us (59%)
  waiting for transfers between devices  94.2 us (16%)
  starting transfers between devices  70.4 us (12%)
  local copies, waits for them, and re-layouts  28.1 us (5%)
  other arithmetic  18.9 us (3%)
  between operations  14.9 us (3%)
    pallas_call x2, Pallas kernels, attend_back(): call(kernel, (last - first,), in_specs + [small, table, table], out_specs...  79.2 us
    pallas_call x3, Pallas kernels, products(): call(kernel, (height // block,), [pl.BlockSpec((block, d.shape[1]), lambd...  51.2 us
    ppermute x21, waiting for transfers between devices, swap_seq(): return lax.ppermute(array, 'seq', [(i, i ^ bit) for i in range(count)])  46.7 us
    pallas_call x1, Pallas kernels, attend(): call(kernel, (count,), [rows, full, full_t, mem_rows, mem_rows], [pl.Bloc...  40.3 us
    pallas_call x2, Pallas kernels, retrieve(): call(kernel, (head_local, blocks // per), [pl.BlockSpec((1, 1, per, slots...  35.7 us
    pallas_call x6, Pallas kernels, project_back(): call(kernel, (steps,), in_specs, rows_of(out), out, 6 * rows * width * gr...  32.3 us
    pallas_call x1, Pallas kernels, norm_back(): call(kernel, (steps + row_steps,), [resident(g.shape, (0, 0)) for g in gr...  27.3 us
    ppermute x15, starting transfers between devices, trade(): lax.ppermute(give, axis, [(i, i ^ bit) for i in range(count)])  27.2 us
  transfers between devices with their start and end apart: 45, of which 12 were waited for; matrix products, arithmetic and copies ran while one was open for 7% of the time, Pallas kernels for 50%

profile of v6, /device:TPU:0, one launch (start us, length us, event | category | flops | bytes accessed | tf_op | source)
XLA Modules:
  0.0 565.4 jit_solution(10285361207557169435)
XLA Ops:
  11.6 3.0 collective-permute-start.1
  15.3 5.8 %all-to-all-start.1 = ((bf16[8,2,128]{2,1,0:T(2,128)(2,1)}), bf16[8,2,128]{2,1,0:T(2,128)(2,1)S(1)}, u32[]{:S(2)}, u32[]{:S(2)}) async-start(bf16[8,2,128]{2,1,0:T(2,128)(2,1)} %broadcast_in_dim.15), calls=%async_computation.1 | async-start | bytes 8192 | tf_op jit(solution)/shard_map/all_to_all | solution.py:74
  21.1 2.0 collective-permute-start.3
  23.1 1.5 collective-permute-start.4
  27.6 1.3 broadcast_in_dim.14
  28.9 4.2 all-to-all-start
  33.2 17.3 %retrieve.2 = (bf16[2,4096,128]{2,1,0:T(8,128)(2,1)}, bf16[2,4096,128]{2,1,0:T(8,128)(2,1)}) custom-call(s32[2,8,4,128]{3,2,1,0:T(4,128)} %bitcast.149, bf16[2,2048,128]{2,1,0:T(8,128)(2,1)} %bitcast.12.k_ref, bf16[2,2048,128]{2,1,0:T(8,128)(2,1)} %bitcast.13.v_ref), custom_call_target="tpu_custom_call" | custom-call | flops 1288490240 | bytes 1258291 | tf_op jit(solution)/shard_map/retrieve/pallas_call | solution.py:188
  51.1 13.8 %collective-permute-done.1.refs_2_ = bf16[1024,1024]{1,0:T(8,128)(2,1)} collective-permute-done((bf16[1024,1024]{1,0:T(8,128)(2,1)}, bf16[1024,1024]{1,0:T(8,128)(2,1)}, u32[]{:S(2)}, u32[]{:S(2)}) %collective-permute-start.1) | collective-permute-done | bytes 2097184 | tf_op jit(solution)/shard_map/ppermute | solution.py:68
  65.7 3.2 pad_maximum_fusion
  69.4 16.3 %collective-permute-done.4.v_ref = bf16[2,2048,128]{2,1,0:T(8,128)(2,1)} collective-permute-done((bf16[2,2048,128]{2,1,0:T(8,128)(2,1)}, bf16[2,2048,128]{2,1,0:T(8,128)(2,1)}, u32[]{:S(2)}, u32[]{:S(2)}) %collective-permute-start.4) | collective-permute-done | bytes 1048608 | tf_op jit(solution)/shard_map/ppermute | solution.py:956
  85.8 18.4 %retrieve.3 = (bf16[2,4096,128]{2,1,0:T(8,128)(2,1)}, bf16[2,4096,128]{2,1,0:T(8,128)(2,1)}) custom-call(s32[2,8,4,128]{3,2,1,0:T(4,128)} %bitcast.150, bf16[2,2048,128]{2,1,0:T(8,128)(2,1)} %copy-done.16, bf16[2,2048,128]{2,1,0:T(8,128)(2,1)} %collective-permute-done.4.v_ref, bf16[2,4096,128]{2,1,0:T(8,128)(2,1)} %get-tuple-element.162.refs_0_, ...), custom_call_target="tpu_custom_call" | custom-call | flops 1288490240 | bytes 1258291 | tf_op jit(solution)/shard_map/retrieve/pallas_call | solution.py:188
  104.2 4.3 all-to-all-done
  109.7 18.9 %project.1 = (bf16[2,4096,128]{2,1,0:T(8,128)(2,1)}, bf16[2,4096,128]{2,1,0:T(8,128)(2,1)}, bf16[2,4096,128]{2,1,0:T(8,128)(2,1)}, bf16[2,128,4096]{2,1,0:T(8,128)(2,1)}, bf16[1024,4096]{1,0:T(8,128)(2,1)}) custom-call(s32[4]{0:T(128)} %iota_xor_fusion.order_ref, bf16[1024,1024]{1,0:T(8,128)(2,1)} %refs_2_.3, ...), custom_call_target="tpu_custom_call" | custom-call | flops 966367616 | bytes 4089446 | tf_op jit(solution)/shard_map/project/pallas_call | solution.py:130
  128.6 40.3 %attend.1 = (bf16[1024,256]{1,0:T(8,128)(2,1)}, bf16[1024,256]{1,0:T(8,128)(2,1)}, bf16[1024,256]{1,0:T(8,128)(2,1)}, bf16[1024,256]{1,0:T(8,128)(2,1)}, f32[8,8,512]{2,1,0:T(8,128)}) custom-call(s32[4]{0:T(128)} %iota_xor_fusion.order_ref, bf16[2,4096,128]{2,1,0:T(8,128)(2,1)} %get-tuple-element.159.q_ref, bf16[2,4096,128]{2,1,0:T(8,128)(2,1)} %get-tuple-element.160.k_ref, ...), custom_call_target="tpu_custom_call" | custom-call | flops 2576980480 | bytes 1887436 | tf_op jit(solution)/shard_map/attend/pallas_call | solution.py:289
  169.0 1.8 collective-permute-start.7
  170.8 2.6 copy.49
  173.4 3.2 copy.50
  176.5 18.6 %collective-permute-done.6.refs_2_ = bf16[1024,256]{1,0:T(8,128)(2,1)S(1)} collective-permute-done((bf16[1024,256]{1,0:T(8,128)(2,1)}, bf16[1024,256]{1,0:T(8,128)(2,1)S(1)}, u32[]{:S(2)}, u32[]{:S(2)}) %collective-permute-start.6) | collective-permute-done | bytes 524320 | tf_op jit(solution)/shard_map/ppermute | solution.py:68
  195.2 11.7 %collective-permute-done.7.refs_3_ = bf16[1024,256]{1,0:T(8,128)(2,1)} collective-permute-done((bf16[1024,256]{1,0:T(8,128)(2,1)}, bf16[1024,256]{1,0:T(8,128)(2,1)}, u32[]{:S(2)}, u32[]{:S(2)}) %collective-permute-start.7) | collective-permute-done | bytes 524320 | tf_op jit(solution)/shard_map/ppermute | solution.py:68
  206.8 7.7 %all-gather.2.cloned.1.call-done.refs_4_.refs_5_.refs_6_.refs_7_.wg_ref.wu_ref.wd_ref.refs_2_.refs_3_.w_ref = bf16[1024,9472]{1,0:T(8,128)(2,1)} async-done(((bf16[32,9472]{1,0:T(8,128)(2,1)}), bf16[1024,9472]{1,0:T(8,128)(2,1)}) %all-gather.2.cloned.1.call-update) | async-done | bytes 19398672 | tf_op jit(solution)/shard_map/all_gather | solution.py:967
  214.6 9.6 %mix.1 = (f32[1024,1024]{1,0:T(8,128)}, bf16[1024,1024]{1,0:T(8,128)(2,1)}, bf16[1024,1024]{1,0:T(8,128)(2,1)}, bf16[1024,1024]{1,0:T(8,128)(2,1)}) custom-call(s32[4]{0:T(128)} %iota_xor_fusion.order_ref, bf16[1024,256]{1,0:T(8,128)(2,1)} %get-tuple-element.166.refs_0_.refs_4_, bf16[1024,256]{1,0:T(8,128)(2,1)} %copy-done.17, bf16[1024,256]{1,0:T(8,128)(2,1)} %copy-done.18, ...), custom_call_target="tpu_custom_call" | custom-call | flops 322122560 | bytes 2516582 | tf_op jit(solution)/shard_map/mix/pallas_call | solution.py:491
  224.2 24.9 %gated.1 = (bf16[1024,2816]{1,0:T(8,128)(2,1)}, bf16[1024,2816]{1,0:T(8,128)(2,1)}, bf16[1024,2816]{1,0:T(8,128)(2,1)}) custom-call(bf16[1024,1024]{1,0:T(8,128)(2,1)} %get-tuple-element.173.n_ref, bf16[1024,1024]{1,0:T(8,128)(2,1)} %refs_9_.1, ...), custom_call_target="tpu_custom_call" | custom-call | flops 2657510912 | bytes 5190451 | tf_op jit(solution)/shard_map/gated/pallas_call | solution.py:527
  249.1 15.5 %products.3 = (bf16[1024,1408]{1,0:T(8,128)(2,1)}, bf16[1024,1408]{1,0:T(8,128)(2,1)}, bf16[1024,1408]{1,0:T(8,128)(2,1)}) custom-call(s32[1]{0:T(128)} %bitcast.16.select_ref, bf16[1024,1024]{1,0:T(8,128)(2,1)} %bitcast.132, bf16[1024,1024]{1,0:T(8,128)(2,1)} %get-tuple-element.172.refs_1_, bf16[1024,2816]{1,0:T(8,128)(2,1)} %get-tuple-element.277.refs_2_.refs_3_.h_ref, ...), custom_call_target="tpu_custom_call" | custom-call | flops 1328755456 | bytes 2595225 | tf_op jit(solution)/shard_map/products/pallas_call | solution.py:678
  265.2 27.3 %norm_back.1 = (f32[1024,1024]{1,0:T(8,128)}, bf16[1024,1024]{1,0:T(8,128)(2,1)}, bf16[1024,256]{1,0:T(8,128)(2,1)}, bf16[1024,256]{1,0:T(8,128)(2,1)}, bf16[102...) custom-call(s32[4]{0:T(128)} %iota_xor_fusion.order_ref, bf16[1024,2816]{1,0:T(8,128)(2,1)} %get-tuple-element.180.refs_3_.refs_0_.refs_4_, ...), custom_call_target="tpu_custom_call" | custom-call | flops 2093796608 | bytes 5976883 | tf_op jit(solution)/shard_map/norm_back/pallas_call | solution.py:597
  293.4 1.2 collective-permute-start.9
  295.3 24.1 %products.4 = (bf16[512,1408]{1,0:T(8,128)(2,1)}, bf16[512,1408]{1,0:T(8,128)(2,1)}, bf16[512,1408]{1,0:T(8,128)(2,1)}, bf16[512,1024]{1,0:T(8,128)(2,1)}, bf16[...) custom-call(s32[5]{0:T(128)} %stack.44.select_ref, ...), custom_call_target="tpu_custom_call" | custom-call | flops 1650878080 | bytes 3224371 | tf_op jit(solution)/shard_map/products/pallas_call | solution.py:678
  319.4 5.8 %collective-permute-start.16 = (bf16[512,1408]{1,0:T(8,128)(2,1)}, bf16[512,1408]{1,0:T(8,128)(2,1)}, u32[]{:S(2)}, u32[]{:S(2)}) collective-permute-start(bf16[512,1408]{1,0:T(8,128)(2,1)} %get-tuple-element.207), channel_id=1, source_target_pairs={{0,8},{4,12},{8,0},{12,4},{16,24},{20,28},{24,16},{28,20},{1,9},{5... | collective-permute-start | bytes 4325384 | tf_op jit(solution)/shard_map/ppermute | solution.py:809
  326.3 9.8 %collective-permute-start.15 = (bf16[512,1408]{1,0:T(8,128)(2,1)}, bf16[512,1408]{1,0:T(8,128)(2,1)}, u32[]{:S(2)}, u32[]{:S(2)}) collective-permute-start(bf16[512,1408]{1,0:T(8,128)(2,1)} %get-tuple-element.205), channel_id=1, source_target_pairs={{0,4},{4,0},{8,12},{12,8},{16,20},{20,16},{24,28},{28,24},{1,5},{5... | collective-permute-start | bytes 4325384 | tf_op jit(solution)/shard_map/ppermute | solution.py:809
  336.4 43.5 %attend_back.2 = (bf16[4096,256]{1,0:T(8,128)(2,1)}, bf16[4096,256]{1,0:T(8,128)(2,1)}, bf16[4096,256]{1,0:T(8,128)(2,1)}, f32[2,128,2560]{2,1,0:T(8,128)}, f32[8,8,512]{2,1,0:T(8,128)}) custom-call(s32[4]{0:T(128)} %iota_xor_fusion.order_ref, bf16[2,4096,128]{2,1,0:T(8,128)(2,1)} %get-tuple-element.159.q_ref, ...), custom_call_target="tpu_custom_call" | custom-call | flops 1879048192 | bytes 3774873 | tf_op jit(solution)/shard_map/attend_back/pallas_call | solution.py:445
  379.9 2.0 fusion.3
  382.0 1.8 fusion
  383.9 1.8 fusion.1
  386.1 6.8 %collective-permute-start.21 = (bf16[2,128,1024]{2,1,0:T(8,128)(2,1)S(1)}, bf16[2,128,1024]{2,1,0:T(8,128)(2,1)S(1)}, u32[]{:S(2)}, u32[]{:S(2)}) collective-permute-start(bf16[2,128,1024]{2,1,0:T(8,128)(2,1)S(1)} %get-tuple-element.309), channel_id=1, source_target_pairs={{0,4},{4,0},{8,12},{12,8},{16,20},{20,16},{24,28},{28,24},{1,5},{5... | collective-permute-start | bytes 1572872 | tf_op jit(solution)/shard_map/ppermute | solution.py:792
  396.6 1.5 collective-permute-start.19
  398.2 35.7 %attend_back.3 = (bf16[4096,256]{1,0:T(8,128)(2,1)}, bf16[4096,256]{1,0:T(8,128)(2,1)}, bf16[4096,256]{1,0:T(8,128)(2,1)}) custom-call(s32[4]{0:T(128)} %iota_xor_fusion.order_ref, bf16[2,4096,128]{2,1,0:T(8,128)(2,1)} %get-tuple-element.159.q_ref, ...), custom_call_target="tpu_custom_call", output_to_operand_aliasing={{0}: (12, {}), {1}: (13, {}), {2}: (14, {})} | custom-call | flops 1342177280 | bytes 3774873 | tf_op jit(solution)/shard_map/attend_back/pallas_call | solution.py:445
  435.0 1.3 add_convert_fusion.2
  436.3 2.1 add_convert_fusion.3
  438.4 5.5 project_back.6
  443.9 5.5 project_back.7
  449.9 4.6 project_back.8
  455.9 1.9 dynamic-slice_bitcast_fusion.17
  458.5 3.4 collective-permute-start.26
  462.7 1.5 collective-permute-start.27
  464.8 11.6 %products.5 = bf16[1024,768]{1,0:T(8,128)(2,1)} custom-call(s32[1]{0:T(128)} %constant.242.clone.1.select_ref, bf16[1024,4096]{1,0:T(8,128)(2,1)} %get-tuple-element.171.refs_0_, bf16[4096,256]{1,0:T(8,128)(2,1)} %get-tuple-element.270.a_ref.refs_1_, bf16[4096,256]{1,0:T(8,128)(2,1)} %get-tuple-element.271.b_ref.refs_2_, ...), custom_call_target="tpu_custom_call" | custom-call | flops 966367616 | bytes 1179648 | tf_op jit(solution)/shard_map/products/pallas_call | solution.py:678
  476.4 4.6 project_back.9
  481.0 1.6 dynamic-slice_bitcast_fusion.1
  482.6 2.1 collective-permute-start.24
  485.3 2.1 collective-permute-start.29
  488.5 3.6 collective-permute-done.24
  492.3 1.2 collective-permute-start.33
  493.7 2.1 collective-permute-start.32
  495.7 1.8 collective-permute-start.31
  497.5 7.2 %collective-permute-done.29 = bf16[2,2,128,768]{3,2,1,0:T(8,128)(2,1)S(1)} collective-permute-done((bf16[2,2,128,768]{3,2,1,0:T(8,128)(2,1)S(1)}, bf16[2,2,128,768]{3,2,1,0:T(8,128)(2,1)S(1)}, u32[]{:S(2)}, u32[]{:S(2)}) %collective-permute-start.29) | collective-permute-done | bytes 786464 | tf_op jit(solution)/shard_map/ppermute | solution.py:792
  504.7 1.8 collective-permute-start.30
  507.0 6.2 %collective-permute-done.30 = bf16[64,1408]{1,0:T(8,128)(2,1)S(1)} collective-permute-done((bf16[64,1408]{1,0:T(8,128)(2,1)S(1)}, bf16[64,1408]{1,0:T(8,128)(2,1)S(1)}, u32[]{:S(2)}, u32[]{:S(2)}) %collective-permute-start.30) | collective-permute-done | bytes 180256 | tf_op jit(solution)/shard_map/ppermute | solution.py:792
  513.3 1.6 collective-permute-start.37
  515.1 6.1 %project_back.10.refs_5_ = bf16[1024,1024]{1,0:T(8,128)(2,1)} custom-call(s32[4]{0:T(128)} %iota_xor_fusion.order_ref, bf16[4096,256]{1,0:T(8,128)(2,1)} %get-tuple-element.270.a_ref.refs_1_, bf16[4096,256]{1,0:T(8,128)(2,1)} %get-tuple-element.271.b_ref.refs_2_, bf16[4096,256]{1,0:T(8,128)(2,1)} %get-tuple-element.272.c_ref.refs_3_, ...), custom_call_target="tpu_custom_call" | custom-call | flops 120795952 | bytes 432537 | tf_op jit(solution)/shard_map/project_back/pallas_call | solution.py:762
  521.2 1.7 collective-permute-done.34
  522.9 6.1 %project_back.11 = bf16[1024,1024]{1,0:T(8,128)(2,1)} custom-call(s32[4]{0:T(128)} %iota_xor_fusion.order_ref, bf16[4096,256]{1,0:T(8,128)(2,1)} %get-tuple-element.270.a_ref.refs_1_, bf16[4096,256]{1,0:T(8,128)(2,1)} %get-tuple-element.271.b_ref.refs_2_, bf16[4096,256]{1,0:T(8,128)(2,1)} %get-tuple-element.272.c_ref.refs_3_, ...), custom_call_target="tpu_custom_call", output_to_operand_aliasing={{}: (10, {})} | custom-call | flops 120795952 | bytes 432537 | tf_op jit(solution)/shard_map/project_back/pallas_call | solution.py:762
  529.5 1.7 collective-permute-start.36
  531.9 11.2 %finish.1 = bf16[1024,1024]{1,0:T(8,128)(2,1)} custom-call(f32[1024,1024]{1,0:T(8,128)} %get-tuple-element.170.refs_8_.r_ref, bf16[1024,2816]{1,0:T(8,128)(2,1)} %get-tuple-element.277.refs_2_.refs_3_.h_ref, bf16[1024,9472]{1,0:T(8,128)(2,1)} %all-gather.2.cloned.1.call-done.refs_4_.refs_5_.refs_6_.refs_7_.wg_ref.wu_ref.wd_ref.refs_2_.refs_3_.w_ref), custom_call_target="tpu_custom_call" | custom-call | flops 885836992 | bytes 2673868 | tf_op jit(solution)/shard_map/finish/pallas_call | solution.py:701
  547.6 5.0 feedforward_ends.1
  552.6 2.5 collective-permute-done.41.refs_3_
  555.1 3.3 projection_ends.1
  (169 shorter events, 32.3 us)
Async XLA Ops:
  7.2 207.4 %all-gather.2.cloned.1.call-start = ((), (), s32[]{:S(2)}) async-start(), calls=%async_computation.2 | async-start | bytes 20004864 | tf_op jit(solution)/shard_map/all_gather | solution.py:967
  8.6 6.1 %copy-start.22 = (bf16[128]{0:T(256)(128)(2,1)S(1)}, bf16[128]{0:T(256)(128)(2,1)}, u32[]{:S(2)}) copy-start(bf16[128]{0:T(256)(128)(2,1)} %param.25) | copy-start | bytes 772
  8.6 6.1 %copy-start.24 = (bf16[128]{0:T(256)(128)(2,1)S(1)}, bf16[128]{0:T(256)(128)(2,1)}, u32[]{:S(2)}) copy-start(bf16[128]{0:T(256)(128)(2,1)} %param.24) | copy-start | bytes 772
  8.6 17.9 %copy-start.20 = (s32[1,2,32,128]{3,2,1,0:T(8,128)S(1)}, s32[1,2,32,128]{3,2,1,0:T(8,128)}, u32[]{:S(2)}) copy-start(s32[1,2,32,128]{3,2,1,0:T(8,128)} %param.28) | copy-start | bytes 98308
  8.6 17.9 %copy-start.21 = (s32[1,2,32,128]{3,2,1,0:T(8,128)S(1)}, s32[1,2,32,128]{3,2,1,0:T(8,128)}, u32[]{:S(2)}) copy-start(s32[1,2,32,128]{3,2,1,0:T(8,128)} %param.29) | copy-start | bytes 98308
  11.6 53.3 %collective-permute-start.1 = (bf16[1024,1024]{1,0:T(8,128)(2,1)}, bf16[1024,1024]{1,0:T(8,128)(2,1)}, u32[]{:S(2)}, u32[]{:S(2)}) collective-permute-start(bf16[1024,1024]{1,0:T(8,128)(2,1)} %refs_2_.3), channel_id=1, source_target_pairs={{0,2},{1,3},{2,0},{3,1},{4,6},{5,7},{6,4},{7,5},{8,10},{9,11},{10,... | collective-permute-start | bytes 6291464 | tf_op jit(solution)/shard_map/ppermute | solution.py:68
  14.7 89.5 %collective-permute-start = (bf16[1024,1024]{1,0:T(8,128)(2,1)}, bf16[1024,1024]{1,0:T(8,128)(2,1)}, u32[]{:S(2)}, u32[]{:S(2)}) collective-permute-start(bf16[1024,1024]{1,0:T(8,128)(2,1)} %refs_2_.3), channel_id=1, source_target_pairs={{0,1},{1,0},{2,3},{3,2},{4,5},{5,4},{6,7},{7,6},{8,9},{9,8},{10,11... | collective-permute-start | bytes 6291464 | tf_op jit(solution)/shard_map/ppermute | solution.py:68
  15.3 12.3 %all-to-all-start.1 = ((bf16[8,2,128]{2,1,0:T(2,128)(2,1)}), bf16[8,2,128]{2,1,0:T(2,128)(2,1)S(1)}, u32[]{:S(2)}, u32[]{:S(2)}) async-start(bf16[8,2,128]{2,1,0:T(2,128)(2,1)} %broadcast_in_dim.15), calls=%async_computation.1 | async-start | bytes 8192 | tf_op jit(solution)/shard_map/all_to_all | solution.py:74
  21.1 48.3 %collective-permute-start.3 = (bf16[2,2048,128]{2,1,0:T(8,128)(2,1)}, bf16[2,2048,128]{2,1,0:T(8,128)(2,1)S(1)}, u32[]{:S(2)}, u32[]{:S(2)}) collective-permute-start(bf16[2,2048,128]{2,1,0:T(8,128)(2,1)} %bitcast.12.k_ref), channel_id=1, source_target_pairs={{0,4},{4,8},{8,12},{12,16},{16,20},{20,24},{24,28},{28,0},{1,5},{5... | collective-permute-start | bytes 3145736 | tf_op jit(solution)/shard_map/ppermute | solution.py:955
  23.1 62.7 %collective-permute-start.4 = (bf16[2,2048,128]{2,1,0:T(8,128)(2,1)}, bf16[2,2048,128]{2,1,0:T(8,128)(2,1)}, u32[]{:S(2)}, u32[]{:S(2)}) collective-permute-start(bf16[2,2048,128]{2,1,0:T(8,128)(2,1)} %bitcast.13.v_ref), channel_id=1, source_target_pairs={{0,4},{4,8},{8,12},{12,16},{16,20},{20,24},{24,28},{28,0},{1,5},{5... | collective-permute-start | bytes 3145736 | tf_op jit(solution)/shard_map/ppermute | solution.py:956
  28.9 79.6 %all-to-all-start = ((bf16[8,128,768]{2,1,0:T(8,128)(2,1)}), bf16[8,128,768]{2,1,0:T(8,128)(2,1)S(1)}, u32[]{:S(2)}, u32[]{:S(2)}) async-start(bf16[8,128,768]{2,1,0:T(8,128)(2,1)} %broadcast_in_dim.14), calls=%async_computation | async-start | bytes 3145728 | tf_op jit(solution)/shard_map/all_to_all | solution.py:74
  64.9 43.6 %collective-permute-start.2 = (bf16[1024,1024]{1,0:T(8,128)(2,1)}, bf16[1024,1024]{1,0:T(8,128)(2,1)}, u32[]{:S(2)}, u32[]{:S(2)}) collective-permute-start(bf16[1024,1024]{1,0:T(8,128)(2,1)} %collective-permute-done.1.refs_2_), channel_id=1, source_target_pairs={{0,1},{1,0},{2,3},{3,2},{4,5},{5,4},{6,7},{7,6},{8,9},{9,8},{10,11... | collective-permute-start | bytes 6291464 | tf_op jit(solution)/shard_map/ppermute | solution.py:68
  69.4 16.3 %copy-start.16 = (bf16[2,2048,128]{2,1,0:T(8,128)(2,1)}, bf16[2,2048,128]{2,1,0:T(8,128)(2,1)S(1)}, u32[]{:S(2)}) copy-start(bf16[2,2048,128]{2,1,0:T(8,128)(2,1)S(1)} %collective-permute-done.3.k_ref) | copy-start | bytes 3145732
  128.6 42.2 %copy-start.3 = (bf16[1024,1024]{1,0:T(8,128)(2,1)S(1)}, bf16[1024,1024]{1,0:T(8,128)(2,1)}, u32[]{:S(2)}) copy-start(bf16[1024,1024]{1,0:T(8,128)(2,1)} %refs_9_.1) | copy-start | bytes 6291460
  168.9 7.7 %collective-permute-start.5 = (bf16[1024,256]{1,0:T(8,128)(2,1)}, bf16[1024,256]{1,0:T(8,128)(2,1)S(1)}, u32[]{:S(2)}, u32[]{:S(2)}) collective-permute-start(bf16[1024,256]{1,0:T(8,128)(2,1)} %get-tuple-element.167.refs_5_), channel_id=1, source_target_pairs={{0,1},{1,0},{2,3},{3,2},{4,5},{5,4},{6,7},{7,6},{8,9},{9,8},{10,11... | collective-permute-start | bytes 1572872 | tf_op jit(solution)/shard_map/ppermute | solution.py:68
  168.9 26.3 %collective-permute-start.6 = (bf16[1024,256]{1,0:T(8,128)(2,1)}, bf16[1024,256]{1,0:T(8,128)(2,1)S(1)}, u32[]{:S(2)}, u32[]{:S(2)}) collective-permute-start(bf16[1024,256]{1,0:T(8,128)(2,1)} %get-tuple-element.168.refs_6_), channel_id=1, source_target_pairs={{0,2},{1,3},{2,0},{3,1},{4,6},{5,7},{6,4},{7,5},{8,10},{9,11},{10,... | collective-permute-start | bytes 1572872 | tf_op jit(solution)/shard_map/ppermute | solution.py:68
  169.0 37.9 %collective-permute-start.7 = (bf16[1024,256]{1,0:T(8,128)(2,1)}, bf16[1024,256]{1,0:T(8,128)(2,1)}, u32[]{:S(2)}, u32[]{:S(2)}) collective-permute-start(bf16[1024,256]{1,0:T(8,128)(2,1)} %get-tuple-element.169.refs_7_), channel_id=1, source_target_pairs={{0,3},{1,2},{2,1},{3,0},{4,7},{5,6},{6,5},{7,4},{8,11},{9,10},{10,... | collective-permute-start | bytes 1572872 | tf_op jit(solution)/shard_map/ppermute | solution.py:68
  176.5 38.0 %copy-start.17 = (bf16[1024,256]{1,0:T(8,128)(2,1)}, bf16[1024,256]{1,0:T(8,128)(2,1)S(1)}, u32[]{:S(2)}) copy-start(bf16[1024,256]{1,0:T(8,128)(2,1)S(1)} %collective-permute-done.5.refs_1_) | copy-start | bytes 1572868
  195.2 19.4 %copy-start.18 = (bf16[1024,256]{1,0:T(8,128)(2,1)}, bf16[1024,256]{1,0:T(8,128)(2,1)S(1)}, u32[]{:S(2)}) copy-start(bf16[1024,256]{1,0:T(8,128)(2,1)S(1)} %collective-permute-done.6.refs_2_) | copy-start | bytes 1572868
  264.6 28.9 %collective-permute-start.11 = (bf16[1024,1408]{1,0:T(8,128)(2,1)}, bf16[1024,1408]{1,0:T(8,128)(2,1)}, u32[]{:S(2)}, u32[]{:S(2)}) collective-permute-start(bf16[1024,1408]{1,0:T(8,128)(2,1)} %get-tuple-element.187), channel_id=1, source_target_pairs={{0,1},{1,0},{2,3},{3,2},{4,5},{5,4},{6,7},{7,6},{8,9},{9,8},{10,11... | collective-permute-start | bytes 8650760 | tf_op jit(solution)/shard_map/ppermute | solution.py:68
  264.6 30.7 %collective-permute-start.12 = (bf16[1024,1408]{1,0:T(8,128)(2,1)}, bf16[1024,1408]{1,0:T(8,128)(2,1)}, u32[]{:S(2)}, u32[]{:S(2)}) collective-permute-start(bf16[1024,1408]{1,0:T(8,128)(2,1)} %get-tuple-element.188), channel_id=1, source_target_pairs={{0,1},{1,0},{2,3},{3,2},{4,5},{5,4},{6,7},{7,6},{8,9},{9,8},{10,11... | collective-permute-start | bytes 8650760 | tf_op jit(solution)/shard_map/ppermute | solution.py:68
  265.1 30.2 %collective-permute-start.13 = (bf16[1024,1408]{1,0:T(8,128)(2,1)}, bf16[1024,1408]{1,0:T(8,128)(2,1)}, u32[]{:S(2)}, u32[]{:S(2)}) collective-permute-start(bf16[1024,1408]{1,0:T(8,128)(2,1)} %get-tuple-element.189), channel_id=1, source_target_pairs={{0,1},{1,0},{2,3},{3,2},{4,5},{5,4},{6,7},{7,6},{8,9},{9,8},{10,11... | collective-permute-start | bytes 8650760 | tf_op jit(solution)/shard_map/ppermute | solution.py:68
  292.5 26.9 %collective-permute-start.10 = (bf16[1024,256]{1,0:T(8,128)(2,1)}, bf16[1024,256]{1,0:T(8,128)(2,1)S(1)}, u32[]{:S(2)}, u32[]{:S(2)}) collective-permute-start(bf16[1024,256]{1,0:T(8,128)(2,1)} %get-tuple-element.184), channel_id=1, source_target_pairs={{0,3},{1,2},{2,1},{3,0},{4,7},{5,6},{6,5},{7,4},{8,11},{9,10},{10,... | collective-permute-start | bytes 1572872 | tf_op jit(solution)/shard_map/ppermute | solution.py:68
  293.4 26.0 %collective-permute-start.8 = (bf16[1024,256]{1,0:T(8,128)(2,1)}, bf16[1024,256]{1,0:T(8,128)(2,1)S(1)}, u32[]{:S(2)}, u32[]{:S(2)}) collective-permute-start(bf16[1024,256]{1,0:T(8,128)(2,1)} %get-tuple-element.182), channel_id=1, source_target_pairs={{0,1},{1,0},{2,3},{3,2},{4,5},{5,4},{6,7},{7,6},{8,9},{9,8},{10,11... | collective-permute-start | bytes 1572872 | tf_op jit(solution)/shard_map/ppermute | solution.py:68
  293.4 26.0 %collective-permute-start.9 = (bf16[1024,256]{1,0:T(8,128)(2,1)}, bf16[1024,256]{1,0:T(8,128)(2,1)S(1)}, u32[]{:S(2)}, u32[]{:S(2)}) collective-permute-start(bf16[1024,256]{1,0:T(8,128)(2,1)} %get-tuple-element.183), channel_id=1, source_target_pairs={{0,2},{1,3},{2,0},{3,1},{4,6},{5,7},{6,4},{7,5},{8,10},{9,11},{10,... | collective-permute-start | bytes 1572872 | tf_op jit(solution)/shard_map/ppermute | solution.py:68
  319.4 17.0 %copy-start.7 = (bf16[1024,256]{1,0:T(8,128)(2,1)}, bf16[1024,256]{1,0:T(8,128)(2,1)S(1)}, u32[]{:S(2)}) copy-start(bf16[1024,256]{1,0:T(8,128)(2,1)S(1)} %collective-permute-done.10.refs_3_) | copy-start | bytes 1572868
  319.4 17.0 %copy-start.8 = (bf16[1024,256]{1,0:T(8,128)(2,1)}, bf16[1024,256]{1,0:T(8,128)(2,1)S(1)}, u32[]{:S(2)}) copy-start(bf16[1024,256]{1,0:T(8,128)(2,1)S(1)} %collective-permute-done.8.refs_1_) | copy-start | bytes 1572868
  319.4 17.0 %copy-start.9 = (bf16[1024,256]{1,0:T(8,128)(2,1)}, bf16[1024,256]{1,0:T(8,128)(2,1)S(1)}, u32[]{:S(2)}) copy-start(bf16[1024,256]{1,0:T(8,128)(2,1)S(1)} %collective-permute-done.9.refs_2_) | copy-start | bytes 1572868
  319.4 62.5 %collective-permute-start.16 = (bf16[512,1408]{1,0:T(8,128)(2,1)}, bf16[512,1408]{1,0:T(8,128)(2,1)}, u32[]{:S(2)}, u32[]{:S(2)}) collective-permute-start(bf16[512,1408]{1,0:T(8,128)(2,1)} %get-tuple-element.207), channel_id=1, source_target_pairs={{0,8},{4,12},{8,0},{12,4},{16,24},{20,28},{24,16},{28,20},{1,9},{5... | collective-permute-start | bytes 4325384 | tf_op jit(solution)/shard_map/ppermute | solution.py:809
  325.3 54.7 %collective-permute-start.17 = (bf16[512,1024]{1,0:T(8,128)(2,1)}, bf16[512,1024]{1,0:T(8,128)(2,1)}, u32[]{:S(2)}, u32[]{:S(2)}) collective-permute-start(bf16[512,1024]{1,0:T(8,128)(2,1)} %get-tuple-element.209), channel_id=1, source_target_pairs={{0,16},{4,20},{8,24},{12,28},{16,0},{20,4},{24,8},{28,12},{1,17},{... | collective-permute-start | bytes 3145736 | tf_op jit(solution)/shard_map/ppermute | solution.py:809
  326.3 57.6 %collective-permute-start.15 = (bf16[512,1408]{1,0:T(8,128)(2,1)}, bf16[512,1408]{1,0:T(8,128)(2,1)}, u32[]{:S(2)}, u32[]{:S(2)}) collective-permute-start(bf16[512,1408]{1,0:T(8,128)(2,1)} %get-tuple-element.205), channel_id=1, source_target_pairs={{0,4},{4,0},{8,12},{12,8},{16,20},{20,16},{24,28},{28,24},{1,5},{5... | collective-permute-start | bytes 4325384 | tf_op jit(solution)/shard_map/ppermute | solution.py:809
  336.1 49.6 %collective-permute-start.14 = (bf16[512,1408]{1,0:T(8,128)(2,1)}, bf16[512,1408]{1,0:T(8,128)(2,1)S(1)}, u32[]{:S(2)}, u32[]{:S(2)}) collective-permute-start(bf16[512,1408]{1,0:T(8,128)(2,1)} %get-tuple-element.203), channel_id=1, source_target_pairs={{0,2},{1,3},{2,0},{3,1},{4,6},{5,7},{6,4},{7,5},{8,10},{9,11},{10,... | collective-permute-start | bytes 4325384 | tf_op jit(solution)/shard_map/ppermute | solution.py:809
  379.9 2.1 copy-start.12
  386.1 47.8 %collective-permute-start.21 = (bf16[2,128,1024]{2,1,0:T(8,128)(2,1)S(1)}, bf16[2,128,1024]{2,1,0:T(8,128)(2,1)S(1)}, u32[]{:S(2)}, u32[]{:S(2)}) collective-permute-start(bf16[2,128,1024]{2,1,0:T(8,128)(2,1)S(1)} %get-tuple-element.309), channel_id=1, source_target_pairs={{0,4},{4,0},{8,12},{12,8},{16,20},{20,16},{24,28},{28,24},{1,5},{5... | collective-permute-start | bytes 1572872 | tf_op jit(solution)/shard_map/ppermute | solution.py:792
  394.0 40.2 %collective-permute-start.20 = (bf16[2,2,64,1408]{3,2,1,0:T(8,128)(2,1)}, bf16[2,2,64,1408]{3,2,1,0:T(8,128)(2,1)S(1)}, u32[]{:S(2)}, u32[]{:S(2)}) collective-permute-start(bf16[2,2,64,1408]{3,2,1,0:T(8,128)(2,1)} %get-tuple-element.301), channel_id=1, source_target_pairs={{0,2},{1,3},{2,0},{3,1},{4,6},{5,7},{6,4},{7,5},{8,10},{9,11},{10,... | collective-permute-start | bytes 2162696 | tf_op jit(solution)/shard_map/ppermute | solution.py:792
  396.6 37.7 %collective-permute-start.19 = (bf16[2,2,64,1408]{3,2,1,0:T(8,128)(2,1)}, bf16[2,2,64,1408]{3,2,1,0:T(8,128)(2,1)}, u32[]{:S(2)}, u32[]{:S(2)}) collective-permute-start(bf16[2,2,64,1408]{3,2,1,0:T(8,128)(2,1)} %get-tuple-element.303), channel_id=1, source_target_pairs={{0,2},{1,3},{2,0},{3,1},{4,6},{5,7},{6,4},{7,5},{8,10},{9,11},{10,... | collective-permute-start | bytes 2162696 | tf_op jit(solution)/shard_map/ppermute | solution.py:792
  398.2 38.1 %collective-permute-start.18 = (bf16[2,2,64,1408]{3,2,1,0:T(8,128)(2,1)}, bf16[2,2,64,1408]{3,2,1,0:T(8,128)(2,1)}, u32[]{:S(2)}, u32[]{:S(2)}) collective-permute-start(bf16[2,2,64,1408]{3,2,1,0:T(8,128)(2,1)} %get-tuple-element.306), channel_id=1, source_target_pairs={{0,4},{4,0},{8,12},{12,8},{16,20},{20,16},{24,28},{28,24},{1,5},{5... | collective-permute-start | bytes 2162696 | tf_op jit(solution)/shard_map/ppermute | solution.py:792
  443.9 6.0 %collective-permute-start.22 = (bf16[1024,1024]{1,0:T(8,128)(2,1)}, bf16[1024,1024]{1,0:T(8,128)(2,1)}, u32[]{:S(2)}, u32[]{:S(2)}) collective-permute-start(bf16[1024,1024]{1,0:T(8,128)(2,1)} %project_back.6), channel_id=1, source_target_pairs={{0,1},{1,0},{2,3},{3,2},{4,5},{5,4},{6,7},{7,6},{8,9},{9,8},{10,11... | collective-permute-start | bytes 6291464 | tf_op jit(solution)/shard_map/ppermute | solution.py:68
  449.4 42.9 %collective-permute-start.28 = (bf16[1024,1024]{1,0:T(8,128)(2,1)}, bf16[1024,1024]{1,0:T(8,128)(2,1)S(1)}, u32[]{:S(2)}, u32[]{:S(2)}) collective-permute-start(bf16[1024,1024]{1,0:T(8,128)(2,1)} %project_back.7), channel_id=1, source_target_pairs={{0,1},{1,0},{2,3},{3,2},{4,5},{5,4},{6,7},{7,6},{8,9},{9,8},{10,11... | collective-permute-start | bytes 6291464 | tf_op jit(solution)/shard_map/ppermute | solution.py:68
  454.4 28.1 %collective-permute-start.23 = (bf16[512,1024]{1,0:T(8,128)(2,1)}, bf16[512,1024]{1,0:T(8,128)(2,1)}, u32[]{:S(2)}, u32[]{:S(2)}) collective-permute-start(bf16[512,1024]{1,0:T(8,128)(2,1)} %project_back.8), channel_id=1, source_target_pairs={{0,2},{1,3},{2,0},{3,1},{4,6},{5,7},{6,4},{7,5},{8,10},{9,11},{10,... | collective-permute-start | bytes 3145736 | tf_op jit(solution)/shard_map/ppermute | solution.py:68
  458.5 26.2 %collective-permute-start.26 = (bf16[2,64,1408]{2,1,0:T(8,128)(2,1)}, bf16[2,64,1408]{2,1,0:T(8,128)(2,1)S(1)}, u32[]{:S(2)}, u32[]{:S(2)}) collective-permute-start(bf16[2,64,1408]{2,1,0:T(8,128)(2,1)} %get-tuple-element.313), channel_id=1, source_target_pairs={{0,16},{4,20},{8,24},{12,28},{16,0},{20,4},{24,8},{28,12},{1,17},{... | collective-permute-start | bytes 1081352 | tf_op jit(solution)/shard_map/ppermute | solution.py:792
  462.7 24.8 %collective-permute-start.27 = (bf16[2,64,1024]{2,1,0:T(8,128)(2,1)}, bf16[2,64,1024]{2,1,0:T(8,128)(2,1)}, u32[]{:S(2)}, u32[]{:S(2)}) collective-permute-start(bf16[2,64,1024]{2,1,0:T(8,128)(2,1)} %get-tuple-element.319), channel_id=1, source_target_pairs={{0,2},{1,3},{2,0},{3,1},{4,6},{5,7},{6,4},{7,5},{8,10},{9,11},{10,... | collective-permute-start | bytes 786440 | tf_op jit(solution)/shard_map/ppermute | solution.py:792
  464.3 21.1 %collective-permute-start.25 = (bf16[2,64,1408]{2,1,0:T(8,128)(2,1)}, bf16[2,64,1408]{2,1,0:T(8,128)(2,1)S(1)}, u32[]{:S(2)}, u32[]{:S(2)}) collective-permute-start(bf16[2,64,1408]{2,1,0:T(8,128)(2,1)} %get-tuple-element.315), channel_id=1, source_target_pairs={{0,8},{4,12},{8,0},{12,4},{16,24},{20,28},{24,16},{28,20},{1,9},{5... | collective-permute-start | bytes 1081352 | tf_op jit(solution)/shard_map/ppermute | solution.py:792
  481.0 6.4 %copy-start.13 = (bf16[2,64,1408]{2,1,0:T(8,128)(2,1)S(1)}, bf16[2,64,1408]{2,1,0:T(8,128)(2,1)}, u32[]{:S(2)}) copy-start(bf16[2,64,1408]{2,1,0:T(8,128)(2,1)} %get-tuple-element.256) | copy-start | bytes 1081348
  481.0 6.5 %copy-start.15 = (bf16[2,64,1024]{2,1,0:T(8,128)(2,1)S(1)}, bf16[2,64,1024]{2,1,0:T(8,128)(2,1)}, u32[]{:S(2)}) copy-start(bf16[2,64,1024]{2,1,0:T(8,128)(2,1)} %get-tuple-element.258) | copy-start | bytes 786436
  482.6 9.6 %collective-permute-start.24 = (bf16[2,64,1408]{2,1,0:T(8,128)(2,1)S(1)}, bf16[2,64,1408]{2,1,0:T(8,128)(2,1)S(1)}, u32[]{:S(2)}, u32[]{:S(2)}) collective-permute-start(bf16[2,64,1408]{2,1,0:T(8,128)(2,1)S(1)} %copy-done.19), channel_id=1, source_target_pairs={{0,8},{4,12},{8,0},{12,4},{16,24},{20,28},{24,16},{28,20},{1,9},{5... | collective-permute-start | bytes 1081352 | tf_op jit(solution)/shard_map/ppermute | solution.py:792
  484.7 38.2 %collective-permute-start.35 = (bf16[512,1024]{1,0:T(8,128)(2,1)}, bf16[512,1024]{1,0:T(8,128)(2,1)}, u32[]{:S(2)}, u32[]{:S(2)}) collective-permute-start(bf16[512,1024]{1,0:T(8,128)(2,1)} %project_back.9), channel_id=1, source_target_pairs={{0,2},{1,3},{2,0},{3,1},{4,6},{5,7},{6,4},{7,5},{8,10},{9,11},{10,... | collective-permute-start | bytes 3145736 | tf_op jit(solution)/shard_map/ppermute | solution.py:68
  485.3 19.4 %collective-permute-start.29 = (bf16[2,2,128,768]{3,2,1,0:T(8,128)(2,1)S(1)}, bf16[2,2,128,768]{3,2,1,0:T(8,128)(2,1)S(1)}, u32[]{:S(2)}, u32[]{:S(2)}) collective-permute-start(bf16[2,2,128,768]{3,2,1,0:T(8,128)(2,1)S(1)} %get-tuple-element.300), channel_id=1, source_target_pairs={{0,4},{4,0},{8,12},{12,8},{16,20},{20,16},{24,28},{28,24},{1,5},{5... | collective-permute-start | bytes 2359304 | tf_op jit(solution)/shard_map/ppermute | solution.py:792
  492.3 14.5 %copy-start.4 = (bf16[1024,1024]{1,0:T(8,128)(2,1)}, bf16[1024,1024]{1,0:T(8,128)(2,1)S(1)}, u32[]{:S(2)}) copy-start(bf16[1024,1024]{1,0:T(8,128)(2,1)S(1)} %collective-permute-done.28.refs_0_) | copy-start | bytes 6291460
  492.3 14.5 %collective-permute-start.33 = (bf16[64,1024]{1,0:T(8,128)(2,1)S(1)}, bf16[64,1024]{1,0:T(8,128)(2,1)S(1)}, u32[]{:S(2)}, u32[]{:S(2)}) collective-permute-start(bf16[64,1024]{1,0:T(8,128)(2,1)S(1)} %get-tuple-element.329), channel_id=1, source_target_pairs={{0,8},{4,12},{8,0},{12,4},{16,24},{20,28},{24,16},{28,20},{1,9},{5... | collective-permute-start | bytes 393224 | tf_op jit(solution)/shard_map/ppermute | solution.py:792
  493.7 13.2 %collective-permute-start.32 = (bf16[64,1408]{1,0:T(8,128)(2,1)S(1)}, bf16[64,1408]{1,0:T(8,128)(2,1)S(1)}, u32[]{:S(2)}, u32[]{:S(2)}) collective-permute-start(bf16[64,1408]{1,0:T(8,128)(2,1)S(1)} %get-tuple-element.323), channel_id=1, source_target_pairs={{0,4},{4,0},{8,12},{12,8},{16,20},{20,16},{24,28},{28,24},{1,5},{5... | collective-permute-start | bytes 540680 | tf_op jit(solution)/shard_map/ppermute | solution.py:792
  495.7 11.2 %collective-permute-start.31 = (bf16[64,1408]{1,0:T(8,128)(2,1)S(1)}, bf16[64,1408]{1,0:T(8,128)(2,1)S(1)}, u32[]{:S(2)}, u32[]{:S(2)}) collective-permute-start(bf16[64,1408]{1,0:T(8,128)(2,1)S(1)} %get-tuple-element.325), channel_id=1, source_target_pairs={{0,16},{4,20},{8,24},{12,28},{16,0},{20,4},{24,8},{28,12},{1,17},{... | collective-permute-start | bytes 540680 | tf_op jit(solution)/shard_map/ppermute | solution.py:792
  504.7 8.4 %collective-permute-start.30 = (bf16[64,1408]{1,0:T(8,128)(2,1)S(1)}, bf16[64,1408]{1,0:T(8,128)(2,1)S(1)}, u32[]{:S(2)}, u32[]{:S(2)}) collective-permute-start(bf16[64,1408]{1,0:T(8,128)(2,1)S(1)} %get-tuple-element.327), channel_id=1, source_target_pairs={{0,16},{4,20},{8,24},{12,28},{16,0},{20,4},{24,8},{28,12},{1,17},{... | collective-permute-start | bytes 540680 | tf_op jit(solution)/shard_map/ppermute | solution.py:792
  513.3 15.7 %collective-permute-start.37 = (bf16[64,5248]{1,0:T(8,128)(2,1)S(1)}, bf16[64,5248]{1,0:T(8,128)(2,1)S(1)}, u32[]{:S(2)}, u32[]{:S(2)}) collective-permute-start(bf16[64,5248]{1,0:T(8,128)(2,1)S(1)} %constant_dynamic-update-slice_fusion), channel_id=1, source_target_pairs={{0,2},{1,3},{2,0},{3,1},{4,6},{5,7},{6,4},{7,5},{8,10},{9,11},{10,... | collective-permute-start | bytes 2015240 | tf_op jit(solution)/shard_map/ppermute | solution.py:68
  515.0 7.8 %collective-permute-start.34 = (bf16[2,128,768]{2,1,0:T(8,128)(2,1)S(1)}, bf16[2,128,768]{2,1,0:T(8,128)(2,1)S(1)}, u32[]{:S(2)}, u32[]{:S(2)}) collective-permute-start(bf16[2,128,768]{2,1,0:T(8,128)(2,1)S(1)} %get-tuple-element.312), channel_id=1, source_target_pairs={{0,8},{4,12},{8,0},{12,4},{16,24},{20,28},{24,16},{28,20},{1,9},{5... | collective-permute-start | bytes 1179656 | tf_op jit(solution)/shard_map/ppermute | solution.py:792
  529.2 2.0 copy-start.23
  529.4 13.8 %copy-start.5 = (bf16[2,64,5248]{2,1,0:T(8,128)(2,1)}, bf16[2,64,5248]{2,1,0:T(8,128)(2,1)S(1)}, u32[]{:S(2)}) copy-start(bf16[2,64,5248]{2,1,0:T(8,128)(2,1)S(1)} %pad_maximum_fusion.2) | copy-start | bytes 4030468
  529.4 17.1 %collective-permute-start.38 = (bf16[128,5248]{1,0:T(8,128)(2,1)S(1)}, bf16[128,5248]{1,0:T(8,128)(2,1)S(1)}, u32[]{:S(2)}, u32[]{:S(2)}) collective-permute-start(bf16[128,5248]{1,0:T(8,128)(2,1)S(1)} %bitcast.140), channel_id=1, source_target_pairs={{0,1},{1,0},{2,3},{3,2},{4,5},{5,4},{6,7},{7,6},{8,9},{9,8},{10,11... | collective-permute-start | bytes 4030472 | tf_op jit(solution)/shard_map/ppermute | solution.py:68
  529.5 13.7 %collective-permute-start.36 = (bf16[128,768]{1,0:T(8,128)(2,1)S(1)}, bf16[128,768]{1,0:T(8,128)(2,1)S(1)}, u32[]{:S(2)}, u32[]{:S(2)}) collective-permute-start(bf16[128,768]{1,0:T(8,128)(2,1)S(1)} %get-tuple-element.322), channel_id=1, source_target_pairs={{0,16},{4,20},{8,24},{12,28},{16,0},{20,4},{24,8},{28,12},{1,17},{... | collective-permute-start | bytes 589832 | tf_op jit(solution)/shard_map/ppermute | solution.py:792
  531.9 13.8 %copy-start.25 = (bf16[128]{0:T(256)(128)(2,1)S(1)}, bf16[128]{0:T(256)(128)(2,1)}, u32[]{:S(2)}) copy-start(bf16[128]{0:T(256)(128)(2,1)} %param.24) | copy-start | bytes 772
  543.9 8.7 %collective-permute-start.39 = (bf16[128,768]{1,0:T(8,128)(2,1)}, bf16[128,768]{1,0:T(8,128)(2,1)}, u32[]{:S(2)}, u32[]{:S(2)}) collective-permute-start(bf16[128,768]{1,0:T(8,128)(2,1)} %add_convert_fusion.10.refs_0_), channel_id=1, source_target_pairs={{0,1},{1,0},{2,3},{3,2},{4,5},{5,4},{6,7},{7,6},{8,9},{9,8},{10,11... | collective-permute-start | bytes 589832 | tf_op jit(solution)/shard_map/ppermute | solution.py:68
  544.1 8.5 %collective-permute-start.40 = (bf16[128,768]{1,0:T(8,128)(2,1)}, bf16[128,768]{1,0:T(8,128)(2,1)}, u32[]{:S(2)}, u32[]{:S(2)}) collective-permute-start(bf16[128,768]{1,0:T(8,128)(2,1)} %add_convert_fusion.10.refs_0_), channel_id=1, source_target_pairs={{0,2},{1,3},{2,0},{3,1},{4,6},{5,7},{6,4},{7,5},{8,10},{9,11},{10,... | collective-permute-start | bytes 589832 | tf_op jit(solution)/shard_map/ppermute | solution.py:68
  544.6 10.6 %collective-permute-start.41 = (bf16[128,768]{1,0:T(8,128)(2,1)}, bf16[128,768]{1,0:T(8,128)(2,1)}, u32[]{:S(2)}, u32[]{:S(2)}) collective-permute-start(bf16[128,768]{1,0:T(8,128)(2,1)} %add_convert_fusion.10.refs_0_), channel_id=1, source_target_pairs={{0,3},{1,2},{2,1},{3,0},{4,7},{5,6},{6,5},{7,4},{8,11},{9,10},{10,... | collective-permute-start | bytes 589832 | tf_op jit(solution)/shard_map/ppermute | solution.py:68
  545.8 12.6 %copy-start.1 = (bf16[2816,128]{1,0:T(8,128)(2,1)S(1)}, bf16[2816,128]{1,0:T(8,128)(2,1)}, u32[]{:S(2)}) copy-start(bf16[2816,128]{1,0:T(8,128)(2,1)} %param.23) | copy-start | bytes 2162692
  (7 other events, 9.8 us)
Sparse Core Ops, SparseCore 0:
  11.8 202.7 all-gather.1
